TPU v7x, 32 devices: a whole 2x2x4 slice. The times are simulated.
32 devices in a mesh: dp: 8 (over z, y), tensor: 4 (over x, core).
Axes of the slice: x: 2, y: 2, z: 4, core: 2. Of those that a mesh axis runs over, the one named last changes fastest.
Arguments:
- block_input: bfloat16 [8192, 1536], P(('dp', 'tensor')), may hold values from -6 to 6
- segment_ids: int32 [8, 1024], P('dp'), may hold values from 0 to 3, as said below
- gain_attn: float32 [1536], replicated, may hold values from 0.5 to 1.5
- w_query: bfloat16 [1536, 1536], P('dp', 'tensor'), may hold values from -0.15625 to 0.15625
- b_query: float32 [1536], P('tensor'), may hold values from -3 to 3
- w_keyval: bfloat16 [1536, 512], P('dp'), may hold values from -0.15625 to 0.15625
- b_keyval: float32 [512], replicated, may hold values from -3 to 3
- w_out: bfloat16 [1536, 1536], P('tensor', 'dp'), may hold values from -0.625 to 0.625
- gain_ffn: float32 [1536], replicated, may hold values from 0.5 to 1.5
- w_gate: bfloat16 [1536, 8960], P('dp', 'tensor'), may hold values from -0.15625 to 0.15625
- w_up: bfloat16 [1536, 8960], P('dp', 'tensor'), may hold values from -0.15625 to 0.15625
- w_down: bfloat16 [8960, 1536], P('tensor', 'dp'), may hold values from -0.0625 to 0.0625
- cotangent: bfloat16 [8192, 1536], P(('dp', 'tensor')), may hold values from -6 to 6
Outputs:
- block_output: bfloat16 [8192, 1536], P(('dp', 'tensor'))
- grad_input: bfloat16 [8192, 1536], P(('dp', 'tensor'))
- grad_gain_attn: float32 [1536], P(('dp', 'tensor'))
- grad_w_query: float32 [1536, 1536], P('dp', 'tensor')
- grad_b_query: float32 [1536], P(('dp', 'tensor'))
- grad_w_keyval: float32 [1536, 512], P(('dp', 'tensor'))
- grad_b_keyval: float32 [512], P(('dp', 'tensor'))
- grad_w_out: float32 [1536, 1536], P('tensor', 'dp')
- grad_gain_ffn: float32 [1536], P(('dp', 'tensor'))
- grad_w_gate: float32 [1536, 8960], P('dp', 'tensor')
- grad_w_up: float32 [1536, 8960], P('dp', 'tensor')
- grad_w_down: float32 [8960, 1536], P('tensor', 'dp')
Inputs may be any that keep to these rules, and one draw needn't show every extreme that they name: `segment_ids`: ids start at 0 and never fall along a sequence, each rising by one at a document's start; a sequence holds 2 to 4 documents, each of 204 tokens or more; some sequence holds 4.
All inputs are finite; a program needn't handle non-finite values.
Results may differ from a plain program's by a relative error of at most 0.018.
Values may be sent and summed in bfloat16 or wider, within the bound.
No kernel may reach another device: no remote copies, remote signals or barrier semaphores. Data moves between devices by JAX's collectives and lax.ppermute only.
A program may use at most 256 MiB of HBM per device.

v0:
```python
import math

import jax
import jax.numpy as jnp
from jax import lax
from jax.sharding import PartitionSpec as P

HQ = 12
KV = 2
HD = 128


epsilon = 1e-06
rope_base = 1000000.0
masked_score = -1e30


def matmul(left, right):
    return jnp.dot(left, right, preferred_element_type=jnp.float32)


def positions_of(segment_row):
    index_row = jnp.arange(segment_row.shape[0], dtype=jnp.int32)
    starts = jnp.concatenate(
        [jnp.ones((1,), jnp.int32), (segment_row[1:] != segment_row[:-1]).astype(jnp.int32)]
    )
    first_index = lax.cummax(jnp.where(starts > 0, index_row, 0), axis=0)
    return index_row - first_index


def allowed_of(segment_row):
    index_row = jnp.arange(segment_row.shape[0], dtype=jnp.int32)
    causal = index_row[:, None] >= index_row[None, :]
    return causal & (segment_row[:, None] == segment_row[None, :])


def rotary(positions):
    inverse = rope_base ** (-(jnp.arange(HD // 2, dtype=jnp.float32) * 2.0 / HD))
    angles = positions.astype(jnp.float32)[:, None] * inverse[None, :]
    angles = jnp.concatenate([angles, angles], axis=1)
    return (jnp.cos(angles), jnp.sin(angles))


def turn(values_in, cosine_table, sine_table):
    half_size = values_in.shape[-1] // 2
    rolled = jnp.concatenate([-values_in[..., half_size:], values_in[..., :half_size]], axis=-1)
    return values_in * cosine_table + rolled * sine_table


def norm_forward(values_in):
    row_scale = lax.rsqrt(jnp.mean(values_in * values_in, axis=-1, keepdims=True) + epsilon)
    return (values_in * row_scale, row_scale)


def norm_backward(grad_out, normed, row_scale, gain_vec):
    grad_normed = grad_out * gain_vec
    grad_in = row_scale * (
        grad_normed - normed * jnp.mean(grad_normed * normed, axis=-1, keepdims=True)
    )
    return (grad_in, jnp.sum(grad_out * normed, axis=0))


def gather_three(first, second, third):
    return (
        lax.all_gather(first, "dp", axis=0, tiled=True),
        lax.all_gather(second, "dp", axis=0, tiled=True),
        lax.all_gather(third, "dp", axis=1, tiled=True),
    )


def masked_scores(query_rot, key_rot, segment_row):
    raw_scores = jnp.einsum(
        "qhd,kd->hqk", query_rot, key_rot, preferred_element_type=jnp.float32
    ) / math.sqrt(HD)
    return jnp.where(allowed_of(segment_row)[None], raw_scores, masked_score)


def attend(query_rot, key_rot, value_rows, segment_row):
    scores = masked_scores(query_rot, key_rot, segment_row)
    row_max = jnp.max(scores, axis=2, keepdims=True)
    log_total = row_max + jnp.log(jnp.sum(jnp.exp(scores - row_max), axis=2, keepdims=True))
    probs_low = jnp.exp(scores - log_total).astype(jnp.bfloat16)
    attn_result = jnp.einsum(
        "hqk,kd->qhd", probs_low, value_rows, preferred_element_type=jnp.float32
    )
    return (attn_result, log_total)


def attend_back(query_rot, key_rot, value_rows, segment_row, log_total, attn_result, grad_context):
    scores = masked_scores(query_rot, key_rot, segment_row)
    attn_probs = jnp.exp(scores - log_total)
    probs_low = attn_probs.astype(jnp.bfloat16)
    grad_probs = jnp.einsum(
        "qhd,kd->hqk", grad_context, value_rows, preferred_element_type=jnp.float32
    )
    row_delta = jnp.sum(grad_context.astype(jnp.float32) * attn_result, axis=2).T[:, :, None]
    grad_scores = (attn_probs * (grad_probs - row_delta)).astype(jnp.bfloat16)
    grad_query_rot = jnp.einsum(
        "hqk,kd->qhd", grad_scores, key_rot, preferred_element_type=jnp.float32
    ) / math.sqrt(HD)
    grad_key_rot = jnp.einsum(
        "hqk,qhd->kd", grad_scores, query_rot, preferred_element_type=jnp.float32
    ) / math.sqrt(HD)
    grad_value = jnp.einsum(
        "hqk,qhd->kd", probs_low, grad_context, preferred_element_type=jnp.float32
    )
    return (grad_query_rot, grad_key_rot, grad_value)


def local(
    block_input,
    segment_ids,
    gain_attn,
    w_query,
    b_query,
    w_keyval,
    b_keyval,
    w_out,
    gain_ffn,
    w_gate,
    w_up,
    w_down,
    cotangent,
):
    tensor_index = lax.axis_index("tensor")
    seq_count = segment_ids.shape[0]
    seq_length = segment_ids.shape[1]
    row_count = seq_count * seq_length
    local_heads = b_query.shape[0] // HD
    head_kv = tensor_index * local_heads // (HQ // KV)
    rows_float = block_input.astype(jnp.float32)
    normed_one, scale_one = norm_forward(rows_float)
    act_one = lax.all_gather(
        (normed_one * gain_attn).astype(jnp.bfloat16), "tensor", axis=0, tiled=True
    )
    query_w, keyval_w, out_w = gather_three(w_query, w_keyval, w_out)
    query_rows = matmul(act_one, query_w) + b_query
    keyval = matmul(act_one, keyval_w) + b_keyval
    key_rows = lax.dynamic_slice_in_dim(keyval, head_kv * HD, HD, 1)
    value_rows = lax.dynamic_slice_in_dim(keyval, KV * HD + head_kv * HD, HD, 1).astype(
        jnp.bfloat16
    )
    positions = jax.vmap(positions_of)(segment_ids).reshape(row_count)
    cosine_table, sine_table = rotary(positions)
    cos_heads = cosine_table[:, None, :]
    sin_heads = sine_table[:, None, :]
    query_rot = turn(query_rows.reshape(row_count, local_heads, HD), cos_heads, sin_heads).astype(
        jnp.bfloat16
    )
    key_rot = turn(key_rows, cosine_table, sine_table).astype(jnp.bfloat16)
    query_seq = query_rot.reshape(seq_count, seq_length, local_heads, HD)
    key_seq = key_rot.reshape(seq_count, seq_length, HD)
    value_seq = value_rows.reshape(seq_count, seq_length, HD)
    attn_result, log_total = lax.map(
        lambda seq_items: attend(*seq_items), (query_seq, key_seq, value_seq, segment_ids)
    )
    context = attn_result.astype(jnp.bfloat16).reshape(row_count, local_heads * HD)
    hidden = rows_float + lax.psum_scatter(
        matmul(context, out_w), "tensor", scatter_dimension=0, tiled=True
    )
    normed_two, scale_two = norm_forward(hidden)
    act_two = lax.all_gather(
        (normed_two * gain_ffn).astype(jnp.bfloat16), "tensor", axis=0, tiled=True
    )
    gate_w, up_w, down_w = gather_three(w_gate, w_up, w_down)
    gate_pre = matmul(act_two, gate_w)
    up_part = matmul(act_two, up_w)
    sigmoid_gate = jax.nn.sigmoid(gate_pre)
    silu_gate = gate_pre * sigmoid_gate
    mixed_rows = (silu_gate * up_part).astype(jnp.bfloat16)
    block_out = (
        hidden
        + lax.psum_scatter(
            matmul(mixed_rows, down_w).astype(jnp.bfloat16),
            "tensor",
            scatter_dimension=0,
            tiled=True,
        ).astype(jnp.float32)
    ).astype(jnp.bfloat16)
    cot_rows = lax.all_gather(cotangent, "tensor", axis=0, tiled=True)
    grad_mixed = matmul(cot_rows, down_w.T)
    grad_gate = (
        grad_mixed * up_part * sigmoid_gate * (1.0 + gate_pre * (1.0 - sigmoid_gate))
    ).astype(jnp.bfloat16)
    grad_up = (grad_mixed * silu_gate).astype(jnp.bfloat16)
    grad_gate_w = matmul(act_two.T, grad_gate)
    grad_up_w = matmul(act_two.T, grad_up)
    grad_down_w = matmul(mixed_rows.T, cot_rows)
    grad_act_two = lax.psum_scatter(
        matmul(grad_gate, gate_w.T) + matmul(grad_up, up_w.T),
        "tensor",
        scatter_dimension=0,
        tiled=True,
    )
    back_two, gain_two = norm_backward(grad_act_two, normed_two, scale_two, gain_ffn)
    grad_hidden = cotangent.astype(jnp.float32) + back_two
    grad_attn = lax.all_gather(grad_hidden.astype(jnp.bfloat16), "tensor", axis=0, tiled=True)
    grad_out_w = matmul(context.T, grad_attn)
    grad_context = (
        matmul(grad_attn, out_w.T)
        .astype(jnp.bfloat16)
        .reshape(seq_count, seq_length, local_heads, HD)
    )
    grad_query_rot, grad_key_rot, grad_value = lax.map(
        lambda seq_items: attend_back(*seq_items),
        (query_seq, key_seq, value_seq, segment_ids, log_total, attn_result, grad_context),
    )
    grad_query = turn(
        grad_query_rot.reshape(row_count, local_heads, HD), cos_heads, -sin_heads
    ).reshape(row_count, local_heads * HD)
    grad_key = turn(grad_key_rot.reshape(row_count, HD), cosine_table, -sine_table)
    grad_value = grad_value.reshape(row_count, HD)
    grad_query_low = grad_query.astype(jnp.bfloat16)
    kv_columns = jnp.zeros((row_count, keyval.shape[1]), jnp.bfloat16)
    kv_columns = lax.dynamic_update_slice_in_dim(
        kv_columns, grad_key.astype(jnp.bfloat16), head_kv * HD, 1
    )
    kv_columns = lax.dynamic_update_slice_in_dim(
        kv_columns, grad_value.astype(jnp.bfloat16), KV * HD + head_kv * HD, 1
    )
    bias_keyval = jnp.zeros((keyval.shape[1],), jnp.float32)
    bias_keyval = lax.dynamic_update_slice_in_dim(
        bias_keyval, jnp.sum(grad_key, axis=0), head_kv * HD, 0
    )
    bias_keyval = lax.dynamic_update_slice_in_dim(
        bias_keyval, jnp.sum(grad_value, axis=0), KV * HD + head_kv * HD, 0
    )
    bias_query = lax.dynamic_update_slice_in_dim(
        jnp.zeros((HQ * HD,), jnp.float32),
        jnp.sum(grad_query, axis=0),
        tensor_index * local_heads * HD,
        0,
    )
    grad_query_w = matmul(act_one.T, grad_query_low)
    grad_keyval_w = matmul(act_one.T, kv_columns)
    grad_act_one = lax.psum_scatter(
        (matmul(grad_query_low, query_w.T) + matmul(kv_columns, keyval_w.T)).astype(jnp.bfloat16),
        "tensor",
        scatter_dimension=0,
        tiled=True,
    ).astype(jnp.float32)
    back_one, gain_one = norm_backward(grad_act_one, normed_one, scale_one, gain_attn)
    grad_rows = (grad_hidden + back_one).astype(jnp.bfloat16)
    keyval_share, gain_one_share, gain_two_share, query_bias_share, keyval_bias_share = (
        lax.psum_scatter(grad_keyval_w, ("dp", "tensor"), scatter_dimension=0, tiled=True),
        lax.psum_scatter(gain_one, ("dp", "tensor"), scatter_dimension=0, tiled=True),
        lax.psum_scatter(gain_two, ("dp", "tensor"), scatter_dimension=0, tiled=True),
        lax.psum_scatter(bias_query, ("dp", "tensor"), scatter_dimension=0, tiled=True),
        lax.psum_scatter(bias_keyval, ("dp", "tensor"), scatter_dimension=0, tiled=True),
    )
    query_share, out_share, gate_share, up_share, down_share = (
        lax.psum_scatter(
            grad_query_w.astype(jnp.bfloat16), "dp", scatter_dimension=0, tiled=True
        ).astype(jnp.float32),
        lax.psum_scatter(
            grad_out_w.astype(jnp.bfloat16), "dp", scatter_dimension=1, tiled=True
        ).astype(jnp.float32),
        lax.psum_scatter(
            grad_gate_w.astype(jnp.bfloat16), "dp", scatter_dimension=0, tiled=True
        ).astype(jnp.float32),
        lax.psum_scatter(
            grad_up_w.astype(jnp.bfloat16), "dp", scatter_dimension=0, tiled=True
        ).astype(jnp.float32),
        lax.psum_scatter(
            grad_down_w.astype(jnp.bfloat16), "dp", scatter_dimension=1, tiled=True
        ).astype(jnp.float32),
    )
    return (
        block_out,
        grad_rows,
        gain_one_share,
        query_share,
        query_bias_share,
        keyval_share,
        keyval_bias_share,
        out_share,
        gain_two_share,
        gate_share,
        up_share,
        down_share,
    )


def solution(mesh):
    placed = (
        P(("dp", "tensor"), None),
        P("dp", None),
        P(),
        P("dp", "tensor"),
        P("tensor"),
        P("dp", None),
        P(),
        P("tensor", "dp"),
        P(),
        P("dp", "tensor"),
        P("dp", "tensor"),
        P("tensor", "dp"),
        P(("dp", "tensor"), None),
    )
    return jax.shard_map(
        local,
        mesh=mesh,
        in_specs=placed,
        out_specs=(
            P(("dp", "tensor"), None),
            P(("dp", "tensor"), None),
            P(("dp", "tensor")),
            P("dp", "tensor"),
            P(("dp", "tensor")),
            P(("dp", "tensor"), None),
            P(("dp", "tensor")),
            P("tensor", "dp"),
            P(("dp", "tensor")),
            P("dp", "tensor"),
            P("dp", "tensor"),
            P("tensor", "dp"),
        ),
        check_vma=False,
    )
```

profile of v0, /device:TPU:0, one launch (start us, length us, event | category | flops | bytes accessed | tf_op | source)
XLA Modules:
  0.0 1481.8 jit_solution(15097303568250098657)
XLA Ops:
  8.0 1.4 fusion.17
  9.4 2.3 fusion.14
  14.6 39.4 %all-gather.15.cloned.1.call-done = bf16[1536,384]{1,0:T(8,128)(2,1)} async-done(((bf16[192,384]{1,0:T(8,128)(2,1)}), bf16[1536,384]{1,0:T(8,128)(2,1)}) %all-gather.15.cloned.1.call-update) | async-done | bytes 1179664 | tf_op jit(solution)/shard_map/all_gather | solution.py:65
  54.0 29.5 %all-gather.11.cloned.1.call-done = bf16[1024,1536]{1,0:T(8,128)(2,1)} async-done(((bf16[256,1536]{1,0:T(8,128)(2,1)}), bf16[1024,1536]{1,0:T(8,128)(2,1)}) %all-gather.11.cloned.1.call-update) | async-done | bytes 3145744 | tf_op jit(solution)/shard_map/all_gather | solution.py:133
  83.5 3.6 convolution_add_fusion.2
  87.1 1.0 slice_negate_fusion.1
  88.2 41.7 %all-gather.13.cloned.1.call-done = bf16[1536,512]{1,0:T(8,128)(2,1)} async-done(((bf16[192,512]{1,0:T(8,128)(2,1)}), bf16[1536,512]{1,0:T(8,128)(2,1)}) %all-gather.13.cloned.1.call-update) | async-done | bytes 1572880 | tf_op jit(solution)/shard_map/all_gather | solution.py:66
  129.9 4.2 convolution_add_fusion.1
  134.9 3.2 broadcast_multiply_fusion
  138.6 6.0 fusion.4
  144.6 7.3 exponential_reduce_fusion
  152.0 9.5 bitcast_convert_fusion
  161.5 10.3 all-gather.17.cloned.1.call-done
  171.8 5.7 fusion.46
  178.2 56.6 %reduce-scatter.11.cloned.1.call-done = f32[256,1536]{1,0:T(8,128)} async-done(((f32[1024,1536]{1,0:T(8,128)}), f32[256,1536]{1,0:T(8,128)}) %reduce-scatter.11.cloned.1.call-update) | async-done | bytes 1572880 | tf_op jit(solution)/shard_map/reduce_scatter | solution.py:158
  234.8 1.7 multiply_reduce_fusion.2
  236.6 1.1 multiply_convert_fusion.3
  239.8 106.2 %all-gather.21.cloned.1.call-done = bf16[1536,2240]{1,0:T(8,128)(2,1)} async-done(((bf16[192,2240]{1,0:T(8,128)(2,1)}), bf16[1536,2240]{1,0:T(8,128)(2,1)}) %all-gather.21.cloned.1.call-update) | async-done | bytes 6881296 | tf_op jit(solution)/shard_map/all_gather | solution.py:65
  346.0 29.0 %all-gather.19.cloned.1.call-done = bf16[1024,1536]{1,0:T(8,128)(2,1)} async-done(((bf16[256,1536]{1,0:T(8,128)(2,1)}), bf16[1024,1536]{1,0:T(8,128)(2,1)}) %all-gather.19.cloned.1.call-update) | async-done | bytes 3145744 | tf_op jit(solution)/shard_map/all_gather | solution.py:162
  374.9 13.7 fusion.47
  388.6 97.5 %all-gather.23.cloned.1.call-done = bf16[1536,2240]{1,0:T(8,128)(2,1)} async-done(((bf16[192,2240]{1,0:T(8,128)(2,1)}), bf16[1536,2240]{1,0:T(8,128)(2,1)}) %all-gather.23.cloned.1.call-update) | async-done | bytes 6881296 | tf_op jit(solution)/shard_map/all_gather | solution.py:66
  486.2 13.2 fusion.48
  499.4 15.2 %all-gather.27.cloned.1.call-done = bf16[1024,1536]{1,0:T(8,128)(2,1)} async-done(((bf16[256,1536]{1,0:T(8,128)(2,1)}), bf16[1024,1536]{1,0:T(8,128)(2,1)}) %all-gather.27.cloned.1.call-update) | async-done | bytes 3145744 | tf_op jit(solution)/shard_map/all_gather | solution.py:180
  514.6 111.1 %all-gather.25.cloned.1.call-done = bf16[2240,1536]{0,1:T(8,128)(2,1)} async-done(((bf16[2240,192]{0,1:T(8,128)(2,1)}), bf16[2240,1536]{0,1:T(8,128)(2,1)}) %all-gather.25.cloned.1.call-update) | async-done | bytes 6881296 | tf_op jit(solution)/shard_map/all_gather | solution.py:67
  625.7 20.1 %multiply_convert_fusion = (bf16[1024,2240]{0,1:T(8,128)(2,1)}, bf16[1024,2240]{0,1:T(8,128)(2,1)}, bf16[1024,2240]{0,1:T(8,128)(2,1)}) fusion(f32[1024,2240]{0,1:T(8,128)} %fusion.47, f32[1024,2240]{0,1:T(8,128)} %fusion.48, bf16[1024,1536]{1,0:T(8,128)(2,1)} %all-gather.27.cloned.1.call-done, bf16[2240,1536]{0,1:T(8,128)(2,1)} %all-gather.25.cloned.1.call-done), kind=kOutput, calls=%fused_computation.10 | convolution fusion | flops 7080837120 | bytes 42139648 | tf_op jit(solution)/shard_map/dot_general | solution.py:19
  645.8 11.4 fusion.49
  657.2 9.9 convolution_add_fusion
  667.2 56.6 %reduce-scatter.15.cloned.1.call-done = f32[256,1536]{1,0:T(8,128)} async-done(((f32[1024,1536]{1,0:T(8,128)}), f32[256,1536]{1,0:T(8,128)}) %reduce-scatter.15.cloned.1.call-update) | async-done | bytes 1572880 | tf_op jit(solution)/shard_map/reduce_scatter | solution.py:189
  723.9 2.0 multiply_reduce_fusion
  725.9 1.4 fusion.42
  727.3 12.3 convolution_convert_fusion.2
  739.7 12.8 convolution_convert_fusion.1
  752.6 12.4 convolution_convert_fusion
  765.1 4.4 convolution_convert_fusion.6
  770.4 2.9 convolution_convert_fusion.4
  773.5 9.4 fusion.1
  782.9 1.1 bitcast_multiply_fusion
  784.0 1.6 copy-done.4
  788.0 2.9 convolution_convert_fusion.5
  791.2 9.1 fusion.45
  800.2 1.1 copy.51
  801.3 5.2 fusion.22
  806.7 2.3 fusion.43
  809.1 1.0 copy-done.16
  810.1 1.8 fusion.50
  812.0 3.6 add_convert_fusion
  816.0 12.5 convolution_convert_fusion.3
  828.6 1.1 copy-done.17
  829.7 5.4 fusion.51
  835.1 53.6 %reduce-scatter.25.cloned.1.call-done = bf16[192,2240]{1,0:T(8,128)(2,1)} async-done(((bf16[1536,2240]{1,0:T(8,128)(2,1)}), bf16[192,2240]{1,0:T(8,128)(2,1)}) %reduce-scatter.25.cloned.1.call-update) | async-done | bytes 860176 | tf_op jit(solution)/shard_map/reduce_scatter | solution.py:258
  888.7 2.5 convert_element_type.154
  891.2 129.6 %reduce-scatter.27.cloned.1.call-done = bf16[192,2240]{1,0:T(8,128)(2,1)} async-done(((bf16[1536,2240]{1,0:T(8,128)(2,1)}), bf16[192,2240]{1,0:T(8,128)(2,1)}) %reduce-scatter.27.cloned.1.call-update) | async-done | bytes 860176 | tf_op jit(solution)/shard_map/reduce_scatter | solution.py:261
  1020.8 2.5 convert_element_type.156
  1023.3 129.1 %reduce-scatter.29.cloned.1.call-done = bf16[2240,192]{0,1:T(8,128)(2,1)} async-done(((bf16[2240,1536]{0,1:T(8,128)(2,1)}), bf16[2240,192]{0,1:T(8,128)(2,1)}) %reduce-scatter.29.cloned.1.call-update) | async-done | bytes 860176 | tf_op jit(solution)/shard_map/reduce_scatter | solution.py:264
  1152.4 2.5 convert_element_type.158
  1155.4 63.8 %reduce-scatter.23.cloned.1.call-done = bf16[384,192]{0,1:T(8,128)(2,1)} async-done(((bf16[384,1536]{0,1:T(8,128)(2,1)}), bf16[384,192]{0,1:T(8,128)(2,1)}) %reduce-scatter.23.cloned.1.call-update) | async-done | bytes 147472 | tf_op jit(solution)/shard_map/reduce_scatter | solution.py:255
  1219.1 1.6 convert_element_type.152
  1220.8 65.0 %reduce-scatter.19.cloned.1.call-done = bf16[192,384]{1,0:T(8,128)(2,1)} async-done(((bf16[1536,384]{1,0:T(8,128)(2,1)}), bf16[192,384]{1,0:T(8,128)(2,1)}) %reduce-scatter.19.cloned.1.call-update) | async-done | bytes 147472 | tf_op jit(solution)/shard_map/reduce_scatter | solution.py:252
  1285.8 1.6 convert_element_type.150
  1287.5 37.9 %reduce-scatter.17.cloned.1.call-done = bf16[256,1536]{1,0:T(8,128)(2,1)} async-done(((bf16[1024,1536]{1,0:T(8,128)(2,1)}), bf16[256,1536]{1,0:T(8,128)(2,1)}) %reduce-scatter.17.cloned.1.call-update) | async-done | bytes 786448 | tf_op jit(solution)/shard_map/reduce_scatter | solution.py:236
  1325.4 1.8 fusion.16
  1327.2 39.9 %all-reduce.4 = (f32[1536]{0:T(1024)S(1)}, f32[1536]{0:T(1024)S(1)}, f32[512]{0:T(512)S(1)}, f32[1536]{0:T(1024)S(1)}) all-reduce(f32[1536]{0:T(1024)S(1)} %get-tuple-element.57, f32[1536]{0:T(1024)S(1)} %bitcast_dynamic-update-slice_fusion, ...), channel_id=6, replica_groups=mesh['dp'=8,'tensor'=4] {'dp','tensor'}, use_global_device_ids=true, to_apply=%region_14.15.clone | all-reduce | flops 5120 | bytes 40960
  1369.4 3.8 fusion.13
  1373.2 101.5 %reduce-scatter.21.cloned.1.call-done = f32[48,512]{1,0:T(8,128)} async-done(((f32[1536,512]{1,0:T(8,128)}), f32[48,512]{1,0:T(8,128)}) %reduce-scatter.21.cloned.1.call-update) | async-done | bytes 98320 | tf_op jit(solution)/shard_map/reduce_scatter | solution.py:245
  (143 shorter events, 15.3 us)
Async XLA Ops:
  7.2 5.9 copy-start.25
  7.2 76.3 %copy-start.32 = (f32[384]{0:T(512)S(1)}, f32[384]{0:T(512)}, u32[]{:S(2)}) copy-start(f32[384]{0:T(512)} %param.17) | copy-start | bytes 4612
  7.2 46.8 %all-gather.15.cloned.1.call-start = ((), (), s32[]{:S(2)}) async-start(), calls=%async_computation.12 | async-start | bytes 1327104 | tf_op jit(solution)/shard_map/all_gather | solution.py:65
  7.9 75.5 %all-gather.11.cloned.1.call-start = ((), (), s32[]{:S(2)}) async-start(), calls=%async_computation.10 | async-start | bytes 3932160 | tf_op jit(solution)/shard_map/all_gather | solution.py:133
  9.4 3.7 copy-start.26
  11.7 118.2 %all-gather.13.cloned.1.call-start = ((), (), s32[]{:S(2)}) async-start(), calls=%async_computation.11 | async-start | bytes 1769472 | tf_op jit(solution)/shard_map/all_gather | solution.py:66
  12.4 159.4 %all-gather.17.cloned.1.call-start = ((), (), s32[]{:S(2)}) async-start(), calls=%async_computation.13 | async-start | bytes 1327104 | tf_op jit(solution)/shard_map/all_gather | solution.py:67
  13.0 221.9 %reduce-scatter.11.cloned.1.call-start = ((), (), s32[]{:S(2)}) async-start(), calls=%async_computation.14 | async-start | bytes 7864320 | tf_op jit(solution)/shard_map/reduce_scatter | solution.py:158
  87.1 42.8 %copy-start.33 = (f32[512]{0:T(512)S(1)}, f32[512]{0:T(512)}, u32[]{:S(2)}) copy-start(f32[512]{0:T(512)} %param.19) | copy-start | bytes 6148
  134.1 17.9 %copy-start.22 = (f32[1024,512]{0,1:T(8,128)}, f32[1024,512]{0,1:T(8,128)S(1)}, u32[]{:S(2)}) copy-start(f32[1024,512]{0,1:T(8,128)S(1)} %convolution_add_fusion.1) | copy-start | bytes 6291460
  134.1 4.0 copy-start.7
  134.2 0.7 copy-start.8
  138.1 6.5 copy-start.18
  138.6 6.0 copy-start.20
  161.5 16.0 %copy-start.13 = (bf16[1024,3,128]{0,2,1:T(8,128)(2,1)}, bf16[1024,3,128]{0,2,1:T(8,128)(2,1)S(1)}, u32[]{:S(2)}) copy-start(bf16[1024,3,128]{0,2,1:T(8,128)(2,1)S(1)} %get-tuple-element.102) | copy-start | bytes 2359300
  177.5 57.3 %copy-start = (bf16[256,1536]{1,0:T(8,128)(2,1)S(1)}, bf16[256,1536]{1,0:T(8,128)(2,1)}, u32[]{:S(2)}) copy-start(bf16[256,1536]{1,0:T(8,128)(2,1)} %param.13) | copy-start | bytes 2359300
  177.6 59.0 %copy-start.23 = (f32[1536]{0:T(1024)S(1)}, f32[1536]{0:T(1024)}, u32[]{:S(2)}) copy-start(f32[1536]{0:T(1024)} %param.21) | copy-start | bytes 18436
  177.6 168.4 %all-gather.21.cloned.1.call-start = ((), (), s32[]{:S(2)}) async-start(), calls=%async_computation.16 | async-start | bytes 7962624 | tf_op jit(solution)/shard_map/all_gather | solution.py:65
  178.2 196.8 %all-gather.19.cloned.1.call-start = ((), (), s32[]{:S(2)}) async-start(), calls=%async_computation.15 | async-start | bytes 3932160 | tf_op jit(solution)/shard_map/all_gather | solution.py:162
  237.7 248.5 %all-gather.23.cloned.1.call-start = ((), (), s32[]{:S(2)}) async-start(), calls=%async_computation.17 | async-start | bytes 7962624 | tf_op jit(solution)/shard_map/all_gather | solution.py:66
  238.4 276.1 %all-gather.27.cloned.1.call-start = ((), (), s32[]{:S(2)}) async-start(), calls=%async_computation.20 | async-start | bytes 3932160 | tf_op jit(solution)/shard_map/all_gather | solution.py:180
  239.1 386.5 %all-gather.25.cloned.1.call-start = ((), (), s32[]{:S(2)}) async-start(), calls=%async_computation.18 | async-start | bytes 7962624 | tf_op jit(solution)/shard_map/all_gather | solution.py:67
  239.7 484.1 %reduce-scatter.15.cloned.1.call-start = ((), (), s32[]{:S(2)}) async-start(), calls=%async_computation.21 | async-start | bytes 7864320 | tf_op jit(solution)/shard_map/reduce_scatter | solution.py:189
  645.8 11.4 copy-start.28
  645.8 11.4 copy-start.34
  667.1 58.7 %copy-start.3 = (bf16[256,1536]{1,0:T(8,128)(2,1)S(1)}, bf16[256,1536]{1,0:T(8,128)(2,1)}, u32[]{:S(2)}) copy-start(bf16[256,1536]{1,0:T(8,128)(2,1)} %param.25) | copy-start | bytes 2359300
  667.2 97.9 %all-gather.29.cloned.1.call-start = ((), (), s32[]{:S(2)}) async-start(), calls=%async_computation.22 | async-start | bytes 3932160 | tf_op jit(solution)/shard_map/all_gather | solution.py:197
  723.9 2.0 copy-start.2
  727.3 161.4 %reduce-scatter.25.cloned.1.call-start = ((), (), s32[]{:S(2)}) async-start(), calls=%async_computation.27 | async-start | bytes 7962624 | tf_op jit(solution)/shard_map/reduce_scatter | solution.py:258
  739.7 281.1 %reduce-scatter.27.cloned.1.call-start = ((), (), s32[]{:S(2)}) async-start(), calls=%async_computation.28 | async-start | bytes 7962624 | tf_op jit(solution)/shard_map/reduce_scatter | solution.py:261
  752.6 399.8 %reduce-scatter.29.cloned.1.call-start = ((), (), s32[]{:S(2)}) async-start(), calls=%async_computation.29 | async-start | bytes 7962624 | tf_op jit(solution)/shard_map/reduce_scatter | solution.py:264
  765.0 454.2 %reduce-scatter.23.cloned.1.call-start = ((), (), s32[]{:S(2)}) async-start(), calls=%async_computation.26 | async-start | bytes 1327104 | tf_op jit(solution)/shard_map/reduce_scatter | solution.py:255
  765.1 4.4 copy-start.12
  765.1 5.3 copy-start.14
  765.1 5.3 copy-start.30
  769.5 0.9 copy-start.21
  773.3 512.5 %reduce-scatter.19.cloned.1.call-start = ((), (), s32[]{:S(2)}) async-start(), calls=%async_computation.24 | async-start | bytes 1327104 | tf_op jit(solution)/shard_map/reduce_scatter | solution.py:252
  773.5 9.4 copy-start.19
  782.9 2.7 copy-start.4
  785.5 1.0 copy-start.10
  785.5 1.2 copy-start.11
  785.7 2.3 copy-start.29
  787.1 0.9 copy-start.5
  790.9 534.5 %reduce-scatter.17.cloned.1.call-start = ((), (), s32[]{:S(2)}) async-start(), calls=%async_computation.23 | async-start | bytes 3932160 | tf_op jit(solution)/shard_map/reduce_scatter | solution.py:236
  801.3 5.3 copy-start.9
  806.6 3.5 copy-start.31
  809.1 1.0 copy-start.16
  810.1 1.9 copy-start.6
  810.1 1.9 copy-start.15
  815.7 553.8 %reduce-scatter.13.cloned.1.call-start = ((), (), s32[]{:S(2)}) async-start(), calls=%async_computation.19 | async-start | bytes 3932160 | tf_op jit(solution)/shard_map/reduce_scatter | solution.py:173
  828.5 1.2 copy-start.17
  828.5 646.2 %reduce-scatter.21.cloned.1.call-start = ((), (), s32[]{:S(2)}) async-start(), calls=%async_computation.25 | async-start | bytes 3244032 | tf_op jit(solution)/shard_map/reduce_scatter | solution.py:245
  891.2 434.2 %copy-start.1 = (bf16[256,1536]{1,0:T(8,128)(2,1)S(1)}, bf16[256,1536]{1,0:T(8,128)(2,1)}, u32[]{:S(2)}) copy-start(bf16[256,1536]{1,0:T(8,128)(2,1)} %param.13) | copy-start | bytes 2359300
  891.2 434.2 %copy-start.24 = (f32[1536]{0:T(1024)S(1)}, f32[1536]{0:T(1024)}, u32[]{:S(2)}) copy-start(f32[1536]{0:T(1024)} %param.15) | copy-start | bytes 18436
  891.2 434.2 %copy-start.27 = (f32[256]{0:T(256)S(1)}, f32[256]{0:T(256)}, u32[]{:S(2)}) copy-start(f32[256]{0:T(256)} %copy-done.26) | copy-start | bytes 3076
Sparse Core Ops, SparseCore 0:
  10.2 43.7 all-gather.14
  56.1 27.2 all-gather.10
  85.7 44.1 all-gather.12
  131.9 39.8 all-gather.16
  177.7 57.1 reduce-scatter.10
  237.1 108.7 all-gather.20
  348.2 26.7 all-gather.18
  377.3 108.7 all-gather.22
  487.8 26.7 all-gather.26
  516.8 108.7 all-gather.24
  667.3 56.5 reduce-scatter.14
  727.4 28.5 all-gather.28
  759.7 129.0 reduce-scatter.24
  892.7 128.0 reduce-scatter.26
  1024.3 128.0 reduce-scatter.28
  1156.0 63.0 reduce-scatter.22
  1222.8 62.9 reduce-scatter.18
  1288.4 36.9 reduce-scatter.16
  1327.9 38.3 reduce-scatter.12
  1373.0 101.6 reduce-scatter.20
where the time goes:
time: 1490 us; the launch traced here: 1480 us
  waiting for transfers between devices  1180 us (79%)
  matrix products  193 us (13%)
  other arithmetic  42.7 us (3%)
  blocking collectives  39.9 us (3%)
  between operations  15.1 us (1%)
    dot_general x18, matrix products, matmul(): return jnp.dot(left, right, preferred_element_type=jnp.float32)  153 us
    all_gather x2, waiting for transfers between devices, gather_three(): lax.all_gather(first, 'dp', axis=0, tiled=True)  146 us
    all_gather x2, waiting for transfers between devices, gather_three(): lax.all_gather(second, 'dp', axis=0, tiled=True)  139 us
    reduce_scatter x1, waiting for transfers between devices, local(): lax.psum_scatter(grad_up_w.astype(jnp.bfloat16), 'dp', scatter_dimension=...  130 us
    reduce_scatter x1, waiting for transfers between devices, local(): lax.psum_scatter(grad_down_w.astype(jnp.bfloat16), 'dp', scatter_dimensio...  129 us
    all_gather x2, waiting for transfers between devices, gather_three(): lax.all_gather(third, 'dp', axis=1, tiled=True)  121 us
    reduce_scatter x1, waiting for transfers between devices, local(): lax.psum_scatter(grad_keyval_w, ('dp', 'tensor'), scatter_dimension=0, ti...  101 us
    reduce_scatter x1, waiting for transfers between devices, local(): lax.psum_scatter(grad_query_w.astype(jnp.bfloat16), 'dp', scatter_dimensi...  65 us
  transfers between devices with their start and end apart: 20, of which 18 were waited for; matrix products, arithmetic and copies ran while one was open for 13% of the time, Pallas kernels for 0%

commit v1 on v0

v1 whole, which is shorter than its diff:
```python
import math

import jax
import jax.numpy as jnp
from jax import lax
from jax.sharding import PartitionSpec as P

HQ = 12
KV = 2
HD = 128


epsilon = 1e-06
rope_base = 1000000.0
masked_score = -1e30
bf16 = jnp.bfloat16
f32 = jnp.float32


def dot(left, right, left_dim, right_dim, out=f32):
    return lax.dot_general(
        left, right, (((left_dim,), (right_dim,)), ((), ())), preferred_element_type=f32
    ).astype(out)


def positions_of(segment_row):
    index_row = jnp.arange(segment_row.shape[0], dtype=jnp.int32)
    starts = jnp.concatenate(
        [jnp.ones((1,), jnp.int32), (segment_row[1:] != segment_row[:-1]).astype(jnp.int32)]
    )
    first_index = lax.cummax(jnp.where(starts > 0, index_row, 0), axis=0)
    return index_row - first_index


def allowed_of(segment_row):
    index_row = jnp.arange(segment_row.shape[0], dtype=jnp.int32)
    causal = index_row[:, None] >= index_row[None, :]
    return causal & (segment_row[:, None] == segment_row[None, :])


def rotary(positions):
    inverse = rope_base ** (-(jnp.arange(HD // 2, dtype=jnp.float32) * 2.0 / HD))
    angles = positions.astype(jnp.float32)[:, None] * inverse[None, :]
    angles = jnp.concatenate([angles, angles], axis=1)
    return (jnp.cos(angles), jnp.sin(angles))


def turn(values_in, cosine_table, sine_table):
    half_size = values_in.shape[-1] // 2
    rolled = jnp.concatenate([-values_in[..., half_size:], values_in[..., :half_size]], axis=-1)
    return values_in * cosine_table + rolled * sine_table


def norm_forward(values_in):
    row_scale = lax.rsqrt(jnp.mean(values_in * values_in, axis=-1, keepdims=True) + epsilon)
    return (values_in * row_scale, row_scale)


def norm_backward(grad_out, normed, row_scale, gain_vec):
    grad_normed = grad_out * gain_vec
    grad_in = row_scale * (
        grad_normed - normed * jnp.mean(grad_normed * normed, axis=-1, keepdims=True)
    )
    return (grad_in, jnp.sum(grad_out * normed, axis=0))


def twist(array, axis, index, codes, bits, back=False):
    count = len(codes)
    blocks = jnp.split(array, count, axis=axis)
    if not back:
        blocks = [blocks[code] for code in codes]
    place = {code: at for at, code in enumerate(codes)}
    bit = 1
    while bit < 2 * count:
        if bits & bit:
            flag = (index & bit) != 0
            blocks = [
                jnp.where(flag, blocks[place[code ^ bit]], blocks[at])
                for at, code in enumerate(codes)
            ]
        bit *= 2
    if back:
        blocks = [blocks[place[at]] for at in range(count)]
    return jnp.concatenate(blocks, axis=axis)


def solution(mesh):
    dp_size = mesh.shape["dp"]
    tensor_size = mesh.shape["tensor"]
    pair_bit = 2
    dp_bits = []
    bit = dp_size // 2
    while bit:
        dp_bits.append(bit)
        bit //= 2
    ring_bits = [bit for bit in dp_bits if bit != pair_bit]
    ring_mask = sum(ring_bits)

    def swap(array, axis, bit):
        size = mesh.shape[axis]
        return lax.ppermute(array, axis, [(i, i ^ bit) for i in range(size)])

    def masks_of(bits):
        masks = [0]
        for bit in bits:
            masks = masks + [mask ^ bit for mask in masks]
        return masks

    def gather_rows(piece, bits):
        pieces = [piece]
        for bit in bits:
            if len(pieces) <= 4:
                pieces = pieces + [swap(part, "dp", bit) for part in pieces]
            else:
                joined = swap(jnp.concatenate(pieces, axis=0), "dp", bit)
                pieces = pieces + jnp.split(joined, len(pieces), axis=0)
        return jnp.concatenate(pieces, axis=0)

    def scatter_rows(total, bits):
        for bit in reversed(bits):
            half = total.shape[0] // 2
            arrived = swap(total[half:].astype(bf16), "dp", bit)
            total = total[:half].astype(f32) + arrived.astype(f32)
        return total

    token_codes = [0, 2, 1, 3]

    def gather_four(rows):
        pair = jnp.concatenate([rows, swap(rows, "tensor", 2)], axis=0)
        return jnp.concatenate([pair, swap(pair, "tensor", 1)], axis=0)

    def scatter_four(partial):
        half = partial.shape[0] // 2
        arrived = swap(partial[half:], "tensor", 1)
        pair = partial[:half].astype(f32) + arrived.astype(f32)
        half = half // 2
        arrived = swap(pair[half:].astype(bf16), "tensor", 2)
        return pair[:half] + arrived.astype(f32)

    def gather_eight(rows):
        half = rows.shape[0] // 2
        over_x = swap(rows, "tensor", 2)
        over_pair = swap(rows, "dp", pair_bit)
        far_a = swap(over_pair[:half], "tensor", 2)
        far_b = swap(over_x[half:], "dp", pair_bit)
        four = jnp.concatenate([rows, over_x, over_pair, far_a, far_b], axis=0)
        return jnp.concatenate([four, swap(four, "tensor", 1)], axis=0)

    def scatter_eight(partial):
        rows = partial.shape[0] // 8
        half = rows // 2
        arrived = swap(partial[4 * rows :], "tensor", 1)
        four = partial[: 4 * rows].astype(f32) + arrived.astype(f32)
        own, to_x, to_pair, far = jnp.split(four, 4, axis=0)
        far_low = far.astype(bf16)
        far_x = swap(far_low[:half], "tensor", 2)
        far_pair = swap(far_low[half:], "dp", pair_bit)
        to_pair = jnp.concatenate([to_pair[:half] + far_x.astype(f32), to_pair[half:]], axis=0)
        to_x = jnp.concatenate([to_x[:half], to_x[half:] + far_pair.astype(f32)], axis=0)
        from_x = swap(to_x.astype(bf16), "tensor", 2)
        from_pair = swap(to_pair.astype(bf16), "dp", pair_bit)
        return own + from_x.astype(f32) + from_pair.astype(f32)

    def local(
        block_input,
        segment_ids,
        gain_attn,
        w_query,
        b_query,
        w_keyval,
        b_keyval,
        w_out,
        gain_ffn,
        w_gate,
        w_up,
        w_down,
        cotangent,
    ):
        dp_index = lax.axis_index("dp")
        tensor_index = lax.axis_index("tensor")
        seq_length = segment_ids.shape[1]
        local_heads = b_query.shape[0] // HD
        head_kv = tensor_index * local_heads // (HQ // KV)
        is_value = tensor_index % 2
        kv_column = is_value * (KV * HD) + head_kv * HD
        width = local_heads * HD
        all_masks = masks_of(dp_bits)
        ring_codes = [mask | low for mask in masks_of(ring_bits) for low in (0, pair_bit)]

        def twist_all(array, back=False):
            return twist(array, 1, dp_index, all_masks, dp_size - 1, back)

        def twist_ring(array, back=False):
            return twist(array, 1, dp_index, ring_codes, ring_mask, back)

        def token_order(array, back=False):
            return twist(array, 0, tensor_index, token_codes, 3, back)

        keyval_cols = lax.dynamic_slice_in_dim(w_keyval, kv_column, HD, 1)
        qkv_w = gather_rows(jnp.concatenate([w_query, keyval_cols], axis=1), dp_bits)
        out_wt = gather_rows(w_out.T, dp_bits)

        pair_flag = (dp_index & pair_bit) != 0

        def ffn_rows(shard):
            half = shard.shape[1] // 2
            low, high = shard[:, :half], shard[:, half:]
            mine = jnp.where(pair_flag, high, low)
            theirs = swap(jnp.where(pair_flag, low, high), "dp", pair_bit)
            piece = jnp.concatenate(
                [jnp.where(pair_flag, theirs, mine), jnp.where(pair_flag, mine, theirs)], axis=0
            )
            return gather_rows(piece, ring_bits)

        gate_w = ffn_rows(w_gate)
        up_w = ffn_rows(w_up)
        down_wt = ffn_rows(w_down.T)

        rows_float = block_input.astype(f32)
        normed_one, scale_one = norm_forward(rows_float)
        act_one = gather_four(twist_all((normed_one * gain_attn).astype(bf16)))
        qkv_bias = jnp.concatenate([b_query, lax.dynamic_slice_in_dim(b_keyval, kv_column, HD, 0)])
        qkv = token_order(dot(act_one, qkv_w, 1, 0) + qkv_bias, back=True)
        cosine_table, sine_table = rotary(positions_of(segment_ids[0]))
        cos_heads = cosine_table[:, None, :]
        sin_heads = sine_table[:, None, :]
        query_rot = turn(
            qkv[:, :width].reshape(seq_length, local_heads, HD), cos_heads, sin_heads
        ).astype(bf16)
        kv_part = qkv[:, width:]
        kv_own = jnp.where(is_value == 1, kv_part, turn(kv_part, cosine_table, sine_table)).astype(
            bf16
        )
        kv_other = swap(kv_own, "tensor", 1)
        key_rot = jnp.where(is_value == 1, kv_other, kv_own)
        value_rows = jnp.where(is_value == 1, kv_own, kv_other)

        allowed = allowed_of(segment_ids[0])[None]
        raw_scores = jnp.einsum(
            "qhd,kd->hqk", query_rot, key_rot, preferred_element_type=f32
        ) / math.sqrt(HD)
        scores = jnp.where(allowed, raw_scores, masked_score)
        row_max = jnp.max(scores, axis=2, keepdims=True)
        log_total = row_max + jnp.log(jnp.sum(jnp.exp(scores - row_max), axis=2, keepdims=True))
        attn_probs = jnp.exp(scores - log_total)
        probs_low = attn_probs.astype(bf16)
        attn_result = jnp.einsum("hqk,kd->qhd", probs_low, value_rows, preferred_element_type=f32)
        context = token_order(attn_result.reshape(seq_length, width).astype(bf16))
        hidden = rows_float + twist_all(
            scatter_four(dot(context, out_wt, 1, 1, bf16)), back=True
        )

        normed_two, scale_two = norm_forward(hidden)
        act_two = gather_eight(twist_ring((normed_two * gain_ffn).astype(bf16)))
        cot_rows = gather_eight(twist_ring(cotangent))
        gate_pre = dot(act_two, gate_w, 1, 0)
        up_part = dot(act_two, up_w, 1, 0)
        sigmoid_gate = jax.nn.sigmoid(gate_pre)
        silu_gate = gate_pre * sigmoid_gate
        mixed_rows = (silu_gate * up_part).astype(bf16)
        grad_mixed = dot(cot_rows, down_wt, 1, 0)
        grad_gate = (
            grad_mixed * up_part * sigmoid_gate * (1.0 + gate_pre * (1.0 - sigmoid_gate))
        ).astype(bf16)
        grad_up = (grad_mixed * silu_gate).astype(bf16)
        grad_act_two = twist_ring(
            scatter_eight((dot(grad_gate, gate_w, 1, 1) + dot(grad_up, up_w, 1, 1)).astype(bf16)),
            back=True,
        )
        block_out = (
            hidden
            + twist_ring(scatter_eight(dot(mixed_rows, down_wt, 1, 1, bf16)), back=True)
        ).astype(bf16)
        back_two, gain_two = norm_backward(grad_act_two, normed_two, scale_two, gain_ffn)
        grad_hidden = cotangent.astype(f32) + back_two

        def ffn_grad(grad_rows_w):
            own = scatter_rows(grad_rows_w, ring_bits).astype(bf16)
            low, high = jnp.split(own, 2, axis=0)
            mine = jnp.where(pair_flag, high, low)
            theirs = swap(jnp.where(pair_flag, low, high), "dp", pair_bit)
            return jnp.concatenate(
                [jnp.where(pair_flag, theirs, mine), jnp.where(pair_flag, mine, theirs)], axis=1
            ).astype(f32)

        down_share = ffn_grad(dot(cot_rows, mixed_rows, 0, 0, bf16)).T
        gate_share = ffn_grad(dot(act_two, grad_gate, 0, 0, bf16))
        up_share = ffn_grad(dot(act_two, grad_up, 0, 0, bf16))

        grad_attn = gather_four(twist_all(grad_hidden.astype(bf16)))
        out_share = scatter_rows(dot(grad_attn, context, 0, 0, bf16), dp_bits).T
        grad_context = token_order(dot(grad_attn, out_wt, 1, 0, bf16), back=True).reshape(
            seq_length, local_heads, HD
        )
        grad_probs = jnp.einsum("qhd,kd->hqk", grad_context, value_rows, preferred_element_type=f32)
        row_delta = jnp.sum(grad_context.astype(f32) * attn_result, axis=2).T[:, :, None]
        grad_scores = (attn_probs * (grad_probs - row_delta)).astype(bf16)
        grad_query_rot = jnp.einsum(
            "hqk,kd->qhd", grad_scores, key_rot, preferred_element_type=f32
        ) / math.sqrt(HD)
        grad_key_rot = jnp.einsum(
            "hqk,qhd->kd", grad_scores, query_rot, preferred_element_type=f32
        ) / math.sqrt(HD)
        grad_value = jnp.einsum("hqk,qhd->kd", probs_low, grad_context, preferred_element_type=f32)
        grad_query = turn(grad_query_rot, cos_heads, -sin_heads).reshape(seq_length, width)
        grad_key = turn(grad_key_rot, cosine_table, -sine_table)

        kv_sent = swap(jnp.where(is_value == 1, grad_key, grad_value).astype(bf16), "tensor", 1)
        kv_kept = jnp.where(is_value == 1, grad_value, grad_key)
        kv_total = (kv_kept + kv_sent.astype(f32)).astype(bf16)
        grad_qkv = token_order(jnp.concatenate([grad_query.astype(bf16), kv_total], axis=1))
        grad_act_one = twist_all(scatter_four(dot(grad_qkv, qkv_w, 1, 1, bf16)), back=True)
        back_one, gain_one = norm_backward(grad_act_one, normed_one, scale_one, gain_attn)
        grad_rows = (grad_hidden + back_one).astype(bf16)

        qkv_share = scatter_rows(dot(act_one, grad_qkv, 0, 0, bf16), dp_bits)
        query_share = qkv_share[:, :width]
        kv_rows = qkv_share[:, width:]
        share_rows = kv_rows.shape[0] // tensor_size
        keyval_share = jnp.zeros((share_rows, 2 * KV * HD), f32)
        for mask in range(tensor_size):
            block = lax.dynamic_slice_in_dim(
                kv_rows, (tensor_index ^ mask) * share_rows, share_rows, 0
            )
            if mask:
                block = swap(block, "tensor", mask)
            sender = tensor_index ^ mask
            column = (sender % 2) * (KV * HD) + (sender * local_heads // (HQ // KV)) * HD
            keyval_share = lax.dynamic_update_slice_in_dim(keyval_share, block, column, 1)

        bias_keyval = jnp.zeros((2 * KV * HD,), f32)
        bias_keyval = lax.dynamic_update_slice_in_dim(
            bias_keyval, jnp.sum(grad_key, axis=0), head_kv * HD, 0
        )
        bias_keyval = lax.dynamic_update_slice_in_dim(
            bias_keyval, jnp.sum(grad_value, axis=0), KV * HD + head_kv * HD, 0
        )
        bias_query = lax.dynamic_update_slice_in_dim(
            jnp.zeros((HQ * HD,), f32), jnp.sum(grad_query, axis=0), tensor_index * width, 0
        )
        devices = dp_size * tensor_size
        sizes = [part.shape[0] // devices for part in (gain_one, gain_two, bias_query, bias_keyval)]
        small = jnp.concatenate(
            [part.reshape(devices, -1) for part in (gain_one, gain_two, bias_query, bias_keyval)],
            axis=1,
        )
        small = lax.all_to_all(small, ("dp", "tensor"), 0, 0, tiled=True)
        small = jnp.sum(small, axis=0)
        ends = [sum(sizes[: at + 1]) for at in range(4)]
        gain_one_share = small[: ends[0]]
        gain_two_share = small[ends[0] : ends[1]]
        query_bias_share = small[ends[1] : ends[2]]
        keyval_bias_share = small[ends[2] :]
        return (
            block_out,
            grad_rows,
            gain_one_share,
            query_share,
            query_bias_share,
            keyval_share,
            keyval_bias_share,
            out_share,
            gain_two_share,
            gate_share,
            up_share,
            down_share,
        )

    placed = (
        P(("dp", "tensor"), None),
        P("dp", None),
        P(),
        P("dp", "tensor"),
        P("tensor"),
        P("dp", None),
        P(),
        P("tensor", "dp"),
        P(),
        P("dp", "tensor"),
        P("dp", "tensor"),
        P("tensor", "dp"),
        P(("dp", "tensor"), None),
    )
    return jax.shard_map(
        local,
        mesh=mesh,
        in_specs=placed,
        out_specs=(
            P(("dp", "tensor"), None),
            P(("dp", "tensor"), None),
            P(("dp", "tensor")),
            P("dp", "tensor"),
            P(("dp", "tensor")),
            P(("dp", "tensor"), None),
            P(("dp", "tensor")),
            P("tensor", "dp"),
            P(("dp", "tensor")),
            P("dp", "tensor"),
            P("dp", "tensor"),
            P("tensor", "dp"),
        ),
        check_vma=False,
    )
```

time: 1490 us -> 806 us (0.54)
  waiting for transfers between devices: 1180 us -> 303 us
  local copies, waits for them, and re-layouts: 11.4 us -> 156 us
  starting transfers between devices: 1.44 us -> 80 us
  other arithmetic: 42.7 us -> 109 us
  matrix products: 193 us -> 145 us
  blocking collectives: 39.9 us -> 0 us
    reduce_scatter x10 -> x0, waiting for transfers between devices: 694 us -> none  [the longest x1 130 us: local(): lax.psum_scatter(grad_up_w.astype(jnp.bfloat16), 'dp', scatter_dimension=...]
    all_gather x10 -> x0, waiting for transfers between devices: 480 us -> none  [the longest x2 146 us: gather_three(): lax.all_gather(first, 'dp', axis=0, tiled=True)]
    ppermute x0 -> x74, waiting for transfers between devices: none -> 300 us  [swap(): return lax.ppermute(array, axis, [(i, i ^ bit) for i in range(size)])]
    ppermute x0 -> x74, starting transfers between devices: none -> 75.5 us  [swap(): return lax.ppermute(array, axis, [(i, i ^ bit) for i in range(size)])]
    unnamed x74 -> x275, local copies, waits for them, and re-layouts: 9.36 us -> 59.7 us
    dot_general x24 -> x21, matrix products: 193 us -> 145 us  [the longest x15 122 us: dot(): lax.dot_general(left, right, (((left_dim,), (right_dim,)), ((), ())), pre...]
    concatenate x0 -> x18, local copies, waits for them, and re-layouts: none -> 44.7 us  [the longest x5 18.6 us: gather_rows(): return jnp.concatenate(pieces, axis=0)]
    unnamed x1 -> x0, blocking collectives: 39.9 us -> none
  transfers between devices with their start and end apart: 20 -> 75, of which waited for: 18 -> 33; matrix products, arithmetic and copies ran while one was open for 13% -> 34% of each run, Pallas kernels for 0% -> 0%
where the time goes in v1:
time: 806 us; the launch traced here: 796 us
  waiting for transfers between devices  303 us (38%)
  local copies, waits for them, and re-layouts  156 us (19%)
  matrix products  145 us (18%)
  other arithmetic  109 us (14%)
  starting transfers between devices  80 us (10%)
    ppermute x74, waiting for transfers between devices, swap(): return lax.ppermute(array, axis, [(i, i ^ bit) for i in range(size)])  300 us
    dot_general x15, matrix products, dot(): lax.dot_general(left, right, (((left_dim,), (right_dim,)), ((), ())), pre...  122 us
    ppermute x74, starting transfers between devices, swap(): return lax.ppermute(array, axis, [(i, i ^ bit) for i in range(size)])  75.5 us
    unnamed x275, local copies, waits for them, and re-layouts  59.7 us
    concatenate x5, local copies, waits for them, and re-layouts, gather_rows(): return jnp.concatenate(pieces, axis=0)  18.6 us
    concatenate x9, local copies, waits for them, and re-layouts, twist(): return jnp.concatenate(blocks, axis=axis)  18.2 us
    another operation x6, other arithmetic  17.3 us
  transfers between devices with their start and end apart: 75, of which 33 were waited for; matrix products, arithmetic and copies ran while one was open for 34% of the time, Pallas kernels for 0%

profile of v1, /device:TPU:0, one launch (start us, length us, event | category | flops | bytes accessed | tf_op | source)
XLA Modules:
  0.0 795.8 jit_solution(13259336280786331066)
XLA Ops:
  3.3 4.0 collective-permute-start.2
  39.4 2.6 collective-permute-done.11
  45.2 2.7 collective-permute-done.12
  50.1 3.2 collective-permute-done.14
  55.5 5.9 collective-permute-done.4
  64.4 4.0 collective-permute-done.6
  79.0 2.9 convolution_add_fusion
  86.7 4.7 broadcast_multiply_fusion
  97.4 2.7 fusion.4
  100.1 4.5 exponential_reduce_fusion
  104.7 6.0 bitcast_convert_fusion
  123.4 2.6 collective-permute-start.33
  143.6 12.4 %collective-permute-done.44 = bf16[128,1536]{1,0:T(8,128)(2,1)S(1)} collective-permute-done((bf16[128,1536]{1,0:T(8,128)(2,1)S(1)}, bf16[128,1536]{1,0:T(8,128)(2,1)S(1)}, u32[]{:S(2)}, u32[]{:S(2)}) %collective-permute-start.44) | collective-permute-done | bytes 393248 | tf_op jit(solution)/shard_map/ppermute | solution.py:101
  165.4 2.5 collective-permute-start.20
  175.3 25.7 %collective-permute-done.20 = bf16[256,1536]{1,0:T(8,128)(2,1)} collective-permute-done((bf16[256,1536]{1,0:T(8,128)(2,1)}, bf16[256,1536]{1,0:T(8,128)(2,1)}, u32[]{:S(2)}, u32[]{:S(2)}) %collective-permute-start.20) | collective-permute-done | bytes 786464 | tf_op jit(solution)/shard_map/ppermute | solution.py:101
  205.7 25.4 %collective-permute-done.29 = bf16[384,1120]{0,1:T(8,128)(2,1)} collective-permute-done((bf16[384,1120]{0,1:T(8,128)(2,1)}, bf16[384,1120]{0,1:T(8,128)(2,1)}, u32[]{:S(2)}, u32[]{:S(2)}) %collective-permute-start.29) | collective-permute-done | bytes 860192 | tf_op jit(solution)/shard_map/ppermute | solution.py:101
  236.7 4.2 collective-permute-done.21
  246.2 2.8 collective-permute-done.25
  250.5 6.7 collective-permute-done.22
  259.5 2.7 copy-done.92
  262.2 6.3 concatenate.183
  268.5 24.9 %collective-permute-done.31 = bf16[384,1120]{0,1:T(8,128)(2,1)} collective-permute-done((bf16[384,1120]{0,1:T(8,128)(2,1)}, bf16[384,1120]{0,1:T(8,128)(2,1)}, u32[]{:S(2)}, u32[]{:S(2)}) %collective-permute-start.31) | collective-permute-done | bytes 860192 | tf_op jit(solution)/shard_map/ppermute | solution.py:101
  293.4 6.2 concatenate.181
  299.5 9.7 %collective-permute-done.27 = bf16[384,1120]{0,1:T(8,128)(2,1)} collective-permute-done((bf16[384,1120]{0,1:T(8,128)(2,1)}, bf16[384,1120]{0,1:T(8,128)(2,1)}, u32[]{:S(2)}, u32[]{:S(2)}) %collective-permute-start.27) | collective-permute-done | bytes 860192 | tf_op jit(solution)/shard_map/ppermute | solution.py:101
  309.2 6.2 concatenate.179
  317.4 3.9 constant_dynamic-update-slice_fusion.32
  321.3 12.0 %fusion.77 = f32[2048,1120]{0,1:T(8,128)} fusion(bf16[2048,1536]{1,0:T(8,128)(2,1)} %constant_dynamic-update-slice_fusion.32, bf16[1536,1120]{0,1:T(8,128)(2,1)S(1)} %copy-done.43), kind=kOutput, calls=%fused_computation.456 | convolution fusion | flops 7046430720 | bytes 18907136 | tf_op jit(solution)/shard_map/dot_general | solution.py:21
  335.5 2.6 copy-done.93
  338.2 9.6 %fusion.76 = f32[2048,1120]{0,1:T(8,128)} fusion(bf16[2048,1536]{1,0:T(8,128)(2,1)S(1)} %constant_dynamic-update-slice_fusion.21, bf16[1536,1120]{0,1:T(8,128)(2,1)S(1)} %copy-done.44), kind=kOutput, calls=%fused_computation.455 | convolution fusion | flops 7046430720 | bytes 18907136 | tf_op jit(solution)/shard_map/dot_general | solution.py:21
  347.8 21.0 %multiply_convert_fusion.1 = (bf16[2048,1120]{0,1:T(8,128)(2,1)}, bf16[2048,1120]{0,1:T(8,128)(2,1)}, bf16[2048,1120]{0,1:T(8,128)(2,1)}) fusion(f32[2048,1120]{0,1:T(8,128)} %fusion.77, f32[2048,1120]{0,1:T(8,128)} %fusion.76, bf16[2048,1536]{1,0:T(8,128)(2,1)} %copy-done.93, bf16[1536,1120]{0,1:T(8,128)(2,1)} %concatenate.179), kind=kOutput, calls=%fused_computation.9 | convolution fusion | flops 7080837120 | bytes 41844736 | tf_op jit(solution)/shard_map/dot_general | solution.py:21
  368.9 13.1 %fusion.78 = f32[2048,1536]{1,0:T(8,128)} fusion(bf16[2048,1120]{0,1:T(8,128)(2,1)} %get-tuple-element.102, bf16[1536,1120]{0,1:T(8,128)(2,1)S(1)} %copy-done.44), kind=kOutput, calls=%fused_computation.457 | convolution fusion | flops 7046430720 | bytes 20611072 | tf_op jit(solution)/shard_map/dot_general | solution.py:21
  381.9 7.6 convolution_convert_fusion.2
  389.5 7.8 convolution_convert_fusion.3
  397.3 12.5 %add_convert_fusion = bf16[2048,1536]{1,0:T(8,128)(2,1)S(1)} fusion(f32[2048,1536]{1,0:T(8,128)} %fusion.78, bf16[2048,1120]{0,1:T(8,128)(2,1)} %get-tuple-element.101, bf16[1536,1120]{0,1:T(8,128)(2,1)S(1)} %copy-done.45), kind=kOutput, calls=%fused_computation.4 | convolution fusion | flops 7052722176 | bytes 26902528 | tf_op jit(solution)/shard_map/dot_general | solution.py:21
  412.2 10.8 %convolution_convert_fusion.1 = bf16[1536,1120]{0,1:T(8,128)(2,1)S(1)} fusion(bf16[2048,1120]{0,1:T(8,128)(2,1)} %get-tuple-element.103, bf16[2048,1536]{1,0:T(8,128)(2,1)} %constant_dynamic-update-slice_fusion.32), kind=kOutput, calls=%fused_computation.15 | convolution fusion | flops 7048151040 | bytes 14319616 | tf_op jit(solution)/shard_map/dot_general | solution.py:21
  424.7 10.7 %convolution_convert_fusion = bf16[2048,1536]{1,0:T(8,128)(2,1)S(1)} fusion(bf16[2048,1120]{0,1:T(8,128)(2,1)} %get-tuple-element.103, bf16[1536,1120]{0,1:T(8,128)(2,1)S(1)} %copy-done.43), kind=kOutput, calls=%fused_computation.14 | convolution fusion | flops 7049576448 | bytes 14319616 | tf_op jit(solution)/shard_map/dot_general | solution.py:21
  440.9 9.8 %collective-permute-done.65 = bf16[768,1120]{0,1:T(8,128)(2,1)} collective-permute-done((bf16[768,1120]{0,1:T(8,128)(2,1)S(1)}, bf16[768,1120]{0,1:T(8,128)(2,1)}, u32[]{:S(2)}, u32[]{:S(2)}) %collective-permute-start.65) | collective-permute-done | bytes 1720352 | tf_op jit(solution)/shard_map/ppermute | solution.py:101
  452.6 34.9 %collective-permute-done.68 = bf16[768,1120]{0,1:T(8,128)(2,1)} collective-permute-done((bf16[768,1120]{0,1:T(8,128)(2,1)S(1)}, bf16[768,1120]{0,1:T(8,128)(2,1)}, u32[]{:S(2)}, u32[]{:S(2)}) %collective-permute-start.68) | collective-permute-done | bytes 1720352 | tf_op jit(solution)/shard_map/ppermute | solution.py:101
  491.1 29.7 %collective-permute-done.71 = bf16[768,1120]{0,1:T(8,128)(2,1)} collective-permute-done((bf16[768,1120]{0,1:T(8,128)(2,1)S(1)}, bf16[768,1120]{0,1:T(8,128)(2,1)}, u32[]{:S(2)}, u32[]{:S(2)}) %collective-permute-start.71) | collective-permute-done | bytes 1720352 | tf_op jit(solution)/shard_map/ppermute | solution.py:101
  525.6 2.6 collective-permute-start.67
  531.2 28.7 %collective-permute-done.72 = bf16[384,1120]{0,1:T(8,128)(2,1)} collective-permute-done((bf16[384,1120]{0,1:T(8,128)(2,1)S(1)}, bf16[384,1120]{0,1:T(8,128)(2,1)}, u32[]{:S(2)}, u32[]{:S(2)}) %collective-permute-start.72) | collective-permute-done | bytes 860192 | tf_op jit(solution)/shard_map/ppermute | solution.py:101
  571.5 6.7 fusion.64
  587.0 2.8 collective-permute-done.47
  594.6 6.7 fusion.63
  605.2 8.4 %collective-permute-done.50 = bf16[256,1536]{1,0:T(8,128)(2,1)S(1)} collective-permute-done((bf16[256,1536]{1,0:T(8,128)(2,1)S(1)}, bf16[256,1536]{1,0:T(8,128)(2,1)S(1)}, u32[]{:S(2)}, u32[]{:S(2)}) %collective-permute-start.50) | collective-permute-done | bytes 786464 | tf_op jit(solution)/shard_map/ppermute | solution.py:101
  633.7 13.2 %collective-permute-done.51 = bf16[256,1536]{1,0:T(8,128)(2,1)S(1)} collective-permute-done((bf16[256,1536]{1,0:T(8,128)(2,1)}, bf16[256,1536]{1,0:T(8,128)(2,1)S(1)}, u32[]{:S(2)}, u32[]{:S(2)}) %collective-permute-start.51) | collective-permute-done | bytes 786464 | tf_op jit(solution)/shard_map/ppermute | solution.py:101
  650.0 2.9 copy.125
  653.6 2.6 collective-permute-done.38
  661.6 3.2 convolution_convert_fusion.8
  670.6 7.6 fusion.1
  681.0 2.9 fusion.65
  684.0 4.2 select_convert_fusion
  694.6 3.9 convolution_convert_fusion.7
  703.7 3.1 convolution_convert_fusion.6
  714.4 3.0 concatenate.186
  720.8 11.4 %collective-permute-done.56 = bf16[768,512]{1,0:T(8,128)(2,1)} collective-permute-done((bf16[768,512]{1,0:T(8,128)(2,1)}, bf16[768,512]{1,0:T(8,128)(2,1)}, u32[]{:S(2)}, u32[]{:S(2)}) %collective-permute-start.56) | collective-permute-done | bytes 786464 | tf_op jit(solution)/shard_map/ppermute | solution.py:101
  738.8 3.0 collective-permute-start.64
  741.8 8.0 %collective-permute-done.57 = bf16[384,512]{1,0:T(8,128)(2,1)} collective-permute-done((bf16[384,512]{1,0:T(8,128)(2,1)}, bf16[384,512]{1,0:T(8,128)(2,1)}, u32[]{:S(2)}, u32[]{:S(2)}) %collective-permute-start.57) | collective-permute-done | bytes 393248 | tf_op jit(solution)/shard_map/ppermute | solution.py:101
  756.4 5.3 collective-permute-done.58
  765.3 8.7 %collective-permute-done.60 = f32[48,128]{1,0:T(8,128)S(1)} collective-permute-done((f32[48,128]{1,0:T(8,128)S(1)}, f32[48,128]{1,0:T(8,128)S(1)}, u32[]{:S(2)}, u32[]{:S(2)}) %collective-permute-start.60) | collective-permute-done | bytes 24608 | tf_op jit(solution)/shard_map/ppermute | solution.py:101
  776.7 2.7 concatenate.201
  782.4 4.5 all-to-all-start
  786.9 4.3 fusion.18
  791.2 2.9 all-to-all-done
  (578 shorter events, 272.3 us)
Async XLA Ops:
  3.3 39.3 %collective-permute-start.2 = (bf16[192,512]{1,0:T(8,128)(2,1)}, bf16[192,512]{1,0:T(8,128)(2,1)}, u32[]{:S(2)}, u32[]{:S(2)}) collective-permute-start(bf16[192,512]{1,0:T(8,128)(2,1)} %get-tuple-element.266), channel_id=1, source_target_pairs={{0,16},{4,20},{8,24},{12,28},{16,0},{20,4},{24,8},{28,12},{1,17},{... | collective-permute-start | bytes 589832 | tf_op jit(solution)/shard_map/ppermute | solution.py:101
  7.3 36.7 %collective-permute-start.3 = (bf16[192,512]{1,0:T(8,128)(2,1)}, bf16[192,512]{1,0:T(8,128)(2,1)}, u32[]{:S(2)}, u32[]{:S(2)}) collective-permute-start(bf16[192,512]{1,0:T(8,128)(2,1)} %get-tuple-element.266), channel_id=1, source_target_pairs={{0,8},{4,12},{8,0},{12,4},{16,24},{20,28},{24,16},{28,20},{1,9},{5... | collective-permute-start | bytes 589832 | tf_op jit(solution)/shard_map/ppermute | solution.py:101
  8.9 54.0 %collective-permute-start.5 = (bf16[192,512]{1,0:T(8,128)(2,1)}, bf16[192,512]{1,0:T(8,128)(2,1)}, u32[]{:S(2)}, u32[]{:S(2)}) collective-permute-start(bf16[192,512]{1,0:T(8,128)(2,1)} %get-tuple-element.266), channel_id=1, source_target_pairs={{0,4},{4,0},{8,12},{12,8},{16,20},{20,16},{24,28},{28,24},{1,5},{5... | collective-permute-start | bytes 589832 | tf_op jit(solution)/shard_map/ppermute | solution.py:101
  14.6 22.0 %collective-permute-start = (bf16[256,1536]{1,0:T(8,128)(2,1)S(1)}, bf16[256,1536]{1,0:T(8,128)(2,1)}, u32[]{:S(2)}, u32[]{:S(2)}) collective-permute-start(bf16[256,1536]{1,0:T(8,128)(2,1)S(1)} %concatenate.160), channel_id=1, source_target_pairs={{0,2},{1,3},{2,0},{3,1},{4,6},{5,7},{6,4},{7,5},{8,10},{9,11},{10,... | collective-permute-start | bytes 2359304 | tf_op jit(solution)/shard_map/ppermute | solution.py:101
  16.2 22.2 %collective-permute-start.10 = (bf16[192,384]{1,0:T(8,128)(2,1)}, bf16[192,384]{1,0:T(8,128)(2,1)}, u32[]{:S(2)}, u32[]{:S(2)}) collective-permute-start(bf16[192,384]{1,0:T(8,128)(2,1)} %bitcast.12), channel_id=1, source_target_pairs={{0,16},{4,20},{8,24},{12,28},{16,0},{20,4},{24,8},{28,12},{1,17},{... | collective-permute-start | bytes 442376 | tf_op jit(solution)/shard_map/ppermute | solution.py:101
  38.4 39.4 %collective-permute-start.1 = (bf16[512,1536]{1,0:T(8,128)(2,1)S(1)}, bf16[512,1536]{1,0:T(8,128)(2,1)S(1)}, u32[]{:S(2)}, u32[]{:S(2)}) collective-permute-start(bf16[512,1536]{1,0:T(8,128)(2,1)S(1)} %pad_maximum_fusion.3), channel_id=1, source_target_pairs={{0,1},{1,0},{2,3},{3,2},{4,5},{5,4},{6,7},{7,6},{8,9},{9,8},{10,11... | collective-permute-start | bytes 4718600 | tf_op jit(solution)/shard_map/ppermute | solution.py:101
  44.0 85.9 %collective-permute-start.41 = (bf16[256,1536]{1,0:T(8,128)(2,1)}, bf16[256,1536]{1,0:T(8,128)(2,1)}, u32[]{:S(2)}, u32[]{:S(2)}) collective-permute-start(bf16[256,1536]{1,0:T(8,128)(2,1)} %concatenate.187), channel_id=1, source_target_pairs={{0,2},{1,3},{2,0},{3,1},{4,6},{5,7},{6,4},{7,5},{8,10},{9,11},{10,... | collective-permute-start | bytes 2359304 | tf_op jit(solution)/shard_map/ppermute | solution.py:101
  53.3 8.0 %collective-permute-start.4 = (bf16[192,512]{1,0:T(8,128)(2,1)}, bf16[192,512]{1,0:T(8,128)(2,1)S(1)}, u32[]{:S(2)}, u32[]{:S(2)}) collective-permute-start(bf16[192,512]{1,0:T(8,128)(2,1)} %collective-permute-done.2), channel_id=1, source_target_pairs={{0,8},{4,12},{8,0},{12,4},{16,24},{20,28},{24,16},{28,20},{1,9},{5... | collective-permute-start | bytes 589832 | tf_op jit(solution)/shard_map/ppermute | solution.py:101
  54.9 73.1 %collective-permute-start.42 = (bf16[256,1536]{1,0:T(8,128)(2,1)}, bf16[256,1536]{1,0:T(8,128)(2,1)}, u32[]{:S(2)}, u32[]{:S(2)}) collective-permute-start(bf16[256,1536]{1,0:T(8,128)(2,1)} %concatenate.187), channel_id=1, source_target_pairs={{0,8},{4,12},{8,0},{12,4},{16,24},{20,28},{24,16},{28,20},{1,9},{5... | collective-permute-start | bytes 2359304 | tf_op jit(solution)/shard_map/ppermute | solution.py:101
  73.5 44.9 %collective-permute-start.32 = (bf16[192,1120]{1,0:T(8,128)(2,1)}, bf16[192,1120]{1,0:T(8,128)(2,1)}, u32[]{:S(2)}, u32[]{:S(2)}) collective-permute-start(bf16[192,1120]{1,0:T(8,128)(2,1)} %copy.98), channel_id=1, source_target_pairs={{0,8},{4,12},{8,0},{12,4},{16,24},{20,28},{24,16},{28,20},{1,9},{5... | collective-permute-start | bytes 1290248 | tf_op jit(solution)/shard_map/ppermute | solution.py:101
  76.2 47.2 %collective-permute-start.28 = (bf16[192,1120]{1,0:T(8,128)(2,1)}, bf16[192,1120]{1,0:T(8,128)(2,1)}, u32[]{:S(2)}, u32[]{:S(2)}) collective-permute-start(bf16[192,1120]{1,0:T(8,128)(2,1)} %copy.94), channel_id=1, source_target_pairs={{0,8},{4,12},{8,0},{12,4},{16,24},{20,28},{24,16},{28,20},{1,9},{5... | collective-permute-start | bytes 1290248 | tf_op jit(solution)/shard_map/ppermute | solution.py:101
  114.1 18.3 %collective-permute-start.17 = (bf16[512,1536]{1,0:T(8,128)(2,1)}, bf16[512,1536]{1,0:T(8,128)(2,1)}, u32[]{:S(2)}, u32[]{:S(2)}) collective-permute-start(bf16[512,1536]{1,0:T(8,128)(2,1)} %slice.354), channel_id=1, source_target_pairs={{0,1},{1,0},{2,3},{3,2},{4,5},{5,4},{6,7},{7,6},{8,9},{9,8},{10,11... | collective-permute-start | bytes 4718600 | tf_op jit(solution)/shard_map/ppermute | solution.py:101
  118.4 52.6 %collective-permute-start.24 = (bf16[192,1120]{1,0:T(8,128)(2,1)}, bf16[192,1120]{1,0:T(8,128)(2,1)}, u32[]{:S(2)}, u32[]{:S(2)}) collective-permute-start(bf16[192,1120]{1,0:T(8,128)(2,1)} %copy.89), channel_id=1, source_target_pairs={{0,8},{4,12},{8,0},{12,4},{16,24},{20,28},{24,16},{28,20},{1,9},{5... | collective-permute-start | bytes 1290248 | tf_op jit(solution)/shard_map/ppermute | solution.py:101
  123.4 80.7 %collective-permute-start.33 = (bf16[384,1120]{0,1:T(8,128)(2,1)}, bf16[384,1120]{0,1:T(8,128)(2,1)}, u32[]{:S(2)}, u32[]{:S(2)}) collective-permute-start(bf16[384,1120]{0,1:T(8,128)(2,1)} %pad_maximum_fusion.12), channel_id=1, source_target_pairs={{0,16},{4,20},{8,24},{12,28},{16,0},{20,4},{24,8},{28,12},{1,17},{... | collective-permute-start | bytes 2580488 | tf_op jit(solution)/shard_map/ppermute | solution.py:101
  129.1 12.1 %collective-permute-start.43 = (bf16[128,1536]{1,0:T(8,128)(2,1)S(1)}, bf16[128,1536]{1,0:T(8,128)(2,1)S(1)}, u32[]{:S(2)}, u32[]{:S(2)}) collective-permute-start(bf16[128,1536]{1,0:T(8,128)(2,1)S(1)} %slice.369), channel_id=1, source_target_pairs={{0,2},{1,3},{2,0},{3,1},{4,6},{5,7},{6,4},{7,5},{8,10},{9,11},{10,... | collective-permute-start | bytes 1179656 | tf_op jit(solution)/shard_map/ppermute | solution.py:101
  130.9 25.1 %collective-permute-start.44 = (bf16[128,1536]{1,0:T(8,128)(2,1)S(1)}, bf16[128,1536]{1,0:T(8,128)(2,1)S(1)}, u32[]{:S(2)}, u32[]{:S(2)}) collective-permute-start(bf16[128,1536]{1,0:T(8,128)(2,1)S(1)} %slice.370), channel_id=1, source_target_pairs={{0,8},{4,12},{8,0},{12,4},{16,24},{20,28},{24,16},{28,20},{1,9},{5... | collective-permute-start | bytes 1179656 | tf_op jit(solution)/shard_map/ppermute | solution.py:101
  134.8 22.3 %collective-permute-start.18 = (bf16[256,1536]{1,0:T(8,128)(2,1)S(1)}, bf16[256,1536]{1,0:T(8,128)(2,1)S(1)}, u32[]{:S(2)}, u32[]{:S(2)}) collective-permute-start(bf16[256,1536]{1,0:T(8,128)(2,1)S(1)} %slice.488), channel_id=1, source_target_pairs={{0,2},{1,3},{2,0},{3,1},{4,6},{5,7},{6,4},{7,5},{8,10},{9,11},{10,... | collective-permute-start | bytes 2359304 | tf_op jit(solution)/shard_map/ppermute | solution.py:101
  141.1 64.6 %collective-permute-start.34 = (bf16[384,1120]{0,1:T(8,128)(2,1)}, bf16[384,1120]{0,1:T(8,128)(2,1)}, u32[]{:S(2)}, u32[]{:S(2)}) collective-permute-start(bf16[384,1120]{0,1:T(8,128)(2,1)} %pad_maximum_fusion.12), channel_id=1, source_target_pairs={{0,4},{4,0},{8,12},{12,8},{16,20},{20,16},{24,28},{28,24},{1,5},{5... | collective-permute-start | bytes 2580488 | tf_op jit(solution)/shard_map/ppermute | solution.py:101
  157.0 160.4 %collective-permute-start.45 = (bf16[1024,1536]{1,0:T(8,128)(2,1)}, bf16[1024,1536]{1,0:T(8,128)(2,1)}, u32[]{:S(2)}, u32[]{:S(2)}) collective-permute-start(bf16[1024,1536]{1,0:T(8,128)(2,1)} %get-tuple-element.258), channel_id=1, source_target_pairs={{0,1},{1,0},{2,3},{3,2},{4,5},{5,4},{6,7},{7,6},{8,9},{9,8},{10,11... | collective-permute-start | bytes 9437192 | tf_op jit(solution)/shard_map/ppermute | solution.py:101
  165.4 35.6 %collective-permute-start.20 = (bf16[256,1536]{1,0:T(8,128)(2,1)}, bf16[256,1536]{1,0:T(8,128)(2,1)}, u32[]{:S(2)}, u32[]{:S(2)}) collective-permute-start(bf16[256,1536]{1,0:T(8,128)(2,1)} %concatenate.175), channel_id=1, source_target_pairs={{0,8},{4,12},{8,0},{12,4},{16,24},{20,28},{24,16},{28,20},{1,9},{5... | collective-permute-start | bytes 2359304 | tf_op jit(solution)/shard_map/ppermute | solution.py:101
  171.1 60.1 %collective-permute-start.29 = (bf16[384,1120]{0,1:T(8,128)(2,1)}, bf16[384,1120]{0,1:T(8,128)(2,1)}, u32[]{:S(2)}, u32[]{:S(2)}) collective-permute-start(bf16[384,1120]{0,1:T(8,128)(2,1)} %pad_maximum_fusion.11), channel_id=1, source_target_pairs={{0,16},{4,20},{8,24},{12,28},{16,0},{20,4},{24,8},{28,12},{1,17},{... | collective-permute-start | bytes 2580488 | tf_op jit(solution)/shard_map/ppermute | solution.py:101
  201.0 33.1 %collective-permute-start.19 = (bf16[256,1536]{1,0:T(8,128)(2,1)}, bf16[256,1536]{1,0:T(8,128)(2,1)S(1)}, u32[]{:S(2)}, u32[]{:S(2)}) collective-permute-start(bf16[256,1536]{1,0:T(8,128)(2,1)} %concatenate.175), channel_id=1, source_target_pairs={{0,2},{1,3},{2,0},{3,1},{4,6},{5,7},{6,4},{7,5},{8,10},{9,11},{10,... | collective-permute-start | bytes 2359304 | tf_op jit(solution)/shard_map/ppermute | solution.py:101
  204.1 40.5 %collective-permute-start.30 = (bf16[384,1120]{0,1:T(8,128)(2,1)}, bf16[384,1120]{0,1:T(8,128)(2,1)S(1)}, u32[]{:S(2)}, u32[]{:S(2)}) collective-permute-start(bf16[384,1120]{0,1:T(8,128)(2,1)} %pad_maximum_fusion.11), channel_id=1, source_target_pairs={{0,4},{4,0},{8,12},{12,8},{16,20},{20,16},{24,28},{28,24},{1,5},{5... | collective-permute-start | bytes 2580488 | tf_op jit(solution)/shard_map/ppermute | solution.py:101
  205.7 43.3 %collective-permute-start.25 = (bf16[384,1120]{0,1:T(8,128)(2,1)S(1)}, bf16[384,1120]{0,1:T(8,128)(2,1)}, u32[]{:S(2)}, u32[]{:S(2)}) collective-permute-start(bf16[384,1120]{0,1:T(8,128)(2,1)S(1)} %pad_maximum_fusion.10), channel_id=1, source_target_pairs={{0,16},{4,20},{8,24},{12,28},{16,0},{20,4},{24,8},{28,12},{1,17},{... | collective-permute-start | bytes 2580488 | tf_op jit(solution)/shard_map/ppermute | solution.py:101
  231.1 9.7 %collective-permute-start.21 = (bf16[128,1536]{1,0:T(8,128)(2,1)S(1)}, bf16[128,1536]{1,0:T(8,128)(2,1)S(1)}, u32[]{:S(2)}, u32[]{:S(2)}) collective-permute-start(bf16[128,1536]{1,0:T(8,128)(2,1)S(1)} %slice.357), channel_id=1, source_target_pairs={{0,2},{1,3},{2,0},{3,1},{4,6},{5,7},{6,4},{7,5},{8,10},{9,11},{10,... | collective-permute-start | bytes 1179656 | tf_op jit(solution)/shard_map/ppermute | solution.py:101
  234.1 28.1 %collective-permute-start.35 = (bf16[384,1120]{0,1:T(8,128)(2,1)}, bf16[384,1120]{0,1:T(8,128)(2,1)}, u32[]{:S(2)}, u32[]{:S(2)}) collective-permute-start(bf16[384,1120]{0,1:T(8,128)(2,1)} %collective-permute-done.33), channel_id=1, source_target_pairs={{0,4},{4,0},{8,12},{12,8},{16,20},{20,16},{24,28},{28,24},{1,5},{5... | collective-permute-start | bytes 2580488 | tf_op jit(solution)/shard_map/ppermute | solution.py:101
  240.9 16.3 %collective-permute-start.22 = (bf16[128,1536]{1,0:T(8,128)(2,1)S(1)}, bf16[128,1536]{1,0:T(8,128)(2,1)S(1)}, u32[]{:S(2)}, u32[]{:S(2)}) collective-permute-start(bf16[128,1536]{1,0:T(8,128)(2,1)S(1)} %slice.358), channel_id=1, source_target_pairs={{0,8},{4,12},{8,0},{12,4},{16,24},{20,28},{24,16},{28,20},{1,9},{5... | collective-permute-start | bytes 1179656 | tf_op jit(solution)/shard_map/ppermute | solution.py:101
  244.6 54.9 %collective-permute-start.26 = (bf16[384,1120]{0,1:T(8,128)(2,1)S(1)}, bf16[384,1120]{0,1:T(8,128)(2,1)}, u32[]{:S(2)}, u32[]{:S(2)}) collective-permute-start(bf16[384,1120]{0,1:T(8,128)(2,1)S(1)} %pad_maximum_fusion.10), channel_id=1, source_target_pairs={{0,4},{4,0},{8,12},{12,8},{16,20},{20,16},{24,28},{28,24},{1,5},{5... | collective-permute-start | bytes 2580488 | tf_op jit(solution)/shard_map/ppermute | solution.py:101
  249.0 44.4 %collective-permute-start.31 = (bf16[384,1120]{0,1:T(8,128)(2,1)}, bf16[384,1120]{0,1:T(8,128)(2,1)}, u32[]{:S(2)}, u32[]{:S(2)}) collective-permute-start(bf16[384,1120]{0,1:T(8,128)(2,1)} %collective-permute-done.29), channel_id=1, source_target_pairs={{0,4},{4,0},{8,12},{12,8},{16,20},{20,16},{24,28},{28,24},{1,5},{5... | collective-permute-start | bytes 2580488 | tf_op jit(solution)/shard_map/ppermute | solution.py:101
  257.2 52.0 %collective-permute-start.27 = (bf16[384,1120]{0,1:T(8,128)(2,1)}, bf16[384,1120]{0,1:T(8,128)(2,1)}, u32[]{:S(2)}, u32[]{:S(2)}) collective-permute-start(bf16[384,1120]{0,1:T(8,128)(2,1)} %collective-permute-done.25), channel_id=1, source_target_pairs={{0,4},{4,0},{8,12},{12,8},{16,20},{20,16},{24,28},{28,24},{1,5},{5... | collective-permute-start | bytes 2580488 | tf_op jit(solution)/shard_map/ppermute | solution.py:101
  262.2 71.1 %collective-permute-start.23 = (bf16[1024,1536]{1,0:T(8,128)(2,1)}, bf16[1024,1536]{1,0:T(8,128)(2,1)}, u32[]{:S(2)}, u32[]{:S(2)}) collective-permute-start(bf16[1024,1536]{1,0:T(8,128)(2,1)} %get-tuple-element.262), channel_id=1, source_target_pairs={{0,1},{1,0},{2,3},{3,2},{4,5},{5,4},{6,7},{7,6},{8,9},{9,8},{10,11... | collective-permute-start | bytes 9437192 | tf_op jit(solution)/shard_map/ppermute | solution.py:101
  410.0 40.7 %collective-permute-start.65 = (bf16[768,1120]{0,1:T(8,128)(2,1)S(1)}, bf16[768,1120]{0,1:T(8,128)(2,1)}, u32[]{:S(2)}, u32[]{:S(2)}) collective-permute-start(bf16[768,1120]{0,1:T(8,128)(2,1)S(1)} %slice.402), channel_id=1, source_target_pairs={{0,4},{4,0},{8,12},{12,8},{16,20},{20,16},{24,28},{28,24},{1,5},{5... | collective-permute-start | bytes 5160968 | tf_op jit(solution)/shard_map/ppermute | solution.py:101
  411.7 75.8 %collective-permute-start.68 = (bf16[768,1120]{0,1:T(8,128)(2,1)S(1)}, bf16[768,1120]{0,1:T(8,128)(2,1)}, u32[]{:S(2)}, u32[]{:S(2)}) collective-permute-start(bf16[768,1120]{0,1:T(8,128)(2,1)S(1)} %slice.406), channel_id=1, source_target_pairs={{0,4},{4,0},{8,12},{12,8},{16,20},{20,16},{24,28},{28,24},{1,5},{5... | collective-permute-start | bytes 5160968 | tf_op jit(solution)/shard_map/ppermute | solution.py:101
  423.1 97.7 %collective-permute-start.71 = (bf16[768,1120]{0,1:T(8,128)(2,1)S(1)}, bf16[768,1120]{0,1:T(8,128)(2,1)}, u32[]{:S(2)}, u32[]{:S(2)}) collective-permute-start(bf16[768,1120]{0,1:T(8,128)(2,1)S(1)} %slice.410), channel_id=1, source_target_pairs={{0,4},{4,0},{8,12},{12,8},{16,20},{20,16},{24,28},{28,24},{1,5},{5... | collective-permute-start | bytes 5160968 | tf_op jit(solution)/shard_map/ppermute | solution.py:101
  437.5 134.0 %collective-permute-start.46 = (bf16[1024,1536]{1,0:T(8,128)(2,1)}, bf16[1024,1536]{1,0:T(8,128)(2,1)}, u32[]{:S(2)}, u32[]{:S(2)}) collective-permute-start(bf16[1024,1536]{1,0:T(8,128)(2,1)} %slice.372), channel_id=1, source_target_pairs={{0,1},{1,0},{2,3},{3,2},{4,5},{5,4},{6,7},{7,6},{8,9},{9,8},{10,11... | collective-permute-start | bytes 9437192 | tf_op jit(solution)/shard_map/ppermute | solution.py:101
  440.9 153.7 %collective-permute-start.36 = (bf16[1024,1536]{1,0:T(8,128)(2,1)}, bf16[1024,1536]{1,0:T(8,128)(2,1)}, u32[]{:S(2)}, u32[]{:S(2)}) collective-permute-start(bf16[1024,1536]{1,0:T(8,128)(2,1)} %slice.362), channel_id=1, source_target_pairs={{0,1},{1,0},{2,3},{3,2},{4,5},{5,4},{6,7},{7,6},{8,9},{9,8},{10,11... | collective-permute-start | bytes 9437192 | tf_op jit(solution)/shard_map/ppermute | solution.py:101
  452.5 70.3 %collective-permute-start.66 = (bf16[384,1120]{0,1:T(8,128)(2,1)S(1)}, bf16[384,1120]{0,1:T(8,128)(2,1)S(1)}, u32[]{:S(2)}, u32[]{:S(2)}) collective-permute-start(bf16[384,1120]{0,1:T(8,128)(2,1)S(1)} %slice.486), channel_id=1, source_target_pairs={{0,16},{4,20},{8,24},{12,28},{16,0},{20,4},{24,8},{28,12},{1,17},{... | collective-permute-start | bytes 2580488 | tf_op jit(solution)/shard_map/ppermute | solution.py:101
  489.4 38.7 %collective-permute-start.69 = (bf16[384,1120]{0,1:T(8,128)(2,1)S(1)}, bf16[384,1120]{0,1:T(8,128)(2,1)}, u32[]{:S(2)}, u32[]{:S(2)}) collective-permute-start(bf16[384,1120]{0,1:T(8,128)(2,1)S(1)} %slice.485), channel_id=1, source_target_pairs={{0,16},{4,20},{8,24},{12,28},{16,0},{20,4},{24,8},{28,12},{1,17},{... | collective-permute-start | bytes 2580488 | tf_op jit(solution)/shard_map/ppermute | solution.py:101
  522.7 37.2 %collective-permute-start.72 = (bf16[384,1120]{0,1:T(8,128)(2,1)S(1)}, bf16[384,1120]{0,1:T(8,128)(2,1)}, u32[]{:S(2)}, u32[]{:S(2)}) collective-permute-start(bf16[384,1120]{0,1:T(8,128)(2,1)S(1)} %slice.484), channel_id=1, source_target_pairs={{0,16},{4,20},{8,24},{12,28},{16,0},{20,4},{24,8},{28,12},{1,17},{... | collective-permute-start | bytes 2580488 | tf_op jit(solution)/shard_map/ppermute | solution.py:101
  525.6 38.4 %collective-permute-start.67 = (bf16[192,1120]{1,0:T(8,128)(2,1)}, bf16[192,1120]{1,0:T(8,128)(2,1)}, u32[]{:S(2)}, u32[]{:S(2)}) collective-permute-start(bf16[192,1120]{1,0:T(8,128)(2,1)} %copy.114), channel_id=1, source_target_pairs={{0,8},{4,12},{8,0},{12,4},{16,24},{20,28},{24,16},{28,20},{1,9},{5... | collective-permute-start | bytes 1290248 | tf_op jit(solution)/shard_map/ppermute | solution.py:101
  531.2 34.0 %collective-permute-start.70 = (bf16[192,1120]{1,0:T(8,128)(2,1)}, bf16[192,1120]{1,0:T(8,128)(2,1)}, u32[]{:S(2)}, u32[]{:S(2)}) collective-permute-start(bf16[192,1120]{1,0:T(8,128)(2,1)} %copy.117), channel_id=1, source_target_pairs={{0,8},{4,12},{8,0},{12,4},{16,24},{20,28},{24,16},{28,20},{1,9},{5... | collective-permute-start | bytes 1290248 | tf_op jit(solution)/shard_map/ppermute | solution.py:101
  563.9 20.9 %collective-permute-start.73 = (bf16[192,1120]{1,0:T(8,128)(2,1)}, bf16[192,1120]{1,0:T(8,128)(2,1)}, u32[]{:S(2)}, u32[]{:S(2)}) collective-permute-start(bf16[192,1120]{1,0:T(8,128)(2,1)} %copy.120), channel_id=1, source_target_pairs={{0,8},{4,12},{8,0},{12,4},{16,24},{20,28},{24,16},{28,20},{1,9},{5... | collective-permute-start | bytes 1290248 | tf_op jit(solution)/shard_map/ppermute | solution.py:101
  579.3 10.5 %collective-permute-start.47 = (bf16[128,1536]{1,0:T(8,128)(2,1)}, bf16[128,1536]{1,0:T(8,128)(2,1)}, u32[]{:S(2)}, u32[]{:S(2)}) collective-permute-start(bf16[128,1536]{1,0:T(8,128)(2,1)} %get-tuple-element.117), channel_id=1, source_target_pairs={{0,8},{4,12},{8,0},{12,4},{16,24},{20,28},{24,16},{28,20},{1,9},{5... | collective-permute-start | bytes 1179656 | tf_op jit(solution)/shard_map/ppermute | solution.py:101
  581.3 10.0 %collective-permute-start.49 = (bf16[128,1536]{1,0:T(8,128)(2,1)}, bf16[128,1536]{1,0:T(8,128)(2,1)}, u32[]{:S(2)}, u32[]{:S(2)}) collective-permute-start(bf16[128,1536]{1,0:T(8,128)(2,1)} %get-tuple-element.116), channel_id=1, source_target_pairs={{0,2},{1,3},{2,0},{3,1},{4,6},{5,7},{6,4},{7,5},{8,10},{9,11},{10,... | collective-permute-start | bytes 1179656 | tf_op jit(solution)/shard_map/ppermute | solution.py:101
  593.1 20.5 %collective-permute-start.50 = (bf16[256,1536]{1,0:T(8,128)(2,1)S(1)}, bf16[256,1536]{1,0:T(8,128)(2,1)S(1)}, u32[]{:S(2)}, u32[]{:S(2)}) collective-permute-start(bf16[256,1536]{1,0:T(8,128)(2,1)S(1)} %pad_maximum_fusion.17), channel_id=1, source_target_pairs={{0,8},{4,12},{8,0},{12,4},{16,24},{20,28},{24,16},{28,20},{1,9},{5... | collective-permute-start | bytes 2359304 | tf_op jit(solution)/shard_map/ppermute | solution.py:101
  593.5 20.5 %collective-permute-start.48 = (bf16[256,1536]{1,0:T(8,128)(2,1)S(1)}, bf16[256,1536]{1,0:T(8,128)(2,1)S(1)}, u32[]{:S(2)}, u32[]{:S(2)}) collective-permute-start(bf16[256,1536]{1,0:T(8,128)(2,1)S(1)} %pad_maximum_fusion.16), channel_id=1, source_target_pairs={{0,2},{1,3},{2,0},{3,1},{4,6},{5,7},{6,4},{7,5},{8,10},{9,11},{10,... | collective-permute-start | bytes 2359304 | tf_op jit(solution)/shard_map/ppermute | solution.py:101
  602.5 24.7 %collective-permute-start.37 = (bf16[128,1536]{1,0:T(8,128)(2,1)}, bf16[128,1536]{1,0:T(8,128)(2,1)}, u32[]{:S(2)}, u32[]{:S(2)}) collective-permute-start(bf16[128,1536]{1,0:T(8,128)(2,1)} %get-tuple-element.121), channel_id=1, source_target_pairs={{0,8},{4,12},{8,0},{12,4},{16,24},{20,28},{24,16},{28,20},{1,9},{5... | collective-permute-start | bytes 1179656 | tf_op jit(solution)/shard_map/ppermute | solution.py:101
  604.2 23.0 %collective-permute-start.39 = (bf16[128,1536]{1,0:T(8,128)(2,1)}, bf16[128,1536]{1,0:T(8,128)(2,1)}, u32[]{:S(2)}, u32[]{:S(2)}) collective-permute-start(bf16[128,1536]{1,0:T(8,128)(2,1)} %get-tuple-element.120), channel_id=1, source_target_pairs={{0,2},{1,3},{2,0},{3,1},{4,6},{5,7},{6,4},{7,5},{8,10},{9,11},{10,... | collective-permute-start | bytes 1179656 | tf_op jit(solution)/shard_map/ppermute | solution.py:101
  626.2 20.7 %collective-permute-start.51 = (bf16[256,1536]{1,0:T(8,128)(2,1)}, bf16[256,1536]{1,0:T(8,128)(2,1)S(1)}, u32[]{:S(2)}, u32[]{:S(2)}) collective-permute-start(bf16[256,1536]{1,0:T(8,128)(2,1)} %concatenate.193), channel_id=1, source_target_pairs={{0,2},{1,3},{2,0},{3,1},{4,6},{5,7},{6,4},{7,5},{8,10},{9,11},{10,... | collective-permute-start | bytes 2359304 | tf_op jit(solution)/shard_map/ppermute | solution.py:101
  630.0 23.6 %collective-permute-start.40 = (bf16[256,1536]{1,0:T(8,128)(2,1)}, bf16[256,1536]{1,0:T(8,128)(2,1)}, u32[]{:S(2)}, u32[]{:S(2)}) collective-permute-start(bf16[256,1536]{1,0:T(8,128)(2,1)} %pad_maximum_fusion.15), channel_id=1, source_target_pairs={{0,8},{4,12},{8,0},{12,4},{16,24},{20,28},{24,16},{28,20},{1,9},{5... | collective-permute-start | bytes 2359304 | tf_op jit(solution)/shard_map/ppermute | solution.py:101
  632.7 23.5 %collective-permute-start.38 = (bf16[256,1536]{1,0:T(8,128)(2,1)}, bf16[256,1536]{1,0:T(8,128)(2,1)}, u32[]{:S(2)}, u32[]{:S(2)}) collective-permute-start(bf16[256,1536]{1,0:T(8,128)(2,1)} %pad_maximum_fusion.14), channel_id=1, source_target_pairs={{0,2},{1,3},{2,0},{3,1},{4,6},{5,7},{6,4},{7,5},{8,10},{9,11},{10,... | collective-permute-start | bytes 2359304 | tf_op jit(solution)/shard_map/ppermute | solution.py:101
  648.2 12.6 %collective-permute-start.52 = (bf16[512,1536]{1,0:T(8,128)(2,1)}, bf16[512,1536]{1,0:T(8,128)(2,1)}, u32[]{:S(2)}, u32[]{:S(2)}) collective-permute-start(bf16[512,1536]{1,0:T(8,128)(2,1)} %pad_maximum_fusion.4), channel_id=1, source_target_pairs={{0,1},{1,0},{2,3},{3,2},{4,5},{5,4},{6,7},{7,6},{8,9},{9,8},{10,11... | collective-permute-start | bytes 4718600 | tf_op jit(solution)/shard_map/ppermute | solution.py:101
  688.1 12.8 %collective-permute-start.53 = (bf16[1024,128]{1,0:T(8,128)(2,1)}, bf16[1024,128]{1,0:T(8,128)(2,1)}, u32[]{:S(2)}, u32[]{:S(2)}) collective-permute-start(bf16[1024,128]{1,0:T(8,128)(2,1)} %get-tuple-element.279), channel_id=1, source_target_pairs={{0,1},{1,0},{2,3},{3,2},{4,5},{5,4},{6,7},{7,6},{8,9},{9,8},{10,11... | collective-permute-start | bytes 786440 | tf_op jit(solution)/shard_map/ppermute | solution.py:101
  699.3 18.0 %collective-permute-start.62 = (bf16[768,384]{1,0:T(8,128)(2,1)}, bf16[768,384]{1,0:T(8,128)(2,1)}, u32[]{:S(2)}, u32[]{:S(2)}) collective-permute-start(bf16[768,384]{1,0:T(8,128)(2,1)} %slice.396), channel_id=1, source_target_pairs={{0,4},{4,0},{8,12},{12,8},{16,20},{20,16},{24,28},{28,24},{1,5},{5... | collective-permute-start | bytes 1769480 | tf_op jit(solution)/shard_map/ppermute | solution.py:101
  708.2 24.1 %collective-permute-start.56 = (bf16[768,512]{1,0:T(8,128)(2,1)}, bf16[768,512]{1,0:T(8,128)(2,1)}, u32[]{:S(2)}, u32[]{:S(2)}) collective-permute-start(bf16[768,512]{1,0:T(8,128)(2,1)} %slice.388), channel_id=1, source_target_pairs={{0,4},{4,0},{8,12},{12,8},{16,20},{20,16},{24,28},{28,24},{1,5},{5... | collective-permute-start | bytes 2359304 | tf_op jit(solution)/shard_map/ppermute | solution.py:101
  711.8 40.9 %collective-permute-start.54 = (bf16[512,1536]{1,0:T(8,128)(2,1)}, bf16[512,1536]{1,0:T(8,128)(2,1)}, u32[]{:S(2)}, u32[]{:S(2)}) collective-permute-start(bf16[512,1536]{1,0:T(8,128)(2,1)} %slice.384), channel_id=1, source_target_pairs={{0,1},{1,0},{2,3},{3,2},{4,5},{5,4},{6,7},{7,6},{8,9},{9,8},{10,11... | collective-permute-start | bytes 4718600 | tf_op jit(solution)/shard_map/ppermute | solution.py:101
  719.6 17.9 %collective-permute-start.63 = (bf16[384,384]{1,0:T(8,128)(2,1)}, bf16[384,384]{1,0:T(8,128)(2,1)}, u32[]{:S(2)}, u32[]{:S(2)}) collective-permute-start(bf16[384,384]{1,0:T(8,128)(2,1)} %slice.490), channel_id=1, source_target_pairs={{0,8},{4,12},{8,0},{12,4},{16,24},{20,28},{24,16},{28,20},{1,9},{5... | collective-permute-start | bytes 884744 | tf_op jit(solution)/shard_map/ppermute | solution.py:101
  735.6 14.2 %collective-permute-start.57 = (bf16[384,512]{1,0:T(8,128)(2,1)}, bf16[384,512]{1,0:T(8,128)(2,1)}, u32[]{:S(2)}, u32[]{:S(2)}) collective-permute-start(bf16[384,512]{1,0:T(8,128)(2,1)} %slice.489), channel_id=1, source_target_pairs={{0,8},{4,12},{8,0},{12,4},{16,24},{20,28},{24,16},{28,20},{1,9},{5... | collective-permute-start | bytes 1179656 | tf_op jit(solution)/shard_map/ppermute | solution.py:101
  738.8 23.1 %collective-permute-start.64 = (bf16[192,384]{1,0:T(8,128)(2,1)S(1)}, bf16[192,384]{1,0:T(8,128)(2,1)S(1)}, u32[]{:S(2)}, u32[]{:S(2)}) collective-permute-start(bf16[192,384]{1,0:T(8,128)(2,1)S(1)} %slice.492), channel_id=1, source_target_pairs={{0,16},{4,20},{8,24},{12,28},{16,0},{20,4},{24,8},{28,12},{1,17},{... | collective-permute-start | bytes 442376 | tf_op jit(solution)/shard_map/ppermute | solution.py:101
  750.9 10.8 %collective-permute-start.58 = (bf16[192,512]{1,0:T(8,128)(2,1)S(1)}, bf16[192,512]{1,0:T(8,128)(2,1)S(1)}, u32[]{:S(2)}, u32[]{:S(2)}) collective-permute-start(bf16[192,512]{1,0:T(8,128)(2,1)S(1)} %slice.491), channel_id=1, source_target_pairs={{0,16},{4,20},{8,24},{12,28},{16,0},{20,4},{24,8},{28,12},{1,17},{... | collective-permute-start | bytes 589832 | tf_op jit(solution)/shard_map/ppermute | solution.py:101
  755.1 18.9 %collective-permute-start.55 = (bf16[256,1536]{1,0:T(8,128)(2,1)S(1)}, bf16[256,1536]{1,0:T(8,128)(2,1)S(1)}, u32[]{:S(2)}, u32[]{:S(2)}) collective-permute-start(bf16[256,1536]{1,0:T(8,128)(2,1)S(1)} %slice.487), channel_id=1, source_target_pairs={{0,2},{1,3},{2,0},{3,1},{4,6},{5,7},{6,4},{7,5},{8,10},{9,11},{10,... | collective-permute-start | bytes 2359304 | tf_op jit(solution)/shard_map/ppermute | solution.py:101
  763.5 10.5 %collective-permute-start.60 = (f32[48,128]{1,0:T(8,128)S(1)}, f32[48,128]{1,0:T(8,128)S(1)}, u32[]{:S(2)}, u32[]{:S(2)}) collective-permute-start(f32[48,128]{1,0:T(8,128)S(1)} %get-tuple-element.269), channel_id=1, source_target_pairs={{0,2},{1,3},{2,0},{3,1},{4,6},{5,7},{6,4},{7,5},{8,10},{9,11},{10,... | collective-permute-start | bytes 73736 | tf_op jit(solution)/shard_map/ppermute | solution.py:101
  764.1 9.9 %collective-permute-start.61 = (f32[48,128]{1,0:T(8,128)S(1)}, f32[48,128]{1,0:T(8,128)S(1)}, u32[]{:S(2)}, u32[]{:S(2)}) collective-permute-start(f32[48,128]{1,0:T(8,128)S(1)} %get-tuple-element.268), channel_id=1, source_target_pairs={{0,3},{1,2},{2,1},{3,0},{4,7},{5,6},{6,5},{7,4},{8,11},{9,10},{10,... | collective-permute-start | bytes 73736 | tf_op jit(solution)/shard_map/ppermute | solution.py:101
  782.4 11.8 %all-to-all-start = ((f32[32,1,160]{2,1,0:T(1,128)}), f32[32,1,160]{2,1,0:T(1,128)S(1)}, u32[]{:S(2)}, u32[]{:S(2)}) async-start(f32[32,1,160]{2,1,0:T(1,128)} %all_to_all.6), calls=%async_computation | async-start | bytes 65536 | tf_op jit(solution)/shard_map/all_to_all | solution.py:347
  (134 other events, 953.0 us)

commit v2 on v1

v2 whole, which is shorter than its diff:
```python
import math

import jax
import jax.numpy as jnp
from jax import lax
from jax.experimental import pallas as pl
from jax.experimental.pallas import tpu as pltpu
from jax.sharding import PartitionSpec as P

HQ = 12
KV = 2
HD = 128


epsilon = 1e-06
rope_base = 1000000.0
masked_score = -1e30
bf16 = jnp.bfloat16
f32 = jnp.float32


def positions_of(segment_row):
    index_row = jnp.arange(segment_row.shape[0], dtype=jnp.int32)
    starts = jnp.concatenate(
        [jnp.ones((1,), jnp.int32), (segment_row[1:] != segment_row[:-1]).astype(jnp.int32)]
    )
    first_index = lax.cummax(jnp.where(starts > 0, index_row, 0), axis=0)
    return index_row - first_index


def rotary(positions):
    inverse = rope_base ** (-(jnp.arange(HD // 2, dtype=jnp.float32) * 2.0 / HD))
    angles = positions.astype(jnp.float32)[:, None] * inverse[None, :]
    angles = jnp.concatenate([angles, angles], axis=1)
    return (jnp.cos(angles), jnp.sin(angles))


def norm_forward(values_in):
    row_scale = lax.rsqrt(jnp.mean(values_in * values_in, axis=-1, keepdims=True) + epsilon)
    return (values_in * row_scale, row_scale)


def norm_backward(grad_out, normed, row_scale, gain_vec):
    grad_normed = grad_out * gain_vec
    grad_in = row_scale * (
        grad_normed - normed * jnp.mean(grad_normed * normed, axis=-1, keepdims=True)
    )
    return (grad_in, jnp.sum(grad_out * normed, axis=0))


ANY = pl.BlockSpec(memory_space=pl.ANY)
WHOLE = pl.BlockSpec(memory_space=pltpu.VMEM)
SCALARS = pl.BlockSpec(memory_space=pltpu.SMEM)


def made(jobs, sems, first=0):
    return [
        pltpu.make_async_copy(src, dst, sems.at[first + at]) for at, (src, dst) in enumerate(jobs)
    ]


def start_all(jobs, sems):
    copies = made(jobs, sems)
    for copy in copies:
        copy.start()
    return copies


def wait_all(copies):
    for copy in copies:
        copy.wait()


def block(ref, at, rows):
    return ref.at[pl.ds(pl.multiple_of(at * rows, rows), rows)]


def turned(values, cosine, sine, sign):
    return values * cosine + sign * (pltpu.roll(values, HD // 2, 1) * sine)


def mm(left, right):
    return lax.dot_general(left, right, (((1,), (0,)), ((), ())), preferred_element_type=f32)


def mm_nt(left, right):
    return lax.dot_general(left, right, (((1,), (1,)), ((), ())), preferred_element_type=f32)


def mm_tn(left, right):
    return lax.dot_general(left, right, (((0,), (0,)), ((), ())), preferred_element_type=f32)


def hold(due, release):
    out = lax.optimization_barrier((tuple(due), tuple(release)))
    return out[1]


def section(body):
    outs = jax.eval_shape(body)
    return lax.cond(
        lax.optimization_barrier(jnp.bool_(True)),
        body,
        lambda: jax.tree.map(lambda out: jnp.zeros(out.shape, out.dtype), outs),
    )


def solution(mesh):
    dp_size = mesh.shape["dp"]
    tensor_size = mesh.shape["tensor"]
    pair_bit = 2
    far_bits = []
    bit = dp_size // 2
    while bit > pair_bit:
        far_bits.append(bit)
        bit //= 2
    ring_bits = far_bits + [1]

    def swap(array, axis, bit):
        size = mesh.shape[axis]
        return lax.ppermute(array, axis, [(i, i ^ bit) for i in range(size)])

    def masks_of(bits):
        masks = [0]
        for bit in bits:
            masks = masks + [mask ^ bit for mask in masks]
        return masks

    def rows_of(*pieces):
        return jnp.concatenate(pieces, axis=0)

    def far_pieces(piece):
        pieces = [piece]
        for bit in far_bits:
            pieces = pieces + [swap(part, "dp", bit) for part in pieces]
        return pieces

    def fold(total, axis, bit):
        half = total.shape[0] // 2
        return total[:half], swap(total[half:].astype(bf16), axis, bit)

    def add(kept, arrived):
        return kept.astype(f32) + arrived.astype(f32)

    ring_masks = masks_of(ring_bits)
    ring_mask = sum(ring_bits)
    count = len(ring_masks)


    def ffn_jobs(dp_index, refs, offsets, held):
        rows = held.shape[0] // dp_size
        jobs = []
        for mask, ref, offset in zip(ring_masks, refs, offsets):
            base = jnp.bitwise_xor(jnp.bitwise_and(dp_index, ring_mask), mask)
            for low in (0, 1):
                jobs.append(
                    (
                        ref.at[pl.ds(offset + low * rows, rows)],
                        block(held, base + low * pair_bit, rows),
                    )
                )
        return jobs

    def row_jobs(refs, held):
        jobs, start = [], 0
        for ref in refs:
            jobs.append((ref, held.at[pl.ds(start, ref.shape[0])]))
            start += ref.shape[0]
        return jobs

    def attn_jobs(dp_index, refs, pieces, held):
        rows = held.shape[0] // dp_size
        return [
            (
                ref.at[pl.ds(first, rows)],
                block(held, jnp.bitwise_xor(dp_index, mask), rows),
            )
            for ref, (_, first, mask) in zip(refs, pieces)
        ]

    def arrays_of(pieces):
        return [piece[0] for piece in pieces]

    token_masks = ((0, 2), (1, 3))

    def token_jobs(tensor_index, pair, other, held):
        rows = held.shape[0] // 4
        jobs = []
        for masks, ref in zip(token_masks, (pair, other)):
            for at, mask in enumerate(masks):
                spot = jnp.bitwise_xor(tensor_index, mask)
                jobs.append((ref.at[pl.ds(at * rows, rows)], block(held, spot, rows)))
        return jobs

    def back(jobs):
        return [(dst, src) for src, dst in jobs]

    def ffn_up(scalars, pieces, gate_pieces, up_pieces):
        tokens, model = sum(piece.shape[0] for piece in pieces), pieces[0].shape[1]
        units = gate_pieces[0][0].shape[1]
        rows = tokens // 2
        many = len(pieces)
        early = 2

        def kernel(scal, *refs):
            parts = refs[:many]
            gates = refs[many : many + count]
            ups = refs[many + count : many + 2 * count]
            acts_ref, mixed_ref, silu_ref, back_ref, acts, gate_w, up_w, sems = refs[
                many + 2 * count :
            ]
            jobs = row_jobs(parts, acts)
            gate_jobs = ffn_jobs(scal[0], gates, [at for _, at in gate_pieces], gate_w)
            up_jobs = ffn_jobs(scal[0], ups, [at for _, at in up_pieces], up_w)
            step = pl.program_id(0)

            @pl.when(step == 0)
            def _():
                copies = start_all(jobs[:early] + gate_jobs + jobs[early:] + up_jobs, sems)
                wait_all(copies[: early + 2 * count])

            @pl.when(step == 1)
            def _():
                wait_all(made(jobs[early:], sems, early + 2 * count))

            spot = pl.ds(pl.multiple_of(step * rows, rows), rows)
            rows_in = acts[spot, :]
            acts_ref[...] = rows_in
            gate = mm(rows_in, gate_w[...])

            @pl.when(step == 0)
            def _():
                wait_all(made(up_jobs, sems, many + 2 * count))

            up = mm(rows_in, up_w[...])
            sig = jax.nn.sigmoid(gate)
            silu = gate * sig
            mixed_ref[...] = (silu * up).astype(bf16)
            silu_ref[...] = silu.astype(bf16)
            back_ref[...] = (up * sig * (1.0 + gate * (1.0 - sig))).astype(bf16)

        out = jax.ShapeDtypeStruct((tokens, units), bf16)
        spec = pl.BlockSpec((rows, units), lambda i: (i, 0))
        return pl.pallas_call(
            kernel,
            grid=(2,),
            in_specs=[SCALARS] + [ANY] * (many + 2 * count),
            out_specs=[pl.BlockSpec((rows, model), lambda i: (i, 0))] + [spec] * 3,
            out_shape=[jax.ShapeDtypeStruct((tokens, model), bf16)] + [out] * 3,
            scratch_shapes=[
                pltpu.VMEM((tokens, model), bf16),
                pltpu.VMEM((model, units), bf16),
                pltpu.VMEM((model, units), bf16),
                pltpu.SemaphoreType.DMA((many + 4 * count,)),
            ],
            name="ffn_up",
        )(
            scalars,
            *pieces,
            *[ref for ref, _ in gate_pieces],
            *[ref for ref, _ in up_pieces],
        )

    def ffn_back(scalars, cots, down_pieces, gate_pieces, up_pieces, silu, back_part):
        many = len(cots)
        tokens, model = sum(piece.shape[0] for piece in cots), cots[0].shape[1]
        units = silu.shape[1]
        rows = tokens // 2
        lists = (down_pieces, gate_pieces, up_pieces)

        def kernel(scal, *refs):
            parts = refs[:many]
            pieces = [refs[many + at * count : many + (at + 1) * count] for at in range(3)]
            silu_ref, back_ref, grad_gate_ref, grad_up_ref, out_ref = refs[
                many + 3 * count : many + 3 * count + 5
            ]
            cot, *held = refs[many + 3 * count + 5 : -1]
            sems = refs[-1]
            jobs = row_jobs(parts, cot)
            for at in range(3):
                jobs += ffn_jobs(scal[0], pieces[at], [spot for _, spot in lists[at]], held[at])
            first = pl.program_id(0) == 0
            early = many + 2 * count

            @pl.when(first)
            def _():
                wait_all(start_all(jobs, sems)[:early])

            spot = pl.ds(pl.multiple_of(pl.program_id(0) * rows, rows), rows)
            grad_mixed = mm(cot[spot, :], held[0][...])
            grad_gate = (grad_mixed * back_ref[...].astype(f32)).astype(bf16)
            grad_up = (grad_mixed * silu_ref[...].astype(f32)).astype(bf16)
            grad_gate_ref[...] = grad_gate
            grad_up_ref[...] = grad_up

            @pl.when(first)
            def _():
                wait_all(made(jobs[early:], sems, early))

            out_ref[...] = (
                mm_nt(grad_gate, held[1][...]) + mm_nt(grad_up, held[2][...])
            ).astype(bf16)

        out = jax.ShapeDtypeStruct((tokens, units), bf16)
        spec = pl.BlockSpec((rows, units), lambda i: (i, 0))
        wide = pl.BlockSpec((rows, model), lambda i: (i, 0))
        return pl.pallas_call(
            kernel,
            grid=(2,),
            in_specs=[SCALARS] + [ANY] * (many + 3 * count) + [spec, spec],
            out_specs=[spec, spec, wide],
            out_shape=[out, out, jax.ShapeDtypeStruct((tokens, model), bf16)],
            scratch_shapes=[pltpu.VMEM((tokens, model), bf16)]
            + [pltpu.VMEM((model, units), bf16)] * 3
            + [pltpu.SemaphoreType.DMA((many + 6 * count,))],
            name="ffn_back",
        )(scalars, *cots, *[ref for pieces in lists for ref, _ in pieces], silu, back_part)

    def ffn_rows(scalars, left, pieces, model, name):
        tokens, units = left.shape
        rows = tokens // 2

        def kernel(scal, left_ref, *refs):
            parts = refs[:count]
            out_ref, held, sems = refs[count:]

            @pl.when(pl.program_id(0) == 0)
            def _():
                wait_all(
                    start_all(ffn_jobs(scal[0], parts, [at for _, at in pieces], held), sems)
                )

            out_ref[...] = mm_nt(left_ref[...], held[...]).astype(bf16)

        return pl.pallas_call(
            kernel,
            grid=(2,),
            in_specs=[SCALARS, pl.BlockSpec((rows, units), lambda i: (i, 0))] + [ANY] * count,
            out_specs=pl.BlockSpec((rows, model), lambda i: (i, 0)),
            out_shape=jax.ShapeDtypeStruct((tokens, model), bf16),
            scratch_shapes=[
                pltpu.VMEM((model, units), bf16),
                pltpu.SemaphoreType.DMA((2 * count,)),
            ],
            name=name,
        )(scalars, left, *[ref for ref, _ in pieces])

    def ffn_grad(scalars, own_pieces, core_pieces, low, high, name):
        pieces = [*own_pieces, *core_pieces]
        many = len(own_pieces)
        tokens, model = low.shape[0], pieces[0].shape[1]
        units = low.shape[1]
        shard = model // dp_size
        wide = 384
        groups = wide // (2 * shard)

        def kernel(scal, *refs):
            def stack(parts):
                values = [part[...] for part in parts]
                return values[0] if len(values) == 1 else jnp.concatenate(values, axis=0)

            low_ref, high_ref, kept_ref, sent_ref = refs[2 * many :]
            total = mm_tn(stack(refs[:many]), low_ref[...])
            total = total + mm_tn(stack(refs[many : 2 * many]), high_ref[...])
            total = total.astype(bf16)
            odd = jnp.bitwise_and(scal[0], 1) == 1
            for group in range(groups):
                first = total[group * 2 * shard : group * 2 * shard + shard]
                second = total[group * 2 * shard + shard : (group + 1) * 2 * shard]
                spot = pl.ds(group * shard, shard)
                kept_ref[spot, :] = jnp.where(odd, second, first)
                sent_ref[spot, :] = jnp.where(odd, first, second)

        out = jax.ShapeDtypeStruct((model // 2, units), bf16)
        spec = pl.BlockSpec((wide // 2, units), lambda i: (i, 0))
        whole = pl.BlockSpec((tokens, units), lambda i: (0, 0))
        return pl.pallas_call(
            kernel,
            grid=(model // wide,),
            in_specs=[SCALARS]
            + [pl.BlockSpec((piece.shape[0], wide), lambda i: (0, i)) for piece in pieces]
            + [whole, whole],
            out_specs=[spec] * 2,
            out_shape=[out] * 2,
            name=name,
        )(scalars, *pieces, low, high)

    def is_high(scal, bit):
        return jnp.bitwise_and(scal[0], bit) != 0

    def whole_call(kernel, outs, name, *args):
        return pl.pallas_call(
            kernel,
            in_specs=[SCALARS] + [WHOLE] * (len(args) - 1),
            out_specs=[WHOLE] * len(outs),
            out_shape=[jax.ShapeDtypeStruct(shape, kind) for shape, kind in outs],
            name=name,
        )(*args)

    def split_cols(scalars, *arrays):
        rows, half = arrays[0].shape[0], arrays[0].shape[1] // 2
        wide = -(-half // 128) * 128
        many = len(arrays)

        def kernel(scal, *refs):
            mine_ref, sent_ref = refs[many:]
            flag = is_high(scal, pair_bit)
            mine_ref[...] = jnp.zeros_like(mine_ref)
            sent_ref[...] = jnp.zeros_like(sent_ref)
            for at in range(many):
                low, high = refs[at][:, :half], refs[at][:, half:]
                mine_ref[at * rows : (at + 1) * rows, :half] = jnp.where(flag, high, low)
                sent_ref[at * rows : (at + 1) * rows, :half] = jnp.where(flag, low, high)

        return whole_call(
            kernel, [((many * rows, wide), bf16)] * 2, "split_cols", scalars, *arrays
        )

    def join_rows(scalars, mine, theirs, at, many):
        rows, columns = mine.shape[0] // many, mine.shape[1]
        spot = pl.ds(at * rows, rows)

        def kernel(scal, mine_ref, theirs_ref, out_ref):
            flag = is_high(scal, pair_bit)
            out_ref[:rows, :] = jnp.where(flag, theirs_ref[spot, :], mine_ref[spot, :])
            out_ref[rows:, :] = jnp.where(flag, mine_ref[spot, :], theirs_ref[spot, :])

        return whole_call(
            kernel, [((2 * rows, columns), bf16)], "join_rows", scalars, mine, theirs
        )[0]

    def join_cols(scalars, mine, theirs, columns):
        rows = mine.shape[0]

        def kernel(scal, mine_ref, theirs_ref, out_ref):
            flag = is_high(scal, pair_bit)
            mine = mine_ref[:, :columns].astype(f32)
            theirs = theirs_ref[:, :columns].astype(f32)
            out_ref[:, :columns] = jnp.where(flag, theirs, mine)
            out_ref[:, columns:] = jnp.where(flag, mine, theirs)

        return whole_call(
            kernel, [((rows, 2 * columns), f32)], "join_cols", scalars, mine, theirs
        )[0]

    def fold_sum(scalars, kept, arrived, bit, outer):
        rows, columns = kept.shape[0] // 2, kept.shape[1]
        part = rows // outer

        def kernel(scal, kept_ref, arrived_ref, own_ref, sent_ref):
            flag = is_high(scal, bit)
            for at in range(outer):
                first = pl.ds(2 * at * part, part)
                second = pl.ds((2 * at + 1) * part, part)
                low = kept_ref[first, :].astype(f32) + arrived_ref[first, :].astype(f32)
                high = kept_ref[second, :].astype(f32) + arrived_ref[second, :].astype(f32)
                spot = pl.ds(at * part, part)
                own_ref[spot, :] = jnp.where(flag, high, low).astype(bf16)
                sent_ref[spot, :] = jnp.where(flag, low, high).astype(bf16)

        return whole_call(
            kernel, [((rows, columns), bf16)] * 2, "fold_sum", scalars, kept, arrived
        )

    def fold_fixed(scalars, kept, arrived, keep, give_away):
        many = len(keep) + len(give_away)
        rows, columns = kept.shape[0] // many, kept.shape[1]

        def kernel(scal, kept_ref, arrived_ref, own_ref, sent_ref):
            for blocks, ref in ((keep, own_ref), (give_away, sent_ref)):
                for at, spot in enumerate(blocks):
                    spot = pl.ds(spot * rows, rows)
                    ref[at * rows : (at + 1) * rows, :] = (
                        kept_ref[spot, :].astype(f32) + arrived_ref[spot, :].astype(f32)
                    ).astype(ref.dtype)

        outs = [((len(keep) * rows, columns), f32), ((len(give_away) * rows, columns), bf16)]
        return whole_call(kernel, outs, "fold_fixed", scalars, kept, arrived)

    def norm_two(scalars, rows_in, own, arrived, gain):
        def kernel(scal, in_ref, own_ref, arrived_ref, gain_ref, hidden_ref, out_ref):
            hidden = in_ref[...].astype(f32) + own_ref[...] + arrived_ref[...].astype(f32)
            hidden_ref[...] = hidden
            out_ref[...] = (norm_forward(hidden)[0] * gain_ref[...]).astype(bf16)

        outs = [(rows_in.shape, f32), (rows_in.shape, bf16)]
        return whole_call(kernel, outs, "norm_two", scalars, rows_in, own, arrived, gain)

    def norm_one_back(scalars, rows_in, own, arrived, gain, given):
        def kernel(scal, in_ref, own_ref, arrived_ref, gain_ref, given_ref, out_ref):
            grad_out = own_ref[...] + arrived_ref[...].astype(f32)
            normed, row_scale = norm_forward(in_ref[...].astype(f32))
            grad_normed = grad_out * gain_ref[...]
            grad_in = row_scale * (
                grad_normed - normed * jnp.mean(grad_normed * normed, axis=-1, keepdims=True)
            )
            out_ref[...] = (given_ref[...] + grad_in).astype(bf16)

        return whole_call(
            kernel, [(rows_in.shape, bf16)], "norm_one_back", scalars, rows_in, own, arrived, gain, given
        )[0]

    def join_both(scalars, first, mine, theirs):
        rows, columns = mine.shape[0] // 2, mine.shape[1]

        def kernel(scal, first_ref, mine_ref, theirs_ref, out_ref, both_ref):
            flag = is_high(scal, pair_bit)
            low = jnp.where(flag, theirs_ref[:rows, :], mine_ref[:rows, :])
            high = jnp.where(flag, mine_ref[:rows, :], theirs_ref[:rows, :])
            out_ref[:rows, :] = low
            out_ref[rows:, :] = high
            both_ref[: 2 * rows, :] = first_ref[...]
            both_ref[2 * rows : 3 * rows, :] = low
            both_ref[3 * rows :, :] = high

        return whole_call(
            kernel,
            [((2 * rows, columns), bf16), ((4 * rows, columns), bf16)],
            "join_both", scalars, first, mine, theirs,
        )

    def spread_eight(scalars, kept, arrived):
        rows, model = kept.shape[0] // 4, kept.shape[1]
        half = rows // 2

        def kernel(scal, kept_ref, arrived_ref, own_ref, x_ref, l_ref, far_a_ref, far_b_ref):
            for at, ref in enumerate((own_ref, x_ref, l_ref)):
                spot = pl.ds(at * rows, rows)
                ref[...] = kept_ref[spot, :].astype(f32) + arrived_ref[spot, :].astype(f32)
            for at, ref in enumerate((far_a_ref, far_b_ref)):
                spot = pl.ds(3 * rows + at * half, half)
                ref[...] = (
                    kept_ref[spot, :].astype(f32) + arrived_ref[spot, :].astype(f32)
                ).astype(bf16)

        outs = [((rows, model), f32)] * 3 + [((half, model), bf16)] * 2
        return whole_call(kernel, outs, "spread_eight", scalars, kept, arrived)

    def spread_two(scalars, to_x, to_l, far_x, far_l):
        rows, model = to_x.shape
        half = rows // 2

        def kernel(scal, x_ref, l_ref, far_x_ref, far_l_ref, out_x_ref, out_l_ref):
            out_x_ref[:half, :] = x_ref[:half, :].astype(bf16)
            out_x_ref[half:, :] = (x_ref[half:, :] + far_l_ref[...].astype(f32)).astype(bf16)
            out_l_ref[:half, :] = (l_ref[:half, :] + far_x_ref[...].astype(f32)).astype(bf16)
            out_l_ref[half:, :] = l_ref[half:, :].astype(bf16)

        return whole_call(
            kernel, [((rows, model), bf16)] * 2, "spread_two", scalars, to_x, to_l, far_x, far_l
        )

    def give(total, scal, kept_ref, sent_ref):
        part = total.shape[0] // dp_size
        flag = is_high(scal, 1)
        for at in range(total.shape[0] // (2 * part)):
            low = total[2 * at * part : (2 * at + 1) * part]
            high = total[(2 * at + 1) * part : (2 * at + 2) * part]
            kept_ref[pl.ds(at * part, part), :] = jnp.where(flag, high, low)
            sent_ref[pl.ds(at * part, part), :] = jnp.where(flag, low, high)

    def project(scalars, pair, core, pieces, bias, cosine, sine):
        tokens, model = 2 * pair.shape[0], pair.shape[1]
        columns = pieces[0][0].shape[1]
        width = columns - HD

        def kernel(scal, pair_ref, core_ref, bias_ref, cos_ref, sin_ref, *refs):
            query_ref, kv_ref, acts, held, sems = refs[dp_size:]
            wait_all(
                start_all(
                    attn_jobs(scal[0], refs[:dp_size], pieces, held)
                    + token_jobs(scal[1], pair_ref, core_ref, acts),
                    sems,
                )
            )
            is_value = jnp.bitwise_and(scal[1], 1) == 1
            rows = tokens // 4
            for at in range(4):
                spot = pl.ds(at * rows, rows)
                out = mm(acts[spot, :], held[...]) + bias_ref[...]
                cosine_rows, sine_rows = cos_ref[spot, :], sin_ref[spot, :]
                for head in range(width // HD):
                    query_ref[spot, head * HD : (head + 1) * HD] = turned(
                        out[:, head * HD : (head + 1) * HD], cosine_rows, sine_rows, 1.0
                    ).astype(bf16)
                kv = out[:, width:]
                kv_ref[spot, :] = jnp.where(
                    is_value, kv, turned(kv, cosine_rows, sine_rows, 1.0)
                ).astype(bf16)

        return pl.pallas_call(
            kernel,
            in_specs=[SCALARS, ANY, ANY, WHOLE, WHOLE, WHOLE] + [ANY] * dp_size,
            out_specs=[WHOLE, WHOLE],
            out_shape=[
                jax.ShapeDtypeStruct((tokens, width), bf16),
                jax.ShapeDtypeStruct((tokens, HD), bf16),
            ],
            scratch_shapes=[
                pltpu.VMEM((tokens, model), bf16),
                pltpu.VMEM((model, columns), bf16),
                pltpu.SemaphoreType.DMA((dp_size + 4,)),
            ],
            name="project",
        )(scalars, pair, core, bias, cosine, sine, *arrays_of(pieces))

    def probabilities(query, keys, start_rows, first):
        scores = mm_nt(query, keys) * (1.0 / math.sqrt(HD))
        column = lax.broadcasted_iota(jnp.int32, scores.shape, 1)
        row = lax.broadcasted_iota(jnp.int32, scores.shape, 0) + first
        allowed = (column <= row) & (column >= start_rows)
        scores = jnp.where(allowed, scores, masked_score)
        top = jnp.max(scores, axis=1, keepdims=True)
        raised = jnp.exp(scores - top)
        return raised * (1.0 / jnp.sum(raised, axis=1, keepdims=True))

    def attend(scalars, query, kv_own, kv_other, starts):
        tokens, width = query.shape
        rows = tokens // 4

        def kernel(scal, query_ref, own_ref, other_ref, start_ref, context_ref):
            is_value = jnp.bitwise_and(scal[1], 1) == 1
            own, other = own_ref[...], other_ref[...]
            keys = jnp.where(is_value, other, own)
            values = jnp.where(is_value, own, other)
            for at in range(4):
                end = (at + 1) * rows
                spot = pl.ds(at * rows, rows)
                for head in range(width // HD):
                    lanes = slice(head * HD, (head + 1) * HD)
                    probs = probabilities(
                        query_ref[spot, lanes], keys[:end], start_ref[spot, :], at * rows
                    )
                    context_ref[spot, lanes] = mm(probs.astype(bf16), values[:end]).astype(bf16)

        return whole_call(
            kernel, [((tokens, width), bf16)], "attend", scalars, query, kv_own, kv_other, starts
        )[0]

    def out_rows(scalars, context, pieces, model):
        tokens, width = context.shape
        rows = tokens // 4

        def kernel(scal, context_ref, *refs):
            kept_ref, sent_ref, held, part, sems, out_sems = refs[dp_size:]
            wait_all(start_all(attn_jobs(scal[0], refs[:dp_size], pieces, held), sems))
            for at in range(4):
                spot = pl.ds(at * rows, rows)
                part[spot, :] = mm_nt(context_ref[spot, :], held[...]).astype(bf16)
            wait_all(start_all(back(token_jobs(scal[1], kept_ref, sent_ref, part)), out_sems))

        half = jax.ShapeDtypeStruct((tokens // 2, model), bf16)
        return pl.pallas_call(
            kernel,
            in_specs=[SCALARS, WHOLE] + [ANY] * dp_size,
            out_specs=[ANY, ANY],
            out_shape=[half, half],
            scratch_shapes=[
                pltpu.VMEM((model, width), bf16),
                pltpu.VMEM((tokens, model), bf16),
                pltpu.SemaphoreType.DMA((dp_size,)),
                pltpu.SemaphoreType.DMA((4,)),
            ],
            name="out_rows",
        )(scalars, context, *arrays_of(pieces))

    def attend_back(
        scalars, query, kv_own, kv_other, starts, pieces, pair, core, context, cosine, sine
    ):
        tokens, width = query.shape
        model = pair.shape[1]
        rows = tokens // 4
        scale = 1.0 / math.sqrt(HD)

        def kernel(
            scal, query_ref, own_ref, other_ref, start_ref, pair_ref, core_ref,
            context_ref, cos_ref, sin_ref, *refs,
        ):
            grad_query_ref, kv_kept_ref, kv_sent_ref, bias_ref, wout_ref, wout_sent_ref = refs[
                dp_size : dp_size + 6
            ]
            held, grads, grad_context, grad_key, grad_value, sems = refs[dp_size + 6 :]
            wait_all(
                start_all(
                    attn_jobs(scal[0], refs[:dp_size], pieces, held)
                    + token_jobs(scal[1], pair_ref, core_ref, grads),
                    sems,
                )
            )
            is_value = jnp.bitwise_and(scal[1], 1) == 1
            own, other = own_ref[...], other_ref[...]
            keys = jnp.where(is_value, other, own)
            values = jnp.where(is_value, own, other)
            for at in range(2):
                spot = pl.ds(at * 2 * rows, 2 * rows)
                grad_context[spot, :] = mm(grads[spot, :], held[...]).astype(bf16)
            give(mm_tn(grads[...], context_ref[...]).astype(bf16), scal, wout_ref, wout_sent_ref)
            grad_key[...] = jnp.zeros_like(grad_key)
            grad_value[...] = jnp.zeros_like(grad_value)
            bias_ref[...] = jnp.zeros_like(bias_ref)
            for at in range(4):
                end = (at + 1) * rows
                spot = pl.ds(at * rows, rows)
                upto = pl.ds(0, end)
                for head in range(width // HD):
                    lanes = slice(head * HD, (head + 1) * HD)
                    queries = query_ref[spot, lanes]
                    given = grad_context[spot, lanes]
                    probs = probabilities(queries, keys[:end], start_ref[spot, :], at * rows)
                    low = probs.astype(bf16)
                    grad_probs = mm_nt(given, values[:end])
                    delta = jnp.sum(low.astype(f32) * grad_probs, axis=1, keepdims=True)
                    grad_scores = (probs * (grad_probs - delta)).astype(bf16)
                    grad_query = turned(
                        mm(grad_scores, keys[:end]) * scale, cos_ref[spot, :], sin_ref[spot, :], -1.0
                    )
                    grad_query_ref[spot, lanes] = grad_query.astype(bf16)
                    bias_ref[0:1, lanes] += jnp.sum(grad_query, axis=0, keepdims=True)
                    grad_key[upto, :] += mm_tn(grad_scores, queries)
                    grad_value[upto, :] += mm_tn(low, given)
            grad_keys = turned(grad_key[...] * scale, cos_ref[...], sin_ref[...], -1.0)
            grad_values = grad_value[...]
            bias_ref[0:1, width : width + HD] = jnp.sum(grad_keys, axis=0, keepdims=True)
            bias_ref[0:1, width + HD :] = jnp.sum(grad_values, axis=0, keepdims=True)
            kv_kept_ref[...] = jnp.where(is_value, grad_values, grad_keys)
            kv_sent_ref[...] = jnp.where(is_value, grad_keys, grad_values).astype(bf16)

        return pl.pallas_call(
            kernel,
            in_specs=[SCALARS] + [WHOLE] * 4 + [ANY] * 2 + [WHOLE] * 3 + [ANY] * dp_size,
            out_specs=[WHOLE] * 6,
            out_shape=[
                jax.ShapeDtypeStruct((tokens, width), bf16),
                jax.ShapeDtypeStruct((tokens, HD), f32),
                jax.ShapeDtypeStruct((tokens, HD), bf16),
                jax.ShapeDtypeStruct((8, width + 2 * HD), f32),
                jax.ShapeDtypeStruct((model // 2, width), bf16),
                jax.ShapeDtypeStruct((model // 2, width), bf16),
            ],
            scratch_shapes=[
                pltpu.VMEM((model, width), bf16),
                pltpu.VMEM((tokens, model), bf16),
                pltpu.VMEM((tokens, width), bf16),
                pltpu.VMEM((tokens, HD), f32),
                pltpu.VMEM((tokens, HD), f32),
                pltpu.SemaphoreType.DMA((dp_size + 4,)),
            ],
            name="attend_back",
        )(
            scalars, query, kv_own, kv_other, starts, pair, core, context, cosine, sine,
            *arrays_of(pieces),
        )

    def project_back(scalars, grad_query, kv_kept, kv_arrived, pieces, pair, core):
        tokens, width = grad_query.shape
        model, columns = pair.shape[1], pieces[0][0].shape[1]
        rows = tokens // 4

        def kernel(
            scal, query_ref, kept_kv_ref, arrived_ref, pair_ref, core_ref, *refs
        ):
            (
                grads_ref, kept_ref, sent_ref, gain_ref, held, part, acts, sems, out_sems,
            ) = refs[dp_size:]
            copies = start_all(
                attn_jobs(scal[0], refs[:dp_size], pieces, held)
                + token_jobs(scal[1], pair_ref, core_ref, acts),
                sems,
            )
            grads_ref[:, :width] = query_ref[...]
            grads_ref[:, width:] = (kept_kv_ref[...] + arrived_ref[...].astype(f32)).astype(bf16)
            wait_all(copies)
            for at in range(4):
                spot = pl.ds(at * rows, rows)
                part[spot, :] = mm_nt(grads_ref[spot, :], held[...]).astype(bf16)
            copies = start_all(back(token_jobs(scal[1], kept_ref, sent_ref, part)), out_sems)
            gain_ref[...] = jnp.zeros_like(gain_ref)
            for at in range(8):
                spot = pl.ds(at * rows // 2, rows // 2)
                gain_ref[0:1, :] += jnp.sum(
                    part[spot, :].astype(f32) * acts[spot, :].astype(f32), axis=0, keepdims=True
                )
            wait_all(copies)

        half = jax.ShapeDtypeStruct((tokens // 2, model), bf16)
        return pl.pallas_call(
            kernel,
            in_specs=[SCALARS, WHOLE, WHOLE, WHOLE, ANY, ANY] + [ANY] * dp_size,
            out_specs=[WHOLE, ANY, ANY, WHOLE],
            out_shape=[
                jax.ShapeDtypeStruct((tokens, columns), bf16),
                half,
                half,
                jax.ShapeDtypeStruct((8, model), f32),
            ],
            scratch_shapes=[
                pltpu.VMEM((model, columns), bf16),
                pltpu.VMEM((tokens, model), bf16),
                pltpu.VMEM((tokens, model), bf16),
                pltpu.SemaphoreType.DMA((dp_size + 4,)),
                pltpu.SemaphoreType.DMA((4,)),
            ],
            name="project_back",
        )(scalars, grad_query, kv_kept, kv_arrived, pair, core, *arrays_of(pieces))

    def project_grad(scalars, pair, core, grads):
        tokens, columns = grads.shape
        model = pair.shape[1]

        def kernel(scal, pair_ref, core_ref, grads_ref, kept_ref, sent_ref, acts, sems):
            wait_all(start_all(token_jobs(scal[1], pair_ref, core_ref, acts), sems))
            give(mm_tn(acts[...], grads_ref[...]).astype(bf16), scal, kept_ref, sent_ref)

        return pl.pallas_call(
            kernel,
            in_specs=[SCALARS, ANY, ANY, WHOLE],
            out_specs=[WHOLE] * 2,
            out_shape=[jax.ShapeDtypeStruct((model // 2, columns), bf16)] * 2,
            scratch_shapes=[
                pltpu.VMEM((tokens, model), bf16),
                pltpu.SemaphoreType.DMA((4,)),
            ],
            name="project_grad",
        )(scalars, pair, core, grads)

    def norm_two_back(scalars, own, from_x, from_l, hidden, gain, given):
        rows, model = own.shape

        def kernel(scal, own_ref, x_ref, l_ref, hidden_ref, gain_ref, given_ref, out_ref, low_ref, sum_ref):
            grad_out = own_ref[...] + x_ref[...].astype(f32) + l_ref[...].astype(f32)
            normed, row_scale = norm_forward(hidden_ref[...])
            grad_normed = grad_out * gain_ref[...]
            grad_in = row_scale * (
                grad_normed - normed * jnp.mean(grad_normed * normed, axis=-1, keepdims=True)
            )
            total = given_ref[...].astype(f32) + grad_in
            out_ref[...] = total
            low_ref[...] = total.astype(bf16)
            sum_ref[0:1, :] = jnp.sum(grad_out * normed, axis=0, keepdims=True)

        outs = [((rows, model), f32), ((rows, model), bf16), ((8, model), f32)]
        return whole_call(
            kernel, outs, "norm_two_back", scalars, own, from_x, from_l, hidden, gain, given
        )

    def local(
        block_input,
        segment_ids,
        gain_attn,
        w_query,
        b_query,
        w_keyval,
        b_keyval,
        w_out,
        gain_ffn,
        w_gate,
        w_up,
        w_down,
        cotangent,
    ):
        dp_index = lax.axis_index("dp")
        tensor_index = lax.axis_index("tensor")
        scalars = jnp.stack([dp_index, tensor_index]).astype(jnp.int32)
        local_heads = b_query.shape[0] // HD
        head_kv = tensor_index * local_heads // (HQ // KV)
        is_value = tensor_index % 2
        kv_column = is_value * (KV * HD) + head_kv * HD
        width = local_heads * HD

        groups = dp_size // 4

        def fold_rows(total, bit):
            flag = ((dp_index & bit) != 0).astype(jnp.int32)
            view = total.reshape(2, -1, total.shape[1])
            kept = lax.dynamic_index_in_dim(view, flag, 0, keepdims=False)
            sent = lax.dynamic_index_in_dim(view, 1 - flag, 0, keepdims=False)
            return kept, swap(sent.astype(bf16), "dp", bit)

        def far_rest(kept, sent):
            arrived = swap(sent, "dp", far_bits[0])
            for bit in far_bits[1:]:
                kept, sent = fold_sum(scalars, kept, arrived, bit, 1)
                arrived = swap(sent, "dp", bit)
            return kept, arrived

        keyval_cols = lax.dynamic_slice_in_dim(w_keyval, kv_column, HD, 1)
        qkv_own = jnp.concatenate([w_query, keyval_cols], axis=1)
        shard = qkv_own.shape[0]
        qkv_far = far_pieces(qkv_own)
        qkv_l = swap(qkv_own, "dp", pair_bit)
        qkv_y = swap(qkv_own, "dp", 1)
        rows_float = block_input.astype(f32)
        normed_one, scale_one = norm_forward(rows_float)
        act_own = (normed_one * gain_attn).astype(bf16)
        act_x = swap(act_own, "tensor", 2)
        gate_mine, gate_sent = split_cols(scalars, w_gate)
        gate_theirs = swap(gate_sent, "dp", pair_bit)

        qkv_far_in, qkv_l, qkv_y, out_own, w_up_in, w_down_in, segments = hold(
            [gate_sent, act_own],
            [tuple(qkv_far[1:]), qkv_l, qkv_y, w_out.T, w_up, w_down, segment_ids],
        )
        far_rows = rows_of(*qkv_far_in)
        qkv_y2 = swap(rows_of(qkv_l, far_rows), "dp", 1)
        qkv_l2 = swap(far_rows, "dp", pair_bit)
        out_far = far_pieces(out_own)
        rest_mine, rest_sent = split_cols(scalars, w_up_in, w_down_in.T)
        positions = positions_of(segments[0])
        cosine, sine = rotary(positions)
        sine = jnp.where(jnp.arange(HD)[None, :] < HD // 2, -sine, sine)
        starts = (jnp.arange(positions.shape[0], dtype=jnp.int32) - positions)[:, None]
        qkv_bias = jnp.concatenate([b_query, lax.dynamic_slice_in_dim(b_keyval, kv_column, HD, 0)])[
            None, :
        ]

        qkv_y2, qkv_l2, act_pair, gate_theirs, out_half, cosine, sine, starts, rest_sent, cot_own = (
            hold(
                [],
                [
                    qkv_y2,
                    qkv_l2,
                    rows_of(act_own, act_x),
                    gate_theirs,
                    rows_of(*out_far),
                    cosine,
                    sine,
                    starts,
                    rest_sent,
                    cotangent,
                ],
            )
        )
        gate_piece = join_rows(scalars, gate_mine, gate_theirs, 0, 1)
        gate_far = far_pieces(gate_piece)
        cot_x = swap(cot_own, "tensor", 2)
        (qkv_l2,) = hold([gate_piece], [qkv_l2])

        def gather_attn():
            return (
                swap(qkv_l2, "dp", 1),
                swap(act_pair, "tensor", 1),
                swap(out_half, "dp", pair_bit),
            )

        qkv_y3, act_c, out_l = section(gather_attn)

        qkv_y3, act_c, out_near, rest_sent, cot_core = hold(
            [], [qkv_y3, act_c, rows_of(out_half, out_l), rest_sent, cotangent]
        )
        rest_theirs = swap(rest_sent, "dp", pair_bit)
        out_y = swap(out_near, "dp", 1)
        far_masks = masks_of(far_bits)
        qkv_pieces = [(part, 0, mask) for part, mask in zip(qkv_far, far_masks)]
        qkv_pieces += [(qkv_l, 0, pair_bit), (qkv_y, 0, 1), (qkv_y2, 0, pair_bit ^ 1)]
        for at, mask in enumerate(far_masks[1:]):
            qkv_pieces += [
                (qkv_y2, (at + 1) * shard, mask ^ 1),
                (qkv_l2, at * shard, mask ^ pair_bit),
                (qkv_y3, at * shard, mask ^ pair_bit ^ 1),
            ]

        def attention():
            query_rot, kv_own = project(
                scalars, act_pair, act_c, qkv_pieces, qkv_bias, cosine, sine
            )
            kv_other = swap(kv_own, "tensor", 1)
            kv_other, cot_given = hold([], [kv_other, cot_core])
            cot_own_c = swap(cot_given, "tensor", 1)
            context = attend(scalars, query_rot, kv_own, kv_other, starts)
            context, cot_own_c = hold([], [context, cot_own_c])
            return query_rot, kv_own, kv_other, context, cot_own_c

        def out_pieces(near, far):
            pieces = []
            masks = masks_of(far_bits + [pair_bit])
            for at, mask in enumerate(masks):
                pieces += [(near, at * shard, mask), (far, at * shard, mask ^ 1)]
            return pieces

        query_rot, kv_own, kv_other, context, cot_own_c = section(attention)
        context, out_y = hold([], [context, out_y])
        out_parts = out_pieces(out_near, out_y)
        attn_kept, attn_sent = out_rows(scalars, context, out_parts, act_pair.shape[1])

        attn_sent, rest_theirs, cot_own_l = hold([cot_x], [attn_sent, rest_theirs, cotangent])

        def sum_cores():
            arrived = swap(attn_sent, "tensor", 1)
            return arrived, join_both(scalars, gate_piece, rest_mine, rest_theirs)

        attn_arrived, (up_piece, own_both) = section(sum_cores)
        attn_arrived, up_piece, own_both = hold([], [attn_arrived, up_piece, own_both])
        up_far = far_pieces(up_piece)
        own_y = swap(own_both, "dp", 1)
        cot_l = swap(cot_own_l, "dp", pair_bit)

        def sum_heads():
            own, sent = fold_fixed(scalars, attn_kept, attn_arrived, [0], [1])
            return norm_two(
                scalars, block_input, own, swap(sent, "tensor", 2), gain_ffn[None, :]
            )

        hidden, two_own = section(sum_heads)

        two_own, gate_halves = hold([cot_l], [two_own, tuple(gate_far[1:])])
        gate_y2 = [swap(part, "dp", 1) for part in gate_halves]

        def gather_near():
            two_x = swap(two_own, "tensor", 2)
            two_l = swap(two_own, "dp", pair_bit)
            return two_x, two_l, join_rows(scalars, rest_mine, rest_theirs, 1, 2)

        two_x, two_l, down_piece = section(gather_near)

        rows = two_own.shape[0]
        two_x, two_l, down_piece, up_halves = hold(
            [own_y, gate_y2], [two_x, two_l, down_piece, tuple(up_far[1:])]
        )
        up_y2 = [swap(part, "dp", 1) for part in up_halves]
        down_far = far_pieces(down_piece)

        def gather_rest():
            far_a = swap(two_l[: rows // 2], "tensor", 2)
            far_b = swap(two_x[rows // 2 :], "dp", pair_bit)

            def cores():
                given, arrived = [two_x, two_l, two_own], []
                for at in range(3):
                    part = swap(given[at], "tensor", 1)
                    part, *given = hold([], [part] + given)
                    arrived.append(part)
                return arrived

            arrived = section(cores)
            far_a, far_b, *arrived = hold([], [far_a, far_b] + arrived)
            return far_a, far_b, *arrived, swap(far_a, "tensor", 1), swap(far_b, "tensor", 1)

        far_a, far_b, two_x_c, two_l_c, two_own_c, far_a_c, far_b_c = section(gather_rest)
        two_pieces = [two_own, two_x, two_l]
        two_pieces_c = [two_own_c, two_x_c, two_l_c]

        size = gate_piece.shape[0]
        gate_pieces = [(part, 0) for part in [*gate_far]] + [
            (part, 0) for part in [own_y, *gate_y2]
        ]
        up_pieces = [(part, 0) for part in [*up_far]] + [(own_y, size)] + [
            (part, 0) for part in up_y2
        ]
        far_a, far_b, far_a_c, far_b_c, down_piece_y, cot_x, cot_l = hold(
            up_y2, [far_a, far_b, far_a_c, far_b_c, down_piece, cot_x, cot_l]
        )
        two_pieces += [far_a, far_b]
        two_pieces_c += [far_a_c, far_b_c]

        def feed_own():
            down_y1 = swap(down_piece_y, "dp", 1)
            cot_far = swap(cot_l, "tensor", 2)
            x_c = swap(cot_x, "tensor", 1)
            own = ffn_up(scalars, two_pieces, gate_pieces, up_pieces)
            down_y1, cot_far, x_c = hold([own], [down_y1, cot_far, x_c])
            return down_y1, cot_far, x_c, own

        down_y1, cot_far, cot_x_c, (acts_a, mixed_a, silu_a, back_a) = section(feed_own)

        mixed_a, down_halves, cot_l_in = hold([], [mixed_a, tuple(down_far[1:]), cot_l])

        cots = [cot_own, cot_x, cot_l, cot_far]

        def feed_core():
            down_y2 = tuple(swap(part, "dp", 1) for part in down_halves)

            def core_half():
                l_c = swap(cot_l_in, "tensor", 1)
                far_c = swap(cot_far, "tensor", 1)
                core = ffn_up(scalars, two_pieces_c, gate_pieces, up_pieces)
                l_c, far_c, *core = hold([], [l_c, far_c, *core])
                grads = ffn_grad(
                    scalars, cots, [cot_own_c, cot_x_c, l_c, far_c], mixed_a, core[1], "grad_down"
                )
                return l_c, far_c, core, grads

            outs = section(core_half)
            down_y2, outs = hold([], [down_y2, outs])
            return (down_y2, *outs)

        (
            down_y2, cot_l_c, cot_far_c, (acts_b, mixed_b, silu_b, back_b), (down_kept, down_sent),
        ) = section(feed_core)
        cots_c = [cot_own_c, cot_x_c, cot_l_c, cot_far_c]
        down_pieces = [(part, 0) for part in [*down_far, down_y1, *down_y2]]

        down_sent, silu_b = hold([], [down_sent, silu_b])
        down_sent = swap(down_sent, "dp", 1)

        def back_all():
            gate_b, up_b, two_sent = ffn_back(
                scalars, cots_c, down_pieces, gate_pieces, up_pieces, silu_b, back_b
            )
            (two_sent,) = hold([], [two_sent])
            arrived = swap(two_sent, "tensor", 1)
            gate_a, up_a, kept = ffn_back(
                scalars, cots, down_pieces, gate_pieces, up_pieces, silu_a, back_a
            )
            return (gate_a, up_a, gate_b, up_b, *spread_eight(scalars, kept, arrived))

        gate_a, up_a, gate_b, up_b, own, to_x, to_l, far_a, far_b = section(back_all)

        far_a, far_b, down_sent = hold([], [far_a, far_b, down_sent])

        def backward():
            def spread_far():
                far_x = swap(far_a, "tensor", 2)
                far_l = swap(far_b, "dp", pair_bit)
                gate_grads = ffn_grad(scalars, [acts_a], [acts_b], gate_a, gate_b, "grad_gate")
                far_x, far_l = hold([gate_grads], [far_x, far_l])
                return (*gate_grads, *spread_two(scalars, to_x, to_l, far_x, far_l))

            gate_kept, gate_sent, given_x, given_l = section(spread_far)

            given_x, given_l, gate_sent = hold([], [given_x, given_l, gate_sent])
            gate_sent = swap(gate_sent, "dp", 1)

            def second_norm():
                def spread_near():
                    from_x = swap(given_x, "tensor", 2)
                    from_l = swap(given_l, "dp", pair_bit)
                    up_grads = ffn_grad(scalars, [acts_a], [acts_b], up_a, up_b, "grad_up")
                    down_pair = fold_sum(scalars, down_kept, down_sent, far_bits[0], 1)
                    from_x, from_l = hold([up_grads, down_pair], [from_x, from_l])
                    return (
                        *up_grads,
                        *down_pair,
                        *norm_two_back(
                            scalars, own, from_x, from_l, hidden, gain_ffn[None, :], cotangent
                        ),
                    )

                up_kept, up_sent, down_own, down_given, grad_hidden, attn_own, gain_two = section(
                    spread_near
                )

                attn_own, down_given = hold([], [attn_own, down_given])
                down_own, down_arrived = far_rest(down_own, down_given)

                def gather_back():
                    attn_x = swap(attn_own, "tensor", 2)
                    model = attn_own.shape[1]
                    block_sent = ffn_rows(scalars, mixed_b, down_pieces, model, "block_rows")
                    block_kept = ffn_rows(scalars, mixed_a, down_pieces, model, "block_rows")
                    (attn_x,) = hold([block_kept, block_sent], [attn_x])
                    return rows_of(attn_own, attn_x), block_kept, block_sent

                attn_half, block_kept, block_sent = section(gather_back)
                attn_half, down_arrived = hold([], [attn_half, down_arrived])
                return (
                    up_kept, up_sent, down_own, down_arrived, grad_hidden, gain_two,
                    attn_half, block_kept, block_sent,
                )

            outs = section(second_norm)
            outs, gate_sent = hold([], [outs, gate_sent])
            return (gate_kept, gate_sent, *outs)

        (
            gate_kept, gate_sent, up_kept, up_sent, down_kept, down_sent, grad_hidden, gain_two,
            attn_half, block_kept, block_sent,
        ) = section(backward)

        attn_half, gate_sent, up_sent, down_sent, block_sent = hold(
            [], [attn_half, gate_sent, up_sent, down_sent, block_sent]
        )
        up_sent = swap(up_sent, "dp", 1)

        def gather_back_core():
            attn_c = swap(attn_half, "tensor", 1)
            gate_pair = fold_sum(scalars, gate_kept, gate_sent, far_bits[0], 1)
            attn_c, block_given = hold([gate_pair], [attn_c, block_sent])
            block_arrived = swap(block_given, "tensor", 1)
            down_pair = fold_sum(scalars, down_kept, down_sent, pair_bit, 1)
            (block_arrived,) = hold([down_pair], [block_arrived])
            block_pair = fold_fixed(scalars, block_kept, block_arrived, [0, 2], [1, 3])
            return attn_c, gate_pair, down_pair, block_pair

        attn_c, (gate_kept, gate_sent), (down_mine, down_given), (block_kept, block_sent) = section(
            gather_back_core
        )

        attn_c, block_sent, gate_sent = hold([], [attn_c, block_sent, gate_sent])
        gate_kept, gate_sent = far_rest(gate_kept, gate_sent)
        block_sent = swap(block_sent, "tensor", 2)

        def attention_back():
            outs = attend_back(
                scalars, query_rot, kv_own, kv_other, starts, out_parts, attn_half, attn_c,
                context, cosine, sine,
            )
            grad_query_low, kv_kept, kv_given, bias_rows, wout_kept, wout_sent = outs
            kv_given, wout_sent = hold([], [kv_given, wout_sent])
            wout_arrived = swap(wout_sent, "dp", 1)

            def project_all():
                kv_arrived = swap(kv_given, "tensor", 1)
                grad_qkv, one_kept, one_sent, gain_rows = project_back(
                    scalars, grad_query_low, kv_kept, kv_arrived, qkv_pieces, act_pair, act_c
                )
                arrived = swap(one_sent, "tensor", 1)
                wqkv_pair = project_grad(scalars, act_pair, act_c, grad_qkv)
                (arrived,) = hold([wqkv_pair], [arrived])
                return (
                    *wqkv_pair,
                    *fold_fixed(scalars, one_kept, arrived, [0], [1]),
                    gain_rows,
                )

            outs = section(project_all)
            outs, wout_arrived = hold([], [outs, wout_arrived])
            return (
                *outs, bias_rows, *fold_sum(scalars, wout_kept, wout_arrived, pair_bit, groups)
            )

        (
            wqkv_kept,
            wqkv_sent,
            one_kept,
            one_sent,
            gain_rows,
            bias_rows,
            wout_kept,
            wout_sent,
        ) = section(attention_back)

        up_sent, one_sent, wqkv_sent, wout_sent, down_given, block_sent = hold(
            [], [up_sent, one_sent, wqkv_sent, wout_sent, down_given, block_sent]
        )
        up_kept, up_sent = fold_sum(scalars, up_kept, up_sent, far_bits[0], 1)
        one_sent, wqkv_sent, up_sent, gate_sent = hold(
            [], [one_sent, wqkv_sent, up_sent, gate_sent]
        )
        up_kept, up_sent = far_rest(up_kept, up_sent)
        devices = dp_size * tensor_size

        def first_norm_back():
            arrived = swap(one_sent, "tensor", 2)
            wqkv_arrived = swap(wqkv_sent, "dp", 1)
            wout_arrived = swap(wout_sent, "dp", pair_bit)
            down_arrived = swap(down_given, "dp", pair_bit)
            gate_pair = fold_sum(scalars, gate_kept, gate_sent, pair_bit, 1)
            block_pair = fold_fixed(scalars, block_kept, block_sent, [0], [1])
            bias_keyval = jnp.zeros((2 * KV * HD,), f32)
            bias_keyval = lax.dynamic_update_slice_in_dim(
                bias_keyval, bias_rows[0, width : width + HD], head_kv * HD, 0
            )
            bias_keyval = lax.dynamic_update_slice_in_dim(
                bias_keyval, bias_rows[0, width + HD :], KV * HD + head_kv * HD, 0
            )
            bias_query = lax.dynamic_update_slice_in_dim(
                jnp.zeros((HQ * HD,), f32), bias_rows[0, :width], tensor_index * width, 0
            )
            parts = (gain_rows[0] / gain_attn, gain_two[0], bias_query, bias_keyval)
            small = jnp.concatenate([part.reshape(devices, -1) for part in parts], axis=1)
            (arrived,) = hold([gate_pair, block_pair, small], [arrived])
            grad_rows = norm_one_back(
                scalars, block_input, one_kept, arrived, gain_attn[None, :], grad_hidden
            )
            wqkv_arrived, wout_arrived, down_arrived = hold(
                [grad_rows], [wqkv_arrived, wout_arrived, down_arrived]
            )
            return (
                grad_rows,
                small,
                gate_pair,
                block_pair,
                fold_sum(scalars, wqkv_kept, wqkv_arrived, pair_bit, groups),
                wout_arrived,
                down_arrived,
            )

        (
            grad_rows,
            small,
            (gate_mine, gate_given),
            (block_kept, block_sent),
            (wqkv_kept, wqkv_sent),
            wout_arrived,
            down_theirs,
        ) = section(first_norm_back)

        wqkv_sent, gate_given, block_sent, small = hold(
            [], [wqkv_sent, gate_given, block_sent, small]
        )
        small = lax.all_to_all(small, ("dp", "tensor"), 0, 0, tiled=True)

        def last_rows():
            wqkv_arrived = swap(wqkv_sent, "dp", pair_bit)
            block_arrived = swap(block_sent, "dp", pair_bit)
            wout_total = add(wout_kept, wout_arrived)
            down_share = join_cols(scalars, down_mine, down_theirs, w_down.shape[0] // 2).T
            (wqkv_arrived,) = hold([down_share, wout_total], [wqkv_arrived])
            total = jnp.concatenate([add(wqkv_kept, wqkv_arrived), wout_total], axis=1)
            total, gate_out = hold([], [total, gate_given])
            for bit in far_bits[:-1]:
                total = add(*fold_rows(total, bit))
            kept, sent = fold_rows(total, far_bits[-1])
            gate_theirs = swap(gate_out, "dp", pair_bit)
            (block_arrived,) = hold([kept], [block_arrived])
            block_out = (hidden + add(block_kept, block_arrived)).astype(bf16)
            (sent,) = hold([block_out], [sent])
            share = add(kept, sent)
            kv_rows = share[:, width : width + HD]
            share_rows = kv_rows.shape[0] // tensor_size
            keyval_share = jnp.zeros((share_rows, 2 * KV * HD), f32)
            moved = []
            for mask in range(tensor_size):
                rows_for = lax.dynamic_slice_in_dim(
                    kv_rows, (tensor_index ^ mask) * share_rows, share_rows, 0
                )
                moved.append(swap(rows_for, "tensor", mask) if mask else rows_for)
            query_share, out_share = share[:, :width], share[:, width + HD :].T
            gate_theirs, *moved = hold([query_share, out_share], [gate_theirs] + moved)
            gate_share = join_cols(scalars, gate_mine, gate_theirs, w_gate.shape[1] // 2)
            for mask in range(tensor_size):
                sender = tensor_index ^ mask
                column = (sender % 2) * (KV * HD) + (sender * local_heads // (HQ // KV)) * HD
                keyval_share = lax.dynamic_update_slice_in_dim(
                    keyval_share, moved[mask], column, 1
                )
            return down_share, gate_share, block_out, query_share, out_share, keyval_share

        down_share, gate_share, block_out, query_share, out_share, keyval_share = section(last_rows)

        up_sent, small = hold([block_out, keyval_share], [up_sent, small])
        up_mine, up_given = fold_sum(scalars, up_kept, up_sent, pair_bit, 1)
        up_theirs = swap(up_given, "dp", pair_bit)
        small = jnp.sum(small, axis=0)
        up_share = join_cols(scalars, up_mine, up_theirs, w_up.shape[1] // 2)
        sizes = [HQ * HD // devices, 2 * KV * HD // devices, gain_attn.shape[0] // devices]
        ends = [sizes[2], 2 * sizes[2], 2 * sizes[2] + sizes[0]]
        gain_one_share = small[: ends[0]]
        gain_two_share = small[ends[0] : ends[1]]
        query_bias_share = small[ends[1] : ends[2]]
        keyval_bias_share = small[ends[2] :]
        return (
            block_out,
            grad_rows,
            gain_one_share,
            query_share,
            query_bias_share,
            keyval_share,
            keyval_bias_share,
            out_share,
            gain_two_share,
            gate_share,
            up_share,
            down_share,
        )

    placed = (
        P(("dp", "tensor"), None),
        P("dp", None),
        P(),
        P("dp", "tensor"),
        P("tensor"),
        P("dp", None),
        P(),
        P("tensor", "dp"),
        P(),
        P("dp", "tensor"),
        P("dp", "tensor"),
        P("tensor", "dp"),
        P(("dp", "tensor"), None),
    )
    return jax.shard_map(
        local,
        mesh=mesh,
        in_specs=placed,
        out_specs=(
            P(("dp", "tensor"), None),
            P(("dp", "tensor"), None),
            P(("dp", "tensor")),
            P("dp", "tensor"),
            P(("dp", "tensor")),
            P(("dp", "tensor"), None),
            P(("dp", "tensor")),
            P("tensor", "dp"),
            P(("dp", "tensor")),
            P("dp", "tensor"),
            P("dp", "tensor"),
            P("tensor", "dp"),
        ),
        check_vma=False,
    )
```

time: 806 us -> 569 us (0.71)
  Pallas kernels: 0 us -> 277 us
  matrix products: 145 us -> 0 us
  waiting for transfers between devices: 303 us -> 163 us
  local copies, waits for them, and re-layouts: 156 us -> 20.1 us
  other arithmetic: 109 us -> 20.5 us
    pallas_call x0 -> x40, Pallas kernels: none -> 277 us  [the longest x26 90.7 us: whole_call(): pl.pallas_call(kernel, in_specs=[SCALARS] + [WHOLE] * (len(args) - 1), ou...]
    dot_general x21 -> x0, matrix products: 145 us -> none  [the longest x15 122 us: dot(): lax.dot_general(left, right, (((left_dim,), (right_dim,)), ((), ())), pre...]
    ppermute x74 -> x70, waiting for transfers between devices: 300 us -> 163 us  [swap(): return lax.ppermute(array, axis, [(i, i ^ bit) for i in range(size)])]
    unnamed x275 -> x41, local copies, waits for them, and re-layouts: 59.7 us -> 1.73 us
    concatenate x18 -> x0, local copies, waits for them, and re-layouts: 44.7 us -> none  [the longest x5 18.6 us: gather_rows(): return jnp.concatenate(pieces, axis=0)]
    select_n x36 -> x1, other arithmetic: 21.4 us -> 2.93 us  [local(): sine = jnp.where(jnp.arange(HD)[None, :] < HD // 2, -sine, sine)]
    add x15 -> x3, other arithmetic: 19.6 us -> 2.28 us  [add(): return kept.astype(f32) + arrived.astype(f32)]
    another operation x6 -> x3, other arithmetic: 17.3 us -> 0.38 us
  transfers between devices with their start and end apart: 75 -> 71, of which waited for: 33 -> 33; matrix products, arithmetic and copies ran while one was open for 34% -> 6% of each run, Pallas kernels for 0% -> 48%
where the time goes in v2:
time: 569 us; the launch traced here: 559 us
  Pallas kernels  277 us (49%)
  waiting for transfers between devices  163 us (29%)
  starting transfers between devices  76.5 us (13%)
  other arithmetic  20.5 us (4%)
  local copies, waits for them, and re-layouts  20.1 us (4%)
    ppermute x70, waiting for transfers between devices, swap(): return lax.ppermute(array, axis, [(i, i ^ bit) for i in range(size)])  163 us
    pallas_call x26, Pallas kernels, whole_call(): pl.pallas_call(kernel, in_specs=[SCALARS] + [WHOLE] * (len(args) - 1), ou...  90.7 us
    ppermute x70, starting transfers between devices, swap(): return lax.ppermute(array, axis, [(i, i ^ bit) for i in range(size)])  72.6 us
    pallas_call x2, Pallas kernels, ffn_back(): pl.pallas_call(kernel, grid=(2,), in_specs=[SCALARS] + [ANY] * (many + 3...  49 us
    pallas_call x3, Pallas kernels, ffn_grad(): pl.pallas_call(kernel, grid=(model // wide,), in_specs=[SCALARS] + [pl.Bl...  39 us
    pallas_call x2, Pallas kernels, ffn_up(): pl.pallas_call(kernel, grid=(2,), in_specs=[SCALARS] + [ANY] * (many + 2...  31.2 us
    pallas_call x1, Pallas kernels, attend_back(): pl.pallas_call(kernel, in_specs=[SCALARS] + [WHOLE] * 4 + [ANY] * 2 + [WH...  21.5 us
    pallas_call x2, Pallas kernels, ffn_rows(): pl.pallas_call(kernel, grid=(2,), in_specs=[SCALARS, pl.BlockSpec((rows,...  18.1 us
  transfers between devices with their start and end apart: 71, of which 33 were waited for; matrix products, arithmetic and copies ran while one was open for 6% of the time, Pallas kernels for 48%

profile of v2, /device:TPU:0, one launch (start us, length us, event | category | flops | bytes accessed | tf_op | source)
XLA Modules:
  0.0 558.6 jit_solution(789269060079849599)
XLA Ops:
  28.9 3.4 split_cols.3
  37.2 9.5 %conditional.21 = (bf16[192,512]{1,0:T(8,128)(2,1)}, bf16[512,1536]{1,0:T(8,128)(2,1)}, bf16[384,384]{1,0:T(8,128)(2,1)}) conditional(s32[]{:T(128)} %convert_element_type.80, () %tuple.229, (bf16[192,512]{1,0:T(8,128)(2,1)}, bf16[512,1536]{1,0:T(8,128)(2,1)S(1)}, bf16[384,384]{1,0:T(8,128)(2,1)S(1)}) %tuple.328), branch_computations={%region_3.4_spmd, %region_4.5_spmd} | conditional | bytes 8257680 | solution.py:101
  38.9 6.3 %collective-permute-done = bf16[192,512]{1,0:T(8,128)(2,1)} collective-permute-done((bf16[192,512]{1,0:T(8,128)(2,1)}, bf16[192,512]{1,0:T(8,128)(2,1)}, u32[]{:S(2)}, u32[]{:S(2)}) %collective-permute-start) | collective-permute-done | bytes 196640 | tf_op jit(solution)/shard_map/cond/branch_1_fun/ppermute | solution.py:121
  53.6 17.8 %conditional.22 = (bf16[1024,384]{1,0:T(8,128)(2,1)}, bf16[1024,128]{1,0:T(8,128)(2,1)}, bf16[1024,128]{1,0:T(8,128)(2,1)}, bf16[1024,384]{1,0:T(8,128)(2,1)}, bf16[256,1536]{1,0:T(8,128)(2,1)}) conditional(s32[]{:T(128)} %convert_element_type.80, () %tuple.228, (f32[512]{0:T(512)S(1)}, s32[2]{0:T(128)S(1)}, bf16[512,1536]{1,0:T(8,128)(2,1)S(1)}, ...), branch_computations={%region_5.6_spmd, %region_6.7_spmd} | conditional | bytes 4194424 | solution.py:101
  53.6 6.8 %project.1 = (bf16[1024,384]{1,0:T(8,128)(2,1)}, bf16[1024,128]{1,0:T(8,128)(2,1)}) custom-call(s32[2]{0:T(128)S(1)} %get-tuple-element.540.scal, bf16[512,1536]{1,0:T(8,128)(2,1)S(1)} %get-tuple-element.541.pair_ref, bf16[512,1536]{1,0:T(8,128)(2,1)} %get-tuple-element.542.core_ref, f32[1,512]{1,0:T(1,128)S(1)} %bitcast.38, ...), custom_call_target="tpu_custom_call" | custom-call | tf_op jit(solution)/shard_map/cond/branch_1_fun/project/pallas_call | solution.py:591
  62.5 8.9 %attend.1 = bf16[1024,384]{1,0:T(8,128)(2,1)} custom-call(s32[2]{0:T(128)S(1)} %get-tuple-element.540.scal, bf16[1024,384]{1,0:T(8,128)(2,1)} %get-tuple-element.1444.query_ref, bf16[1024,128]{1,0:T(8,128)(2,1)} %get-tuple-element.1445.own_ref, bf16[1024,128]{1,0:T(8,128)(2,1)} %collective-permute-done.3.other_ref, s32[1024,1]{1,0:T(8,128)} %get-tuple-element.557.start_ref), custom_call_target="tpu_custom_call" | custom-call | tf_op jit(solution)/shard_map/cond/branch_1_fun/attend/pallas_call | solution.py:392
  71.4 6.5 %out_rows.1 = (bf16[512,1536]{1,0:T(8,128)(2,1)}, bf16[512,1536]{1,0:T(8,128)(2,1)}) custom-call(s32[2]{0:T(128)S(1)} %pad_add_fusion.scal, bf16[1024,384]{1,0:T(8,128)(2,1)} %get-tuple-element.1196.context_ref, bf16[768,384]{1,0:T(8,128)(2,1)S(1)} %pad_maximum_fusion.4.refs_0_.refs_2_.refs_4_.refs_6_, ...), custom_call_target="tpu_custom_call" | custom-call | tf_op jit(solution)/shard_map/out_rows/pallas_call | solution.py:653
  78.0 6.7 %collective-permute-done.56 = bf16[384,1152]{1,0:T(8,128)(2,1)} collective-permute-done((bf16[384,1152]{1,0:T(8,128)(2,1)}, bf16[384,1152]{1,0:T(8,128)(2,1)}, u32[]{:S(2)}, u32[]{:S(2)}) %collective-permute-start.56) | collective-permute-done | bytes 884768 | tf_op jit(solution)/shard_map/ppermute | solution.py:121
  84.7 3.8 conditional.23
  91.2 27.9 %conditional.24 = ((f32[256,1536]{1,0:T(8,128)}, bf16[256,1536]{1,0:T(8,128)(2,1)})) conditional(s32[]{:T(128)} %convert_element_type.80, () %tuple.236, (s32[2]{0:T(128)S(1)}, bf16[512,1536]{1,0:T(8,128)(2,1)}, bf16[512,1536]{1,0:T(8,128)(2,1)}, f32[1536]{0:T(1024)S(1)}, bf16[256,1536]{1,0:T(8,128)(2,1)}) %tuple.332), branch_computations={%region_9.10_spmd, %region_10.11_spmd} | conditional | bytes 3158064 | solution.py:101
  91.2 3.4 fold_fixed.4
  94.7 3.5 collective-permute-start.6
  98.8 16.7 %collective-permute-done.6.arrived_ref = bf16[256,1536]{1,0:T(8,128)(2,1)} collective-permute-done((bf16[256,1536]{1,0:T(8,128)(2,1)}, bf16[256,1536]{1,0:T(8,128)(2,1)}, u32[]{:S(2)}, u32[]{:S(2)}) %collective-permute-start.6) | collective-permute-done | bytes 786464 | tf_op jit(solution)/shard_map/cond/branch_1_fun/ppermute | solution.py:121
  115.5 3.6 norm_two.1
  119.1 5.4 collective-permute-done.57
  125.1 23.4 %conditional.25 = (bf16[256,1536]{1,0:T(8,128)(2,1)}, bf16[256,1536]{1,0:T(8,128)(2,1)}, bf16[384,1152]{1,0:T(8,128)(2,1)}) conditional(s32[]{:T(128)} %convert_element_type.80, () %tuple.241, (bf16[256,1536]{1,0:T(8,128)(2,1)}, s32[2]{0:T(128)S(1)}, bf16[384,1152]{1,0:T(8,128)(2,1)}, bf16[384,1152]{1,0:T(8,128)(2,1)}) %tuple.242), branch_computations={%region_11.12_spmd, %region_12.13_spmd} | conditional | bytes 6291560 | solution.py:101
  125.1 3.2 collective-permute-start.7
  130.8 17.7 %collective-permute-done.8 = bf16[256,1536]{1,0:T(8,128)(2,1)} collective-permute-done((bf16[256,1536]{1,0:T(8,128)(2,1)}, bf16[256,1536]{1,0:T(8,128)(2,1)}, u32[]{:S(2)}, u32[]{:S(2)}) %collective-permute-start.8) | collective-permute-done | bytes 786464 | tf_op jit(solution)/shard_map/cond/branch_1_fun/ppermute | solution.py:121
  150.7 29.5 %conditional.26 = (bf16[128,1536]{1,0:T(8,128)(2,1)}, bf16[128,1536]{1,0:T(8,128)(2,1)}, bf16[256,1536]{1,0:T(8,128)(2,1)}, bf16[256,1536]{1,0:T(8,128)(2,1)}, b...) conditional(s32[]{:T(128)} %convert_element_type.80, () %tuple.244, ...), branch_computations={%region_13.14_spmd, %region_14.17_spmd} | conditional | flops 1 | bytes 17301892 | solution.py:101
  158.2 7.9 %conditional = (bf16[256,1536]{1,0:T(8,128)(2,1)}, bf16[256,1536]{1,0:T(8,128)(2,1)}, bf16[256,1536]{1,0:T(8,128)(2,1)}) conditional(s32[]{:T(128)} %convert_element_type.13, () %tuple.109, (bf16[256,1536]{1,0:T(8,128)(2,1)}, bf16[256,1536]{1,0:T(8,128)(2,1)}, bf16[256,1536]{1,0:T(8,128)(2,1)}) %tuple.110), branch_computations={%region_15.15_spmd, %region_16.16_spmd} | conditional | bytes 9437328 | solution.py:101
  166.1 11.5 %collective-permute-done.13 = bf16[128,1536]{1,0:T(8,128)(2,1)} collective-permute-done((bf16[128,1536]{1,0:T(8,128)(2,1)}, bf16[128,1536]{1,0:T(8,128)(2,1)}, u32[]{:S(2)}, u32[]{:S(2)}) %collective-permute-start.13) | collective-permute-done | bytes 393248 | tf_op jit(solution)/shard_map/cond/branch_1_fun/ppermute | solution.py:121
  180.3 22.0 %conditional.27 = (bf16[384,1152]{1,0:T(8,128)(2,1)}, bf16[256,1536]{1,0:T(8,128)(2,1)}, bf16[256,1536]{1,0:T(8,128)(2,1)}, bf16[1024,1536]{1,0:T(8,128)(2,1)}, ...) conditional(s32[]{:T(128)} %convert_element_type.80, () %tuple.225, ...), branch_computations={%region_17.18_spmd, %region_18.19_spmd} | conditional | bytes 12681286 | solution.py:101
  184.0 15.4 %ffn_up.2 = (bf16[1024,1536]{1,0:T(8,128)(2,1)}, bf16[1024,1152]{1,0:T(8,128)(2,1)}, bf16[1024,1152]{1,0:T(8,128)(2,1)}, bf16[1024,1152]{1,0:T(8,128)(2,1)}) custom-call(s32[2]{0:T(128)S(1)} %get-tuple-element.599.scal, bf16[256,1536]{1,0:T(8,128)(2,1)} %get-tuple-element.600.refs_0_, bf16[256,1536]{1,0:T(8,128)(2,1)} %get-tuple-element.601.refs_1_, ...), custom_call_target="tpu_custom_call" | custom-call | tf_op jit(solution)/shard_map/cond/branch_1_fun/ffn_up/pallas_call | solution.py:244
  202.3 30.7 %conditional.28 = (bf16[384,1152]{1,0:T(8,128)(2,1)}, bf16[256,1536]{1,0:T(8,128)(2,1)}, bf16[256,1536]{1,0:T(8,128)(2,1)}, bf16[1024,1536]{1,0:T(8,128)(2,1)}, ...) conditional(s32[]{:T(128)} %convert_element_type.80, () %tuple.248, ...), branch_computations={%region_19.20_spmd, %region_20.23_spmd} | conditional | flops 1 | bytes 18874732 | solution.py:101
  203.4 29.6 %conditional.1 = (bf16[256,1536]{1,0:T(8,128)(2,1)}, bf16[256,1536]{1,0:T(8,128)(2,1)}, bf16[1024,1536]{1,0:T(8,128)(2,1)}, bf16[1024,1152]{1,0:T(8,128)(2,1)}, ...) conditional(s32[]{:T(128)} %convert_element_type.16, () %tuple.120, ...), branch_computations={%region_21.21_spmd, %region_22.22_spmd} | conditional | bytes 15335504 | solution.py:101
  203.9 15.8 %ffn_up.3 = (bf16[1024,1536]{1,0:T(8,128)(2,1)}, bf16[1024,1152]{1,0:T(8,128)(2,1)}, bf16[1024,1152]{1,0:T(8,128)(2,1)}, bf16[1024,1152]{1,0:T(8,128)(2,1)}) custom-call(s32[2]{0:T(128)S(1)} %get-tuple-element.624.scal, bf16[256,1536]{1,0:T(8,128)(2,1)} %get-tuple-element.625.refs_0_, bf16[256,1536]{1,0:T(8,128)(2,1)} %get-tuple-element.626.refs_1_, ...), custom_call_target="tpu_custom_call" | custom-call | tf_op jit(solution)/shard_map/cond/branch_1_fun/cond/branch_1_fun/ffn_up/pallas_call | solution.py:244
  219.7 13.2 %grad_down.1 = (bf16[768,1152]{1,0:T(8,128)(2,1)}, bf16[768,1152]{1,0:T(8,128)(2,1)}) custom-call(s32[2]{0:T(128)S(1)} %get-tuple-element.624.scal, bf16[256,1536]{1,0:T(8,128)(2,1)} %get-tuple-element.647.refs_0_, bf16[256,1536]{1,0:T(8,128)(2,1)} %get-tuple-element.648.refs_1_, bf16[256,1536]{1,0:T(8,128)(2,1)} %get-tuple-element.649.refs_2_, ...), custom_call_target="tpu_custom_call" | custom-call | tf_op jit(solution)/shard_map/cond/branch_1_fun/cond/branch_1_fun/grad_down/pallas_call | solution.py:377
  234.0 54.5 %conditional.29 = (bf16[1024,1152]{1,0:T(8,128)(2,1)}, bf16[1024,1152]{1,0:T(8,128)(2,1)}, bf16[1024,1152]{1,0:T(8,128)(2,1)}, bf16[1024,1152]{1,0:T(8,128)(2,1)...) conditional(s32[]{:T(128)} %convert_element_type.80, () %tuple.251, ...), branch_computations={%region_23.24_spmd, %region_24.25_spmd} | conditional | bytes 14942304 | solution.py:101
  234.0 24.4 %ffn_back.3 = (bf16[1024,1152]{1,0:T(8,128)(2,1)}, bf16[1024,1152]{1,0:T(8,128)(2,1)}, bf16[1024,1536]{1,0:T(8,128)(2,1)}) custom-call(s32[2]{0:T(128)S(1)} %get-tuple-element.685.scal, bf16[256,1536]{1,0:T(8,128)(2,1)} %get-tuple-element.705.refs_0_, bf16[256,1536]{1,0:T(8,128)(2,1)} %get-tuple-element.706.refs_1_, ...), custom_call_target="tpu_custom_call" | custom-call | tf_op jit(solution)/shard_map/cond/branch_1_fun/ffn_back/pallas_call | solution.py:307
  258.4 24.6 %ffn_back.2 = (bf16[1024,1152]{1,0:T(8,128)(2,1)}, bf16[1024,1152]{1,0:T(8,128)(2,1)}, bf16[1024,1536]{1,0:T(8,128)(2,1)}) custom-call(s32[2]{0:T(128)S(1)} %get-tuple-element.685.scal, bf16[256,1536]{1,0:T(8,128)(2,1)} %get-tuple-element.686.refs_0_, bf16[256,1536]{1,0:T(8,128)(2,1)} %get-tuple-element.687.refs_1_, ...), custom_call_target="tpu_custom_call" | custom-call | tf_op jit(solution)/shard_map/cond/branch_1_fun/ffn_back/pallas_call | solution.py:307
  283.1 5.4 spread_eight.1
  288.5 87.1 %conditional.30 = (bf16[768,1152]{1,0:T(8,128)(2,1)}, bf16[768,1152]{1,0:T(8,128)(2,1)}, bf16[768,1152]{1,0:T(8,128)(2,1)}, bf16[768,1152]{1,0:T(8,128)(2,1)}, b...) conditional(s32[]{:T(128)} %convert_element_type.80, () %tuple.224, ...), branch_computations={%region_25.26_spmd, %region_26.35_spmd} | conditional | flops 3145730 | bytes 37602092 | solution.py:101
  288.5 21.9 %conditional.4 = (bf16[768,1152]{1,0:T(8,128)(2,1)}, bf16[768,1152]{1,0:T(8,128)(2,1)}, bf16[256,1536]{1,0:T(8,128)(2,1)}, bf16[256,1536]{1,0:T(8,128)(2,1)}) conditional(s32[]{:T(128)} %convert_element_type.18, () %tuple.143, (s32[2]{0:T(128)S(1)}, bf16[1024,1536]{1,0:T(8,128)(2,1)}, bf16[1024,1536]{1,0:T(8,128)(2,1)}, ...), branch_computations={%region_27.27_spmd, %region_28.28_spmd} | conditional | bytes 5111848 | solution.py:101
  294.2 12.8 %grad_gate.1 = (bf16[768,1152]{1,0:T(8,128)(2,1)}, bf16[768,1152]{1,0:T(8,128)(2,1)}) custom-call(s32[2]{0:T(128)S(1)} %get-tuple-element.720.scal, bf16[1024,1536]{1,0:T(8,128)(2,1)} %get-tuple-element.721.refs_0_, bf16[1024,1536]{1,0:T(8,128)(2,1)} %get-tuple-element.722.refs_1_, bf16[1024,1152]{1,0:T(8,128)(2,1)} %get-tuple-element.723.refs_2_, ...), custom_call_target="tpu_custom_call" | custom-call | tf_op jit(solution)/shard_map/cond/branch_1_fun/cond/branch_1_fun/grad_gate/pallas_call | solution.py:377
  307.0 3.4 spread_two.1
  311.0 64.5 %conditional.5 = (bf16[768,1152]{1,0:T(8,128)(2,1)}, bf16[768,1152]{1,0:T(8,128)(2,1)}, bf16[384,1152]{1,0:T(8,128)(2,1)}, bf16[384,1152]{1,0:T(8,128)(2,1)}, f3...) conditional(s32[]{:T(128)} %convert_element_type.18, () %tuple.145, ...), branch_computations={%region_29.29_spmd, %region_30.34_spmd} | conditional | flops 3145729 | bytes 19120516 | solution.py:101
  311.0 24.1 %conditional.2 = (bf16[768,1152]{1,0:T(8,128)(2,1)}, bf16[768,1152]{1,0:T(8,128)(2,1)}, bf16[384,1152]{1,0:T(8,128)(2,1)}, bf16[384,1152]{1,0:T(8,128)(2,1)}, f3...) conditional(s32[]{:T(128)} %convert_element_type.17, () %tuple.136, (s32[2]{0:T(128)S(1)}, ...), branch_computations={%region_31.30_spmd, %region_32.31_spmd} | conditional | bytes 7716938 | solution.py:101
  311.8 3.7 fold_sum.8
  315.5 12.9 %grad_up.1 = (bf16[768,1152]{1,0:T(8,128)(2,1)}, bf16[768,1152]{1,0:T(8,128)(2,1)}) custom-call(s32[2]{0:T(128)S(1)} %get-tuple-element.735.scal, bf16[1024,1536]{1,0:T(8,128)(2,1)} %get-tuple-element.736.refs_0_, bf16[1024,1536]{1,0:T(8,128)(2,1)} %get-tuple-element.737.refs_1_, bf16[1024,1152]{1,0:T(8,128)(2,1)} %get-tuple-element.738.refs_2_, ...), custom_call_target="tpu_custom_call" | custom-call | tf_op jit(solution)/shard_map/cond/branch_1_fun/cond/branch_1_fun/cond/branch_1_fun/grad_up/pallas_call | solution.py:377
  330.5 4.6 norm_two_back.1
  335.7 22.1 %conditional.3 = (bf16[512,1536]{1,0:T(8,128)(2,1)}, bf16[1024,1536]{1,0:T(8,128)(2,1)}, bf16[1024,1536]{1,0:T(8,128)(2,1)}) conditional(s32[]{:T(128)} %convert_element_type.17, () %tuple.138, (s32[2]{0:T(128)S(1)}, bf16[1024,1152]{1,0:T(8,128)(2,1)}, bf16[384,1152]{1,0:T(8,128)(2,1)}, bf16[384,1152]{1,0:T(8,128)(2,1)}, ...), branch_computations={%region_33.32_spmd, %region_34.33_spmd} | conditional | flops 3145728 | bytes 7864350 | solution.py:101
  337.2 9.0 %block_rows.2 = bf16[1024,1536]{1,0:T(8,128)(2,1)} custom-call(s32[2]{0:T(128)S(1)} %get-tuple-element.758.scal, bf16[1024,1152]{1,0:T(8,128)(2,1)} %get-tuple-element.759.left_ref, bf16[384,1152]{1,0:T(8,128)(2,1)} %get-tuple-element.760.refs_0_, bf16[384,1152]{1,0:T(8,128)(2,1)} %get-tuple-element.761.refs_1_, ...), custom_call_target="tpu_custom_call" | custom-call | tf_op jit(solution)/shard_map/cond/branch_1_fun/cond/branch_1_fun/cond/branch_1_fun/block_rows/pallas_call | solution.py:335
  346.3 9.0 %block_rows.3 = bf16[1024,1536]{1,0:T(8,128)(2,1)} custom-call(s32[2]{0:T(128)S(1)} %get-tuple-element.758.scal, bf16[1024,1152]{1,0:T(8,128)(2,1)} %get-tuple-element.764.left_ref, bf16[384,1152]{1,0:T(8,128)(2,1)} %get-tuple-element.760.refs_0_, bf16[384,1152]{1,0:T(8,128)(2,1)} %get-tuple-element.761.refs_1_, ...), custom_call_target="tpu_custom_call" | custom-call | tf_op jit(solution)/shard_map/cond/branch_1_fun/cond/branch_1_fun/cond/branch_1_fun/block_rows/pallas_call | solution.py:335
  357.8 17.8 %collective-permute-done.33 = bf16[384,1152]{1,0:T(8,128)(2,1)} collective-permute-done((bf16[384,1152]{1,0:T(8,128)(2,1)}, bf16[384,1152]{1,0:T(8,128)(2,1)}, u32[]{:S(2)}, u32[]{:S(2)}) %collective-permute-start.33) | collective-permute-done | bytes 884768 | tf_op jit(solution)/shard_map/cond/branch_1_fun/cond/branch_1_fun/ppermute | solution.py:121
  377.0 15.2 %conditional.31 = (bf16[512,1536]{1,0:T(8,128)(2,1)}, bf16[384,1152]{1,0:T(8,128)(2,1)}, bf16[384,1152]{1,0:T(8,128)(2,1)}, bf16[192,1152]{1,0:T(8,128)(2,1)}, b...) conditional(s32[]{:T(128)} %convert_element_type.80, () %tuple.223, ...), branch_computations={%region_35.36_spmd, %region_36.37_spmd} | conditional | bytes 18874504 | solution.py:101
  377.0 3.8 fold_sum.9
  386.8 5.3 fold_fixed.5
  393.6 45.8 %conditional.32 = (bf16[768,512]{1,0:T(8,128)(2,1)}, bf16[768,512]{1,0:T(8,128)(2,1)}, f32[256,1536]{1,0:T(8,128)}, bf16[256,1536]{1,0:T(8,128)(2,1)}, f32[8,153...) conditional(s32[]{:T(128)} %convert_element_type.80, () %tuple.259, ...), branch_computations={%region_37.38_spmd, %region_38.41_spmd} | conditional | flops 1 | bytes 13107589 | solution.py:101
  393.6 21.5 %attend_back.1 = (bf16[1024,384]{1,0:T(8,128)(2,1)}, f32[1024,128]{1,0:T(8,128)}, bf16[1024,128]{1,0:T(8,128)(2,1)}, f32[8,640]{1,0:T(8,128)}, bf16[768,384]{1,0:T(8,128)(2,1)}, /*index=5*/bf16[768,384]{1,0:T(8,128)(2,1)}) custom-call(s32[2]{0:T(128)S(1)} %get-tuple-element.887.scal, bf16[1024,384]{1,0:T(8,128)(2,1)} %get-tuple-element.888.query_ref, ...), custom_call_target="tpu_custom_call" | custom-call | tf_op jit(solution)/shard_map/cond/branch_1_fun/attend_back/pallas_call | solution.py:728
  415.7 20.6 %conditional.6 = (bf16[768,512]{1,0:T(8,128)(2,1)}, bf16[768,512]{1,0:T(8,128)(2,1)}, f32[256,1536]{1,0:T(8,128)}, bf16[256,1536]{1,0:T(8,128)(2,1)}, f32[8,1536]{1,0:T(8,128)}) conditional(s32[]{:T(128)} %convert_element_type.19, () %tuple.158, (bf16[1024,128]{1,0:T(8,128)(2,1)}, s32[2]{0:T(128)S(1)}, bf16[1024,384]{1,0:T(8,128)(2,1)}, ...), branch_computations={%region_39.39_spmd, %region_40.40_spmd} | conditional | bytes 8388756 | solution.py:101
  418.2 8.6 %project_back.1 = (bf16[1024,512]{1,0:T(8,128)(2,1)}, bf16[512,1536]{1,0:T(8,128)(2,1)}, bf16[512,1536]{1,0:T(8,128)(2,1)}, f32[8,1536]{1,0:T(8,128)}) custom-call(s32[2]{0:T(128)S(1)} %get-tuple-element.865.scal, bf16[1024,384]{1,0:T(8,128)(2,1)} %get-tuple-element.868.query_ref, f32[1024,128]{1,0:T(8,128)} %get-tuple-element.869.kept_kv_ref, ...), custom_call_target="tpu_custom_call" | custom-call | tf_op jit(solution)/shard_map/cond/branch_1_fun/cond/branch_1_fun/project_back/pallas_call | solution.py:786
  427.0 5.8 %project_grad.1 = (bf16[768,512]{1,0:T(8,128)(2,1)}, bf16[768,512]{1,0:T(8,128)(2,1)}) custom-call(s32[2]{0:T(128)S(1)} %get-tuple-element.865.scal, bf16[512,1536]{1,0:T(8,128)(2,1)S(1)} %get-tuple-element.866.pair_ref, bf16[512,1536]{1,0:T(8,128)(2,1)} %get-tuple-element.867.core_ref, bf16[1024,512]{1,0:T(8,128)(2,1)} %get-tuple-element.878.grads_ref), custom_call_target="tpu_custom_call" | custom-call | tf_op jit(solution)/shard_map/cond/branch_1_fun/cond/branch_1_fun/project_grad/pallas_call | solution.py:814
  432.8 3.5 fold_fixed.6
  439.4 3.7 fold_sum.14
  446.1 37.9 %conditional.33 = (bf16[256,1536]{1,0:T(8,128)(2,1)}, f32[32,160]{1,0:T(8,128)S(1)}, bf16[192,1152]{1,0:T(8,128)(2,1)S(1)}, bf16[192,1152]{1,0:T(8,128)(2,1)}, f...) conditional(s32[]{:T(128)} %convert_element_type.80, () %tuple.258, ...), branch_computations={%region_41.42_spmd, %region_42.43_spmd} | conditional | flops 16908 | bytes 9394574 | solution.py:101
  457.0 3.9 fold_fixed.7
  461.0 6.5 %collective-permute-done.42.arrived_ref = bf16[256,1536]{1,0:T(8,128)(2,1)} collective-permute-done((bf16[256,1536]{1,0:T(8,128)(2,1)}, bf16[256,1536]{1,0:T(8,128)(2,1)}, u32[]{:S(2)}, u32[]{:S(2)}) %collective-permute-start.42) | collective-permute-done | bytes 786464 | tf_op jit(solution)/shard_map/cond/branch_1_fun/ppermute | solution.py:121
  467.4 3.8 norm_one_back.1
  472.7 8.9 %collective-permute-done.45 = bf16[192,1152]{1,0:T(8,128)(2,1)} collective-permute-done((bf16[192,1152]{1,0:T(8,128)(2,1)}, bf16[192,1152]{1,0:T(8,128)(2,1)}, u32[]{:S(2)}, u32[]{:S(2)}) %collective-permute-start.45) | collective-permute-done | bytes 442400 | tf_op jit(solution)/shard_map/cond/branch_1_fun/ppermute | solution.py:121
  484.6 4.0 all-to-all-start
  488.6 52.0 %conditional.34 = (f32[2240,192]{0,1:T(8,128)}, f32[192,2240]{1,0:T(8,128)}, bf16[256,1536]{1,0:T(8,128)(2,1)}, f32[192,384]{1,0:T(8,128)}, f32[384,192]{0,1:T(8,128)}, /*index=5*/f32[48,512]{1,0:T(8,128)}) conditional(s32[]{:T(128)} %convert_element_type.80, () %tuple.222, (s32[2]{0:T(128)S(1)}, bf16[192,1152]{1,0:T(8,128)(2,1)}, ...), branch_computations={%region_43.44_spmd, %region_44.45_spmd} | conditional | flops 3293317 | bytes 24430296 | solution.py:101
  494.6 6.7 %collective-permute-done.35 = bf16[384,512]{1,0:T(8,128)(2,1)} collective-permute-done((bf16[384,512]{1,0:T(8,128)(2,1)}, bf16[384,512]{1,0:T(8,128)(2,1)}, u32[]{:S(2)}, u32[]{:S(2)}) %collective-permute-start.35) | collective-permute-done | bytes 393248 | tf_op jit(solution)/shard_map/cond/branch_1_fun/ppermute | solution.py:121
  506.5 19.0 %collective-permute-done.36 = bf16[256,1536]{1,0:T(8,128)(2,1)} collective-permute-done((bf16[256,1536]{1,0:T(8,128)(2,1)}, bf16[256,1536]{1,0:T(8,128)(2,1)}, u32[]{:S(2)}, u32[]{:S(2)}) %collective-permute-start.36) | collective-permute-done | bytes 786464 | tf_op jit(solution)/shard_map/cond/branch_1_fun/ppermute | solution.py:121
  545.7 9.4 %collective-permute-done.69.theirs_ref = bf16[192,1152]{1,0:T(8,128)(2,1)S(1)} collective-permute-done((bf16[192,1152]{1,0:T(8,128)(2,1)}, bf16[192,1152]{1,0:T(8,128)(2,1)S(1)}, u32[]{:S(2)}, u32[]{:S(2)}) %collective-permute-start.69) | collective-permute-done | bytes 442400 | tf_op jit(solution)/shard_map/ppermute | solution.py:121
  (250 shorter events, 166.6 us)
Async XLA Ops:
  2.6 14.1 %collective-permute-start.48 = (bf16[192,512]{1,0:T(8,128)(2,1)S(1)}, bf16[192,512]{1,0:T(8,128)(2,1)S(1)}, u32[]{:S(2)}, u32[]{:S(2)}) collective-permute-start(bf16[192,512]{1,0:T(8,128)(2,1)S(1)} %pad_maximum_fusion.8), channel_id=1, source_target_pairs={{0,4},{4,0},{8,12},{12,8},{16,20},{20,16},{24,28},{28,24},{1,5},{5... | collective-permute-start | bytes 589832 | tf_op jit(solution)/shard_map/ppermute | solution.py:121
  5.6 11.0 %collective-permute-start.47 = (bf16[192,512]{1,0:T(8,128)(2,1)S(1)}, bf16[192,512]{1,0:T(8,128)(2,1)S(1)}, u32[]{:S(2)}, u32[]{:S(2)}) collective-permute-start(bf16[192,512]{1,0:T(8,128)(2,1)S(1)} %pad_maximum_fusion.8), channel_id=1, source_target_pairs={{0,8},{4,12},{8,0},{12,4},{16,24},{20,28},{24,16},{28,20},{1,9},{5... | collective-permute-start | bytes 589832 | tf_op jit(solution)/shard_map/ppermute | solution.py:121
  7.2 10.8 %collective-permute-start.46 = (bf16[192,512]{1,0:T(8,128)(2,1)S(1)}, bf16[192,512]{1,0:T(8,128)(2,1)}, u32[]{:S(2)}, u32[]{:S(2)}) collective-permute-start(bf16[192,512]{1,0:T(8,128)(2,1)S(1)} %pad_maximum_fusion.8), channel_id=1, source_target_pairs={{0,16},{4,20},{8,24},{12,28},{16,0},{20,4},{24,8},{28,12},{1,17},{... | collective-permute-start | bytes 589832 | tf_op jit(solution)/shard_map/ppermute | solution.py:121
  12.1 21.0 %collective-permute-start.51 = (bf16[256,1536]{1,0:T(8,128)(2,1)S(1)}, bf16[256,1536]{1,0:T(8,128)(2,1)}, u32[]{:S(2)}, u32[]{:S(2)}) collective-permute-start(bf16[256,1536]{1,0:T(8,128)(2,1)S(1)} %fusion.3), channel_id=1, source_target_pairs={{0,2},{1,3},{2,0},{3,1},{4,6},{5,7},{6,4},{7,5},{8,10},{9,11},{10,... | collective-permute-start | bytes 2359304 | tf_op jit(solution)/shard_map/ppermute | solution.py:121
  16.2 18.6 %collective-permute-start.52 = (bf16[192,1152]{1,0:T(8,128)(2,1)}, bf16[192,1152]{1,0:T(8,128)(2,1)}, u32[]{:S(2)}, u32[]{:S(2)}) collective-permute-start(bf16[192,1152]{1,0:T(8,128)(2,1)} %get-tuple-element.1167), channel_id=1, source_target_pairs={{0,8},{4,12},{8,0},{12,4},{16,24},{20,28},{24,16},{28,20},{1,9},{5... | collective-permute-start | bytes 1327112 | tf_op jit(solution)/shard_map/ppermute | solution.py:121
  18.7 13.7 %collective-permute-start.53 = (bf16[192,384]{1,0:T(8,128)(2,1)S(1)}, bf16[192,384]{1,0:T(8,128)(2,1)S(1)}, u32[]{:S(2)}, u32[]{:S(2)}) collective-permute-start(bf16[192,384]{1,0:T(8,128)(2,1)S(1)} %bitcast.34), channel_id=1, source_target_pairs={{0,16},{4,20},{8,24},{12,28},{16,0},{20,4},{24,8},{28,12},{1,17},{... | collective-permute-start | bytes 442376 | tf_op jit(solution)/shard_map/ppermute | solution.py:121
  19.6 15.1 %collective-permute-start.50 = (bf16[192,512]{1,0:T(8,128)(2,1)}, bf16[192,512]{1,0:T(8,128)(2,1)}, u32[]{:S(2)}, u32[]{:S(2)}) collective-permute-start(bf16[192,512]{1,0:T(8,128)(2,1)} %collective-permute-done.46), channel_id=1, source_target_pairs={{0,8},{4,12},{8,0},{12,4},{16,24},{20,28},{24,16},{28,20},{1,9},{5... | collective-permute-start | bytes 589832 | tf_op jit(solution)/shard_map/ppermute | solution.py:121
  24.2 10.6 %collective-permute-start.49 = (bf16[384,512]{1,0:T(8,128)(2,1)}, bf16[384,512]{1,0:T(8,128)(2,1)S(1)}, u32[]{:S(2)}, u32[]{:S(2)}) collective-permute-start(bf16[384,512]{1,0:T(8,128)(2,1)} %pad_maximum_fusion.6), channel_id=1, source_target_pairs={{0,4},{4,0},{8,12},{12,8},{16,20},{20,16},{24,28},{28,24},{1,5},{5... | collective-permute-start | bytes 1179656 | tf_op jit(solution)/shard_map/ppermute | solution.py:121
  37.2 9.5 %collective-permute-start.1 = (bf16[512,1536]{1,0:T(8,128)(2,1)S(1)}, bf16[512,1536]{1,0:T(8,128)(2,1)}, u32[]{:S(2)}, u32[]{:S(2)}) collective-permute-start(bf16[512,1536]{1,0:T(8,128)(2,1)S(1)} %get-tuple-element.538), channel_id=1, source_target_pairs={{0,1},{1,0},{2,3},{3,2},{4,5},{5,4},{6,7},{7,6},{8,9},{9,8},{10,11... | collective-permute-start | bytes 4718600 | tf_op jit(solution)/shard_map/cond/branch_1_fun/ppermute | solution.py:121
  37.2 9.5 %collective-permute-start.2 = (bf16[384,384]{1,0:T(8,128)(2,1)S(1)}, bf16[384,384]{1,0:T(8,128)(2,1)}, u32[]{:S(2)}, u32[]{:S(2)}) collective-permute-start(bf16[384,384]{1,0:T(8,128)(2,1)S(1)} %get-tuple-element.539), channel_id=1, source_target_pairs={{0,8},{4,12},{8,0},{12,4},{16,24},{20,28},{24,16},{28,20},{1,9},{5... | collective-permute-start | bytes 884744 | tf_op jit(solution)/shard_map/cond/branch_1_fun/ppermute | solution.py:121
  37.8 7.3 %collective-permute-start = (bf16[192,512]{1,0:T(8,128)(2,1)}, bf16[192,512]{1,0:T(8,128)(2,1)}, u32[]{:S(2)}, u32[]{:S(2)}) collective-permute-start(bf16[192,512]{1,0:T(8,128)(2,1)} %get-tuple-element.537), channel_id=1, source_target_pairs={{0,4},{4,0},{8,12},{12,8},{16,20},{20,16},{24,28},{28,24},{1,5},{5... | collective-permute-start | bytes 589832 | tf_op jit(solution)/shard_map/cond/branch_1_fun/ppermute | solution.py:121
  47.7 37.0 %collective-permute-start.56 = (bf16[384,1152]{1,0:T(8,128)(2,1)}, bf16[384,1152]{1,0:T(8,128)(2,1)}, u32[]{:S(2)}, u32[]{:S(2)}) collective-permute-start(bf16[384,1152]{1,0:T(8,128)(2,1)} %get-tuple-element.1199), channel_id=1, source_target_pairs={{0,8},{4,12},{8,0},{12,4},{16,24},{20,28},{24,16},{28,20},{1,9},{5... | collective-permute-start | bytes 2654216 | tf_op jit(solution)/shard_map/ppermute | solution.py:121
  48.4 29.6 %collective-permute-start.54 = (bf16[256,1536]{1,0:T(8,128)(2,1)}, bf16[256,1536]{1,0:T(8,128)(2,1)}, u32[]{:S(2)}, u32[]{:S(2)}) collective-permute-start(bf16[256,1536]{1,0:T(8,128)(2,1)} %param.67), channel_id=1, source_target_pairs={{0,2},{1,3},{2,0},{3,1},{4,6},{5,7},{6,4},{7,5},{8,10},{9,11},{10,... | collective-permute-start | bytes 2359304 | tf_op jit(solution)/shard_map/ppermute | solution.py:121
  49.8 21.6 %collective-permute-start.55 = (bf16[768,384]{1,0:T(8,128)(2,1)S(1)}, bf16[768,384]{1,0:T(8,128)(2,1)S(1)}, u32[]{:S(2)}, u32[]{:S(2)}) collective-permute-start(bf16[768,384]{1,0:T(8,128)(2,1)S(1)} %pad_maximum_fusion.4.refs_0_.refs_2_.refs_4_.refs_6_), channel_id=1, source_target_pairs={{0,4},{4,0},{8,12},{12,8},{16,20},{20,16},{24,28},{28,24},{1,5},{5... | collective-permute-start | bytes 1769480 | tf_op jit(solution)/shard_map/ppermute | solution.py:121
  51.9 67.2 %collective-permute-start.58 = (bf16[384,1152]{1,0:T(8,128)(2,1)}, bf16[384,1152]{1,0:T(8,128)(2,1)}, u32[]{:S(2)}, u32[]{:S(2)}) collective-permute-start(bf16[384,1152]{1,0:T(8,128)(2,1)} %join_rows.3), channel_id=1, source_target_pairs={{0,16},{4,20},{8,24},{12,28},{16,0},{20,4},{24,8},{28,12},{1,17},{... | collective-permute-start | bytes 2654216 | tf_op jit(solution)/shard_map/ppermute | solution.py:121
  62.4 9.1 %collective-permute-start.4 = (bf16[256,1536]{1,0:T(8,128)(2,1)}, bf16[256,1536]{1,0:T(8,128)(2,1)}, u32[]{:S(2)}, u32[]{:S(2)}) collective-permute-start(bf16[256,1536]{1,0:T(8,128)(2,1)} %get-tuple-element.558), channel_id=1, source_target_pairs={{0,1},{1,0},{2,3},{3,2},{4,5},{5,4},{6,7},{7,6},{8,9},{9,8},{10,11... | collective-permute-start | bytes 2359304 | tf_op jit(solution)/shard_map/cond/branch_1_fun/ppermute | solution.py:121
  84.7 3.8 collective-permute-start.5
  88.5 60.2 %collective-permute-start.59 = (bf16[768,1152]{1,0:T(8,128)(2,1)}, bf16[768,1152]{1,0:T(8,128)(2,1)S(1)}, u32[]{:S(2)}, u32[]{:S(2)}) collective-permute-start(bf16[768,1152]{1,0:T(8,128)(2,1)} %get-tuple-element.1208), channel_id=1, source_target_pairs={{0,4},{4,0},{8,12},{12,8},{16,20},{20,16},{24,28},{28,24},{1,5},{5... | collective-permute-start | bytes 5308424 | tf_op jit(solution)/shard_map/ppermute | solution.py:121
  90.5 34.0 %collective-permute-start.57 = (bf16[256,1536]{1,0:T(8,128)(2,1)}, bf16[256,1536]{1,0:T(8,128)(2,1)}, u32[]{:S(2)}, u32[]{:S(2)}) collective-permute-start(bf16[256,1536]{1,0:T(8,128)(2,1)} %param.67), channel_id=1, source_target_pairs={{0,8},{4,12},{8,0},{12,4},{16,24},{20,28},{24,16},{28,20},{1,9},{5... | collective-permute-start | bytes 2359304 | tf_op jit(solution)/shard_map/ppermute | solution.py:121
  90.5 58.0 %collective-permute-start.61 = (bf16[384,1152]{1,0:T(8,128)(2,1)}, bf16[384,1152]{1,0:T(8,128)(2,1)}, u32[]{:S(2)}, u32[]{:S(2)}) collective-permute-start(bf16[384,1152]{1,0:T(8,128)(2,1)} %get-tuple-element.1213), channel_id=1, source_target_pairs={{0,16},{4,20},{8,24},{12,28},{16,0},{20,4},{24,8},{28,12},{1,17},{... | collective-permute-start | bytes 2654216 | tf_op jit(solution)/shard_map/ppermute | solution.py:121
  94.7 20.9 %collective-permute-start.6 = (bf16[256,1536]{1,0:T(8,128)(2,1)}, bf16[256,1536]{1,0:T(8,128)(2,1)}, u32[]{:S(2)}, u32[]{:S(2)}) collective-permute-start(bf16[256,1536]{1,0:T(8,128)(2,1)} %get-tuple-element.573), channel_id=1, source_target_pairs={{0,2},{1,3},{2,0},{3,1},{4,6},{5,7},{6,4},{7,5},{8,10},{9,11},{10,... | collective-permute-start | bytes 2359304 | tf_op jit(solution)/shard_map/cond/branch_1_fun/ppermute | solution.py:121
  124.5 24.2 %collective-permute-start.60 = (bf16[384,1152]{1,0:T(8,128)(2,1)}, bf16[384,1152]{1,0:T(8,128)(2,1)}, u32[]{:S(2)}, u32[]{:S(2)}) collective-permute-start(bf16[384,1152]{1,0:T(8,128)(2,1)} %collective-permute-done.58), channel_id=1, source_target_pairs={{0,4},{4,0},{8,12},{12,8},{16,20},{20,16},{24,28},{28,24},{1,5},{5... | collective-permute-start | bytes 2654216 | tf_op jit(solution)/shard_map/ppermute | solution.py:121
  125.1 23.4 %collective-permute-start.8 = (bf16[256,1536]{1,0:T(8,128)(2,1)}, bf16[256,1536]{1,0:T(8,128)(2,1)}, u32[]{:S(2)}, u32[]{:S(2)}) collective-permute-start(bf16[256,1536]{1,0:T(8,128)(2,1)} %get-tuple-element.575), channel_id=1, source_target_pairs={{0,8},{4,12},{8,0},{12,4},{16,24},{20,28},{24,16},{28,20},{1,9},{5... | collective-permute-start | bytes 2359304 | tf_op jit(solution)/shard_map/cond/branch_1_fun/ppermute | solution.py:121
  125.1 23.4 %collective-permute-start.7 = (bf16[256,1536]{1,0:T(8,128)(2,1)}, bf16[256,1536]{1,0:T(8,128)(2,1)}, u32[]{:S(2)}, u32[]{:S(2)}) collective-permute-start(bf16[256,1536]{1,0:T(8,128)(2,1)} %get-tuple-element.575), channel_id=1, source_target_pairs={{0,2},{1,3},{2,0},{3,1},{4,6},{5,7},{6,4},{7,5},{8,10},{9,11},{10,... | collective-permute-start | bytes 2359304 | tf_op jit(solution)/shard_map/cond/branch_1_fun/ppermute | solution.py:121
  148.7 31.6 %collective-permute-start.62 = (bf16[384,1152]{1,0:T(8,128)(2,1)}, bf16[384,1152]{1,0:T(8,128)(2,1)}, u32[]{:S(2)}, u32[]{:S(2)}) collective-permute-start(bf16[384,1152]{1,0:T(8,128)(2,1)} %collective-permute-done.61), channel_id=1, source_target_pairs={{0,4},{4,0},{8,12},{12,8},{16,20},{20,16},{24,28},{28,24},{1,5},{5... | collective-permute-start | bytes 2654216 | tf_op jit(solution)/shard_map/ppermute | solution.py:121
  150.5 51.8 %collective-permute-start.63 = (bf16[384,1152]{1,0:T(8,128)(2,1)}, bf16[384,1152]{1,0:T(8,128)(2,1)}, u32[]{:S(2)}, u32[]{:S(2)}) collective-permute-start(bf16[384,1152]{1,0:T(8,128)(2,1)} %get-tuple-element.1224), channel_id=1, source_target_pairs={{0,16},{4,20},{8,24},{12,28},{16,0},{20,4},{24,8},{28,12},{1,17},{... | collective-permute-start | bytes 2654216 | tf_op jit(solution)/shard_map/ppermute | solution.py:121
  152.5 25.1 %collective-permute-start.13 = (bf16[128,1536]{1,0:T(8,128)(2,1)}, bf16[128,1536]{1,0:T(8,128)(2,1)}, u32[]{:S(2)}, u32[]{:S(2)}) collective-permute-start(bf16[128,1536]{1,0:T(8,128)(2,1)} %slice.40), channel_id=1, source_target_pairs={{0,8},{4,12},{8,0},{12,4},{16,24},{20,28},{24,16},{28,20},{1,9},{5... | collective-permute-start | bytes 1179656 | tf_op jit(solution)/shard_map/cond/branch_1_fun/ppermute | solution.py:121
  155.3 22.3 %collective-permute-start.12 = (bf16[128,1536]{1,0:T(8,128)(2,1)}, bf16[128,1536]{1,0:T(8,128)(2,1)}, u32[]{:S(2)}, u32[]{:S(2)}) collective-permute-start(bf16[128,1536]{1,0:T(8,128)(2,1)} %slice.39), channel_id=1, source_target_pairs={{0,2},{1,3},{2,0},{3,1},{4,6},{5,7},{6,4},{7,5},{8,10},{9,11},{10,... | collective-permute-start | bytes 1179656 | tf_op jit(solution)/shard_map/cond/branch_1_fun/ppermute | solution.py:121
  158.2 2.6 collective-permute-start.9
  180.3 22.0 %collective-permute-start.16 = (bf16[384,1152]{1,0:T(8,128)(2,1)}, bf16[384,1152]{1,0:T(8,128)(2,1)}, u32[]{:S(2)}, u32[]{:S(2)}) collective-permute-start(bf16[384,1152]{1,0:T(8,128)(2,1)} %get-tuple-element.616), channel_id=1, source_target_pairs={{0,4},{4,0},{8,12},{12,8},{16,20},{20,16},{24,28},{28,24},{1,5},{5... | collective-permute-start | bytes 2654216 | tf_op jit(solution)/shard_map/cond/branch_1_fun/ppermute | solution.py:121
  180.9 21.0 %collective-permute-start.17 = (bf16[256,1536]{1,0:T(8,128)(2,1)}, bf16[256,1536]{1,0:T(8,128)(2,1)}, u32[]{:S(2)}, u32[]{:S(2)}) collective-permute-start(bf16[256,1536]{1,0:T(8,128)(2,1)} %get-tuple-element.617), channel_id=1, source_target_pairs={{0,2},{1,3},{2,0},{3,1},{4,6},{5,7},{6,4},{7,5},{8,10},{9,11},{10,... | collective-permute-start | bytes 2359304 | tf_op jit(solution)/shard_map/cond/branch_1_fun/ppermute | solution.py:121
  184.0 17.9 %collective-permute-start.18 = (bf16[256,1536]{1,0:T(8,128)(2,1)}, bf16[256,1536]{1,0:T(8,128)(2,1)}, u32[]{:S(2)}, u32[]{:S(2)}) collective-permute-start(bf16[256,1536]{1,0:T(8,128)(2,1)} %get-tuple-element.618), channel_id=1, source_target_pairs={{0,1},{1,0},{2,3},{3,2},{4,5},{5,4},{6,7},{7,6},{8,9},{9,8},{10,11... | collective-permute-start | bytes 2359304 | tf_op jit(solution)/shard_map/cond/branch_1_fun/ppermute | solution.py:121
  202.3 30.7 %collective-permute-start.21 = (bf16[384,1152]{1,0:T(8,128)(2,1)}, bf16[384,1152]{1,0:T(8,128)(2,1)}, u32[]{:S(2)}, u32[]{:S(2)}) collective-permute-start(bf16[384,1152]{1,0:T(8,128)(2,1)} %get-tuple-element.655), channel_id=1, source_target_pairs={{0,4},{4,0},{8,12},{12,8},{16,20},{20,16},{24,28},{28,24},{1,5},{5... | collective-permute-start | bytes 2654216 | tf_op jit(solution)/shard_map/cond/branch_1_fun/ppermute | solution.py:121
  203.4 16.3 %collective-permute-start.19 = (bf16[256,1536]{1,0:T(8,128)(2,1)}, bf16[256,1536]{1,0:T(8,128)(2,1)}, u32[]{:S(2)}, u32[]{:S(2)}) collective-permute-start(bf16[256,1536]{1,0:T(8,128)(2,1)} %get-tuple-element.622), channel_id=1, source_target_pairs={{0,1},{1,0},{2,3},{3,2},{4,5},{5,4},{6,7},{7,6},{8,9},{9,8},{10,11... | collective-permute-start | bytes 2359304 | tf_op jit(solution)/shard_map/cond/branch_1_fun/cond/branch_1_fun/ppermute | solution.py:121
  203.4 16.3 %collective-permute-start.20 = (bf16[256,1536]{1,0:T(8,128)(2,1)}, bf16[256,1536]{1,0:T(8,128)(2,1)}, u32[]{:S(2)}, u32[]{:S(2)}) collective-permute-start(bf16[256,1536]{1,0:T(8,128)(2,1)} %get-tuple-element.623.refs_3_), channel_id=1, source_target_pairs={{0,1},{1,0},{2,3},{3,2},{4,5},{5,4},{6,7},{7,6},{8,9},{9,8},{10,11... | collective-permute-start | bytes 2359304 | tf_op jit(solution)/shard_map/cond/branch_1_fun/cond/branch_1_fun/ppermute | solution.py:121
  233.0 55.5 %collective-permute-start.64 = (bf16[768,1152]{1,0:T(8,128)(2,1)}, bf16[768,1152]{1,0:T(8,128)(2,1)}, u32[]{:S(2)}, u32[]{:S(2)}) collective-permute-start(bf16[768,1152]{1,0:T(8,128)(2,1)} %get-tuple-element.1255), channel_id=1, source_target_pairs={{0,4},{4,0},{8,12},{12,8},{16,20},{20,16},{24,28},{28,24},{1,5},{5... | collective-permute-start | bytes 5308424 | tf_op jit(solution)/shard_map/ppermute | solution.py:121
  258.4 24.7 %collective-permute-start.22 = (bf16[1024,1536]{1,0:T(8,128)(2,1)}, bf16[1024,1536]{1,0:T(8,128)(2,1)}, u32[]{:S(2)}, u32[]{:S(2)}) collective-permute-start(bf16[1024,1536]{1,0:T(8,128)(2,1)} %get-tuple-element.714), channel_id=1, source_target_pairs={{0,1},{1,0},{2,3},{3,2},{4,5},{5,4},{6,7},{7,6},{8,9},{9,8},{10,11... | collective-permute-start | bytes 9437192 | tf_op jit(solution)/shard_map/cond/branch_1_fun/ppermute | solution.py:121
  288.5 18.5 %collective-permute-start.23 = (bf16[128,1536]{1,0:T(8,128)(2,1)}, bf16[128,1536]{1,0:T(8,128)(2,1)}, u32[]{:S(2)}, u32[]{:S(2)}) collective-permute-start(bf16[128,1536]{1,0:T(8,128)(2,1)} %get-tuple-element.729), channel_id=1, source_target_pairs={{0,2},{1,3},{2,0},{3,1},{4,6},{5,7},{6,4},{7,5},{8,10},{9,11},{10,... | collective-permute-start | bytes 1179656 | tf_op jit(solution)/shard_map/cond/branch_1_fun/cond/branch_1_fun/ppermute | solution.py:121
  291.7 15.3 %collective-permute-start.24 = (bf16[128,1536]{1,0:T(8,128)(2,1)}, bf16[128,1536]{1,0:T(8,128)(2,1)}, u32[]{:S(2)}, u32[]{:S(2)}) collective-permute-start(bf16[128,1536]{1,0:T(8,128)(2,1)} %get-tuple-element.730), channel_id=1, source_target_pairs={{0,8},{4,12},{8,0},{12,4},{16,24},{20,28},{24,16},{28,20},{1,9},{5... | collective-permute-start | bytes 1179656 | tf_op jit(solution)/shard_map/cond/branch_1_fun/cond/branch_1_fun/ppermute | solution.py:121
  310.4 65.1 %collective-permute-start.34 = (bf16[768,1152]{1,0:T(8,128)(2,1)}, bf16[768,1152]{1,0:T(8,128)(2,1)}, u32[]{:S(2)}, u32[]{:S(2)}) collective-permute-start(bf16[768,1152]{1,0:T(8,128)(2,1)} %get-tuple-element.837), channel_id=1, source_target_pairs={{0,4},{4,0},{8,12},{12,8},{16,20},{20,16},{24,28},{28,24},{1,5},{5... | collective-permute-start | bytes 5308424 | tf_op jit(solution)/shard_map/cond/branch_1_fun/ppermute | solution.py:121
  311.0 19.4 %collective-permute-start.25 = (bf16[256,1536]{1,0:T(8,128)(2,1)}, bf16[256,1536]{1,0:T(8,128)(2,1)}, u32[]{:S(2)}, u32[]{:S(2)}) collective-permute-start(bf16[256,1536]{1,0:T(8,128)(2,1)} %get-tuple-element.747), channel_id=1, source_target_pairs={{0,2},{1,3},{2,0},{3,1},{4,6},{5,7},{6,4},{7,5},{8,10},{9,11},{10,... | collective-permute-start | bytes 2359304 | tf_op jit(solution)/shard_map/cond/branch_1_fun/cond/branch_1_fun/cond/branch_1_fun/ppermute | solution.py:121
  311.1 19.4 %collective-permute-start.26 = (bf16[256,1536]{1,0:T(8,128)(2,1)}, bf16[256,1536]{1,0:T(8,128)(2,1)}, u32[]{:S(2)}, u32[]{:S(2)}) collective-permute-start(bf16[256,1536]{1,0:T(8,128)(2,1)} %get-tuple-element.748), channel_id=1, source_target_pairs={{0,8},{4,12},{8,0},{12,4},{16,24},{20,28},{24,16},{28,20},{1,9},{5... | collective-permute-start | bytes 2359304 | tf_op jit(solution)/shard_map/cond/branch_1_fun/cond/branch_1_fun/cond/branch_1_fun/ppermute | solution.py:121
  335.1 40.4 %collective-permute-start.33 = (bf16[384,1152]{1,0:T(8,128)(2,1)}, bf16[384,1152]{1,0:T(8,128)(2,1)}, u32[]{:S(2)}, u32[]{:S(2)}) collective-permute-start(bf16[384,1152]{1,0:T(8,128)(2,1)} %get-tuple-element.792), channel_id=1, source_target_pairs={{0,16},{4,20},{8,24},{12,28},{16,0},{20,4},{24,8},{28,12},{1,17},{... | collective-permute-start | bytes 2654216 | tf_op jit(solution)/shard_map/cond/branch_1_fun/cond/branch_1_fun/ppermute | solution.py:121
  335.7 19.7 %collective-permute-start.32 = (bf16[256,1536]{1,0:T(8,128)(2,1)}, bf16[256,1536]{1,0:T(8,128)(2,1)S(1)}, u32[]{:S(2)}, u32[]{:S(2)}) collective-permute-start(bf16[256,1536]{1,0:T(8,128)(2,1)} %get-tuple-element.757), channel_id=1, source_target_pairs={{0,2},{1,3},{2,0},{3,1},{4,6},{5,7},{6,4},{7,5},{8,10},{9,11},{10,... | collective-permute-start | bytes 2359304 | tf_op jit(solution)/shard_map/cond/branch_1_fun/cond/branch_1_fun/cond/branch_1_fun/ppermute | solution.py:121
  375.5 63.9 %collective-permute-start.65 = (bf16[768,1152]{1,0:T(8,128)(2,1)}, bf16[768,1152]{1,0:T(8,128)(2,1)}, u32[]{:S(2)}, u32[]{:S(2)}) collective-permute-start(bf16[768,1152]{1,0:T(8,128)(2,1)} %get-tuple-element.1281), channel_id=1, source_target_pairs={{0,4},{4,0},{8,12},{12,8},{16,20},{20,16},{24,28},{28,24},{1,5},{5... | collective-permute-start | bytes 5308424 | tf_op jit(solution)/shard_map/ppermute | solution.py:121
  377.0 3.8 collective-permute-start.27
  380.8 6.0 %collective-permute-start.28 = (bf16[1024,1536]{1,0:T(8,128)(2,1)}, bf16[1024,1536]{1,0:T(8,128)(2,1)}, u32[]{:S(2)}, u32[]{:S(2)}) collective-permute-start(bf16[1024,1536]{1,0:T(8,128)(2,1)} %get-tuple-element.861), channel_id=1, source_target_pairs={{0,1},{1,0},{2,3},{3,2},{4,5},{5,4},{6,7},{7,6},{8,9},{9,8},{10,11... | collective-permute-start | bytes 9437192 | tf_op jit(solution)/shard_map/cond/branch_1_fun/ppermute | solution.py:121
  392.2 47.2 %collective-permute-start.66 = (bf16[512,1536]{1,0:T(8,128)(2,1)}, bf16[512,1536]{1,0:T(8,128)(2,1)}, u32[]{:S(2)}, u32[]{:S(2)}) collective-permute-start(bf16[512,1536]{1,0:T(8,128)(2,1)} %get-tuple-element.1293), channel_id=1, source_target_pairs={{0,2},{1,3},{2,0},{3,1},{4,6},{5,7},{6,4},{7,5},{8,10},{9,11},{10,... | collective-permute-start | bytes 4718600 | tf_op jit(solution)/shard_map/ppermute | solution.py:121
  393.5 49.6 %collective-permute-start.67 = (bf16[384,1152]{1,0:T(8,128)(2,1)}, bf16[384,1152]{1,0:T(8,128)(2,1)}, u32[]{:S(2)}, u32[]{:S(2)}) collective-permute-start(bf16[384,1152]{1,0:T(8,128)(2,1)} %get-tuple-element.1299), channel_id=1, source_target_pairs={{0,16},{4,20},{8,24},{12,28},{16,0},{20,4},{24,8},{28,12},{1,17},{... | collective-permute-start | bytes 2654216 | tf_op jit(solution)/shard_map/ppermute | solution.py:121
  415.0 21.3 %collective-permute-start.31 = (bf16[768,384]{1,0:T(8,128)(2,1)}, bf16[768,384]{1,0:T(8,128)(2,1)S(1)}, u32[]{:S(2)}, u32[]{:S(2)}) collective-permute-start(bf16[768,384]{1,0:T(8,128)(2,1)} %get-tuple-element.918), channel_id=1, source_target_pairs={{0,4},{4,0},{8,12},{12,8},{16,20},{20,16},{24,28},{28,24},{1,5},{5... | collective-permute-start | bytes 1769480 | tf_op jit(solution)/shard_map/cond/branch_1_fun/ppermute | solution.py:121
  426.8 6.0 %collective-permute-start.30 = (bf16[512,1536]{1,0:T(8,128)(2,1)}, bf16[512,1536]{1,0:T(8,128)(2,1)}, u32[]{:S(2)}, u32[]{:S(2)}) collective-permute-start(bf16[512,1536]{1,0:T(8,128)(2,1)} %get-tuple-element.882), channel_id=1, source_target_pairs={{0,1},{1,0},{2,3},{3,2},{4,5},{5,4},{6,7},{7,6},{8,9},{9,8},{10,11... | collective-permute-start | bytes 4718600 | tf_op jit(solution)/shard_map/cond/branch_1_fun/cond/branch_1_fun/ppermute | solution.py:121
  443.2 97.5 %collective-permute-start.68 = (bf16[384,1152]{1,0:T(8,128)(2,1)}, bf16[384,1152]{1,0:T(8,128)(2,1)}, u32[]{:S(2)}, u32[]{:S(2)}) collective-permute-start(bf16[384,1152]{1,0:T(8,128)(2,1)} %get-tuple-element.1329), channel_id=1, source_target_pairs={{0,16},{4,20},{8,24},{12,28},{16,0},{20,4},{24,8},{28,12},{1,17},{... | collective-permute-start | bytes 2654216 | tf_op jit(solution)/shard_map/ppermute | solution.py:121
  446.1 26.7 %collective-permute-start.44 = (bf16[384,384]{1,0:T(8,128)(2,1)}, bf16[384,384]{1,0:T(8,128)(2,1)}, u32[]{:S(2)}, u32[]{:S(2)}) collective-permute-start(bf16[384,384]{1,0:T(8,128)(2,1)} %get-tuple-element.951), channel_id=1, source_target_pairs={{0,8},{4,12},{8,0},{12,4},{16,24},{20,28},{24,16},{28,20},{1,9},{5... | collective-permute-start | bytes 884744 | tf_op jit(solution)/shard_map/cond/branch_1_fun/ppermute | solution.py:121
  446.2 35.5 %collective-permute-start.45 = (bf16[192,1152]{1,0:T(8,128)(2,1)}, bf16[192,1152]{1,0:T(8,128)(2,1)}, u32[]{:S(2)}, u32[]{:S(2)}) collective-permute-start(bf16[192,1152]{1,0:T(8,128)(2,1)} %get-tuple-element.952), channel_id=1, source_target_pairs={{0,8},{4,12},{8,0},{12,4},{16,24},{20,28},{24,16},{28,20},{1,9},{5... | collective-permute-start | bytes 1327112 | tf_op jit(solution)/shard_map/cond/branch_1_fun/ppermute | solution.py:121
  448.2 19.3 %collective-permute-start.42 = (bf16[256,1536]{1,0:T(8,128)(2,1)}, bf16[256,1536]{1,0:T(8,128)(2,1)}, u32[]{:S(2)}, u32[]{:S(2)}) collective-permute-start(bf16[256,1536]{1,0:T(8,128)(2,1)} %get-tuple-element.946), channel_id=1, source_target_pairs={{0,2},{1,3},{2,0},{3,1},{4,6},{5,7},{6,4},{7,5},{8,10},{9,11},{10,... | collective-permute-start | bytes 2359304 | tf_op jit(solution)/shard_map/cond/branch_1_fun/ppermute | solution.py:121
  448.8 32.8 %collective-permute-start.43 = (bf16[768,512]{1,0:T(8,128)(2,1)}, bf16[768,512]{1,0:T(8,128)(2,1)}, u32[]{:S(2)}, u32[]{:S(2)}) collective-permute-start(bf16[768,512]{1,0:T(8,128)(2,1)} %get-tuple-element.950), channel_id=1, source_target_pairs={{0,4},{4,0},{8,12},{12,8},{16,20},{20,16},{24,28},{28,24},{1,5},{5... | collective-permute-start | bytes 2359304 | tf_op jit(solution)/shard_map/cond/branch_1_fun/ppermute | solution.py:121
  484.6 56.0 %all-to-all-start = ((f32[32,1,160]{2,1,0:T(1,128)}), f32[32,1,160]{2,1,0:T(1,128)S(1)}, u32[]{:S(2)}, u32[]{:S(2)}) async-start(f32[32,1,160]{2,1,0:T(1,128)} %all_to_all.8), calls=%async_computation | async-start | bytes 65536 | tf_op jit(solution)/shard_map/all_to_all | solution.py:1291
  488.6 12.7 %collective-permute-start.35 = (bf16[384,512]{1,0:T(8,128)(2,1)}, bf16[384,512]{1,0:T(8,128)(2,1)}, u32[]{:S(2)}, u32[]{:S(2)}) collective-permute-start(bf16[384,512]{1,0:T(8,128)(2,1)} %get-tuple-element.965), channel_id=1, source_target_pairs={{0,8},{4,12},{8,0},{12,4},{16,24},{20,28},{24,16},{28,20},{1,9},{5... | collective-permute-start | bytes 1179656 | tf_op jit(solution)/shard_map/cond/branch_1_fun/ppermute | solution.py:121
  490.5 35.1 %collective-permute-start.36 = (bf16[256,1536]{1,0:T(8,128)(2,1)}, bf16[256,1536]{1,0:T(8,128)(2,1)}, u32[]{:S(2)}, u32[]{:S(2)}) collective-permute-start(bf16[256,1536]{1,0:T(8,128)(2,1)} %get-tuple-element.972), channel_id=1, source_target_pairs={{0,8},{4,12},{8,0},{12,4},{16,24},{20,28},{24,16},{28,20},{1,9},{5... | collective-permute-start | bytes 2359304 | tf_op jit(solution)/shard_map/cond/branch_1_fun/ppermute | solution.py:121
  502.5 25.8 %collective-permute-start.37 = (bf16[192,896]{1,0:T(8,128)(2,1)S(1)}, bf16[192,896]{1,0:T(8,128)(2,1)S(1)}, u32[]{:S(2)}, u32[]{:S(2)}) collective-permute-start(bf16[192,896]{1,0:T(8,128)(2,1)S(1)} %fusion), channel_id=1, source_target_pairs={{0,16},{4,20},{8,24},{12,28},{16,0},{20,4},{24,8},{28,12},{1,17},{... | collective-permute-start | bytes 1032200 | tf_op jit(solution)/shard_map/cond/branch_1_fun/ppermute | solution.py:121
  505.0 29.3 %collective-permute-start.38 = (bf16[192,1152]{1,0:T(8,128)(2,1)}, bf16[192,1152]{1,0:T(8,128)(2,1)S(1)}, u32[]{:S(2)}, u32[]{:S(2)}) collective-permute-start(bf16[192,1152]{1,0:T(8,128)(2,1)} %get-tuple-element.975), channel_id=1, source_target_pairs={{0,8},{4,12},{8,0},{12,4},{16,24},{20,28},{24,16},{28,20},{1,9},{5... | collective-permute-start | bytes 1327112 | tf_op jit(solution)/shard_map/cond/branch_1_fun/ppermute | solution.py:121
  528.5 3.3 collective-permute-start.41
  528.7 3.8 collective-permute-start.40
  543.3 11.8 %collective-permute-start.69 = (bf16[192,1152]{1,0:T(8,128)(2,1)}, bf16[192,1152]{1,0:T(8,128)(2,1)S(1)}, u32[]{:S(2)}, u32[]{:S(2)}) collective-permute-start(bf16[192,1152]{1,0:T(8,128)(2,1)} %get-tuple-element.1338), channel_id=1, source_target_pairs={{0,8},{4,12},{8,0},{12,4},{16,24},{20,28},{24,16},{28,20},{1,9},{5... | collective-permute-start | bytes 1327112 | tf_op jit(solution)/shard_map/ppermute | solution.py:121
  (31 other events, 313.8 us)

commit v3 on v2

--- a/solution.py
+++ b/solution.py
@@ -118,7 +118,8 @@
 
     def swap(array, axis, bit):
         size = mesh.shape[axis]
-        return lax.ppermute(array, axis, [(i, i ^ bit) for i in range(size)])
+        with jax.named_scope(f"swap_{axis}_{bit}"):
+            return lax.ppermute(array, axis, [(i, i ^ bit) for i in range(size)])
 
     def masks_of(bits):
         masks = [0]
@@ -519,6 +520,27 @@
             "join_both", scalars, first, mine, theirs,
         )
 
+    def halves(scalars, first, second):
+        rows, columns = first.shape[0] // 2, first.shape[1]
+
+        def kernel(scal, first_ref, second_ref, out_a_ref, out_b_ref):
+            out_a_ref[...] = first_ref[:rows, :]
+            out_b_ref[...] = second_ref[rows:, :]
+
+        return whole_call(
+            kernel, [((rows, columns), bf16)] * 2, "halves", scalars, first, second
+        )
+
+    def block_step(scalars, kept, arrived):
+        rows, columns = arrived.shape[0] // 2, arrived.shape[1]
+
+        def kernel(scal, kept_ref, arrived_ref, own_ref, sent_ref):
+            own_ref[...] = kept_ref[:rows, :] + arrived_ref[:rows, :].astype(f32)
+            sent_ref[...] = (kept_ref[rows:, :] + arrived_ref[rows:, :].astype(f32)).astype(bf16)
+
+        outs = [((rows, columns), f32), ((rows, columns), bf16)]
+        return whole_call(kernel, outs, "block_step", scalars, kept, arrived)
+
     def spread_eight(scalars, kept, arrived):
         rows, model = kept.shape[0] // 4, kept.shape[1]
         half = rows // 2
@@ -551,8 +573,8 @@
         )
 
     def give(total, scal, kept_ref, sent_ref):
-        part = total.shape[0] // dp_size
-        flag = is_high(scal, 1)
+        part = pair_bit * (total.shape[0] // dp_size)
+        flag = is_high(scal, pair_bit)
         for at in range(total.shape[0] // (2 * part)):
             low = total[2 * at * part : (2 * at + 1) * part]
             high = total[(2 * at + 1) * part : (2 * at + 2) * part]
@@ -931,8 +953,6 @@
             )
         )
         gate_piece = join_rows(scalars, gate_mine, gate_theirs, 0, 1)
-        gate_far = far_pieces(gate_piece)
-        cot_x = swap(cot_own, "tensor", 2)
         (qkv_l2,) = hold([gate_piece], [qkv_l2])
 
         def gather_attn():
@@ -944,9 +964,11 @@
 
         qkv_y3, act_c, out_l = section(gather_attn)
 
-        qkv_y3, act_c, out_near, rest_sent, cot_core = hold(
-            [], [qkv_y3, act_c, rows_of(out_half, out_l), rest_sent, cotangent]
-        )
+        qkv_y3, act_c, out_near, rest_sent, cot_core, gate_piece = hold(
+            [], [qkv_y3, act_c, rows_of(out_half, out_l), rest_sent, cotangent, gate_piece]
+        )
+        gate_far = far_pieces(gate_piece)
+        cot_x = swap(cot_core, "tensor", 2)
         rest_theirs = swap(rest_sent, "dp", pair_bit)
         out_y = swap(out_near, "dp", 1)
         far_masks = masks_of(far_bits)
@@ -1013,15 +1035,13 @@
         two_x, two_l, down_piece = section(gather_near)
 
         rows = two_own.shape[0]
-        two_x, two_l, down_piece, up_halves = hold(
-            [own_y, gate_y2], [two_x, two_l, down_piece, tuple(up_far[1:])]
-        )
+        two_x, two_l, up_halves = hold([own_y, gate_y2], [two_x, two_l, tuple(up_far[1:])])
         up_y2 = [swap(part, "dp", 1) for part in up_halves]
-        down_far = far_pieces(down_piece)
 
         def gather_rest():
-            far_a = swap(two_l[: rows // 2], "tensor", 2)
-            far_b = swap(two_x[rows // 2 :], "dp", pair_bit)
+            given_a, given_b = halves(scalars, two_l, two_x)
+            far_a = swap(given_a, "tensor", 2)
+            far_b = swap(given_b, "dp", pair_bit)
 
             def cores():
                 given, arrived = [two_x, two_l, two_own], []
@@ -1032,10 +1052,16 @@
                 return arrived
 
             arrived = section(cores)
-            far_a, far_b, *arrived = hold([], [far_a, far_b] + arrived)
-            return far_a, far_b, *arrived, swap(far_a, "tensor", 1), swap(far_b, "tensor", 1)
-
-        far_a, far_b, two_x_c, two_l_c, two_own_c, far_a_c, far_b_c = section(gather_rest)
+            return hold([], [far_a, far_b, *arrived])
+
+        far_a, far_b, two_x_c, two_l_c, two_own_c = section(gather_rest)
+        far_a, far_b, down_piece = hold(up_y2, [far_a, far_b, down_piece])
+        down_far = far_pieces(down_piece)
+
+        def gather_far():
+            return swap(far_a, "tensor", 1), swap(far_b, "tensor", 1)
+
+        far_a_c, far_b_c = section(gather_far)
         two_pieces = [two_own, two_x, two_l]
         two_pieces_c = [two_own_c, two_x_c, two_l_c]
 
@@ -1047,7 +1073,7 @@
             (part, 0) for part in up_y2
         ]
         far_a, far_b, far_a_c, far_b_c, down_piece_y, cot_x, cot_l = hold(
-            up_y2, [far_a, far_b, far_a_c, far_b_c, down_piece, cot_x, cot_l]
+            [], [far_a, far_b, far_a_c, far_b_c, down_piece, cot_x, cot_l]
         )
         two_pieces += [far_a, far_b]
         two_pieces_c += [far_a_c, far_b_c]
@@ -1062,31 +1088,25 @@
 
         down_y1, cot_far, cot_x_c, (acts_a, mixed_a, silu_a, back_a) = section(feed_own)
 
-        mixed_a, down_halves, cot_l_in = hold([], [mixed_a, tuple(down_far[1:]), cot_l])
-
-        cots = [cot_own, cot_x, cot_l, cot_far]
+        mixed_a, cot_l_in = hold([], [mixed_a, cot_l])
 
         def feed_core():
-            down_y2 = tuple(swap(part, "dp", 1) for part in down_halves)
-
-            def core_half():
-                l_c = swap(cot_l_in, "tensor", 1)
-                far_c = swap(cot_far, "tensor", 1)
-                core = ffn_up(scalars, two_pieces_c, gate_pieces, up_pieces)
-                l_c, far_c, *core = hold([], [l_c, far_c, *core])
-                grads = ffn_grad(
-                    scalars, cots, [cot_own_c, cot_x_c, l_c, far_c], mixed_a, core[1], "grad_down"
-                )
-                return l_c, far_c, core, grads
-
-            outs = section(core_half)
-            down_y2, outs = hold([], [down_y2, outs])
-            return (down_y2, *outs)
-
-        (
-            down_y2, cot_l_c, cot_far_c, (acts_b, mixed_b, silu_b, back_b), (down_kept, down_sent),
-        ) = section(feed_core)
+            l_c = swap(cot_l_in, "tensor", 1)
+            far_c = swap(cot_far, "tensor", 1)
+            core = ffn_up(scalars, two_pieces_c, gate_pieces, up_pieces)
+            l_c, far_c = hold([core], [l_c, far_c])
+            return l_c, far_c, core
+
+        cot_l_c, cot_far_c, (acts_b, mixed_b, silu_b, back_b) = section(feed_core)
+
+        cots = [cotangent, cot_x, cot_l, cot_far]
         cots_c = [cot_own_c, cot_x_c, cot_l_c, cot_far_c]
+        mixed_b, down_halves = hold([down_y1], [mixed_b, tuple(down_far[1:])])
+        down_y2 = tuple(swap(part, "dp", 1) for part in down_halves)
+        down_kept, down_sent = section(
+            lambda: ffn_grad(scalars, cots, cots_c, mixed_a, mixed_b, "grad_down")
+        )
+        down_sent, down_y2 = hold([], [down_sent, down_y2])
         down_pieces = [(part, 0) for part in [*down_far, down_y1, *down_y2]]
 
         down_sent, silu_b = hold([], [down_sent, silu_b])
@@ -1105,234 +1125,201 @@
 
         gate_a, up_a, gate_b, up_b, own, to_x, to_l, far_a, far_b = section(back_all)
 
-        far_a, far_b, down_sent = hold([], [far_a, far_b, down_sent])
-
-        def backward():
-            def spread_far():
-                far_x = swap(far_a, "tensor", 2)
-                far_l = swap(far_b, "dp", pair_bit)
+        far_a, far_b, mixed_b = hold([], [far_a, far_b, mixed_b])
+        model = far_a.shape[1]
+
+        def spread_far():
+            far_x = swap(far_a, "tensor", 2)
+            far_l = swap(far_b, "dp", pair_bit)
+
+            def block_rows():
+                sent = ffn_rows(scalars, mixed_b, down_pieces, model, "block_rows")
+                (sent,) = hold([], [sent])
+                arrived = swap(sent, "tensor", 1)
+                kept = ffn_rows(scalars, mixed_a, down_pieces, model, "block_rows")
+                return hold([], [kept, arrived])
+
+            outs = section(block_rows)
+            outs, far_x, far_l = hold([], [outs, far_x, far_l])
+            return (*outs, *spread_two(scalars, to_x, to_l, far_x, far_l))
+
+        block_kept, block_arrived, to_x, to_l = section(spread_far)
+
+        to_x, to_l, down_sent = hold([], [to_x, to_l, down_sent])
+
+        def spread_near():
+            from_x = swap(to_x, "tensor", 2)
+            from_l = swap(to_l, "dp", pair_bit)
+            up_grads = ffn_grad(scalars, [acts_a], [acts_b], up_a, up_b, "grad_up")
+            down_pair = fold_sum(scalars, down_kept, down_sent, far_bits[0], 1)
+            block_pair = fold_fixed(scalars, block_kept, block_arrived, [0, 1], [2, 3])
+            from_x, from_l = hold([up_grads, down_pair, block_pair], [from_x, from_l])
+            return (
+                *up_grads,
+                *down_pair,
+                *block_pair,
+                *norm_two_back(
+                    scalars, own, from_x, from_l, hidden, gain_ffn[None, :], cotangent
+                ),
+            )
+
+        (
+            up_kept, up_sent, down_kept, down_sent, block_kept, block_sent,
+            grad_hidden, attn_own, gain_two,
+        ) = section(spread_near)
+
+        attn_own, down_sent, up_sent, block_sent, gate_b = hold(
+            [], [attn_own, down_sent, up_sent, block_sent, gate_b]
+        )
+        down_kept, down_sent = far_rest(down_kept, down_sent)
+        up_sent = swap(up_sent, "dp", 1)
+        block_sent = swap(block_sent, "dp", pair_bit)
+
+        def attention_back():
+            def gather_back():
+                attn_x = swap(attn_own, "tensor", 2)
                 gate_grads = ffn_grad(scalars, [acts_a], [acts_b], gate_a, gate_b, "grad_gate")
-                far_x, far_l = hold([gate_grads], [far_x, far_l])
-                return (*gate_grads, *spread_two(scalars, to_x, to_l, far_x, far_l))
-
-            gate_kept, gate_sent, given_x, given_l = section(spread_far)
-
-            given_x, given_l, gate_sent = hold([], [given_x, given_l, gate_sent])
-            gate_sent = swap(gate_sent, "dp", 1)
-
-            def second_norm():
-                def spread_near():
-                    from_x = swap(given_x, "tensor", 2)
-                    from_l = swap(given_l, "dp", pair_bit)
-                    up_grads = ffn_grad(scalars, [acts_a], [acts_b], up_a, up_b, "grad_up")
-                    down_pair = fold_sum(scalars, down_kept, down_sent, far_bits[0], 1)
-                    from_x, from_l = hold([up_grads, down_pair], [from_x, from_l])
-                    return (
-                        *up_grads,
-                        *down_pair,
-                        *norm_two_back(
-                            scalars, own, from_x, from_l, hidden, gain_ffn[None, :], cotangent
-                        ),
-                    )
-
-                up_kept, up_sent, down_own, down_given, grad_hidden, attn_own, gain_two = section(
-                    spread_near
-                )
-
-                attn_own, down_given = hold([], [attn_own, down_given])
-                down_own, down_arrived = far_rest(down_own, down_given)
-
-                def gather_back():
-                    attn_x = swap(attn_own, "tensor", 2)
-                    model = attn_own.shape[1]
-                    block_sent = ffn_rows(scalars, mixed_b, down_pieces, model, "block_rows")
-                    block_kept = ffn_rows(scalars, mixed_a, down_pieces, model, "block_rows")
-                    (attn_x,) = hold([block_kept, block_sent], [attn_x])
-                    return rows_of(attn_own, attn_x), block_kept, block_sent
-
-                attn_half, block_kept, block_sent = section(gather_back)
-                attn_half, down_arrived = hold([], [attn_half, down_arrived])
-                return (
-                    up_kept, up_sent, down_own, down_arrived, grad_hidden, gain_two,
-                    attn_half, block_kept, block_sent,
-                )
-
-            outs = section(second_norm)
-            outs, gate_sent = hold([], [outs, gate_sent])
-            return (gate_kept, gate_sent, *outs)
-
-        (
-            gate_kept, gate_sent, up_kept, up_sent, down_kept, down_sent, grad_hidden, gain_two,
-            attn_half, block_kept, block_sent,
-        ) = section(backward)
-
-        attn_half, gate_sent, up_sent, down_sent, block_sent = hold(
-            [], [attn_half, gate_sent, up_sent, down_sent, block_sent]
-        )
-        up_sent = swap(up_sent, "dp", 1)
-
-        def gather_back_core():
+                (attn_x,) = hold([gate_grads], [attn_x])
+                return (rows_of(attn_own, attn_x), *gate_grads)
+
+            attn_half, gate_kept, gate_sent = section(gather_back)
+            attn_half, gate_sent = hold([], [attn_half, gate_sent])
             attn_c = swap(attn_half, "tensor", 1)
-            gate_pair = fold_sum(scalars, gate_kept, gate_sent, far_bits[0], 1)
-            attn_c, block_given = hold([gate_pair], [attn_c, block_sent])
-            block_arrived = swap(block_given, "tensor", 1)
-            down_pair = fold_sum(scalars, down_kept, down_sent, pair_bit, 1)
-            (block_arrived,) = hold([down_pair], [block_arrived])
-            block_pair = fold_fixed(scalars, block_kept, block_arrived, [0, 2], [1, 3])
-            return attn_c, gate_pair, down_pair, block_pair
-
-        attn_c, (gate_kept, gate_sent), (down_mine, down_given), (block_kept, block_sent) = section(
-            gather_back_core
-        )
-
-        attn_c, block_sent, gate_sent = hold([], [attn_c, block_sent, gate_sent])
-        gate_kept, gate_sent = far_rest(gate_kept, gate_sent)
-        block_sent = swap(block_sent, "tensor", 2)
-
-        def attention_back():
             outs = attend_back(
                 scalars, query_rot, kv_own, kv_other, starts, out_parts, attn_half, attn_c,
                 context, cosine, sine,
             )
-            grad_query_low, kv_kept, kv_given, bias_rows, wout_kept, wout_sent = outs
-            kv_given, wout_sent = hold([], [kv_given, wout_sent])
-            wout_arrived = swap(wout_sent, "dp", 1)
+            return gate_kept, gate_sent, outs
+
+        gate_kept, gate_sent, outs = section(attention_back)
+        grad_query_low, kv_kept, kv_given, bias_rows, wout_kept, wout_sent = outs
+
+        kv_given, wout_sent, gate_sent, down_sent, up_sent, block_sent = hold(
+            [], [kv_given, wout_sent, gate_sent, down_sent, up_sent, block_sent]
+        )
+        wout_arrived = swap(wout_sent, "dp", pair_bit)
+        devices = dp_size * tensor_size
+
+        def input_grads():
+            up_own, up_given = fold_sum(scalars, up_kept, up_sent, far_bits[0], 1)
+            kv_in, gate_in, up_given = hold([], [kv_given, gate_sent, up_given])
+            gate_y = swap(gate_in, "dp", 1)
+            up_own, up_far_sum = far_rest(up_own, up_given)
 
             def project_all():
-                kv_arrived = swap(kv_given, "tensor", 1)
+                kv_arrived = swap(kv_in, "tensor", 1)
+                down_pair = fold_sum(scalars, down_kept, down_sent, pair_bit, 1)
+                (kv_arrived,) = hold([down_pair], [kv_arrived])
                 grad_qkv, one_kept, one_sent, gain_rows = project_back(
                     scalars, grad_query_low, kv_kept, kv_arrived, qkv_pieces, act_pair, act_c
                 )
                 arrived = swap(one_sent, "tensor", 1)
                 wqkv_pair = project_grad(scalars, act_pair, act_c, grad_qkv)
                 (arrived,) = hold([wqkv_pair], [arrived])
-                return (
-                    *wqkv_pair,
-                    *fold_fixed(scalars, one_kept, arrived, [0], [1]),
-                    gain_rows,
-                )
+                wqkv_kept, wqkv_sent = wqkv_pair
+                one_kept, one_sent = fold_fixed(scalars, one_kept, arrived, [0], [1])
+
+                def first_norm_back():
+                    arrived = swap(one_sent, "tensor", 2)
+                    wqkv_arrived = swap(wqkv_sent, "dp", pair_bit)
+                    block = block_step(scalars, block_kept, block_sent)
+                    bias_keyval = jnp.zeros((2 * KV * HD,), f32)
+                    bias_keyval = lax.dynamic_update_slice_in_dim(
+                        bias_keyval, bias_rows[0, width : width + HD], head_kv * HD, 0
+                    )
+                    bias_keyval = lax.dynamic_update_slice_in_dim(
+                        bias_keyval, bias_rows[0, width + HD :], KV * HD + head_kv * HD, 0
+                    )
+                    bias_query = lax.dynamic_update_slice_in_dim(
+                        jnp.zeros((HQ * HD,), f32), bias_rows[0, :width], tensor_index * width, 0
+                    )
+                    parts = (gain_rows[0] / gain_attn, gain_two[0], bias_query, bias_keyval)
+                    small = jnp.concatenate([part.reshape(devices, -1) for part in parts], axis=1)
+                    (arrived,) = hold([block, small], [arrived])
+                    grad_rows = norm_one_back(
+                        scalars, block_input, one_kept, arrived, gain_attn[None, :], grad_hidden
+                    )
+                    (wqkv_arrived,) = hold([grad_rows], [wqkv_arrived])
+                    return grad_rows, small, *block, wqkv_arrived
+
+                return (*down_pair, wqkv_kept, *section(first_norm_back))
 
             outs = section(project_all)
-            outs, wout_arrived = hold([], [outs, wout_arrived])
-            return (
-                *outs, bias_rows, *fold_sum(scalars, wout_kept, wout_arrived, pair_bit, groups)
-            )
+            outs, gate_y, up_far_sum = hold([], [outs, gate_y, up_far_sum])
+            return (up_own, up_far_sum, gate_y, *outs)
 
         (
-            wqkv_kept,
-            wqkv_sent,
-            one_kept,
-            one_sent,
-            gain_rows,
-            bias_rows,
-            wout_kept,
-            wout_sent,
-        ) = section(attention_back)
-
-        up_sent, one_sent, wqkv_sent, wout_sent, down_given, block_sent = hold(
-            [], [up_sent, one_sent, wqkv_sent, wout_sent, down_given, block_sent]
-        )
-        up_kept, up_sent = fold_sum(scalars, up_kept, up_sent, far_bits[0], 1)
-        one_sent, wqkv_sent, up_sent, gate_sent = hold(
-            [], [one_sent, wqkv_sent, up_sent, gate_sent]
-        )
-        up_kept, up_sent = far_rest(up_kept, up_sent)
-        devices = dp_size * tensor_size
-
-        def first_norm_back():
-            arrived = swap(one_sent, "tensor", 2)
-            wqkv_arrived = swap(wqkv_sent, "dp", 1)
-            wout_arrived = swap(wout_sent, "dp", pair_bit)
-            down_arrived = swap(down_given, "dp", pair_bit)
-            gate_pair = fold_sum(scalars, gate_kept, gate_sent, pair_bit, 1)
-            block_pair = fold_fixed(scalars, block_kept, block_sent, [0], [1])
-            bias_keyval = jnp.zeros((2 * KV * HD,), f32)
-            bias_keyval = lax.dynamic_update_slice_in_dim(
-                bias_keyval, bias_rows[0, width : width + HD], head_kv * HD, 0
-            )
-            bias_keyval = lax.dynamic_update_slice_in_dim(
-                bias_keyval, bias_rows[0, width + HD :], KV * HD + head_kv * HD, 0
-            )
-            bias_query = lax.dynamic_update_slice_in_dim(
-                jnp.zeros((HQ * HD,), f32), bias_rows[0, :width], tensor_index * width, 0
-            )
-            parts = (gain_rows[0] / gain_attn, gain_two[0], bias_query, bias_keyval)
-            small = jnp.concatenate([part.reshape(devices, -1) for part in parts], axis=1)
-            (arrived,) = hold([gate_pair, block_pair, small], [arrived])
-            grad_rows = norm_one_back(
-                scalars, block_input, one_kept, arrived, gain_attn[None, :], grad_hidden
-            )
-            wqkv_arrived, wout_arrived, down_arrived = hold(
-                [grad_rows], [wqkv_arrived, wout_arrived, down_arrived]
-            )
-            return (
-                grad_rows,
-                small,
-                gate_pair,
-                block_pair,
-                fold_sum(scalars, wqkv_kept, wqkv_arrived, pair_bit, groups),
-                wout_arrived,
-                down_arrived,
-            )
-
-        (
-            grad_rows,
-            small,
-            (gate_mine, gate_given),
-            (block_kept, block_sent),
-            (wqkv_kept, wqkv_sent),
-            wout_arrived,
-            down_theirs,
-        ) = section(first_norm_back)
-
-        wqkv_sent, gate_given, block_sent, small = hold(
-            [], [wqkv_sent, gate_given, block_sent, small]
-        )
+            up_kept, up_sent, gate_sent, down_mine, down_given, wqkv_kept, grad_rows, small,
+            block_own, block_sent, wqkv_arrived,
+        ) = section(input_grads)
+
+        wqkv_arrived, wout_arrived, gate_sent, small, down_given = hold(
+            [], [wqkv_arrived, wout_arrived, gate_sent, small, down_given]
+        )
+        gate_kept, gate_sent = fold_sum(scalars, gate_kept, gate_sent, far_bits[0], 1)
+        wqkv_arrived, gate_sent, small = hold([], [wqkv_arrived, gate_sent, small])
+        gate_kept, gate_sent = far_rest(gate_kept, gate_sent)
         small = lax.all_to_all(small, ("dp", "tensor"), 0, 0, tiled=True)
 
         def last_rows():
-            wqkv_arrived = swap(wqkv_sent, "dp", pair_bit)
-            block_arrived = swap(block_sent, "dp", pair_bit)
-            wout_total = add(wout_kept, wout_arrived)
-            down_share = join_cols(scalars, down_mine, down_theirs, w_down.shape[0] // 2).T
-            (wqkv_arrived,) = hold([down_share, wout_total], [wqkv_arrived])
-            total = jnp.concatenate([add(wqkv_kept, wqkv_arrived), wout_total], axis=1)
-            total, gate_out = hold([], [total, gate_given])
+            down_theirs = swap(down_given, "dp", pair_bit)
+            block_x = swap(block_sent, "tensor", 2)
+
+            def attn_step():
+                wqkv_own, wqkv_sent = fold_sum(scalars, wqkv_kept, wqkv_arrived, 1, groups)
+                wout_own, wout_sent = fold_sum(scalars, wout_kept, wout_arrived, 1, groups)
+                wqkv_y = swap(wqkv_sent, "dp", 1)
+                wout_y = swap(wout_sent, "dp", 1)
+                up_pair = fold_sum(scalars, up_kept, up_sent, pair_bit, 1)
+                wqkv_y, wout_y = hold([up_pair], [wqkv_y, wout_y])
+                total = jnp.concatenate([add(wqkv_own, wqkv_y), add(wout_own, wout_y)], axis=1)
+                return total, up_pair
+
+            total, up_pair = section(attn_step)
+            total, down_theirs, block_x, up_given = hold(
+                [], [total, down_theirs, block_x, up_pair[1]]
+            )
+            up_theirs = swap(up_given, "dp", pair_bit)
             for bit in far_bits[:-1]:
                 total = add(*fold_rows(total, bit))
-            kept, sent = fold_rows(total, far_bits[-1])
-            gate_theirs = swap(gate_out, "dp", pair_bit)
-            (block_arrived,) = hold([kept], [block_arrived])
-            block_out = (hidden + add(block_kept, block_arrived)).astype(bf16)
-            (sent,) = hold([block_out], [sent])
-            share = add(kept, sent)
-            kv_rows = share[:, width : width + HD]
-            share_rows = kv_rows.shape[0] // tensor_size
-            keyval_share = jnp.zeros((share_rows, 2 * KV * HD), f32)
-            moved = []
-            for mask in range(tensor_size):
-                rows_for = lax.dynamic_slice_in_dim(
-                    kv_rows, (tensor_index ^ mask) * share_rows, share_rows, 0
-                )
-                moved.append(swap(rows_for, "tensor", mask) if mask else rows_for)
-            query_share, out_share = share[:, :width], share[:, width + HD :].T
-            gate_theirs, *moved = hold([query_share, out_share], [gate_theirs] + moved)
-            gate_share = join_cols(scalars, gate_mine, gate_theirs, w_gate.shape[1] // 2)
-            for mask in range(tensor_size):
-                sender = tensor_index ^ mask
-                column = (sender % 2) * (KV * HD) + (sender * local_heads // (HQ // KV)) * HD
-                keyval_share = lax.dynamic_update_slice_in_dim(
-                    keyval_share, moved[mask], column, 1
-                )
-            return down_share, gate_share, block_out, query_share, out_share, keyval_share
-
-        down_share, gate_share, block_out, query_share, out_share, keyval_share = section(last_rows)
-
-        up_sent, small = hold([block_out, keyval_share], [up_sent, small])
-        up_mine, up_given = fold_sum(scalars, up_kept, up_sent, pair_bit, 1)
-        up_theirs = swap(up_given, "dp", pair_bit)
+            flag = ((dp_index & far_bits[-1]) != 0).astype(jnp.int32)
+            view = total.reshape(2, -1, total.shape[1])
+            kept = lax.dynamic_index_in_dim(view, flag, 0, keepdims=False)
+            sent = lax.dynamic_index_in_dim(view, 1 - flag, 0, keepdims=False).astype(bf16)
+            block_out = (hidden + add(block_own, block_x)).astype(bf16)
+            down_share = join_cols(scalars, down_mine, down_theirs, w_down.shape[0] // 2).T
+            (up_theirs,) = hold([kept, sent, block_out, down_share], [up_theirs])
+            return kept, sent, up_pair[0], up_theirs, block_out, down_share
+
+        attn_kept, attn_sent, up_mine, up_theirs, block_out, down_share = section(last_rows)
+
+        gate_sent, attn_sent, up_theirs, small = hold(
+            [block_out, down_share], [gate_sent, attn_sent, up_theirs, small]
+        )
         small = jnp.sum(small, axis=0)
+        attn_sent = swap(attn_sent, "dp", far_bits[-1])
+        gate_mine, gate_given = fold_sum(scalars, gate_kept, gate_sent, pair_bit, 1)
+        gate_theirs = swap(gate_given, "dp", pair_bit)
+        (up_theirs,) = hold([gate_given], [up_theirs])
         up_share = join_cols(scalars, up_mine, up_theirs, w_up.shape[1] // 2)
+        (attn_sent,) = hold([up_share], [attn_sent])
+        share = add(attn_kept, attn_sent)
+        kv_rows = share[:, width : width + HD]
+        share_rows = kv_rows.shape[0] // tensor_size
+        moved = []
+        for mask in range(tensor_size):
+            rows_for = lax.dynamic_slice_in_dim(
+                kv_rows, (tensor_index ^ mask) * share_rows, share_rows, 0
+            )
+            moved.append(swap(rows_for, "tensor", mask) if mask else rows_for)
+        query_share, out_share = share[:, :width], share[:, width + HD :].T
+        gate_theirs, *moved = hold([query_share, out_share], [gate_theirs] + moved)
+        gate_share = join_cols(scalars, gate_mine, gate_theirs, w_gate.shape[1] // 2)
+        keyval_share = jnp.zeros((share_rows, 2 * KV * HD), f32)
+        for mask in range(tensor_size):
+            sender = tensor_index ^ mask
+            column = (sender % 2) * (KV * HD) + (sender * local_heads // (HQ // KV)) * HD
+            keyval_share = lax.dynamic_update_slice_in_dim(keyval_share, moved[mask], column, 1)
         sizes = [HQ * HD // devices, 2 * KV * HD // devices, gain_attn.shape[0] // devices]
         ends = [sizes[2], 2 * sizes[2], 2 * sizes[2] + sizes[0]]
         gain_one_share = small[: ends[0]]

time: 569 us -> 553 us (0.972)
  waiting for transfers between devices: 163 us -> 152 us
  local copies, waits for them, and re-layouts: 20.1 us -> 14.3 us
    ppermute x70, waiting for transfers between devices: 163 us -> 152 us  [swap(): return lax.ppermute(array, axis, [(i, i ^ bit) for i in range(size)])]
    pallas_call x26 -> x27, Pallas kernels: 90.7 us -> 92.9 us  [whole_call(): pl.pallas_call(kernel, in_specs=[SCALARS] + [WHOLE] * (len(args) - 1), ou...]
  transfers between devices with their start and end apart: 71 -> 71, of which waited for: 33 -> 34; matrix products, arithmetic and copies ran while one was open for 6% -> 5% of each run, Pallas kernels for 48% -> 49%
where the time goes in v3:
time: 553 us; the launch traced here: 543 us
  Pallas kernels  280 us (51%)
  waiting for transfers between devices  152 us (27%)
  starting transfers between devices  75.4 us (14%)
  other arithmetic  19.4 us (4%)
  local copies, waits for them, and re-layouts  14.3 us (3%)
    ppermute x70, waiting for transfers between devices, swap(): return lax.ppermute(array, axis, [(i, i ^ bit) for i in range(size)])  152 us
    pallas_call x27, Pallas kernels, whole_call(): pl.pallas_call(kernel, in_specs=[SCALARS] + [WHOLE] * (len(args) - 1), ou...  92.9 us
    ppermute x70, starting transfers between devices, swap(): return lax.ppermute(array, axis, [(i, i ^ bit) for i in range(size)])  70.5 us
    pallas_call x2, Pallas kernels, ffn_back(): pl.pallas_call(kernel, grid=(2,), in_specs=[SCALARS] + [ANY] * (many + 3...  49 us
    pallas_call x3, Pallas kernels, ffn_grad(): pl.pallas_call(kernel, grid=(model // wide,), in_specs=[SCALARS] + [pl.Bl...  39 us
    pallas_call x2, Pallas kernels, ffn_up(): pl.pallas_call(kernel, grid=(2,), in_specs=[SCALARS] + [ANY] * (many + 2...  31.1 us
    pallas_call x1, Pallas kernels, attend_back(): pl.pallas_call(kernel, in_specs=[SCALARS] + [WHOLE] * 4 + [ANY] * 2 + [WH...  21.5 us
    pallas_call x2, Pallas kernels, ffn_rows(): pl.pallas_call(kernel, grid=(2,), in_specs=[SCALARS, pl.BlockSpec((rows,...  18.1 us
  transfers between devices with their start and end apart: 71, of which 34 were waited for; matrix products, arithmetic and copies ran while one was open for 5% of the time, Pallas kernels for 49%

profile of v3, /device:TPU:0, one launch (start us, length us, event | category | flops | bytes accessed | tf_op | source)
XLA Modules:
  0.0 542.6 jit_solution(9611161413346244962)
XLA Ops:
  2.5 4.1 collective-permute-start.40
  37.3 10.2 %conditional.22 = (bf16[192,512]{1,0:T(8,128)(2,1)}, bf16[512,1536]{1,0:T(8,128)(2,1)}, bf16[384,384]{1,0:T(8,128)(2,1)}) conditional(s32[]{:T(128)} %convert_element_type.83, () %tuple.232, (bf16[192,512]{1,0:T(8,128)(2,1)}, bf16[512,1536]{1,0:T(8,128)(2,1)S(1)}, bf16[384,384]{1,0:T(8,128)(2,1)S(1)}) %tuple.351), branch_computations={%region_3.4_spmd, %region_4.5_spmd} | conditional | bytes 8257680 | solution.py:101
  40.7 6.4 %collective-permute-done = bf16[192,512]{1,0:T(8,128)(2,1)} collective-permute-done((bf16[192,512]{1,0:T(8,128)(2,1)}, bf16[192,512]{1,0:T(8,128)(2,1)}, u32[]{:S(2)}, u32[]{:S(2)}) %collective-permute-start) | collective-permute-done | bytes 196640 | tf_op jit(solution)/shard_map/cond/branch_1_fun/swap_dp_1/ppermute | solution.py:122
  54.8 17.9 %conditional.23 = (bf16[1024,384]{1,0:T(8,128)(2,1)}, bf16[1024,128]{1,0:T(8,128)(2,1)}, bf16[1024,128]{1,0:T(8,128)(2,1)}, bf16[1024,384]{1,0:T(8,128)(2,1)}, bf16[256,1536]{1,0:T(8,128)(2,1)}) conditional(s32[]{:T(128)} %convert_element_type.83, () %tuple.238, (f32[512]{0:T(512)S(1)}, s32[2]{0:T(128)S(1)}, bf16[512,1536]{1,0:T(8,128)(2,1)S(1)}, ...), branch_computations={%region_5.6_spmd, %region_6.7_spmd} | conditional | bytes 4194424 | solution.py:101
  54.8 6.8 %project.1 = (bf16[1024,384]{1,0:T(8,128)(2,1)}, bf16[1024,128]{1,0:T(8,128)(2,1)}) custom-call(s32[2]{0:T(128)S(1)} %get-tuple-element.496.scal, bf16[512,1536]{1,0:T(8,128)(2,1)S(1)} %get-tuple-element.497.pair_ref, bf16[512,1536]{1,0:T(8,128)(2,1)} %get-tuple-element.498.core_ref, f32[1,512]{1,0:T(1,128)S(1)} %bitcast.36, ...), custom_call_target="tpu_custom_call" | custom-call | tf_op jit(solution)/shard_map/cond/branch_1_fun/project/pallas_call | solution.py:613
  63.8 8.9 %attend.1 = bf16[1024,384]{1,0:T(8,128)(2,1)} custom-call(s32[2]{0:T(128)S(1)} %get-tuple-element.496.scal, bf16[1024,384]{1,0:T(8,128)(2,1)} %get-tuple-element.1327.query_ref, bf16[1024,128]{1,0:T(8,128)(2,1)} %get-tuple-element.1328.own_ref, bf16[1024,128]{1,0:T(8,128)(2,1)} %collective-permute-done.3.other_ref, s32[1024,1]{1,0:T(8,128)} %get-tuple-element.513.start_ref), custom_call_target="tpu_custom_call" | custom-call | tf_op jit(solution)/shard_map/cond/branch_1_fun/attend/pallas_call | solution.py:393
  72.7 6.6 %out_rows.1 = (bf16[512,1536]{1,0:T(8,128)(2,1)}, bf16[512,1536]{1,0:T(8,128)(2,1)}) custom-call(s32[2]{0:T(128)S(1)} %pad_add_fusion.scal, bf16[1024,384]{1,0:T(8,128)(2,1)} %get-tuple-element.1099.context_ref, bf16[768,384]{1,0:T(8,128)(2,1)S(1)} %pad_maximum_fusion.4.refs_0_.refs_2_.refs_4_.refs_6_, ...), custom_call_target="tpu_custom_call" | custom-call | tf_op jit(solution)/shard_map/out_rows/pallas_call | solution.py:675
  79.3 7.2 %collective-permute-done.50 = bf16[384,1152]{1,0:T(8,128)(2,1)} collective-permute-done((bf16[384,1152]{1,0:T(8,128)(2,1)}, bf16[384,1152]{1,0:T(8,128)(2,1)}, u32[]{:S(2)}, u32[]{:S(2)}) %collective-permute-start.50) | collective-permute-done | bytes 884768 | tf_op jit(solution)/shard_map/swap_dp_2/ppermute | solution.py:122
  86.5 3.8 conditional.24
  93.4 26.2 %conditional.25 = ((f32[256,1536]{1,0:T(8,128)}, bf16[256,1536]{1,0:T(8,128)(2,1)})) conditional(s32[]{:T(128)} %convert_element_type.83, () %tuple.242, (s32[2]{0:T(128)S(1)}, bf16[512,1536]{1,0:T(8,128)(2,1)}, bf16[512,1536]{1,0:T(8,128)(2,1)}, f32[1536]{0:T(1024)S(1)}, bf16[256,1536]{1,0:T(8,128)(2,1)}) %tuple.356), branch_computations={%region_9.10_spmd, %region_10.11_spmd} | conditional | bytes 3158064 | solution.py:101
  93.4 3.5 fold_fixed.3
  99.3 16.7 %collective-permute-done.6.arrived_ref = bf16[256,1536]{1,0:T(8,128)(2,1)} collective-permute-done((bf16[256,1536]{1,0:T(8,128)(2,1)}, bf16[256,1536]{1,0:T(8,128)(2,1)}, u32[]{:S(2)}, u32[]{:S(2)}) %collective-permute-start.6) | collective-permute-done | bytes 786464 | tf_op jit(solution)/shard_map/cond/branch_1_fun/swap_tensor_2/ppermute | solution.py:122
  116.0 3.6 norm_two.1
  119.6 7.1 %collective-permute-done.51 = bf16[256,1536]{1,0:T(8,128)(2,1)} collective-permute-done((bf16[256,1536]{1,0:T(8,128)(2,1)}, bf16[256,1536]{1,0:T(8,128)(2,1)}, u32[]{:S(2)}, u32[]{:S(2)}) %collective-permute-start.51) | collective-permute-done | bytes 786464 | tf_op jit(solution)/shard_map/swap_dp_2/ppermute | solution.py:122
  127.5 22.5 %conditional.26 = (bf16[256,1536]{1,0:T(8,128)(2,1)}, bf16[256,1536]{1,0:T(8,128)(2,1)}, bf16[384,1152]{1,0:T(8,128)(2,1)}) conditional(s32[]{:T(128)} %convert_element_type.83, () %tuple.247, (bf16[256,1536]{1,0:T(8,128)(2,1)}, s32[2]{0:T(128)S(1)}, bf16[384,1152]{1,0:T(8,128)(2,1)}, bf16[384,1152]{1,0:T(8,128)(2,1)}) %tuple.248), branch_computations={%region_11.12_spmd, %region_12.13_spmd} | conditional | bytes 6291560 | solution.py:101
  131.3 14.8 %collective-permute-done.7 = bf16[256,1536]{1,0:T(8,128)(2,1)} collective-permute-done((bf16[256,1536]{1,0:T(8,128)(2,1)}, bf16[256,1536]{1,0:T(8,128)(2,1)}, u32[]{:S(2)}, u32[]{:S(2)}) %collective-permute-start.7) | collective-permute-done | bytes 786464 | tf_op jit(solution)/shard_map/cond/branch_1_fun/swap_tensor_2/ppermute | solution.py:122
  146.1 3.9 collective-permute-done.8
  151.4 14.2 %conditional.27 = (bf16[128,1536]{1,0:T(8,128)(2,1)}, bf16[128,1536]{1,0:T(8,128)(2,1)}, bf16[256,1536]{1,0:T(8,128)(2,1)}, bf16[256,1536]{1,0:T(8,128)(2,1)}, bf16[256,1536]{1,0:T(8,128)(2,1)}) conditional(s32[]{:T(128)} %convert_element_type.83, () %tuple.250, (s32[2]{0:T(128)S(1)}, bf16[256,1536]{1,0:T(8,128)(2,1)}, ...), branch_computations={%region_13.14_spmd, %region_14.17_spmd} | conditional | flops 1 | bytes 12583205 | solution.py:101
  155.5 7.9 %conditional = (bf16[256,1536]{1,0:T(8,128)(2,1)}, bf16[256,1536]{1,0:T(8,128)(2,1)}, bf16[256,1536]{1,0:T(8,128)(2,1)}) conditional(s32[]{:T(128)} %convert_element_type.16, () %tuple.113, (bf16[256,1536]{1,0:T(8,128)(2,1)}, bf16[256,1536]{1,0:T(8,128)(2,1)}, bf16[256,1536]{1,0:T(8,128)(2,1)}) %tuple.114), branch_computations={%region_15.15_spmd, %region_16.16_spmd} | conditional | bytes 9437328 | solution.py:101
  165.6 6.4 %collective-permute-done.56 = bf16[384,1152]{1,0:T(8,128)(2,1)} collective-permute-done((bf16[384,1152]{1,0:T(8,128)(2,1)}, bf16[384,1152]{1,0:T(8,128)(2,1)}, u32[]{:S(2)}, u32[]{:S(2)}) %collective-permute-start.56) | collective-permute-done | bytes 884768 | tf_op jit(solution)/shard_map/swap_dp_1/ppermute | solution.py:122
  174.6 22.0 %conditional.29 = (bf16[384,1152]{1,0:T(8,128)(2,1)}, bf16[256,1536]{1,0:T(8,128)(2,1)}, bf16[256,1536]{1,0:T(8,128)(2,1)}, bf16[1024,1536]{1,0:T(8,128)(2,1)}, ...) conditional(s32[]{:T(128)} %convert_element_type.83, () %tuple.231, ...), branch_computations={%region_19.20_spmd, %region_20.21_spmd} | conditional | bytes 12681286 | solution.py:101
  177.1 15.4 %ffn_up.2 = (bf16[1024,1536]{1,0:T(8,128)(2,1)}, bf16[1024,1152]{1,0:T(8,128)(2,1)}, bf16[1024,1152]{1,0:T(8,128)(2,1)}, bf16[1024,1152]{1,0:T(8,128)(2,1)}) custom-call(s32[2]{0:T(128)S(1)} %get-tuple-element.555.scal, bf16[256,1536]{1,0:T(8,128)(2,1)} %get-tuple-element.556.refs_0_, bf16[256,1536]{1,0:T(8,128)(2,1)} %get-tuple-element.557.refs_1_, ...), custom_call_target="tpu_custom_call" | custom-call | tf_op jit(solution)/shard_map/cond/branch_1_fun/ffn_up/pallas_call | solution.py:245
  196.6 16.3 %conditional.30 = (bf16[256,1536]{1,0:T(8,128)(2,1)}, bf16[256,1536]{1,0:T(8,128)(2,1)}, bf16[1024,1536]{1,0:T(8,128)(2,1)}, bf16[1024,1152]{1,0:T(8,128)(2,1)},...) conditional(s32[]{:T(128)} %convert_element_type.83, () %tuple.257, (s32[2]{0:T(128)S(1)}, ...), branch_computations={%region_21.22_spmd, %region_22.23_spmd} | conditional | bytes 11796540 | solution.py:101
  197.1 15.8 %ffn_up.3 = (bf16[1024,1536]{1,0:T(8,128)(2,1)}, bf16[1024,1152]{1,0:T(8,128)(2,1)}, bf16[1024,1152]{1,0:T(8,128)(2,1)}, bf16[1024,1152]{1,0:T(8,128)(2,1)}) custom-call(s32[2]{0:T(128)S(1)} %get-tuple-element.578.scal, bf16[256,1536]{1,0:T(8,128)(2,1)} %get-tuple-element.579.refs_0_, bf16[256,1536]{1,0:T(8,128)(2,1)} %get-tuple-element.580.refs_1_, ...), custom_call_target="tpu_custom_call" | custom-call | tf_op jit(solution)/shard_map/cond/branch_1_fun/ffn_up/pallas_call | solution.py:245
  213.6 13.2 %conditional.31 = ((bf16[768,1152]{1,0:T(8,128)(2,1)}, bf16[768,1152]{1,0:T(8,128)(2,1)})) conditional(s32[]{:T(128)} %convert_element_type.83, () %tuple.261, (s32[2]{0:T(128)S(1)}, bf16[256,1536]{1,0:T(8,128)(2,1)}, bf16[256,1536]{1,0:T(8,128)(2,1)}, bf16[256,1536]{1,0:T(8,128)(2,1)}, bf16[256,1536]{1,0:T(8,128)(2,1)}, ...), branch_computations={%region_23.24_spmd, %region_24.25_spmd} | conditional | bytes 3538972 | solution.py:101
  213.6 13.2 %grad_down.1 = (bf16[768,1152]{1,0:T(8,128)(2,1)}, bf16[768,1152]{1,0:T(8,128)(2,1)}) custom-call(s32[2]{0:T(128)S(1)} %get-tuple-element.599.scal, bf16[256,1536]{1,0:T(8,128)(2,1)} %get-tuple-element.600.refs_0_, bf16[256,1536]{1,0:T(8,128)(2,1)} %get-tuple-element.601.refs_1_, bf16[256,1536]{1,0:T(8,128)(2,1)} %get-tuple-element.602.refs_2_, ...), custom_call_target="tpu_custom_call" | custom-call | tf_op jit(solution)/shard_map/cond/branch_1_fun/grad_down/pallas_call | solution.py:378
  226.9 8.0 %collective-permute-done.58 = bf16[384,1152]{1,0:T(8,128)(2,1)} collective-permute-done((bf16[384,1152]{1,0:T(8,128)(2,1)}, bf16[384,1152]{1,0:T(8,128)(2,1)}, u32[]{:S(2)}, u32[]{:S(2)}) %collective-permute-start.58) | collective-permute-done | bytes 884768 | tf_op jit(solution)/shard_map/swap_dp_1/ppermute | solution.py:122
  235.5 54.6 %conditional.32 = (bf16[1024,1152]{1,0:T(8,128)(2,1)}, bf16[1024,1152]{1,0:T(8,128)(2,1)}, bf16[1024,1152]{1,0:T(8,128)(2,1)}, bf16[1024,1152]{1,0:T(8,128)(2,1)...) conditional(s32[]{:T(128)} %convert_element_type.83, () %tuple.260, ...), branch_computations={%region_25.26_spmd, %region_26.27_spmd} | conditional | bytes 14942304 | solution.py:101
  235.5 24.4 %ffn_back.3 = (bf16[1024,1152]{1,0:T(8,128)(2,1)}, bf16[1024,1152]{1,0:T(8,128)(2,1)}, bf16[1024,1536]{1,0:T(8,128)(2,1)}) custom-call(s32[2]{0:T(128)S(1)} %get-tuple-element.610.scal, bf16[256,1536]{1,0:T(8,128)(2,1)} %get-tuple-element.630.refs_0_, bf16[256,1536]{1,0:T(8,128)(2,1)} %get-tuple-element.631.refs_1_, ...), custom_call_target="tpu_custom_call" | custom-call | tf_op jit(solution)/shard_map/cond/branch_1_fun/ffn_back/pallas_call | solution.py:308
  260.0 24.6 %ffn_back.2 = (bf16[1024,1152]{1,0:T(8,128)(2,1)}, bf16[1024,1152]{1,0:T(8,128)(2,1)}, bf16[1024,1536]{1,0:T(8,128)(2,1)}) custom-call(s32[2]{0:T(128)S(1)} %get-tuple-element.610.scal, bf16[256,1536]{1,0:T(8,128)(2,1)} %get-tuple-element.611.refs_0_, bf16[256,1536]{1,0:T(8,128)(2,1)} %get-tuple-element.612.refs_1_, ...), custom_call_target="tpu_custom_call" | custom-call | tf_op jit(solution)/shard_map/cond/branch_1_fun/ffn_back/pallas_call | solution.py:308
  284.6 5.5 %spread_eight.1 = (f32[256,1536]{1,0:T(8,128)}, f32[256,1536]{1,0:T(8,128)}, f32[256,1536]{1,0:T(8,128)}, bf16[128,1536]{1,0:T(8,128)(2,1)}, bf16[128,1536]{1,0:T(8,128)(2,1)}) custom-call(s32[2]{0:T(128)S(1)} %get-tuple-element.610.scal, bf16[1024,1536]{1,0:T(8,128)(2,1)} %get-tuple-element.638.kept_ref, bf16[1024,1536]{1,0:T(8,128)(2,1)} %collective-permute-done.21.arrived_ref), custom_call_target="tpu_custom_call" | custom-call | tf_op jit(solution)/shard_map/cond/branch_1_fun/spread_eight/pallas_call | solution.py:393
  290.1 25.3 %conditional.33 = (bf16[1024,1536]{1,0:T(8,128)(2,1)}, bf16[1024,1536]{1,0:T(8,128)(2,1)}, bf16[256,1536]{1,0:T(8,128)(2,1)}, bf16[256,1536]{1,0:T(8,128)(2,1)}) conditional(s32[]{:T(128)} %convert_element_type.83, () %tuple.267, (s32[2]{0:T(128)S(1)}, bf16[1024,1152]{1,0:T(8,128)(2,1)}, bf16[384,1152]{1,0:T(8,128)(2,1)}, ...), branch_computations={%region_27.28_spmd, %region_28.31_spmd} | conditional | flops 1 | bytes 15728869 | solution.py:101
  293.8 18.2 %conditional.1 = (bf16[1024,1536]{1,0:T(8,128)(2,1)}, bf16[1024,1536]{1,0:T(8,128)(2,1)}) conditional(s32[]{:T(128)} %convert_element_type.17, () %tuple.130, (s32[2]{0:T(128)S(1)}, bf16[1024,1152]{1,0:T(8,128)(2,1)}, bf16[384,1152]{1,0:T(8,128)(2,1)}, bf16[384,1152]{1,0:T(8,128)(2,1)}, bf16[384,1152]{1,0:T(8,128)(2,1)}, ...), branch_computations={%region_29.29_spmd, %region_30.30_spmd} | conditional | bytes 12582968 | solution.py:101
  293.8 9.0 %block_rows.3 = bf16[1024,1536]{1,0:T(8,128)(2,1)} custom-call(s32[2]{0:T(128)S(1)} %get-tuple-element.645.scal, bf16[1024,1152]{1,0:T(8,128)(2,1)} %get-tuple-element.651.left_ref, bf16[384,1152]{1,0:T(8,128)(2,1)} %get-tuple-element.647.refs_0_, bf16[384,1152]{1,0:T(8,128)(2,1)} %get-tuple-element.648.refs_1_, ...), custom_call_target="tpu_custom_call" | custom-call | tf_op jit(solution)/shard_map/cond/branch_1_fun/cond/branch_1_fun/block_rows/pallas_call | solution.py:336
  302.9 9.1 %block_rows.2 = bf16[1024,1536]{1,0:T(8,128)(2,1)} custom-call(s32[2]{0:T(128)S(1)} %get-tuple-element.645.scal, bf16[1024,1152]{1,0:T(8,128)(2,1)} %get-tuple-element.646.left_ref, bf16[384,1152]{1,0:T(8,128)(2,1)} %get-tuple-element.647.refs_0_, bf16[384,1152]{1,0:T(8,128)(2,1)} %get-tuple-element.648.refs_1_, ...), custom_call_target="tpu_custom_call" | custom-call | tf_op jit(solution)/shard_map/cond/branch_1_fun/cond/branch_1_fun/block_rows/pallas_call | solution.py:336
  315.4 28.0 %conditional.34 = (bf16[768,1152]{1,0:T(8,128)(2,1)}, bf16[768,1152]{1,0:T(8,128)(2,1)}, bf16[384,1152]{1,0:T(8,128)(2,1)}, bf16[384,1152]{1,0:T(8,128)(2,1)}, f...) conditional(s32[]{:T(128)} %convert_element_type.83, () %tuple.230, ...), branch_computations={%region_31.32_spmd, %region_32.33_spmd} | conditional | bytes 12435552 | solution.py:101
  316.7 3.7 fold_sum.8
  320.3 5.4 fold_fixed.4
  325.7 12.9 %grad_up.1 = (bf16[768,1152]{1,0:T(8,128)(2,1)}, bf16[768,1152]{1,0:T(8,128)(2,1)}) custom-call(s32[2]{0:T(128)S(1)} %get-tuple-element.671.scal, bf16[1024,1536]{1,0:T(8,128)(2,1)} %get-tuple-element.672.refs_0_, bf16[1024,1536]{1,0:T(8,128)(2,1)} %get-tuple-element.673.refs_1_, bf16[1024,1152]{1,0:T(8,128)(2,1)} %get-tuple-element.674.refs_2_, ...), custom_call_target="tpu_custom_call" | custom-call | tf_op jit(solution)/shard_map/cond/branch_1_fun/grad_up/pallas_call | solution.py:378
  338.7 4.7 norm_two_back.1
  347.5 46.9 %conditional.35 = (bf16[768,1152]{1,0:T(8,128)(2,1)}, bf16[768,1152]{1,0:T(8,128)(2,1)}, bf16[1024,384]{1,0:T(8,128)(2,1)}, f32[1024,128]{1,0:T(8,128)}, bf16[10...) conditional(s32[]{:T(128)} %convert_element_type.83, () %tuple.272, ...), branch_computations={%region_33.34_spmd, %region_34.37_spmd} | conditional | flops 3145729 | bytes 12583133 | solution.py:101
  347.5 21.6 %conditional.2 = (bf16[512,1536]{1,0:T(8,128)(2,1)}, bf16[768,1152]{1,0:T(8,128)(2,1)}, bf16[768,1152]{1,0:T(8,128)(2,1)}) conditional(s32[]{:T(128)} %convert_element_type.18, () %tuple.141, (s32[2]{0:T(128)S(1)}, bf16[1024,1536]{1,0:T(8,128)(2,1)}, bf16[1024,1536]{1,0:T(8,128)(2,1)}, bf16[1024,1152]{1,0:T(8,128)(2,1)}, ...), branch_computations={%region_35.35_spmd, %region_36.36_spmd} | conditional | flops 3145728 | bytes 6291520 | solution.py:101
  348.4 12.8 %grad_gate.1 = (bf16[768,1152]{1,0:T(8,128)(2,1)}, bf16[768,1152]{1,0:T(8,128)(2,1)}) custom-call(s32[2]{0:T(128)S(1)} %get-tuple-element.698.scal, bf16[1024,1536]{1,0:T(8,128)(2,1)} %get-tuple-element.699.refs_0_, bf16[1024,1536]{1,0:T(8,128)(2,1)} %get-tuple-element.700.refs_1_, bf16[1024,1152]{1,0:T(8,128)(2,1)} %get-tuple-element.701.refs_2_, ...), custom_call_target="tpu_custom_call" | custom-call | tf_op jit(solution)/shard_map/cond/branch_1_fun/cond/branch_1_fun/grad_gate/pallas_call | solution.py:378
  361.3 5.2 collective-permute-done.27
  369.2 3.7 collective-permute-done.28.core_ref
  372.9 21.5 %attend_back.1 = (bf16[1024,384]{1,0:T(8,128)(2,1)}, f32[1024,128]{1,0:T(8,128)}, bf16[1024,128]{1,0:T(8,128)(2,1)}, f32[8,640]{1,0:T(8,128)}, bf16[768,384]{1,0:T(8,128)(2,1)}, /*index=5*/bf16[768,384]{1,0:T(8,128)(2,1)}) custom-call(s32[2]{0:T(128)S(1)} %get-tuple-element.706.scal, bf16[1024,384]{1,0:T(8,128)(2,1)} %get-tuple-element.716.query_ref, ...), custom_call_target="tpu_custom_call" | custom-call | tf_op jit(solution)/shard_map/cond/branch_1_fun/attend_back/pallas_call | solution.py:750
  394.4 4.9 collective-permute-done.60
  402.6 59.1 %conditional.36 = (bf16[384,1152]{1,0:T(8,128)(2,1)}, bf16[384,1152]{1,0:T(8,128)(2,1)}, bf16[768,1152]{1,0:T(8,128)(2,1)}, bf16[192,1152]{1,0:T(8,128)(2,1)}, b...) conditional(s32[]{:T(128)} %convert_element_type.83, () %tuple.229, ...), branch_computations={%region_37.38_spmd, %region_38.43_spmd} | conditional | flops 16910 | bytes 32267256 | solution.py:101
  402.7 3.8 fold_sum.10
  407.6 54.1 %conditional.4 = (bf16[192,1152]{1,0:T(8,128)(2,1)}, bf16[192,1152]{1,0:T(8,128)(2,1)}, bf16[768,512]{1,0:T(8,128)(2,1)}, bf16[256,1536]{1,0:T(8,128)(2,1)}, f32...) conditional(s32[]{:T(128)} %convert_element_type.25, () %tuple.156, ...), branch_computations={%region_39.39_spmd, %region_40.42_spmd} | conditional | flops 16909 | bytes 16931384 | solution.py:101
  410.2 9.2 %project_back.1 = (bf16[1024,512]{1,0:T(8,128)(2,1)}, bf16[512,1536]{1,0:T(8,128)(2,1)}, bf16[512,1536]{1,0:T(8,128)(2,1)}, f32[8,1536]{1,0:T(8,128)}) custom-call(s32[2]{0:T(128)S(1)} %get-tuple-element.750.scal, bf16[1024,384]{1,0:T(8,128)(2,1)} %get-tuple-element.757.query_ref, f32[1024,128]{1,0:T(8,128)} %get-tuple-element.758.kept_kv_ref, ...), custom_call_target="tpu_custom_call" | custom-call | tf_op jit(solution)/shard_map/cond/branch_1_fun/cond/branch_1_fun/project_back/pallas_call | solution.py:808
  420.0 5.7 %project_grad.1 = (bf16[768,512]{1,0:T(8,128)(2,1)}, bf16[768,512]{1,0:T(8,128)(2,1)}) custom-call(s32[2]{0:T(128)S(1)} %get-tuple-element.750.scal, bf16[512,1536]{1,0:T(8,128)(2,1)S(1)} %get-tuple-element.755.pair_ref, bf16[512,1536]{1,0:T(8,128)(2,1)} %get-tuple-element.756.core_ref, bf16[1024,512]{1,0:T(8,128)(2,1)} %get-tuple-element.768.grads_ref), custom_call_target="tpu_custom_call" | custom-call | tf_op jit(solution)/shard_map/cond/branch_1_fun/cond/branch_1_fun/project_grad/pallas_call | solution.py:836
  428.8 32.9 %conditional.3 = (bf16[256,1536]{1,0:T(8,128)(2,1)}, f32[32,160]{1,0:T(8,128)}, f32[256,1536]{1,0:T(8,128)}, bf16[256,1536]{1,0:T(8,128)(2,1)}, bf16[768,512]{1,0:T(8,128)(2,1)}) conditional(s32[]{:T(128)} %convert_element_type.24, () %tuple.152, (s32[2]{0:T(128)S(1)}, f32[512,1536]{1,0:T(8,128)}, bf16[512,1536]{1,0:T(8,128)(2,1)}, ...), branch_computations={%region_41.40_spmd, %region_42.41_spmd} | conditional | flops 16908 | bytes 9591090 | solution.py:101
  436.4 3.9 block_step.1
  441.0 7.4 %collective-permute-done.34.arrived_ref = bf16[256,1536]{1,0:T(8,128)(2,1)S(1)} collective-permute-done((bf16[256,1536]{1,0:T(8,128)(2,1)}, bf16[256,1536]{1,0:T(8,128)(2,1)S(1)}, u32[]{:S(2)}, u32[]{:S(2)}) %collective-permute-start.34) | collective-permute-done | bytes 786464 | tf_op jit(solution)/shard_map/cond/branch_1_fun/cond/branch_1_fun/cond/branch_1_fun/swap_tensor_2/ppermute | solution.py:122
  452.6 9.0 %collective-permute-done.35 = bf16[768,512]{1,0:T(8,128)(2,1)} collective-permute-done((bf16[768,512]{1,0:T(8,128)(2,1)}, bf16[768,512]{1,0:T(8,128)(2,1)}, u32[]{:S(2)}, u32[]{:S(2)}) %collective-permute-start.35) | collective-permute-done | bytes 786464 | tf_op jit(solution)/shard_map/cond/branch_1_fun/cond/branch_1_fun/cond/branch_1_fun/swap_dp_2/ppermute | solution.py:122
  461.7 3.8 fold_sum.14
  466.9 4.8 all-to-all-start
  471.8 43.5 %conditional.37 = (f32[192,896]{1,0:T(8,128)}, bf16[192,896]{1,0:T(8,128)(2,1)S(1)}, bf16[192,1152]{1,0:T(8,128)(2,1)}, bf16[192,1152]{1,0:T(8,128)(2,1)}, bf16[...) conditional(s32[]{:T(128)} %convert_element_type.83, () %tuple.228, (s32[2]{0:T(128)S(1)}, ...), branch_computations={%region_43.44_spmd, %region_44.47_spmd} | conditional | flops 2949131 | bytes 24478200 | solution.py:101
  475.2 20.0 %conditional.5 = (f32[384,896]{1,0:T(8,128)S(1)}, bf16[192,1152]{1,0:T(8,128)(2,1)}, bf16[192,1152]{1,0:T(8,128)(2,1)}) conditional(s32[]{:T(128)} %convert_element_type.71, () %tuple.165, (s32[2]{0:T(128)S(1)}, bf16[768,512]{1,0:T(8,128)(2,1)}, bf16[768,512]{1,0:T(8,128)(2,1)}, bf16[384,1152]{1,0:T(8,128)(2,1)}, bf16[384,1152]{1,0:T(8,128)(2,1)}, ...), branch_computations={%region_45.45_spmd, %region_46.46_spmd} | conditional | flops 1376256 | bytes 11010208 | solution.py:101
  484.5 10.4 %collective-permute-done.30 = bf16[384,384]{1,0:T(8,128)(2,1)S(1)} collective-permute-done((bf16[384,384]{1,0:T(8,128)(2,1)}, bf16[384,384]{1,0:T(8,128)(2,1)S(1)}, u32[]{:S(2)}, u32[]{:S(2)}) %collective-permute-start.30) | collective-permute-done | bytes 294944 | tf_op jit(solution)/shard_map/cond/branch_1_fun/cond/branch_1_fun/swap_dp_1/ppermute | solution.py:122
  503.0 12.3 %collective-permute-done.33 = bf16[192,1152]{1,0:T(8,128)(2,1)} collective-permute-done((bf16[192,1152]{1,0:T(8,128)(2,1)}, bf16[192,1152]{1,0:T(8,128)(2,1)}, u32[]{:S(2)}, u32[]{:S(2)}) %collective-permute-start.33) | collective-permute-done | bytes 442400 | tf_op jit(solution)/shard_map/cond/branch_1_fun/swap_dp_2/ppermute | solution.py:122
  515.3 3.6 collective-permute-start.65
  527.8 4.9 collective-permute-done.65
  (259 shorter events, 168.9 us)
Async XLA Ops:
  2.5 14.1 %collective-permute-start.40 = (bf16[192,512]{1,0:T(8,128)(2,1)S(1)}, bf16[192,512]{1,0:T(8,128)(2,1)S(1)}, u32[]{:S(2)}, u32[]{:S(2)}) collective-permute-start(bf16[192,512]{1,0:T(8,128)(2,1)S(1)} %pad_maximum_fusion.8), channel_id=1, source_target_pairs={{0,16},{4,20},{8,24},{12,28},{16,0},{20,4},{24,8},{28,12},{1,17},{... | collective-permute-start | bytes 589832 | tf_op jit(solution)/shard_map/swap_dp_4/ppermute | solution.py:122
  6.6 10.0 %collective-permute-start.41 = (bf16[192,512]{1,0:T(8,128)(2,1)S(1)}, bf16[192,512]{1,0:T(8,128)(2,1)S(1)}, u32[]{:S(2)}, u32[]{:S(2)}) collective-permute-start(bf16[192,512]{1,0:T(8,128)(2,1)S(1)} %pad_maximum_fusion.8), channel_id=1, source_target_pairs={{0,8},{4,12},{8,0},{12,4},{16,24},{20,28},{24,16},{28,20},{1,9},{5... | collective-permute-start | bytes 589832 | tf_op jit(solution)/shard_map/swap_dp_2/ppermute | solution.py:122
  8.2 8.5 %collective-permute-start.42 = (bf16[192,512]{1,0:T(8,128)(2,1)S(1)}, bf16[192,512]{1,0:T(8,128)(2,1)S(1)}, u32[]{:S(2)}, u32[]{:S(2)}) collective-permute-start(bf16[192,512]{1,0:T(8,128)(2,1)S(1)} %pad_maximum_fusion.8), channel_id=1, source_target_pairs={{0,4},{4,0},{8,12},{12,8},{16,20},{20,16},{24,28},{28,24},{1,5},{5... | collective-permute-start | bytes 589832 | tf_op jit(solution)/shard_map/swap_dp_1/ppermute | solution.py:122
  12.1 21.1 %collective-permute-start.45 = (bf16[256,1536]{1,0:T(8,128)(2,1)S(1)}, bf16[256,1536]{1,0:T(8,128)(2,1)}, u32[]{:S(2)}, u32[]{:S(2)}) collective-permute-start(bf16[256,1536]{1,0:T(8,128)(2,1)S(1)} %fusion.3), channel_id=1, source_target_pairs={{0,2},{1,3},{2,0},{3,1},{4,6},{5,7},{6,4},{7,5},{8,10},{9,11},{10,... | collective-permute-start | bytes 2359304 | tf_op jit(solution)/shard_map/swap_tensor_2/ppermute | solution.py:122
  16.2 18.5 %collective-permute-start.46 = (bf16[192,1152]{1,0:T(8,128)(2,1)}, bf16[192,1152]{1,0:T(8,128)(2,1)}, u32[]{:S(2)}, u32[]{:S(2)}) collective-permute-start(bf16[192,1152]{1,0:T(8,128)(2,1)} %get-tuple-element.1072), channel_id=1, source_target_pairs={{0,8},{4,12},{8,0},{12,4},{16,24},{20,28},{24,16},{28,20},{1,9},{5... | collective-permute-start | bytes 1327112 | tf_op jit(solution)/shard_map/swap_dp_2/ppermute | solution.py:122
  16.7 18.0 %collective-permute-start.44 = (bf16[192,512]{1,0:T(8,128)(2,1)S(1)}, bf16[192,512]{1,0:T(8,128)(2,1)}, u32[]{:S(2)}, u32[]{:S(2)}) collective-permute-start(bf16[192,512]{1,0:T(8,128)(2,1)S(1)} %collective-permute-done.40), channel_id=1, source_target_pairs={{0,8},{4,12},{8,0},{12,4},{16,24},{20,28},{24,16},{28,20},{1,9},{5... | collective-permute-start | bytes 589832 | tf_op jit(solution)/shard_map/swap_dp_2/ppermute | solution.py:122
  19.1 15.5 %collective-permute-start.43 = (bf16[384,512]{1,0:T(8,128)(2,1)}, bf16[384,512]{1,0:T(8,128)(2,1)S(1)}, u32[]{:S(2)}, u32[]{:S(2)}) collective-permute-start(bf16[384,512]{1,0:T(8,128)(2,1)} %pad_maximum_fusion.6), channel_id=1, source_target_pairs={{0,4},{4,0},{8,12},{12,8},{16,20},{20,16},{24,28},{28,24},{1,5},{5... | collective-permute-start | bytes 1179656 | tf_op jit(solution)/shard_map/swap_dp_1/ppermute | solution.py:122
  20.2 12.3 %collective-permute-start.47 = (bf16[192,384]{1,0:T(8,128)(2,1)S(1)}, bf16[192,384]{1,0:T(8,128)(2,1)S(1)}, u32[]{:S(2)}, u32[]{:S(2)}) collective-permute-start(bf16[192,384]{1,0:T(8,128)(2,1)S(1)} %bitcast.32), channel_id=1, source_target_pairs={{0,16},{4,20},{8,24},{12,28},{16,0},{20,4},{24,8},{28,12},{1,17},{... | collective-permute-start | bytes 442376 | tf_op jit(solution)/shard_map/swap_dp_4/ppermute | solution.py:122
  37.3 10.2 %collective-permute-start.1 = (bf16[512,1536]{1,0:T(8,128)(2,1)S(1)}, bf16[512,1536]{1,0:T(8,128)(2,1)}, u32[]{:S(2)}, u32[]{:S(2)}) collective-permute-start(bf16[512,1536]{1,0:T(8,128)(2,1)S(1)} %get-tuple-element.494), channel_id=1, source_target_pairs={{0,1},{1,0},{2,3},{3,2},{4,5},{5,4},{6,7},{7,6},{8,9},{9,8},{10,11... | collective-permute-start | bytes 4718600 | tf_op jit(solution)/shard_map/cond/branch_1_fun/swap_tensor_1/ppermute | solution.py:122
  37.3 10.2 %collective-permute-start.2 = (bf16[384,384]{1,0:T(8,128)(2,1)S(1)}, bf16[384,384]{1,0:T(8,128)(2,1)}, u32[]{:S(2)}, u32[]{:S(2)}) collective-permute-start(bf16[384,384]{1,0:T(8,128)(2,1)S(1)} %get-tuple-element.495), channel_id=1, source_target_pairs={{0,8},{4,12},{8,0},{12,4},{16,24},{20,28},{24,16},{28,20},{1,9},{5... | collective-permute-start | bytes 884744 | tf_op jit(solution)/shard_map/cond/branch_1_fun/swap_dp_2/ppermute | solution.py:122
  39.8 7.3 %collective-permute-start = (bf16[192,512]{1,0:T(8,128)(2,1)}, bf16[192,512]{1,0:T(8,128)(2,1)}, u32[]{:S(2)}, u32[]{:S(2)}) collective-permute-start(bf16[192,512]{1,0:T(8,128)(2,1)} %get-tuple-element.493), channel_id=1, source_target_pairs={{0,4},{4,0},{8,12},{12,8},{16,20},{20,16},{24,28},{28,24},{1,5},{5... | collective-permute-start | bytes 589832 | tf_op jit(solution)/shard_map/cond/branch_1_fun/swap_dp_1/ppermute | solution.py:122
  48.5 38.0 %collective-permute-start.50 = (bf16[384,1152]{1,0:T(8,128)(2,1)}, bf16[384,1152]{1,0:T(8,128)(2,1)}, u32[]{:S(2)}, u32[]{:S(2)}) collective-permute-start(bf16[384,1152]{1,0:T(8,128)(2,1)} %get-tuple-element.1102), channel_id=1, source_target_pairs={{0,8},{4,12},{8,0},{12,4},{16,24},{20,28},{24,16},{28,20},{1,9},{5... | collective-permute-start | bytes 2654216 | tf_op jit(solution)/shard_map/swap_dp_2/ppermute | solution.py:122
  50.3 28.9 %collective-permute-start.48 = (bf16[256,1536]{1,0:T(8,128)(2,1)}, bf16[256,1536]{1,0:T(8,128)(2,1)}, u32[]{:S(2)}, u32[]{:S(2)}) collective-permute-start(bf16[256,1536]{1,0:T(8,128)(2,1)} %param.69), channel_id=1, source_target_pairs={{0,2},{1,3},{2,0},{3,1},{4,6},{5,7},{6,4},{7,5},{8,10},{9,11},{10,... | collective-permute-start | bytes 2359304 | tf_op jit(solution)/shard_map/swap_tensor_2/ppermute | solution.py:122
  51.2 21.5 %collective-permute-start.49 = (bf16[768,384]{1,0:T(8,128)(2,1)S(1)}, bf16[768,384]{1,0:T(8,128)(2,1)S(1)}, u32[]{:S(2)}, u32[]{:S(2)}) collective-permute-start(bf16[768,384]{1,0:T(8,128)(2,1)S(1)} %pad_maximum_fusion.4.refs_0_.refs_2_.refs_4_.refs_6_), channel_id=1, source_target_pairs={{0,4},{4,0},{8,12},{12,8},{16,20},{20,16},{24,28},{28,24},{1,5},{5... | collective-permute-start | bytes 1769480 | tf_op jit(solution)/shard_map/swap_dp_1/ppermute | solution.py:122
  53.5 66.2 %collective-permute-start.52 = (bf16[384,1152]{1,0:T(8,128)(2,1)}, bf16[384,1152]{1,0:T(8,128)(2,1)}, u32[]{:S(2)}, u32[]{:S(2)}) collective-permute-start(bf16[384,1152]{1,0:T(8,128)(2,1)} %join_rows.3), channel_id=1, source_target_pairs={{0,16},{4,20},{8,24},{12,28},{16,0},{20,4},{24,8},{28,12},{1,17},{... | collective-permute-start | bytes 2654216 | tf_op jit(solution)/shard_map/swap_dp_4/ppermute | solution.py:122
  63.6 9.1 %collective-permute-start.4 = (bf16[256,1536]{1,0:T(8,128)(2,1)}, bf16[256,1536]{1,0:T(8,128)(2,1)}, u32[]{:S(2)}, u32[]{:S(2)}) collective-permute-start(bf16[256,1536]{1,0:T(8,128)(2,1)} %get-tuple-element.514), channel_id=1, source_target_pairs={{0,1},{1,0},{2,3},{3,2},{4,5},{5,4},{6,7},{7,6},{8,9},{9,8},{10,11... | collective-permute-start | bytes 2359304 | tf_op jit(solution)/shard_map/cond/branch_1_fun/swap_tensor_1/ppermute | solution.py:122
  86.5 3.8 collective-permute-start.5
  90.2 59.9 %collective-permute-start.53 = (bf16[768,1152]{1,0:T(8,128)(2,1)}, bf16[768,1152]{1,0:T(8,128)(2,1)S(1)}, u32[]{:S(2)}, u32[]{:S(2)}) collective-permute-start(bf16[768,1152]{1,0:T(8,128)(2,1)} %get-tuple-element.1112), channel_id=1, source_target_pairs={{0,4},{4,0},{8,12},{12,8},{16,20},{20,16},{24,28},{28,24},{1,5},{5... | collective-permute-start | bytes 5308424 | tf_op jit(solution)/shard_map/swap_dp_1/ppermute | solution.py:122
  91.5 35.2 %collective-permute-start.51 = (bf16[256,1536]{1,0:T(8,128)(2,1)}, bf16[256,1536]{1,0:T(8,128)(2,1)}, u32[]{:S(2)}, u32[]{:S(2)}) collective-permute-start(bf16[256,1536]{1,0:T(8,128)(2,1)} %param.69), channel_id=1, source_target_pairs={{0,8},{4,12},{8,0},{12,4},{16,24},{20,28},{24,16},{28,20},{1,9},{5... | collective-permute-start | bytes 2359304 | tf_op jit(solution)/shard_map/swap_dp_2/ppermute | solution.py:122
  91.5 58.5 %collective-permute-start.55 = (bf16[384,1152]{1,0:T(8,128)(2,1)}, bf16[384,1152]{1,0:T(8,128)(2,1)}, u32[]{:S(2)}, u32[]{:S(2)}) collective-permute-start(bf16[384,1152]{1,0:T(8,128)(2,1)} %get-tuple-element.1116), channel_id=1, source_target_pairs={{0,16},{4,20},{8,24},{12,28},{16,0},{20,4},{24,8},{28,12},{1,17},{... | collective-permute-start | bytes 2654216 | tf_op jit(solution)/shard_map/swap_dp_4/ppermute | solution.py:122
  96.9 19.1 %collective-permute-start.6 = (bf16[256,1536]{1,0:T(8,128)(2,1)}, bf16[256,1536]{1,0:T(8,128)(2,1)}, u32[]{:S(2)}, u32[]{:S(2)}) collective-permute-start(bf16[256,1536]{1,0:T(8,128)(2,1)} %get-tuple-element.529), channel_id=1, source_target_pairs={{0,2},{1,3},{2,0},{3,1},{4,6},{5,7},{6,4},{7,5},{8,10},{9,11},{10,... | collective-permute-start | bytes 2359304 | tf_op jit(solution)/shard_map/cond/branch_1_fun/swap_tensor_2/ppermute | solution.py:122
  126.7 23.4 %collective-permute-start.54 = (bf16[384,1152]{1,0:T(8,128)(2,1)}, bf16[384,1152]{1,0:T(8,128)(2,1)}, u32[]{:S(2)}, u32[]{:S(2)}) collective-permute-start(bf16[384,1152]{1,0:T(8,128)(2,1)} %collective-permute-done.52), channel_id=1, source_target_pairs={{0,4},{4,0},{8,12},{12,8},{16,20},{20,16},{24,28},{28,24},{1,5},{5... | collective-permute-start | bytes 2654216 | tf_op jit(solution)/shard_map/swap_dp_1/ppermute | solution.py:122
  127.5 18.6 %collective-permute-start.7 = (bf16[256,1536]{1,0:T(8,128)(2,1)}, bf16[256,1536]{1,0:T(8,128)(2,1)}, u32[]{:S(2)}, u32[]{:S(2)}) collective-permute-start(bf16[256,1536]{1,0:T(8,128)(2,1)} %get-tuple-element.531), channel_id=1, source_target_pairs={{0,2},{1,3},{2,0},{3,1},{4,6},{5,7},{6,4},{7,5},{8,10},{9,11},{10,... | collective-permute-start | bytes 2359304 | tf_op jit(solution)/shard_map/cond/branch_1_fun/swap_tensor_2/ppermute | solution.py:122
  128.9 21.1 %collective-permute-start.8 = (bf16[256,1536]{1,0:T(8,128)(2,1)}, bf16[256,1536]{1,0:T(8,128)(2,1)}, u32[]{:S(2)}, u32[]{:S(2)}) collective-permute-start(bf16[256,1536]{1,0:T(8,128)(2,1)} %get-tuple-element.531), channel_id=1, source_target_pairs={{0,8},{4,12},{8,0},{12,4},{16,24},{20,28},{24,16},{28,20},{1,9},{5... | collective-permute-start | bytes 2359304 | tf_op jit(solution)/shard_map/cond/branch_1_fun/swap_dp_2/ppermute | solution.py:122
  150.2 21.8 %collective-permute-start.56 = (bf16[384,1152]{1,0:T(8,128)(2,1)}, bf16[384,1152]{1,0:T(8,128)(2,1)}, u32[]{:S(2)}, u32[]{:S(2)}) collective-permute-start(bf16[384,1152]{1,0:T(8,128)(2,1)} %collective-permute-done.55), channel_id=1, source_target_pairs={{0,4},{4,0},{8,12},{12,8},{16,20},{20,16},{24,28},{28,24},{1,5},{5... | collective-permute-start | bytes 2654216 | tf_op jit(solution)/shard_map/swap_dp_1/ppermute | solution.py:122
  153.7 10.4 %collective-permute-start.12 = (bf16[128,1536]{1,0:T(8,128)(2,1)}, bf16[128,1536]{1,0:T(8,128)(2,1)}, u32[]{:S(2)}, u32[]{:S(2)}) collective-permute-start(bf16[128,1536]{1,0:T(8,128)(2,1)} %get-tuple-element.547), channel_id=1, source_target_pairs={{0,2},{1,3},{2,0},{3,1},{4,6},{5,7},{6,4},{7,5},{8,10},{9,11},{10,... | collective-permute-start | bytes 1179656 | tf_op jit(solution)/shard_map/cond/branch_1_fun/swap_tensor_2/ppermute | solution.py:122
  155.5 10.1 %collective-permute-start.13 = (bf16[128,1536]{1,0:T(8,128)(2,1)}, bf16[128,1536]{1,0:T(8,128)(2,1)}, u32[]{:S(2)}, u32[]{:S(2)}) collective-permute-start(bf16[128,1536]{1,0:T(8,128)(2,1)} %get-tuple-element.548), channel_id=1, source_target_pairs={{0,8},{4,12},{8,0},{12,4},{16,24},{20,28},{24,16},{28,20},{1,9},{5... | collective-permute-start | bytes 1179656 | tf_op jit(solution)/shard_map/cond/branch_1_fun/swap_dp_2/ppermute | solution.py:122
  172.0 40.9 %collective-permute-start.57 = (bf16[384,1152]{1,0:T(8,128)(2,1)}, bf16[384,1152]{1,0:T(8,128)(2,1)}, u32[]{:S(2)}, u32[]{:S(2)}) collective-permute-start(bf16[384,1152]{1,0:T(8,128)(2,1)} %get-tuple-element.1130), channel_id=1, source_target_pairs={{0,16},{4,20},{8,24},{12,28},{16,0},{20,4},{24,8},{28,12},{1,17},{... | collective-permute-start | bytes 2654216 | tf_op jit(solution)/shard_map/swap_dp_4/ppermute | solution.py:122
  174.6 22.0 %collective-permute-start.16 = (bf16[384,1152]{1,0:T(8,128)(2,1)}, bf16[384,1152]{1,0:T(8,128)(2,1)}, u32[]{:S(2)}, u32[]{:S(2)}) collective-permute-start(bf16[384,1152]{1,0:T(8,128)(2,1)} %get-tuple-element.572), channel_id=1, source_target_pairs={{0,4},{4,0},{8,12},{12,8},{16,20},{20,16},{24,28},{28,24},{1,5},{5... | collective-permute-start | bytes 2654216 | tf_op jit(solution)/shard_map/cond/branch_1_fun/swap_dp_1/ppermute | solution.py:122
  175.3 19.7 %collective-permute-start.17 = (bf16[256,1536]{1,0:T(8,128)(2,1)}, bf16[256,1536]{1,0:T(8,128)(2,1)}, u32[]{:S(2)}, u32[]{:S(2)}) collective-permute-start(bf16[256,1536]{1,0:T(8,128)(2,1)} %get-tuple-element.573), channel_id=1, source_target_pairs={{0,2},{1,3},{2,0},{3,1},{4,6},{5,7},{6,4},{7,5},{8,10},{9,11},{10,... | collective-permute-start | bytes 2359304 | tf_op jit(solution)/shard_map/cond/branch_1_fun/swap_tensor_2/ppermute | solution.py:122
  177.1 17.9 %collective-permute-start.18 = (bf16[256,1536]{1,0:T(8,128)(2,1)}, bf16[256,1536]{1,0:T(8,128)(2,1)}, u32[]{:S(2)}, u32[]{:S(2)}) collective-permute-start(bf16[256,1536]{1,0:T(8,128)(2,1)} %get-tuple-element.574), channel_id=1, source_target_pairs={{0,1},{1,0},{2,3},{3,2},{4,5},{5,4},{6,7},{7,6},{8,9},{9,8},{10,11... | collective-permute-start | bytes 2359304 | tf_op jit(solution)/shard_map/cond/branch_1_fun/swap_tensor_1/ppermute | solution.py:122
  196.6 16.3 %collective-permute-start.19 = (bf16[256,1536]{1,0:T(8,128)(2,1)}, bf16[256,1536]{1,0:T(8,128)(2,1)}, u32[]{:S(2)}, u32[]{:S(2)}) collective-permute-start(bf16[256,1536]{1,0:T(8,128)(2,1)} %get-tuple-element.595), channel_id=1, source_target_pairs={{0,1},{1,0},{2,3},{3,2},{4,5},{5,4},{6,7},{7,6},{8,9},{9,8},{10,11... | collective-permute-start | bytes 2359304 | tf_op jit(solution)/shard_map/cond/branch_1_fun/swap_tensor_1/ppermute | solution.py:122
  196.6 16.3 %collective-permute-start.20 = (bf16[256,1536]{1,0:T(8,128)(2,1)}, bf16[256,1536]{1,0:T(8,128)(2,1)}, u32[]{:S(2)}, u32[]{:S(2)}) collective-permute-start(bf16[256,1536]{1,0:T(8,128)(2,1)} %get-tuple-element.596), channel_id=1, source_target_pairs={{0,1},{1,0},{2,3},{3,2},{4,5},{5,4},{6,7},{7,6},{8,9},{9,8},{10,11... | collective-permute-start | bytes 2359304 | tf_op jit(solution)/shard_map/cond/branch_1_fun/swap_tensor_1/ppermute | solution.py:122
  212.9 21.9 %collective-permute-start.58 = (bf16[384,1152]{1,0:T(8,128)(2,1)}, bf16[384,1152]{1,0:T(8,128)(2,1)}, u32[]{:S(2)}, u32[]{:S(2)}) collective-permute-start(bf16[384,1152]{1,0:T(8,128)(2,1)} %collective-permute-done.57), channel_id=1, source_target_pairs={{0,4},{4,0},{8,12},{12,8},{16,20},{20,16},{24,28},{28,24},{1,5},{5... | collective-permute-start | bytes 2654216 | tf_op jit(solution)/shard_map/swap_dp_1/ppermute | solution.py:122
  234.9 80.5 %collective-permute-start.59 = (bf16[768,1152]{1,0:T(8,128)(2,1)}, bf16[768,1152]{1,0:T(8,128)(2,1)}, u32[]{:S(2)}, u32[]{:S(2)}) collective-permute-start(bf16[768,1152]{1,0:T(8,128)(2,1)} %get-tuple-element.1172), channel_id=1, source_target_pairs={{0,4},{4,0},{8,12},{12,8},{16,20},{20,16},{24,28},{28,24},{1,5},{5... | collective-permute-start | bytes 5308424 | tf_op jit(solution)/shard_map/swap_dp_1/ppermute | solution.py:122
  259.9 24.7 %collective-permute-start.21 = (bf16[1024,1536]{1,0:T(8,128)(2,1)}, bf16[1024,1536]{1,0:T(8,128)(2,1)}, u32[]{:S(2)}, u32[]{:S(2)}) collective-permute-start(bf16[1024,1536]{1,0:T(8,128)(2,1)} %get-tuple-element.639), channel_id=1, source_target_pairs={{0,1},{1,0},{2,3},{3,2},{4,5},{5,4},{6,7},{7,6},{8,9},{9,8},{10,11... | collective-permute-start | bytes 9437192 | tf_op jit(solution)/shard_map/cond/branch_1_fun/swap_tensor_1/ppermute | solution.py:122
  290.1 22.0 %collective-permute-start.23 = (bf16[128,1536]{1,0:T(8,128)(2,1)}, bf16[128,1536]{1,0:T(8,128)(2,1)}, u32[]{:S(2)}, u32[]{:S(2)}) collective-permute-start(bf16[128,1536]{1,0:T(8,128)(2,1)} %get-tuple-element.661), channel_id=1, source_target_pairs={{0,2},{1,3},{2,0},{3,1},{4,6},{5,7},{6,4},{7,5},{8,10},{9,11},{10,... | collective-permute-start | bytes 1179656 | tf_op jit(solution)/shard_map/cond/branch_1_fun/swap_tensor_2/ppermute | solution.py:122
  291.9 20.2 %collective-permute-start.24 = (bf16[128,1536]{1,0:T(8,128)(2,1)}, bf16[128,1536]{1,0:T(8,128)(2,1)}, u32[]{:S(2)}, u32[]{:S(2)}) collective-permute-start(bf16[128,1536]{1,0:T(8,128)(2,1)} %get-tuple-element.662), channel_id=1, source_target_pairs={{0,8},{4,12},{8,0},{12,4},{16,24},{20,28},{24,16},{28,20},{1,9},{5... | collective-permute-start | bytes 1179656 | tf_op jit(solution)/shard_map/cond/branch_1_fun/swap_dp_2/ppermute | solution.py:122
  302.9 9.2 %collective-permute-start.22 = (bf16[1024,1536]{1,0:T(8,128)(2,1)}, bf16[1024,1536]{1,0:T(8,128)(2,1)}, u32[]{:S(2)}, u32[]{:S(2)}) collective-permute-start(bf16[1024,1536]{1,0:T(8,128)(2,1)} %block_rows.3), channel_id=1, source_target_pairs={{0,1},{1,0},{2,3},{3,2},{4,5},{5,4},{6,7},{7,6},{8,9},{9,8},{10,11... | collective-permute-start | bytes 9437192 | tf_op jit(solution)/shard_map/cond/branch_1_fun/cond/branch_1_fun/swap_tensor_1/ppermute | solution.py:122
  315.4 23.3 %collective-permute-start.25 = (bf16[256,1536]{1,0:T(8,128)(2,1)}, bf16[256,1536]{1,0:T(8,128)(2,1)}, u32[]{:S(2)}, u32[]{:S(2)}) collective-permute-start(bf16[256,1536]{1,0:T(8,128)(2,1)} %get-tuple-element.687), channel_id=1, source_target_pairs={{0,2},{1,3},{2,0},{3,1},{4,6},{5,7},{6,4},{7,5},{8,10},{9,11},{10,... | collective-permute-start | bytes 2359304 | tf_op jit(solution)/shard_map/cond/branch_1_fun/swap_tensor_2/ppermute | solution.py:122
  315.8 22.9 %collective-permute-start.26 = (bf16[256,1536]{1,0:T(8,128)(2,1)}, bf16[256,1536]{1,0:T(8,128)(2,1)}, u32[]{:S(2)}, u32[]{:S(2)}) collective-permute-start(bf16[256,1536]{1,0:T(8,128)(2,1)} %get-tuple-element.688), channel_id=1, source_target_pairs={{0,8},{4,12},{8,0},{12,4},{16,24},{20,28},{24,16},{28,20},{1,9},{5... | collective-permute-start | bytes 2359304 | tf_op jit(solution)/shard_map/cond/branch_1_fun/swap_dp_2/ppermute | solution.py:122
  343.4 56.7 %collective-permute-start.61 = (bf16[768,1152]{1,0:T(8,128)(2,1)}, bf16[768,1152]{1,0:T(8,128)(2,1)}, u32[]{:S(2)}, u32[]{:S(2)}) collective-permute-start(bf16[768,1152]{1,0:T(8,128)(2,1)} %get-tuple-element.1196), channel_id=1, source_target_pairs={{0,4},{4,0},{8,12},{12,8},{16,20},{20,16},{24,28},{28,24},{1,5},{5... | collective-permute-start | bytes 5308424 | tf_op jit(solution)/shard_map/swap_dp_1/ppermute | solution.py:122
  344.8 55.2 %collective-permute-start.62 = (bf16[512,1536]{1,0:T(8,128)(2,1)}, bf16[512,1536]{1,0:T(8,128)(2,1)}, u32[]{:S(2)}, u32[]{:S(2)}) collective-permute-start(bf16[512,1536]{1,0:T(8,128)(2,1)} %get-tuple-element.1197), channel_id=1, source_target_pairs={{0,8},{4,12},{8,0},{12,4},{16,24},{20,28},{24,16},{28,20},{1,9},{5... | collective-permute-start | bytes 4718600 | tf_op jit(solution)/shard_map/swap_dp_2/ppermute | solution.py:122
  346.4 52.9 %collective-permute-start.60 = (bf16[384,1152]{1,0:T(8,128)(2,1)}, bf16[384,1152]{1,0:T(8,128)(2,1)}, u32[]{:S(2)}, u32[]{:S(2)}) collective-permute-start(bf16[384,1152]{1,0:T(8,128)(2,1)} %get-tuple-element.1195), channel_id=1, source_target_pairs={{0,16},{4,20},{8,24},{12,28},{16,0},{20,4},{24,8},{28,12},{1,17},{... | collective-permute-start | bytes 2654216 | tf_op jit(solution)/shard_map/swap_dp_4/ppermute | solution.py:122
  347.5 19.0 %collective-permute-start.27 = (bf16[256,1536]{1,0:T(8,128)(2,1)}, bf16[256,1536]{1,0:T(8,128)(2,1)}, u32[]{:S(2)}, u32[]{:S(2)}) collective-permute-start(bf16[256,1536]{1,0:T(8,128)(2,1)} %get-tuple-element.697), channel_id=1, source_target_pairs={{0,2},{1,3},{2,0},{3,1},{4,6},{5,7},{6,4},{7,5},{8,10},{9,11},{10,... | collective-permute-start | bytes 2359304 | tf_op jit(solution)/shard_map/cond/branch_1_fun/cond/branch_1_fun/swap_tensor_2/ppermute | solution.py:122
  369.2 3.8 collective-permute-start.28
  400.1 61.6 %collective-permute-start.63 = (bf16[768,384]{1,0:T(8,128)(2,1)}, bf16[768,384]{1,0:T(8,128)(2,1)}, u32[]{:S(2)}, u32[]{:S(2)}) collective-permute-start(bf16[768,384]{1,0:T(8,128)(2,1)} %get-tuple-element.1212), channel_id=1, source_target_pairs={{0,8},{4,12},{8,0},{12,4},{16,24},{20,28},{24,16},{28,20},{1,9},{5... | collective-permute-start | bytes 1769480 | tf_op jit(solution)/shard_map/swap_dp_2/ppermute | solution.py:122
  406.5 55.2 %collective-permute-start.38 = (bf16[768,1152]{1,0:T(8,128)(2,1)}, bf16[768,1152]{1,0:T(8,128)(2,1)}, u32[]{:S(2)}, u32[]{:S(2)}) collective-permute-start(bf16[768,1152]{1,0:T(8,128)(2,1)} %get-tuple-element.829), channel_id=1, source_target_pairs={{0,4},{4,0},{8,12},{12,8},{16,20},{20,16},{24,28},{28,24},{1,5},{5... | collective-permute-start | bytes 5308424 | tf_op jit(solution)/shard_map/cond/branch_1_fun/swap_dp_1/ppermute | solution.py:122
  407.3 54.4 %collective-permute-start.39 = (bf16[384,1152]{1,0:T(8,128)(2,1)}, bf16[384,1152]{1,0:T(8,128)(2,1)}, u32[]{:S(2)}, u32[]{:S(2)}) collective-permute-start(bf16[384,1152]{1,0:T(8,128)(2,1)} %get-tuple-element.830), channel_id=1, source_target_pairs={{0,16},{4,20},{8,24},{12,28},{16,0},{20,4},{24,8},{28,12},{1,17},{... | collective-permute-start | bytes 2654216 | tf_op jit(solution)/shard_map/cond/branch_1_fun/swap_dp_4/ppermute | solution.py:122
  419.4 6.3 %collective-permute-start.37 = (bf16[512,1536]{1,0:T(8,128)(2,1)}, bf16[512,1536]{1,0:T(8,128)(2,1)}, u32[]{:S(2)}, u32[]{:S(2)}) collective-permute-start(bf16[512,1536]{1,0:T(8,128)(2,1)} %get-tuple-element.780), channel_id=1, source_target_pairs={{0,1},{1,0},{2,3},{3,2},{4,5},{5,4},{6,7},{7,6},{8,9},{9,8},{10,11... | collective-permute-start | bytes 4718600 | tf_op jit(solution)/shard_map/cond/branch_1_fun/cond/branch_1_fun/swap_tensor_1/ppermute | solution.py:122
  428.8 19.7 %collective-permute-start.34 = (bf16[256,1536]{1,0:T(8,128)(2,1)}, bf16[256,1536]{1,0:T(8,128)(2,1)S(1)}, u32[]{:S(2)}, u32[]{:S(2)}) collective-permute-start(bf16[256,1536]{1,0:T(8,128)(2,1)} %get-tuple-element.745), channel_id=1, source_target_pairs={{0,2},{1,3},{2,0},{3,1},{4,6},{5,7},{6,4},{7,5},{8,10},{9,11},{10,... | collective-permute-start | bytes 2359304 | tf_op jit(solution)/shard_map/cond/branch_1_fun/cond/branch_1_fun/cond/branch_1_fun/swap_tensor_2/ppermute | solution.py:122
  430.4 31.2 %collective-permute-start.35 = (bf16[768,512]{1,0:T(8,128)(2,1)}, bf16[768,512]{1,0:T(8,128)(2,1)}, u32[]{:S(2)}, u32[]{:S(2)}) collective-permute-start(bf16[768,512]{1,0:T(8,128)(2,1)} %get-tuple-element.748), channel_id=1, source_target_pairs={{0,8},{4,12},{8,0},{12,4},{16,24},{20,28},{24,16},{28,20},{1,9},{5... | collective-permute-start | bytes 2359304 | tf_op jit(solution)/shard_map/cond/branch_1_fun/cond/branch_1_fun/cond/branch_1_fun/swap_dp_2/ppermute | solution.py:122
  465.5 49.8 %collective-permute-start.64 = (bf16[384,1152]{1,0:T(8,128)(2,1)}, bf16[384,1152]{1,0:T(8,128)(2,1)}, u32[]{:S(2)}, u32[]{:S(2)}) collective-permute-start(bf16[384,1152]{1,0:T(8,128)(2,1)} %get-tuple-element.1233), channel_id=1, source_target_pairs={{0,16},{4,20},{8,24},{12,28},{16,0},{20,4},{24,8},{28,12},{1,17},{... | collective-permute-start | bytes 2654216 | tf_op jit(solution)/shard_map/swap_dp_4/ppermute | solution.py:122
  466.9 48.4 %all-to-all-start = ((f32[32,1,160]{2,1,0:T(1,128)}), f32[32,1,160]{2,1,0:T(1,128)S(1)}, u32[]{:S(2)}, u32[]{:S(2)}) async-start(f32[32,1,160]{2,1,0:T(1,128)} %all_to_all.8), calls=%async_computation | async-start | bytes 65536 | tf_op jit(solution)/shard_map/all_to_all | solution.py:1262
  471.8 23.4 %collective-permute-start.32 = (bf16[256,1536]{1,0:T(8,128)(2,1)}, bf16[256,1536]{1,0:T(8,128)(2,1)}, u32[]{:S(2)}, u32[]{:S(2)}) collective-permute-start(bf16[256,1536]{1,0:T(8,128)(2,1)} %get-tuple-element.865), channel_id=1, source_target_pairs={{0,2},{1,3},{2,0},{3,1},{4,6},{5,7},{6,4},{7,5},{8,10},{9,11},{10,... | collective-permute-start | bytes 2359304 | tf_op jit(solution)/shard_map/cond/branch_1_fun/swap_tensor_2/ppermute | solution.py:122
  473.7 21.5 %collective-permute-start.31 = (bf16[192,1152]{1,0:T(8,128)(2,1)}, bf16[192,1152]{1,0:T(8,128)(2,1)}, u32[]{:S(2)}, u32[]{:S(2)}) collective-permute-start(bf16[192,1152]{1,0:T(8,128)(2,1)} %get-tuple-element.864), channel_id=1, source_target_pairs={{0,8},{4,12},{8,0},{12,4},{16,24},{20,28},{24,16},{28,20},{1,9},{5... | collective-permute-start | bytes 1327112 | tf_op jit(solution)/shard_map/cond/branch_1_fun/swap_dp_2/ppermute | solution.py:122
  477.6 17.2 %collective-permute-start.29 = (bf16[384,512]{1,0:T(8,128)(2,1)}, bf16[384,512]{1,0:T(8,128)(2,1)S(1)}, u32[]{:S(2)}, u32[]{:S(2)}) collective-permute-start(bf16[384,512]{1,0:T(8,128)(2,1)} %get-tuple-element.849), channel_id=1, source_target_pairs={{0,4},{4,0},{8,12},{12,8},{16,20},{20,16},{24,28},{28,24},{1,5},{5... | collective-permute-start | bytes 1179656 | tf_op jit(solution)/shard_map/cond/branch_1_fun/cond/branch_1_fun/swap_dp_1/ppermute | solution.py:122
  481.4 13.5 %collective-permute-start.30 = (bf16[384,384]{1,0:T(8,128)(2,1)}, bf16[384,384]{1,0:T(8,128)(2,1)S(1)}, u32[]{:S(2)}, u32[]{:S(2)}) collective-permute-start(bf16[384,384]{1,0:T(8,128)(2,1)} %get-tuple-element.852), channel_id=1, source_target_pairs={{0,4},{4,0},{8,12},{12,8},{16,20},{20,16},{24,28},{28,24},{1,5},{5... | collective-permute-start | bytes 884744 | tf_op jit(solution)/shard_map/cond/branch_1_fun/cond/branch_1_fun/swap_dp_1/ppermute | solution.py:122
  496.2 19.1 %collective-permute-start.33 = (bf16[192,1152]{1,0:T(8,128)(2,1)}, bf16[192,1152]{1,0:T(8,128)(2,1)}, u32[]{:S(2)}, u32[]{:S(2)}) collective-permute-start(bf16[192,1152]{1,0:T(8,128)(2,1)} %get-tuple-element.875), channel_id=1, source_target_pairs={{0,8},{4,12},{8,0},{12,4},{16,24},{20,28},{24,16},{28,20},{1,9},{5... | collective-permute-start | bytes 1327112 | tf_op jit(solution)/shard_map/cond/branch_1_fun/swap_dp_2/ppermute | solution.py:122
  515.3 17.4 %collective-permute-start.65 = (bf16[192,896]{1,0:T(8,128)(2,1)S(1)}, bf16[192,896]{1,0:T(8,128)(2,1)S(1)}, u32[]{:S(2)}, u32[]{:S(2)}) collective-permute-start(bf16[192,896]{1,0:T(8,128)(2,1)S(1)} %get-tuple-element.1245), channel_id=1, source_target_pairs={{0,16},{4,20},{8,24},{12,28},{16,0},{20,4},{24,8},{28,12},{1,17},{... | collective-permute-start | bytes 1032200 | tf_op jit(solution)/shard_map/swap_dp_4/ppermute | solution.py:122
  521.5 16.9 %collective-permute-start.66 = (bf16[192,1152]{1,0:T(8,128)(2,1)}, bf16[192,1152]{1,0:T(8,128)(2,1)S(1)}, u32[]{:S(2)}, u32[]{:S(2)}) collective-permute-start(bf16[192,1152]{1,0:T(8,128)(2,1)} %get-tuple-element.1242), channel_id=1, source_target_pairs={{0,8},{4,12},{8,0},{12,4},{16,24},{20,28},{24,16},{28,20},{1,9},{5... | collective-permute-start | bytes 1327112 | tf_op jit(solution)/shard_map/swap_dp_2/ppermute | solution.py:122
  533.8 2.8 collective-permute-start.67
  533.9 3.9 collective-permute-start.68
  535.1 3.3 collective-permute-start.69
  (35 other events, 428.4 us)

commit v4 on v3

--- a/solution.py
+++ b/solution.py
@@ -192,6 +192,13 @@
                 spot = jnp.bitwise_xor(tensor_index, mask)
                 jobs.append((ref.at[pl.ds(at * rows, rows)], block(held, spot, rows)))
         return jobs
+
+    def quarter_jobs(tensor_index, refs, held):
+        rows = held.shape[0] // 4
+        return [
+            (ref, block(held, jnp.bitwise_xor(tensor_index, mask), rows))
+            for ref, mask in zip(refs, (0, 2, 1, 3))
+        ]
 
     def back(jobs):
         return [(dst, src) for src, dst in jobs]
@@ -463,33 +470,26 @@
             kernel, [((rows, columns), bf16)] * 2, "fold_sum", scalars, kept, arrived
         )
 
-    def fold_fixed(scalars, kept, arrived, keep, give_away):
-        many = len(keep) + len(give_away)
-        rows, columns = kept.shape[0] // many, kept.shape[1]
-
-        def kernel(scal, kept_ref, arrived_ref, own_ref, sent_ref):
-            for blocks, ref in ((keep, own_ref), (give_away, sent_ref)):
-                for at, spot in enumerate(blocks):
-                    spot = pl.ds(spot * rows, rows)
-                    ref[at * rows : (at + 1) * rows, :] = (
-                        kept_ref[spot, :].astype(f32) + arrived_ref[spot, :].astype(f32)
-                    ).astype(ref.dtype)
-
-        outs = [((len(keep) * rows, columns), f32), ((len(give_away) * rows, columns), bf16)]
-        return whole_call(kernel, outs, "fold_fixed", scalars, kept, arrived)
-
-    def norm_two(scalars, rows_in, own, arrived, gain):
-        def kernel(scal, in_ref, own_ref, arrived_ref, gain_ref, hidden_ref, out_ref):
-            hidden = in_ref[...].astype(f32) + own_ref[...] + arrived_ref[...].astype(f32)
+    def norm_two(scalars, rows_in, kept, sums, arrived, gain):
+        rows, columns = rows_in.shape
+
+        def kernel(scal, kept_ref, sums_ref, in_ref, arrived_ref, gain_ref, hidden_ref, out_ref):
+            hidden = in_ref[...].astype(f32) + kept_ref[...].astype(f32)
+            hidden = hidden + sums_ref[...].astype(f32) + arrived_ref[...].astype(f32)
             hidden_ref[...] = hidden
             out_ref[...] = (norm_forward(hidden)[0] * gain_ref[...]).astype(bf16)
 
-        outs = [(rows_in.shape, f32), (rows_in.shape, bf16)]
-        return whole_call(kernel, outs, "norm_two", scalars, rows_in, own, arrived, gain)
-
-    def norm_one_back(scalars, rows_in, own, arrived, gain, given):
-        def kernel(scal, in_ref, own_ref, arrived_ref, gain_ref, given_ref, out_ref):
-            grad_out = own_ref[...] + arrived_ref[...].astype(f32)
+        return part_call(
+            kernel, [((rows, columns), f32), ((rows, columns), bf16)], "norm_two", scalars,
+            [(kept, rows, 0), (sums, rows, 0)], [rows_in, arrived, gain],
+        )
+
+    def norm_one_back(scalars, rows_in, kept, sums, arrived, gain, given):
+        rows, columns = rows_in.shape
+
+        def kernel(scal, kept_ref, sums_ref, in_ref, arrived_ref, gain_ref, given_ref, out_ref):
+            grad_out = kept_ref[...].astype(f32) + sums_ref[...].astype(f32)
+            grad_out = grad_out + arrived_ref[...].astype(f32)
             normed, row_scale = norm_forward(in_ref[...].astype(f32))
             grad_normed = grad_out * gain_ref[...]
             grad_in = row_scale * (
@@ -497,8 +497,9 @@
             )
             out_ref[...] = (given_ref[...] + grad_in).astype(bf16)
 
-        return whole_call(
-            kernel, [(rows_in.shape, bf16)], "norm_one_back", scalars, rows_in, own, arrived, gain, given
+        return part_call(
+            kernel, [((rows, columns), bf16)], "norm_one_back", scalars,
+            [(kept, rows, 0), (sums, rows, 0)], [rows_in, arrived, gain, given],
         )[0]
 
     def join_both(scalars, first, mine, theirs):
@@ -531,46 +532,108 @@
             kernel, [((rows, columns), bf16)] * 2, "halves", scalars, first, second
         )
 
-    def block_step(scalars, kept, arrived):
-        rows, columns = arrived.shape[0] // 2, arrived.shape[1]
-
-        def kernel(scal, kept_ref, arrived_ref, own_ref, sent_ref):
-            own_ref[...] = kept_ref[:rows, :] + arrived_ref[:rows, :].astype(f32)
-            sent_ref[...] = (kept_ref[rows:, :] + arrived_ref[rows:, :].astype(f32)).astype(bf16)
-
-        outs = [((rows, columns), f32), ((rows, columns), bf16)]
-        return whole_call(kernel, outs, "block_step", scalars, kept, arrived)
-
-    def spread_eight(scalars, kept, arrived):
-        rows, model = kept.shape[0] // 4, kept.shape[1]
-        half = rows // 2
-
-        def kernel(scal, kept_ref, arrived_ref, own_ref, x_ref, l_ref, far_a_ref, far_b_ref):
-            for at, ref in enumerate((own_ref, x_ref, l_ref)):
-                spot = pl.ds(at * rows, rows)
-                ref[...] = kept_ref[spot, :].astype(f32) + arrived_ref[spot, :].astype(f32)
-            for at, ref in enumerate((far_a_ref, far_b_ref)):
-                spot = pl.ds(3 * rows + at * half, half)
+    def fold_both(scalars, first, first_arrived, second, second_arrived, bit, outer):
+        rows = first.shape[0] // 2
+        columns = (first.shape[1], second.shape[1])
+        part = rows // outer
+
+        def kernel(scal, first_ref, first_in_ref, second_ref, second_in_ref, own_ref, sent_ref):
+            flag = is_high(scal, bit)
+            for lanes, kept_ref, arrived_ref in (
+                (slice(0, columns[0]), first_ref, first_in_ref),
+                (slice(columns[0], columns[0] + columns[1]), second_ref, second_in_ref),
+            ):
+                for at in range(outer):
+                    low_spot = pl.ds(2 * at * part, part)
+                    high_spot = pl.ds((2 * at + 1) * part, part)
+                    low = kept_ref[low_spot, :].astype(f32) + arrived_ref[low_spot, :].astype(f32)
+                    high = kept_ref[high_spot, :].astype(f32) + arrived_ref[high_spot, :].astype(f32)
+                    spot = pl.ds(at * part, part)
+                    own_ref[spot, lanes] = jnp.where(flag, high, low)
+                    sent_ref[spot, lanes] = jnp.where(flag, low, high).astype(bf16)
+
+        outs = [((rows, sum(columns)), f32), ((rows, sum(columns)), bf16)]
+        return whole_call(
+            kernel, outs, "fold_both", scalars, first, first_arrived, second, second_arrived
+        )
+
+    def rows_block(rows, columns, at):
+        return pl.BlockSpec((rows, columns), lambda i: (at, 0))
+
+    def part_call(kernel, outs, name, scalars, parts, rest):
+        return pl.pallas_call(
+            kernel,
+            grid=(1,),
+            in_specs=[SCALARS]
+            + [rows_block(rows, array.shape[1], at) for array, rows, at in parts]
+            + [WHOLE] * len(rest),
+            out_specs=[WHOLE] * len(outs),
+            out_shape=[jax.ShapeDtypeStruct(shape, kind) for shape, kind in outs],
+            name=name,
+        )(scalars, *[array for array, _, _ in parts], *rest)
+
+    def part_sum(scalars, kept, arrived, rows, at, pieces):
+        columns, size = kept.shape[1], rows // pieces
+
+        def kernel(scal, kept_ref, arrived_ref, *out_refs):
+            for piece, ref in enumerate(out_refs):
+                spot = pl.ds(piece * size, size)
                 ref[...] = (
                     kept_ref[spot, :].astype(f32) + arrived_ref[spot, :].astype(f32)
                 ).astype(bf16)
 
-        outs = [((rows, model), f32)] * 3 + [((half, model), bf16)] * 2
-        return whole_call(kernel, outs, "spread_eight", scalars, kept, arrived)
-
-    def spread_two(scalars, to_x, to_l, far_x, far_l):
-        rows, model = to_x.shape
+        return part_call(
+            kernel, [((size, columns), bf16)] * pieces, "part_sum", scalars,
+            [(kept, rows, at), (arrived, rows, at)], [],
+        )
+
+    def spread_rest(scalars, kept, arrived, far_x, far_l):
+        rows, columns = kept.shape[0] // 4, kept.shape[1]
         half = rows // 2
 
-        def kernel(scal, x_ref, l_ref, far_x_ref, far_l_ref, out_x_ref, out_l_ref):
-            out_x_ref[:half, :] = x_ref[:half, :].astype(bf16)
-            out_x_ref[half:, :] = (x_ref[half:, :] + far_l_ref[...].astype(f32)).astype(bf16)
-            out_l_ref[:half, :] = (l_ref[:half, :] + far_x_ref[...].astype(f32)).astype(bf16)
-            out_l_ref[half:, :] = l_ref[half:, :].astype(bf16)
-
-        return whole_call(
-            kernel, [((rows, model), bf16)] * 2, "spread_two", scalars, to_x, to_l, far_x, far_l
-        )
+        def kernel(scal, *refs):
+            keeps, arrives = refs[:3], refs[3:6]
+            far_x_ref, far_l_ref, own_ref, x_ref, l_ref = refs[6:]
+            own_ref[...] = keeps[0][...].astype(f32) + arrives[0][...].astype(f32)
+            to_x = keeps[1][...].astype(f32) + arrives[1][...].astype(f32)
+            x_ref[:half, :] = to_x[:half].astype(bf16)
+            x_ref[half:, :] = (to_x[half:] + far_l_ref[...].astype(f32)).astype(bf16)
+            to_l = keeps[2][...].astype(f32) + arrives[2][...].astype(f32)
+            l_ref[:half, :] = (to_l[:half] + far_x_ref[...].astype(f32)).astype(bf16)
+            l_ref[half:, :] = to_l[half:].astype(bf16)
+
+        outs = [((rows, columns), f32), ((rows, columns), bf16), ((rows, columns), bf16)]
+        return part_call(
+            kernel, outs, "spread_rest", scalars,
+            [(array, rows, at) for array in (kept, arrived) for at in range(3)], [far_x, far_l],
+        )
+
+    def block_x_sum(scalars, kept, arrived, from_l):
+        rows, columns = kept.shape[0] // 4, kept.shape[1]
+
+        def kernel(scal, kept_ref, arrived_ref, from_ref, out_ref):
+            out_ref[...] = (
+                kept_ref[...].astype(f32)
+                + arrived_ref[...].astype(f32)
+                + from_ref[...].astype(f32)
+            ).astype(bf16)
+
+        return part_call(
+            kernel, [((rows, columns), bf16)], "block_x_sum", scalars,
+            [(kept, rows, 1), (arrived, rows, 1), (from_l, rows, 1)], [],
+        )[0]
+
+    def block_final(scalars, kept, arrived, from_l, hidden, from_x):
+        rows, columns = hidden.shape
+
+        def kernel(scal, kept_ref, arrived_ref, from_ref, hidden_ref, x_ref, out_ref):
+            total = hidden_ref[...] + kept_ref[...].astype(f32) + arrived_ref[...].astype(f32)
+            out_ref[...] = (total + from_ref[...].astype(f32) + x_ref[...].astype(f32)).astype(bf16)
+
+        return part_call(
+            kernel, [((rows, columns), bf16)], "block_final", scalars,
+            [(kept, rows, 0), (arrived, rows, 0), (from_l, rows, 0)], [hidden, from_x],
+        )[0]
 
     def give(total, scal, kept_ref, sent_ref):
         part = pair_bit * (total.shape[0] // dp_size)
@@ -687,15 +750,15 @@
         )(scalars, context, *arrays_of(pieces))
 
     def attend_back(
-        scalars, query, kv_own, kv_other, starts, pieces, pair, core, context, cosine, sine
+        scalars, query, kv_own, kv_other, starts, pieces, attn, context, cosine, sine
     ):
         tokens, width = query.shape
-        model = pair.shape[1]
+        model = attn[0].shape[1]
         rows = tokens // 4
         scale = 1.0 / math.sqrt(HD)
 
         def kernel(
-            scal, query_ref, own_ref, other_ref, start_ref, pair_ref, core_ref,
+            scal, query_ref, own_ref, other_ref, start_ref, attn_a, attn_b, attn_c, attn_d,
             context_ref, cos_ref, sin_ref, *refs,
         ):
             grad_query_ref, kv_kept_ref, kv_sent_ref, bias_ref, wout_ref, wout_sent_ref = refs[
@@ -705,7 +768,7 @@
             wait_all(
                 start_all(
                     attn_jobs(scal[0], refs[:dp_size], pieces, held)
-                    + token_jobs(scal[1], pair_ref, core_ref, grads),
+                    + quarter_jobs(scal[1], (attn_a, attn_b, attn_c, attn_d), grads),
                     sems,
                 )
             )
@@ -749,7 +812,7 @@
 
         return pl.pallas_call(
             kernel,
-            in_specs=[SCALARS] + [WHOLE] * 4 + [ANY] * 2 + [WHOLE] * 3 + [ANY] * dp_size,
+            in_specs=[SCALARS] + [WHOLE] * 4 + [ANY] * 4 + [WHOLE] * 3 + [ANY] * dp_size,
             out_specs=[WHOLE] * 6,
             out_shape=[
                 jax.ShapeDtypeStruct((tokens, width), bf16),
@@ -769,7 +832,7 @@
             ],
             name="attend_back",
         )(
-            scalars, query, kv_own, kv_other, starts, pair, core, context, cosine, sine,
+            scalars, query, kv_own, kv_other, starts, *attn, context, cosine, sine,
             *arrays_of(pieces),
         )
 
@@ -891,13 +954,6 @@
 
         groups = dp_size // 4
 
-        def fold_rows(total, bit):
-            flag = ((dp_index & bit) != 0).astype(jnp.int32)
-            view = total.reshape(2, -1, total.shape[1])
-            kept = lax.dynamic_index_in_dim(view, flag, 0, keepdims=False)
-            sent = lax.dynamic_index_in_dim(view, 1 - flag, 0, keepdims=False)
-            return kept, swap(sent.astype(bf16), "dp", bit)
-
         def far_rest(kept, sent):
             arrived = swap(sent, "dp", far_bits[0])
             for bit in far_bits[1:]:
@@ -952,17 +1008,16 @@
                 ],
             )
         )
-        gate_piece = join_rows(scalars, gate_mine, gate_theirs, 0, 1)
-        (qkv_l2,) = hold([gate_piece], [qkv_l2])
 
         def gather_attn():
             return (
                 swap(qkv_l2, "dp", 1),
                 swap(act_pair, "tensor", 1),
                 swap(out_half, "dp", pair_bit),
-            )
-
-        qkv_y3, act_c, out_l = section(gather_attn)
+                join_rows(scalars, gate_mine, gate_theirs, 0, 1),
+            )
+
+        qkv_y3, act_c, out_l, gate_piece = section(gather_attn)
 
         qkv_y3, act_c, out_near, rest_sent, cot_core, gate_piece = hold(
             [], [qkv_y3, act_c, rows_of(out_half, out_l), rest_sent, cotangent, gate_piece]
@@ -1017,9 +1072,10 @@
         cot_l = swap(cot_own_l, "dp", pair_bit)
 
         def sum_heads():
-            own, sent = fold_fixed(scalars, attn_kept, attn_arrived, [0], [1])
+            (sent,) = part_sum(scalars, attn_kept, attn_arrived, block_input.shape[0], 1, 1)
             return norm_two(
-                scalars, block_input, own, swap(sent, "tensor", 2), gain_ffn[None, :]
+                scalars, block_input, attn_kept, attn_arrived, swap(sent, "tensor", 2),
+                gain_ffn[None, :],
             )
 
         hidden, two_own = section(sum_heads)
@@ -1121,9 +1177,11 @@
             gate_a, up_a, kept = ffn_back(
                 scalars, cots, down_pieces, gate_pieces, up_pieces, silu_a, back_a
             )
-            return (gate_a, up_a, gate_b, up_b, *spread_eight(scalars, kept, arrived))
-
-        gate_a, up_a, gate_b, up_b, own, to_x, to_l, far_a, far_b = section(back_all)
+            (kept,) = hold([], [kept])
+            far = part_sum(scalars, kept, arrived, kept.shape[0] // 4, 3, 2)
+            return gate_a, up_a, gate_b, up_b, kept, arrived, *far
+
+        gate_a, up_a, gate_b, up_b, two_kept, two_arrived, far_a, far_b = section(back_all)
 
         far_a, far_b, mixed_b = hold([], [far_a, far_b, mixed_b])
         model = far_a.shape[1]
@@ -1141,9 +1199,9 @@
 
             outs = section(block_rows)
             outs, far_x, far_l = hold([], [outs, far_x, far_l])
-            return (*outs, *spread_two(scalars, to_x, to_l, far_x, far_l))
-
-        block_kept, block_arrived, to_x, to_l = section(spread_far)
+            return (*outs, *spread_rest(scalars, two_kept, two_arrived, far_x, far_l))
+
+        block_kept, block_arrived, own, to_x, to_l = section(spread_far)
 
         to_x, to_l, down_sent = hold([], [to_x, to_l, down_sent])
 
@@ -1152,7 +1210,8 @@
             from_l = swap(to_l, "dp", pair_bit)
             up_grads = ffn_grad(scalars, [acts_a], [acts_b], up_a, up_b, "grad_up")
             down_pair = fold_sum(scalars, down_kept, down_sent, far_bits[0], 1)
-            block_pair = fold_fixed(scalars, block_kept, block_arrived, [0, 1], [2, 3])
+            block_rows = 2 * own.shape[0]
+            block_pair = part_sum(scalars, block_kept, block_arrived, block_rows, 1, 1)
             from_x, from_l = hold([up_grads, down_pair, block_pair], [from_x, from_l])
             return (
                 *up_grads,
@@ -1164,38 +1223,38 @@
             )
 
         (
-            up_kept, up_sent, down_kept, down_sent, block_kept, block_sent,
-            grad_hidden, attn_own, gain_two,
+            up_kept, up_sent, down_kept, down_sent, block_sent, grad_hidden, attn_own, gain_two,
         ) = section(spread_near)
 
-        attn_own, down_sent, up_sent, block_sent, gate_b = hold(
-            [], [attn_own, down_sent, up_sent, block_sent, gate_b]
+        attn_own, down_sent, up_sent, gate_b, block_sent = hold(
+            [], [attn_own, down_sent, up_sent, gate_b, block_sent]
         )
         down_kept, down_sent = far_rest(down_kept, down_sent)
         up_sent = swap(up_sent, "dp", 1)
-        block_sent = swap(block_sent, "dp", pair_bit)
+        block_from_l = swap(block_sent, "dp", pair_bit)
 
         def attention_back():
             def gather_back():
                 attn_x = swap(attn_own, "tensor", 2)
+                own_c = swap(attn_own, "tensor", 1)
                 gate_grads = ffn_grad(scalars, [acts_a], [acts_b], gate_a, gate_b, "grad_gate")
-                (attn_x,) = hold([gate_grads], [attn_x])
-                return (rows_of(attn_own, attn_x), *gate_grads)
-
-            attn_half, gate_kept, gate_sent = section(gather_back)
-            attn_half, gate_sent = hold([], [attn_half, gate_sent])
-            attn_c = swap(attn_half, "tensor", 1)
+                attn_x, own_c = hold([gate_grads], [attn_x, own_c])
+                return (attn_x, own_c, *gate_grads)
+
+            attn_x, own_c, gate_kept, gate_sent = section(gather_back)
+            attn_x, own_c, gate_sent = hold([], [attn_x, own_c, gate_sent])
+            x_c = swap(attn_x, "tensor", 1)
             outs = attend_back(
-                scalars, query_rot, kv_own, kv_other, starts, out_parts, attn_half, attn_c,
-                context, cosine, sine,
+                scalars, query_rot, kv_own, kv_other, starts, out_parts,
+                [attn_own, attn_x, own_c, x_c], context, cosine, sine,
             )
             return gate_kept, gate_sent, outs
 
         gate_kept, gate_sent, outs = section(attention_back)
         grad_query_low, kv_kept, kv_given, bias_rows, wout_kept, wout_sent = outs
 
-        kv_given, wout_sent, gate_sent, down_sent, up_sent, block_sent = hold(
-            [], [kv_given, wout_sent, gate_sent, down_sent, up_sent, block_sent]
+        kv_given, wout_sent, gate_sent, down_sent, up_sent, block_from_l = hold(
+            [], [kv_given, wout_sent, gate_sent, down_sent, up_sent, block_from_l]
         )
         wout_arrived = swap(wout_sent, "dp", pair_bit)
         devices = dp_size * tensor_size
@@ -1217,12 +1276,13 @@
                 wqkv_pair = project_grad(scalars, act_pair, act_c, grad_qkv)
                 (arrived,) = hold([wqkv_pair], [arrived])
                 wqkv_kept, wqkv_sent = wqkv_pair
-                one_kept, one_sent = fold_fixed(scalars, one_kept, arrived, [0], [1])
+                (one_given,) = part_sum(scalars, one_kept, arrived, block_input.shape[0], 1, 1)
+                one_arrived = arrived
 
                 def first_norm_back():
-                    arrived = swap(one_sent, "tensor", 2)
+                    arrived = swap(one_given, "tensor", 2)
                     wqkv_arrived = swap(wqkv_sent, "dp", pair_bit)
-                    block = block_step(scalars, block_kept, block_sent)
+                    block = block_x_sum(scalars, block_kept, block_arrived, block_from_l)
                     bias_keyval = jnp.zeros((2 * KV * HD,), f32)
                     bias_keyval = lax.dynamic_update_slice_in_dim(
                         bias_keyval, bias_rows[0, width : width + HD], head_kv * HD, 0
@@ -1237,10 +1297,11 @@
                     small = jnp.concatenate([part.reshape(devices, -1) for part in parts], axis=1)
                     (arrived,) = hold([block, small], [arrived])
                     grad_rows = norm_one_back(
-                        scalars, block_input, one_kept, arrived, gain_attn[None, :], grad_hidden
+                        scalars, block_input, one_kept, one_arrived, arrived, gain_attn[None, :],
+                        grad_hidden,
                     )
                     (wqkv_arrived,) = hold([grad_rows], [wqkv_arrived])
-                    return grad_rows, small, *block, wqkv_arrived
+                    return grad_rows, small, block, wqkv_arrived
 
                 return (*down_pair, wqkv_kept, *section(first_norm_back))
 
@@ -1250,7 +1311,7 @@
 
         (
             up_kept, up_sent, gate_sent, down_mine, down_given, wqkv_kept, grad_rows, small,
-            block_own, block_sent, wqkv_arrived,
+            block_to_x, wqkv_arrived,
         ) = section(input_grads)
 
         wqkv_arrived, wout_arrived, gate_sent, small, down_given = hold(
@@ -1262,45 +1323,38 @@
         small = lax.all_to_all(small, ("dp", "tensor"), 0, 0, tiled=True)
 
         def last_rows():
+            block_x = swap(block_to_x, "tensor", 2)
             down_theirs = swap(down_given, "dp", pair_bit)
-            block_x = swap(block_sent, "tensor", 2)
 
             def attn_step():
-                wqkv_own, wqkv_sent = fold_sum(scalars, wqkv_kept, wqkv_arrived, 1, groups)
-                wout_own, wout_sent = fold_sum(scalars, wout_kept, wout_arrived, 1, groups)
-                wqkv_y = swap(wqkv_sent, "dp", 1)
-                wout_y = swap(wout_sent, "dp", 1)
+                own, sent = fold_both(
+                    scalars, wqkv_kept, wqkv_arrived, wout_kept, wout_arrived, 1, groups
+                )
+                arrived = swap(sent, "dp", 1)
                 up_pair = fold_sum(scalars, up_kept, up_sent, pair_bit, 1)
-                wqkv_y, wout_y = hold([up_pair], [wqkv_y, wout_y])
-                total = jnp.concatenate([add(wqkv_own, wqkv_y), add(wout_own, wout_y)], axis=1)
-                return total, up_pair
-
-            total, up_pair = section(attn_step)
-            total, down_theirs, block_x, up_given = hold(
-                [], [total, down_theirs, block_x, up_pair[1]]
-            )
-            up_theirs = swap(up_given, "dp", pair_bit)
-            for bit in far_bits[:-1]:
-                total = add(*fold_rows(total, bit))
-            flag = ((dp_index & far_bits[-1]) != 0).astype(jnp.int32)
-            view = total.reshape(2, -1, total.shape[1])
-            kept = lax.dynamic_index_in_dim(view, flag, 0, keepdims=False)
-            sent = lax.dynamic_index_in_dim(view, 1 - flag, 0, keepdims=False).astype(bf16)
-            block_out = (hidden + add(block_own, block_x)).astype(bf16)
+                (arrived,) = hold([up_pair], [arrived])
+                return (*fold_sum(scalars, own, arrived, far_bits[0], 1), *up_pair)
+
+            *attn_outs, block_x, down_theirs = hold(
+                [], [*section(attn_step), block_x, down_theirs]
+            )
+            block_out = block_final(
+                scalars, block_kept, block_arrived, block_from_l, hidden, block_x
+            )
             down_share = join_cols(scalars, down_mine, down_theirs, w_down.shape[0] // 2).T
-            (up_theirs,) = hold([kept, sent, block_out, down_share], [up_theirs])
-            return kept, sent, up_pair[0], up_theirs, block_out, down_share
-
-        attn_kept, attn_sent, up_mine, up_theirs, block_out, down_share = section(last_rows)
-
-        gate_sent, attn_sent, up_theirs, small = hold(
-            [block_out, down_share], [gate_sent, attn_sent, up_theirs, small]
-        )
-        small = jnp.sum(small, axis=0)
-        attn_sent = swap(attn_sent, "dp", far_bits[-1])
+            return *attn_outs, block_out, down_share
+
+        attn_kept, attn_sent, up_mine, up_given, block_out, down_share = section(last_rows)
+
+        gate_sent, attn_sent, up_given, small = hold(
+            [block_out, down_share], [gate_sent, attn_sent, up_given, small]
+        )
+        attn_kept, attn_sent = far_rest(attn_kept, attn_sent)
+        up_theirs = swap(up_given, "dp", pair_bit)
         gate_mine, gate_given = fold_sum(scalars, gate_kept, gate_sent, pair_bit, 1)
         gate_theirs = swap(gate_given, "dp", pair_bit)
-        (up_theirs,) = hold([gate_given], [up_theirs])
+        small = jnp.sum(small, axis=0)
+        up_theirs = hold([gate_given, small], [up_theirs])[0]
         up_share = join_cols(scalars, up_mine, up_theirs, w_up.shape[1] // 2)
         (attn_sent,) = hold([up_share], [attn_sent])
         share = add(attn_kept, attn_sent)

time: 553 us -> 544 us (0.984)
  other arithmetic: 19.4 us -> 13.6 us
    pallas_call x27 -> x19, Pallas kernels: 92.9 us -> 61.1 us  [whole_call(): pl.pallas_call(kernel, in_specs=[SCALARS] + [WHOLE] * (len(args) - 1), ou...]
    pallas_call x1 -> x10, Pallas kernels: 21.5 us -> 50.2 us  [the longest x9 28.7 us: part_call(): pl.pallas_call(kernel, grid=(1,), in_specs=[SCALARS] + [rows_block(rows,...]
  transfers between devices with their start and end apart: 71 -> 71, of which waited for: 34 -> 35; matrix products, arithmetic and copies ran while one was open for 5% -> 4% of each run, Pallas kernels for 49% -> 50%
where the time goes in v4:
time: 544 us; the launch traced here: 534 us
  Pallas kernels  276 us (51%)
  waiting for transfers between devices  152 us (28%)
  starting transfers between devices  75.7 us (14%)
  local copies, waits for them, and re-layouts  14.8 us (3%)
  other arithmetic  13.6 us (2%)
    ppermute x70, waiting for transfers between devices, swap(): return lax.ppermute(array, axis, [(i, i ^ bit) for i in range(size)])  151 us
    ppermute x70, starting transfers between devices, swap(): return lax.ppermute(array, axis, [(i, i ^ bit) for i in range(size)])  70.9 us
    pallas_call x19, Pallas kernels, whole_call(): pl.pallas_call(kernel, in_specs=[SCALARS] + [WHOLE] * (len(args) - 1), ou...  61.1 us
    pallas_call x2, Pallas kernels, ffn_back(): pl.pallas_call(kernel, grid=(2,), in_specs=[SCALARS] + [ANY] * (many + 3...  49 us
    pallas_call x3, Pallas kernels, ffn_grad(): pl.pallas_call(kernel, grid=(model // wide,), in_specs=[SCALARS] + [pl.Bl...  38.9 us
    pallas_call x2, Pallas kernels, ffn_up(): pl.pallas_call(kernel, grid=(2,), in_specs=[SCALARS] + [ANY] * (many + 2...  31.4 us
    pallas_call x9, Pallas kernels, part_call(): pl.pallas_call(kernel, grid=(1,), in_specs=[SCALARS] + [rows_block(rows,...  28.7 us
    pallas_call x1, Pallas kernels, attend_back(): pl.pallas_call(kernel, in_specs=[SCALARS] + [WHOLE] * 4 + [ANY] * 4 + [WH...  21.5 us
  transfers between devices with their start and end apart: 71, of which 35 were waited for; matrix products, arithmetic and copies ran while one was open for 4% of the time, Pallas kernels for 50%

profile of v4, /device:TPU:0, one launch (start us, length us, event | category | flops | bytes accessed | tf_op | source)
XLA Modules:
  0.0 534.2 jit_solution(2672856389987025846)
XLA Ops:
  2.5 4.1 collective-permute-start.39
  27.3 3.4 split_cols.3
  34.7 10.4 %conditional.22 = (bf16[192,512]{1,0:T(8,128)(2,1)}, bf16[512,1536]{1,0:T(8,128)(2,1)}, bf16[384,384]{1,0:T(8,128)(2,1)}, bf16[384,1152]{1,0:T(8,128)(2,1)}) conditional(s32[]{:T(128)} %convert_element_type.62, () %tuple.232, (bf16[192,512]{1,0:T(8,128)(2,1)}, bf16[512,1536]{1,0:T(8,128)(2,1)S(1)}, bf16[384,384]{1,0:T(8,128)(2,1)}, s32[2]{0:T(128)S(1)}, ...), branch_computations={%region_3.4_spmd, %region_4.5_spmd} | conditional | bytes 8257688 | solution.py:101
  40.1 4.2 collective-permute-done
  52.4 17.0 %conditional.23 = (bf16[1024,384]{1,0:T(8,128)(2,1)}, bf16[1024,128]{1,0:T(8,128)(2,1)}, bf16[1024,128]{1,0:T(8,128)(2,1)}, bf16[1024,384]{1,0:T(8,128)(2,1)S(1)}, bf16[256,1536]{1,0:T(8,128)(2,1)}) conditional(s32[]{:T(128)} %convert_element_type.62, () %tuple.237, (f32[512]{0:T(512)S(1)}, s32[2]{0:T(128)S(1)}, bf16[512,1536]{1,0:T(8,128)(2,1)S(1)}, ...), branch_computations={%region_5.6_spmd, %region_6.7_spmd} | conditional | bytes 4194424 | solution.py:101
  52.4 6.8 %project.1 = (bf16[1024,384]{1,0:T(8,128)(2,1)}, bf16[1024,128]{1,0:T(8,128)(2,1)}) custom-call(s32[2]{0:T(128)S(1)} %get-tuple-element.516.scal, bf16[512,1536]{1,0:T(8,128)(2,1)S(1)} %get-tuple-element.517.pair_ref, bf16[512,1536]{1,0:T(8,128)(2,1)} %get-tuple-element.518.core_ref, f32[1,512]{1,0:T(1,128)S(1)} %bitcast.29, ...), custom_call_target="tpu_custom_call" | custom-call | tf_op jit(solution)/shard_map/cond/branch_1_fun/project/pallas_call | solution.py:676
  61.4 8.0 %attend.1 = bf16[1024,384]{1,0:T(8,128)(2,1)S(1)} custom-call(s32[2]{0:T(128)S(1)} %get-tuple-element.516.scal, bf16[1024,384]{1,0:T(8,128)(2,1)} %get-tuple-element.1341.query_ref, bf16[1024,128]{1,0:T(8,128)(2,1)} %get-tuple-element.1342.own_ref, bf16[1024,128]{1,0:T(8,128)(2,1)} %collective-permute-done.3.other_ref, s32[1024,1]{1,0:T(8,128)} %get-tuple-element.533.start_ref), custom_call_target="tpu_custom_call" | custom-call | tf_op jit(solution)/shard_map/cond/branch_1_fun/attend/pallas_call | solution.py:400
  69.5 6.0 %out_rows.1 = (bf16[512,1536]{1,0:T(8,128)(2,1)}, bf16[512,1536]{1,0:T(8,128)(2,1)}) custom-call(s32[2]{0:T(128)S(1)} %pad_add_fusion.scal, bf16[1024,384]{1,0:T(8,128)(2,1)S(1)} %get-tuple-element.1113.context_ref, bf16[768,384]{1,0:T(8,128)(2,1)S(1)} %pad_maximum_fusion.2.refs_0_.refs_2_.refs_4_.refs_6_, ...), custom_call_target="tpu_custom_call" | custom-call | tf_op jit(solution)/shard_map/out_rows/pallas_call | solution.py:738
  75.5 8.6 %collective-permute-done.49 = bf16[384,1152]{1,0:T(8,128)(2,1)} collective-permute-done((bf16[384,1152]{1,0:T(8,128)(2,1)}, bf16[384,1152]{1,0:T(8,128)(2,1)}, u32[]{:S(2)}, u32[]{:S(2)}) %collective-permute-start.49) | collective-permute-done | bytes 884768 | tf_op jit(solution)/shard_map/swap_dp_2/ppermute | solution.py:122
  84.1 3.8 conditional.24
  91.0 25.3 %conditional.25 = ((f32[256,1536]{1,0:T(8,128)}, bf16[256,1536]{1,0:T(8,128)(2,1)})) conditional(s32[]{:T(128)} %convert_element_type.62, () %tuple.241, (s32[2]{0:T(128)S(1)}, bf16[512,1536]{1,0:T(8,128)(2,1)}, bf16[512,1536]{1,0:T(8,128)(2,1)}, f32[1536]{0:T(1024)S(1)}, bf16[256,1536]{1,0:T(8,128)(2,1)}) %tuple.356), branch_computations={%region_9.10_spmd, %region_10.11_spmd} | conditional | bytes 3158064 | solution.py:101
  95.9 16.7 %collective-permute-done.6.arrived_ref = bf16[256,1536]{1,0:T(8,128)(2,1)} collective-permute-done((bf16[256,1536]{1,0:T(8,128)(2,1)}, bf16[256,1536]{1,0:T(8,128)(2,1)}, u32[]{:S(2)}, u32[]{:S(2)}) %collective-permute-start.6) | collective-permute-done | bytes 786464 | tf_op jit(solution)/shard_map/cond/branch_1_fun/swap_tensor_2/ppermute | solution.py:122
  112.6 3.7 norm_two.1
  116.3 8.0 %collective-permute-done.50 = bf16[256,1536]{1,0:T(8,128)(2,1)} collective-permute-done((bf16[256,1536]{1,0:T(8,128)(2,1)}, bf16[256,1536]{1,0:T(8,128)(2,1)}, u32[]{:S(2)}, u32[]{:S(2)}) %collective-permute-start.50) | collective-permute-done | bytes 786464 | tf_op jit(solution)/shard_map/swap_dp_2/ppermute | solution.py:122
  125.1 22.5 %conditional.26 = (bf16[256,1536]{1,0:T(8,128)(2,1)}, bf16[256,1536]{1,0:T(8,128)(2,1)}, bf16[384,1152]{1,0:T(8,128)(2,1)}) conditional(s32[]{:T(128)} %convert_element_type.62, () %tuple.246, (bf16[256,1536]{1,0:T(8,128)(2,1)}, s32[2]{0:T(128)S(1)}, bf16[384,1152]{1,0:T(8,128)(2,1)}, bf16[384,1152]{1,0:T(8,128)(2,1)}) %tuple.247), branch_computations={%region_11.12_spmd, %region_12.13_spmd} | conditional | bytes 6291560 | solution.py:101
  128.9 14.8 %collective-permute-done.7 = bf16[256,1536]{1,0:T(8,128)(2,1)} collective-permute-done((bf16[256,1536]{1,0:T(8,128)(2,1)}, bf16[256,1536]{1,0:T(8,128)(2,1)}, u32[]{:S(2)}, u32[]{:S(2)}) %collective-permute-start.7) | collective-permute-done | bytes 786464 | tf_op jit(solution)/shard_map/cond/branch_1_fun/swap_tensor_2/ppermute | solution.py:122
  143.7 3.9 collective-permute-done.8
  149.1 14.2 %conditional.27 = (bf16[128,1536]{1,0:T(8,128)(2,1)}, bf16[128,1536]{1,0:T(8,128)(2,1)}, bf16[256,1536]{1,0:T(8,128)(2,1)}, bf16[256,1536]{1,0:T(8,128)(2,1)}, bf16[256,1536]{1,0:T(8,128)(2,1)}) conditional(s32[]{:T(128)} %convert_element_type.62, () %tuple.249, (s32[2]{0:T(128)S(1)}, bf16[256,1536]{1,0:T(8,128)(2,1)}, ...), branch_computations={%region_13.14_spmd, %region_14.17_spmd} | conditional | flops 1 | bytes 12583205 | solution.py:101
  153.1 7.9 %conditional = (bf16[256,1536]{1,0:T(8,128)(2,1)}, bf16[256,1536]{1,0:T(8,128)(2,1)}, bf16[256,1536]{1,0:T(8,128)(2,1)}) conditional(s32[]{:T(128)} %convert_element_type.15, () %tuple.115, (bf16[256,1536]{1,0:T(8,128)(2,1)}, bf16[256,1536]{1,0:T(8,128)(2,1)}, bf16[256,1536]{1,0:T(8,128)(2,1)}) %tuple.116), branch_computations={%region_15.15_spmd, %region_16.16_spmd} | conditional | bytes 9437328 | solution.py:101
  163.2 6.4 %collective-permute-done.55 = bf16[384,1152]{1,0:T(8,128)(2,1)} collective-permute-done((bf16[384,1152]{1,0:T(8,128)(2,1)}, bf16[384,1152]{1,0:T(8,128)(2,1)}, u32[]{:S(2)}, u32[]{:S(2)}) %collective-permute-start.55) | collective-permute-done | bytes 884768 | tf_op jit(solution)/shard_map/swap_dp_1/ppermute | solution.py:122
  172.2 22.0 %conditional.29 = (bf16[384,1152]{1,0:T(8,128)(2,1)}, bf16[256,1536]{1,0:T(8,128)(2,1)}, bf16[256,1536]{1,0:T(8,128)(2,1)}, bf16[1024,1536]{1,0:T(8,128)(2,1)}, ...) conditional(s32[]{:T(128)} %convert_element_type.62, () %tuple.231, ...), branch_computations={%region_19.20_spmd, %region_20.21_spmd} | conditional | bytes 12681286 | solution.py:101
  174.7 15.4 %ffn_up.2 = (bf16[1024,1536]{1,0:T(8,128)(2,1)}, bf16[1024,1152]{1,0:T(8,128)(2,1)}, bf16[1024,1152]{1,0:T(8,128)(2,1)}, bf16[1024,1152]{1,0:T(8,128)(2,1)}) custom-call(s32[2]{0:T(128)S(1)} %get-tuple-element.573.scal, bf16[256,1536]{1,0:T(8,128)(2,1)} %get-tuple-element.574.refs_0_, bf16[256,1536]{1,0:T(8,128)(2,1)} %get-tuple-element.575.refs_1_, ...), custom_call_target="tpu_custom_call" | custom-call | tf_op jit(solution)/shard_map/cond/branch_1_fun/ffn_up/pallas_call | solution.py:252
  194.2 16.5 %conditional.30 = (bf16[256,1536]{1,0:T(8,128)(2,1)}, bf16[256,1536]{1,0:T(8,128)(2,1)}, bf16[1024,1536]{1,0:T(8,128)(2,1)}, bf16[1024,1152]{1,0:T(8,128)(2,1)},...) conditional(s32[]{:T(128)} %convert_element_type.62, () %tuple.256, (s32[2]{0:T(128)S(1)}, ...), branch_computations={%region_21.22_spmd, %region_22.23_spmd} | conditional | bytes 11796540 | solution.py:101
  194.7 16.0 %ffn_up.3 = (bf16[1024,1536]{1,0:T(8,128)(2,1)}, bf16[1024,1152]{1,0:T(8,128)(2,1)}, bf16[1024,1152]{1,0:T(8,128)(2,1)}, bf16[1024,1152]{1,0:T(8,128)(2,1)}) custom-call(s32[2]{0:T(128)S(1)} %get-tuple-element.596.scal, bf16[256,1536]{1,0:T(8,128)(2,1)} %get-tuple-element.597.refs_0_, bf16[256,1536]{1,0:T(8,128)(2,1)} %get-tuple-element.598.refs_1_, ...), custom_call_target="tpu_custom_call" | custom-call | tf_op jit(solution)/shard_map/cond/branch_1_fun/ffn_up/pallas_call | solution.py:252
  211.5 13.2 %conditional.31 = ((bf16[768,1152]{1,0:T(8,128)(2,1)}, bf16[768,1152]{1,0:T(8,128)(2,1)})) conditional(s32[]{:T(128)} %convert_element_type.62, () %tuple.260, (s32[2]{0:T(128)S(1)}, bf16[256,1536]{1,0:T(8,128)(2,1)}, bf16[256,1536]{1,0:T(8,128)(2,1)}, bf16[256,1536]{1,0:T(8,128)(2,1)}, bf16[256,1536]{1,0:T(8,128)(2,1)}, ...), branch_computations={%region_23.24_spmd, %region_24.25_spmd} | conditional | bytes 3538972 | solution.py:101
  211.5 13.2 %grad_down.1 = (bf16[768,1152]{1,0:T(8,128)(2,1)}, bf16[768,1152]{1,0:T(8,128)(2,1)}) custom-call(s32[2]{0:T(128)S(1)} %get-tuple-element.617.scal, bf16[256,1536]{1,0:T(8,128)(2,1)} %get-tuple-element.618.refs_0_, bf16[256,1536]{1,0:T(8,128)(2,1)} %get-tuple-element.619.refs_1_, bf16[256,1536]{1,0:T(8,128)(2,1)} %get-tuple-element.620.refs_2_, ...), custom_call_target="tpu_custom_call" | custom-call | tf_op jit(solution)/shard_map/cond/branch_1_fun/grad_down/pallas_call | solution.py:385
  224.7 8.0 %collective-permute-done.57 = bf16[384,1152]{1,0:T(8,128)(2,1)} collective-permute-done((bf16[384,1152]{1,0:T(8,128)(2,1)}, bf16[384,1152]{1,0:T(8,128)(2,1)}, u32[]{:S(2)}, u32[]{:S(2)}) %collective-permute-start.57) | collective-permute-done | bytes 884768 | tf_op jit(solution)/shard_map/swap_dp_1/ppermute | solution.py:122
  233.3 51.5 %conditional.32 = (bf16[1024,1152]{1,0:T(8,128)(2,1)}, bf16[1024,1152]{1,0:T(8,128)(2,1)}, bf16[1024,1152]{1,0:T(8,128)(2,1)}, bf16[1024,1152]{1,0:T(8,128)(2,1)...) conditional(s32[]{:T(128)} %convert_element_type.62, () %tuple.259, ...), branch_computations={%region_25.26_spmd, %region_26.27_spmd} | conditional | bytes 16515152 | solution.py:101
  233.3 24.4 %ffn_back.3 = (bf16[1024,1152]{1,0:T(8,128)(2,1)}, bf16[1024,1152]{1,0:T(8,128)(2,1)}, bf16[1024,1536]{1,0:T(8,128)(2,1)}) custom-call(s32[2]{0:T(128)S(1)} %get-tuple-element.628.scal, bf16[256,1536]{1,0:T(8,128)(2,1)} %get-tuple-element.648.refs_0_, bf16[256,1536]{1,0:T(8,128)(2,1)} %get-tuple-element.649.refs_1_, ...), custom_call_target="tpu_custom_call" | custom-call | tf_op jit(solution)/shard_map/cond/branch_1_fun/ffn_back/pallas_call | solution.py:315
  257.8 24.6 %ffn_back.2 = (bf16[1024,1152]{1,0:T(8,128)(2,1)}, bf16[1024,1152]{1,0:T(8,128)(2,1)}, bf16[1024,1536]{1,0:T(8,128)(2,1)}) custom-call(s32[2]{0:T(128)S(1)} %get-tuple-element.628.scal, bf16[256,1536]{1,0:T(8,128)(2,1)} %get-tuple-element.629.refs_0_, bf16[256,1536]{1,0:T(8,128)(2,1)} %get-tuple-element.630.refs_1_, ...), custom_call_target="tpu_custom_call" | custom-call | tf_op jit(solution)/shard_map/cond/branch_1_fun/ffn_back/pallas_call | solution.py:315
  284.8 26.4 %conditional.33 = (bf16[1024,1536]{1,0:T(8,128)(2,1)}, bf16[1024,1536]{1,0:T(8,128)(2,1)}, f32[256,1536]{1,0:T(8,128)}, bf16[256,1536]{1,0:T(8,128)(2,1)}, bf16[256,1536]{1,0:T(8,128)(2,1)}) conditional(s32[]{:T(128)} %convert_element_type.62, () %tuple.266, (s32[2]{0:T(128)S(1)}, bf16[1024,1152]{1,0:T(8,128)(2,1)}, bf16[384,1152]{1,0:T(8,128)(2,1)}, ...), branch_computations={%region_27.28_spmd, %region_28.31_spmd} | conditional | flops 1 | bytes 15728877 | solution.py:101
  288.6 18.2 %conditional.1 = (bf16[1024,1536]{1,0:T(8,128)(2,1)}, bf16[1024,1536]{1,0:T(8,128)(2,1)}) conditional(s32[]{:T(128)} %convert_element_type.16, () %tuple.132, (s32[2]{0:T(128)S(1)}, bf16[1024,1152]{1,0:T(8,128)(2,1)}, bf16[384,1152]{1,0:T(8,128)(2,1)}, bf16[384,1152]{1,0:T(8,128)(2,1)}, bf16[384,1152]{1,0:T(8,128)(2,1)}, ...), branch_computations={%region_29.29_spmd, %region_30.30_spmd} | conditional | bytes 12582968 | solution.py:101
  288.6 9.0 %block_rows.3 = bf16[1024,1536]{1,0:T(8,128)(2,1)} custom-call(s32[2]{0:T(128)S(1)} %get-tuple-element.660.scal, bf16[1024,1152]{1,0:T(8,128)(2,1)} %get-tuple-element.666.left_ref, bf16[384,1152]{1,0:T(8,128)(2,1)} %get-tuple-element.662.refs_0_, bf16[384,1152]{1,0:T(8,128)(2,1)} %get-tuple-element.663.refs_1_, ...), custom_call_target="tpu_custom_call" | custom-call | tf_op jit(solution)/shard_map/cond/branch_1_fun/cond/branch_1_fun/block_rows/pallas_call | solution.py:343
  297.7 9.0 %block_rows.2 = bf16[1024,1536]{1,0:T(8,128)(2,1)} custom-call(s32[2]{0:T(128)S(1)} %get-tuple-element.660.scal, bf16[1024,1152]{1,0:T(8,128)(2,1)} %get-tuple-element.661.left_ref, bf16[384,1152]{1,0:T(8,128)(2,1)} %get-tuple-element.662.refs_0_, bf16[384,1152]{1,0:T(8,128)(2,1)} %get-tuple-element.663.refs_1_, ...), custom_call_target="tpu_custom_call" | custom-call | tf_op jit(solution)/shard_map/cond/branch_1_fun/cond/branch_1_fun/block_rows/pallas_call | solution.py:343
  306.8 4.4 spread_rest.1
  311.2 25.9 %conditional.34 = (bf16[768,1152]{1,0:T(8,128)(2,1)}, bf16[768,1152]{1,0:T(8,128)(2,1)}, bf16[384,1152]{1,0:T(8,128)(2,1)}, bf16[384,1152]{1,0:T(8,128)(2,1)}, b...) conditional(s32[]{:T(128)} %convert_element_type.62, () %tuple.230, ...), branch_computations={%region_31.32_spmd, %region_32.33_spmd} | conditional | bytes 9289812 | solution.py:101
  312.5 3.7 fold_sum.7
  316.2 3.4 part_sum.6
  319.6 12.9 %grad_up.1 = (bf16[768,1152]{1,0:T(8,128)(2,1)}, bf16[768,1152]{1,0:T(8,128)(2,1)}) custom-call(s32[2]{0:T(128)S(1)} %get-tuple-element.687.scal, bf16[1024,1536]{1,0:T(8,128)(2,1)} %get-tuple-element.688.refs_0_, bf16[1024,1536]{1,0:T(8,128)(2,1)} %get-tuple-element.689.refs_1_, bf16[1024,1152]{1,0:T(8,128)(2,1)} %get-tuple-element.690.refs_2_, ...), custom_call_target="tpu_custom_call" | custom-call | tf_op jit(solution)/shard_map/cond/branch_1_fun/grad_up/pallas_call | solution.py:385
  332.5 4.7 norm_two_back.1
  341.3 43.1 %conditional.35 = (bf16[768,1152]{1,0:T(8,128)(2,1)}, bf16[768,1152]{1,0:T(8,128)(2,1)}, bf16[1024,384]{1,0:T(8,128)(2,1)}, f32[1024,128]{1,0:T(8,128)}, bf16[10...) conditional(s32[]{:T(128)} %convert_element_type.62, () %tuple.271, ...), branch_computations={%region_33.34_spmd, %region_34.37_spmd} | conditional | flops 1 | bytes 9437453 | solution.py:101
  341.3 19.0 %conditional.2 = (bf16[256,1536]{1,0:T(8,128)(2,1)}, bf16[256,1536]{1,0:T(8,128)(2,1)}, bf16[768,1152]{1,0:T(8,128)(2,1)}, bf16[768,1152]{1,0:T(8,128)(2,1)}) conditional(s32[]{:T(128)} %convert_element_type.26, () %tuple.143, (s32[2]{0:T(128)S(1)}, bf16[1024,1536]{1,0:T(8,128)(2,1)}, bf16[1024,1536]{1,0:T(8,128)(2,1)}, ...), branch_computations={%region_35.35_spmd, %region_36.36_spmd} | conditional | bytes 6291568 | solution.py:101
  342.2 12.9 %grad_gate.1 = (bf16[768,1152]{1,0:T(8,128)(2,1)}, bf16[768,1152]{1,0:T(8,128)(2,1)}) custom-call(s32[2]{0:T(128)S(1)} %get-tuple-element.711.scal, bf16[1024,1536]{1,0:T(8,128)(2,1)} %get-tuple-element.712.refs_0_, bf16[1024,1536]{1,0:T(8,128)(2,1)} %get-tuple-element.713.refs_1_, bf16[1024,1152]{1,0:T(8,128)(2,1)} %get-tuple-element.714.refs_2_, ...), custom_call_target="tpu_custom_call" | custom-call | tf_op jit(solution)/shard_map/cond/branch_1_fun/cond/branch_1_fun/grad_gate/pallas_call | solution.py:385
  355.0 5.2 collective-permute-done.27
  362.9 21.5 %attend_back.1 = (bf16[1024,384]{1,0:T(8,128)(2,1)}, f32[1024,128]{1,0:T(8,128)}, bf16[1024,128]{1,0:T(8,128)(2,1)}, f32[8,640]{1,0:T(8,128)}, bf16[768,384]{1,0:T(8,128)(2,1)}, /*index=5*/bf16[768,384]{1,0:T(8,128)(2,1)}) custom-call(s32[2]{0:T(128)S(1)} %get-tuple-element.721.scal, bf16[1024,384]{1,0:T(8,128)(2,1)} %get-tuple-element.732.query_ref, ...), custom_call_target="tpu_custom_call" | custom-call | tf_op jit(solution)/shard_map/cond/branch_1_fun/attend_back/pallas_call | solution.py:813
  384.4 8.6 %collective-permute-done.59 = bf16[384,1152]{1,0:T(8,128)(2,1)} collective-permute-done((bf16[384,1152]{1,0:T(8,128)(2,1)}, bf16[384,1152]{1,0:T(8,128)(2,1)}, u32[]{:S(2)}, u32[]{:S(2)}) %collective-permute-start.59) | collective-permute-done | bytes 884768 | tf_op jit(solution)/shard_map/swap_dp_4/ppermute | solution.py:122
  396.4 58.7 %conditional.36 = (bf16[384,1152]{1,0:T(8,128)(2,1)}, bf16[384,1152]{1,0:T(8,128)(2,1)}, bf16[768,1152]{1,0:T(8,128)(2,1)}, bf16[192,1152]{1,0:T(8,128)(2,1)}, b...) conditional(s32[]{:T(128)} %convert_element_type.62, () %tuple.229, ...), branch_computations={%region_37.38_spmd, %region_38.43_spmd} | conditional | flops 16910 | bytes 35412984 | solution.py:101
  396.4 3.9 fold_sum.9
  401.3 53.7 %conditional.4 = (bf16[192,1152]{1,0:T(8,128)(2,1)}, bf16[192,1152]{1,0:T(8,128)(2,1)}, bf16[768,512]{1,0:T(8,128)(2,1)}, bf16[256,1536]{1,0:T(8,128)(2,1)}, f32...) conditional(s32[]{:T(128)} %convert_element_type.30, () %tuple.158, ...), branch_computations={%region_39.39_spmd, %region_40.42_spmd} | conditional | flops 16909 | bytes 20077112 | solution.py:101
  404.0 9.2 %project_back.1 = (bf16[1024,512]{1,0:T(8,128)(2,1)}, bf16[512,1536]{1,0:T(8,128)(2,1)}, bf16[512,1536]{1,0:T(8,128)(2,1)}, f32[8,1536]{1,0:T(8,128)}) custom-call(s32[2]{0:T(128)S(1)} %get-tuple-element.767.scal, bf16[1024,384]{1,0:T(8,128)(2,1)} %get-tuple-element.774.query_ref, f32[1024,128]{1,0:T(8,128)} %get-tuple-element.775.kept_kv_ref, ...), custom_call_target="tpu_custom_call" | custom-call | tf_op jit(solution)/shard_map/cond/branch_1_fun/cond/branch_1_fun/project_back/pallas_call | solution.py:871
  413.8 5.7 %project_grad.1 = (bf16[768,512]{1,0:T(8,128)(2,1)}, bf16[768,512]{1,0:T(8,128)(2,1)}) custom-call(s32[2]{0:T(128)S(1)} %get-tuple-element.767.scal, bf16[512,1536]{1,0:T(8,128)(2,1)S(1)} %get-tuple-element.772.pair_ref, bf16[512,1536]{1,0:T(8,128)(2,1)} %get-tuple-element.773.core_ref, bf16[1024,512]{1,0:T(8,128)(2,1)} %get-tuple-element.785.grads_ref), custom_call_target="tpu_custom_call" | custom-call | tf_op jit(solution)/shard_map/cond/branch_1_fun/cond/branch_1_fun/project_grad/pallas_call | solution.py:899
  422.1 32.9 %conditional.3 = (bf16[256,1536]{1,0:T(8,128)(2,1)}, f32[32,160]{1,0:T(8,128)}, bf16[256,1536]{1,0:T(8,128)(2,1)}, bf16[768,512]{1,0:T(8,128)(2,1)}) conditional(s32[]{:T(128)} %convert_element_type.29, () %tuple.154, (s32[2]{0:T(128)S(1)}, bf16[1024,1536]{1,0:T(8,128)(2,1)}, bf16[1024,1536]{1,0:T(8,128)(2,1)}, bf16[512,1536]{1,0:T(8,128)(2,1)}, ...), branch_computations={%region_41.40_spmd, %region_42.41_spmd} | conditional | flops 16908 | bytes 6445326 | solution.py:101
  433.2 8.6 %collective-permute-done.33.arrived_ref = bf16[256,1536]{1,0:T(8,128)(2,1)} collective-permute-done((bf16[256,1536]{1,0:T(8,128)(2,1)}, bf16[256,1536]{1,0:T(8,128)(2,1)}, u32[]{:S(2)}, u32[]{:S(2)}) %collective-permute-start.33) | collective-permute-done | bytes 786464 | tf_op jit(solution)/shard_map/cond/branch_1_fun/cond/branch_1_fun/cond/branch_1_fun/swap_tensor_2/ppermute | solution.py:122
  441.9 3.7 norm_one_back.1
  445.6 9.4 %collective-permute-done.34 = bf16[768,512]{1,0:T(8,128)(2,1)} collective-permute-done((bf16[768,512]{1,0:T(8,128)(2,1)}, bf16[768,512]{1,0:T(8,128)(2,1)}, u32[]{:S(2)}, u32[]{:S(2)}) %collective-permute-start.34) | collective-permute-done | bytes 786464 | tf_op jit(solution)/shard_map/cond/branch_1_fun/cond/branch_1_fun/cond/branch_1_fun/swap_dp_2/ppermute | solution.py:122
  455.0 3.8 fold_sum.12
  460.2 4.8 all-to-all-start
  465.0 33.9 %conditional.37 = (bf16[192,896]{1,0:T(8,128)(2,1)}, bf16[192,1152]{1,0:T(8,128)(2,1)S(1)}, bf16[192,1152]{1,0:T(8,128)(2,1)S(1)}, bf16[256,1536]{1,0:T(8,128)(2...) conditional(s32[]{:T(128)} %convert_element_type.62, () %tuple.228, (s32[2]{0:T(128)S(1)}, ...), branch_computations={%region_43.44_spmd, %region_44.47_spmd} | conditional | flops 172033 | bytes 16761205 | solution.py:101
  468.5 23.9 %conditional.5 = (bf16[192,896]{1,0:T(8,128)(2,1)S(1)}, bf16[192,896]{1,0:T(8,128)(2,1)}, bf16[192,1152]{1,0:T(8,128)(2,1)}, bf16[192,1152]{1,0:T(8,128)(2,1)}) conditional(s32[]{:T(128)} %convert_element_type.32, () %tuple.167, (s32[2]{0:T(128)S(1)}, bf16[768,512]{1,0:T(8,128)(2,1)}, bf16[768,512]{1,0:T(8,128)(2,1)}, bf16[768,384]{1,0:T(8,128)(2,1)}, ...), branch_computations={%region_45.45_spmd, %region_46.46_spmd} | conditional | bytes 5505124 | solution.py:101
  468.5 3.4 fold_both.1
  476.0 13.2 %collective-permute-done.30.arrived_ref = bf16[384,896]{1,0:T(8,128)(2,1)S(1)} collective-permute-done((bf16[384,896]{1,0:T(8,128)(2,1)}, bf16[384,896]{1,0:T(8,128)(2,1)S(1)}, u32[]{:S(2)}, u32[]{:S(2)}) %collective-permute-start.30) | collective-permute-done | bytes 688160 | tf_op jit(solution)/shard_map/cond/branch_1_fun/cond/branch_1_fun/swap_dp_1/ppermute | solution.py:122
  495.7 3.2 block_final.1
  501.1 7.9 %collective-permute-start.65 = (bf16[192,896]{1,0:T(8,128)(2,1)}, bf16[192,896]{1,0:T(8,128)(2,1)S(1)}, u32[]{:S(2)}, u32[]{:S(2)}) collective-permute-start(bf16[192,896]{1,0:T(8,128)(2,1)} %get-tuple-element.1257), channel_id=1, source_target_pairs={{0,16},{4,20},{8,24},{12,28},{16,0},{20,4},{24,8},{28,12},{1,17},{... | collective-permute-start | bytes 1032200 | tf_op jit(solution)/shard_map/swap_dp_4/ppermute | solution.py:122
  512.8 8.1 %collective-permute-done.64.theirs_ref = bf16[192,1152]{1,0:T(8,128)(2,1)S(1)} collective-permute-done((bf16[192,1152]{1,0:T(8,128)(2,1)S(1)}, bf16[192,1152]{1,0:T(8,128)(2,1)S(1)}, u32[]{:S(2)}, u32[]{:S(2)}) %collective-permute-start.64) | collective-permute-done | bytes 442400 | tf_op jit(solution)/shard_map/swap_dp_2/ppermute | solution.py:122
  (262 shorter events, 158.6 us)
Async XLA Ops:
  2.5 14.1 %collective-permute-start.39 = (bf16[192,512]{1,0:T(8,128)(2,1)S(1)}, bf16[192,512]{1,0:T(8,128)(2,1)S(1)}, u32[]{:S(2)}, u32[]{:S(2)}) collective-permute-start(bf16[192,512]{1,0:T(8,128)(2,1)S(1)} %pad_maximum_fusion.6), channel_id=1, source_target_pairs={{0,16},{4,20},{8,24},{12,28},{16,0},{20,4},{24,8},{28,12},{1,17},{... | collective-permute-start | bytes 589832 | tf_op jit(solution)/shard_map/swap_dp_4/ppermute | solution.py:122
  6.6 10.0 %collective-permute-start.40 = (bf16[192,512]{1,0:T(8,128)(2,1)S(1)}, bf16[192,512]{1,0:T(8,128)(2,1)S(1)}, u32[]{:S(2)}, u32[]{:S(2)}) collective-permute-start(bf16[192,512]{1,0:T(8,128)(2,1)S(1)} %pad_maximum_fusion.6), channel_id=1, source_target_pairs={{0,8},{4,12},{8,0},{12,4},{16,24},{20,28},{24,16},{28,20},{1,9},{5... | collective-permute-start | bytes 589832 | tf_op jit(solution)/shard_map/swap_dp_2/ppermute | solution.py:122
  8.2 8.5 %collective-permute-start.41 = (bf16[192,512]{1,0:T(8,128)(2,1)S(1)}, bf16[192,512]{1,0:T(8,128)(2,1)S(1)}, u32[]{:S(2)}, u32[]{:S(2)}) collective-permute-start(bf16[192,512]{1,0:T(8,128)(2,1)S(1)} %pad_maximum_fusion.6), channel_id=1, source_target_pairs={{0,4},{4,0},{8,12},{12,8},{16,20},{20,16},{24,28},{28,24},{1,5},{5... | collective-permute-start | bytes 589832 | tf_op jit(solution)/shard_map/swap_dp_1/ppermute | solution.py:122
  12.1 21.1 %collective-permute-start.44 = (bf16[256,1536]{1,0:T(8,128)(2,1)S(1)}, bf16[256,1536]{1,0:T(8,128)(2,1)}, u32[]{:S(2)}, u32[]{:S(2)}) collective-permute-start(bf16[256,1536]{1,0:T(8,128)(2,1)S(1)} %fusion.2), channel_id=1, source_target_pairs={{0,2},{1,3},{2,0},{3,1},{4,6},{5,7},{6,4},{7,5},{8,10},{9,11},{10,... | collective-permute-start | bytes 2359304 | tf_op jit(solution)/shard_map/swap_tensor_2/ppermute | solution.py:122
  16.2 18.5 %collective-permute-start.45 = (bf16[192,1152]{1,0:T(8,128)(2,1)}, bf16[192,1152]{1,0:T(8,128)(2,1)}, u32[]{:S(2)}, u32[]{:S(2)}) collective-permute-start(bf16[192,1152]{1,0:T(8,128)(2,1)} %get-tuple-element.1085), channel_id=1, source_target_pairs={{0,8},{4,12},{8,0},{12,4},{16,24},{20,28},{24,16},{28,20},{1,9},{5... | collective-permute-start | bytes 1327112 | tf_op jit(solution)/shard_map/swap_dp_2/ppermute | solution.py:122
  16.7 18.0 %collective-permute-start.43 = (bf16[192,512]{1,0:T(8,128)(2,1)S(1)}, bf16[192,512]{1,0:T(8,128)(2,1)}, u32[]{:S(2)}, u32[]{:S(2)}) collective-permute-start(bf16[192,512]{1,0:T(8,128)(2,1)S(1)} %collective-permute-done.39), channel_id=1, source_target_pairs={{0,8},{4,12},{8,0},{12,4},{16,24},{20,28},{24,16},{28,20},{1,9},{5... | collective-permute-start | bytes 589832 | tf_op jit(solution)/shard_map/swap_dp_2/ppermute | solution.py:122
  19.1 15.5 %collective-permute-start.42 = (bf16[384,512]{1,0:T(8,128)(2,1)}, bf16[384,512]{1,0:T(8,128)(2,1)S(1)}, u32[]{:S(2)}, u32[]{:S(2)}) collective-permute-start(bf16[384,512]{1,0:T(8,128)(2,1)} %pad_maximum_fusion.4), channel_id=1, source_target_pairs={{0,4},{4,0},{8,12},{12,8},{16,20},{20,16},{24,28},{28,24},{1,5},{5... | collective-permute-start | bytes 1179656 | tf_op jit(solution)/shard_map/swap_dp_1/ppermute | solution.py:122
  20.2 12.3 %collective-permute-start.46 = (bf16[192,384]{1,0:T(8,128)(2,1)S(1)}, bf16[192,384]{1,0:T(8,128)(2,1)S(1)}, u32[]{:S(2)}, u32[]{:S(2)}) collective-permute-start(bf16[192,384]{1,0:T(8,128)(2,1)S(1)} %bitcast.25), channel_id=1, source_target_pairs={{0,16},{4,20},{8,24},{12,28},{16,0},{20,4},{24,8},{28,12},{1,17},{... | collective-permute-start | bytes 442376 | tf_op jit(solution)/shard_map/swap_dp_4/ppermute | solution.py:122
  34.7 10.3 %collective-permute-start.1 = (bf16[512,1536]{1,0:T(8,128)(2,1)S(1)}, bf16[512,1536]{1,0:T(8,128)(2,1)}, u32[]{:S(2)}, u32[]{:S(2)}) collective-permute-start(bf16[512,1536]{1,0:T(8,128)(2,1)S(1)} %get-tuple-element.511), channel_id=1, source_target_pairs={{0,1},{1,0},{2,3},{3,2},{4,5},{5,4},{6,7},{7,6},{8,9},{9,8},{10,11... | collective-permute-start | bytes 4718600 | tf_op jit(solution)/shard_map/cond/branch_1_fun/swap_tensor_1/ppermute | solution.py:122
  34.7 10.3 %collective-permute-start.2 = (bf16[384,384]{1,0:T(8,128)(2,1)}, bf16[384,384]{1,0:T(8,128)(2,1)}, u32[]{:S(2)}, u32[]{:S(2)}) collective-permute-start(bf16[384,384]{1,0:T(8,128)(2,1)} %get-tuple-element.512), channel_id=1, source_target_pairs={{0,8},{4,12},{8,0},{12,4},{16,24},{20,28},{24,16},{28,20},{1,9},{5... | collective-permute-start | bytes 884744 | tf_op jit(solution)/shard_map/cond/branch_1_fun/swap_dp_2/ppermute | solution.py:122
  37.1 7.3 %collective-permute-start = (bf16[192,512]{1,0:T(8,128)(2,1)}, bf16[192,512]{1,0:T(8,128)(2,1)}, u32[]{:S(2)}, u32[]{:S(2)}) collective-permute-start(bf16[192,512]{1,0:T(8,128)(2,1)} %get-tuple-element.510), channel_id=1, source_target_pairs={{0,4},{4,0},{8,12},{12,8},{16,20},{20,16},{24,28},{28,24},{1,5},{5... | collective-permute-start | bytes 589832 | tf_op jit(solution)/shard_map/cond/branch_1_fun/swap_dp_1/ppermute | solution.py:122
  46.1 38.0 %collective-permute-start.49 = (bf16[384,1152]{1,0:T(8,128)(2,1)}, bf16[384,1152]{1,0:T(8,128)(2,1)}, u32[]{:S(2)}, u32[]{:S(2)}) collective-permute-start(bf16[384,1152]{1,0:T(8,128)(2,1)} %get-tuple-element.1116), channel_id=1, source_target_pairs={{0,8},{4,12},{8,0},{12,4},{16,24},{20,28},{24,16},{28,20},{1,9},{5... | collective-permute-start | bytes 2654216 | tf_op jit(solution)/shard_map/swap_dp_2/ppermute | solution.py:122
  48.0 27.5 %collective-permute-start.47 = (bf16[256,1536]{1,0:T(8,128)(2,1)}, bf16[256,1536]{1,0:T(8,128)(2,1)}, u32[]{:S(2)}, u32[]{:S(2)}) collective-permute-start(bf16[256,1536]{1,0:T(8,128)(2,1)} %param.69), channel_id=1, source_target_pairs={{0,2},{1,3},{2,0},{3,1},{4,6},{5,7},{6,4},{7,5},{8,10},{9,11},{10,... | collective-permute-start | bytes 2359304 | tf_op jit(solution)/shard_map/swap_tensor_2/ppermute | solution.py:122
  48.8 20.6 %collective-permute-start.48 = (bf16[768,384]{1,0:T(8,128)(2,1)S(1)}, bf16[768,384]{1,0:T(8,128)(2,1)S(1)}, u32[]{:S(2)}, u32[]{:S(2)}) collective-permute-start(bf16[768,384]{1,0:T(8,128)(2,1)S(1)} %pad_maximum_fusion.2.refs_0_.refs_2_.refs_4_.refs_6_), channel_id=1, source_target_pairs={{0,4},{4,0},{8,12},{12,8},{16,20},{20,16},{24,28},{28,24},{1,5},{5... | collective-permute-start | bytes 1769480 | tf_op jit(solution)/shard_map/swap_dp_1/ppermute | solution.py:122
  51.1 65.2 %collective-permute-start.51 = (bf16[384,1152]{1,0:T(8,128)(2,1)}, bf16[384,1152]{1,0:T(8,128)(2,1)}, u32[]{:S(2)}, u32[]{:S(2)}) collective-permute-start(bf16[384,1152]{1,0:T(8,128)(2,1)} %get-tuple-element.1120), channel_id=1, source_target_pairs={{0,16},{4,20},{8,24},{12,28},{16,0},{20,4},{24,8},{28,12},{1,17},{... | collective-permute-start | bytes 2654216 | tf_op jit(solution)/shard_map/swap_dp_4/ppermute | solution.py:122
  61.2 8.2 %collective-permute-start.4 = (bf16[256,1536]{1,0:T(8,128)(2,1)}, bf16[256,1536]{1,0:T(8,128)(2,1)}, u32[]{:S(2)}, u32[]{:S(2)}) collective-permute-start(bf16[256,1536]{1,0:T(8,128)(2,1)} %get-tuple-element.534), channel_id=1, source_target_pairs={{0,1},{1,0},{2,3},{3,2},{4,5},{5,4},{6,7},{7,6},{8,9},{9,8},{10,11... | collective-permute-start | bytes 2359304 | tf_op jit(solution)/shard_map/cond/branch_1_fun/swap_tensor_1/ppermute | solution.py:122
  84.1 3.8 collective-permute-start.5
  87.9 59.9 %collective-permute-start.52 = (bf16[768,1152]{1,0:T(8,128)(2,1)}, bf16[768,1152]{1,0:T(8,128)(2,1)S(1)}, u32[]{:S(2)}, u32[]{:S(2)}) collective-permute-start(bf16[768,1152]{1,0:T(8,128)(2,1)} %get-tuple-element.1126), channel_id=1, source_target_pairs={{0,4},{4,0},{8,12},{12,8},{16,20},{20,16},{24,28},{28,24},{1,5},{5... | collective-permute-start | bytes 5308424 | tf_op jit(solution)/shard_map/swap_dp_1/ppermute | solution.py:122
  89.1 35.2 %collective-permute-start.50 = (bf16[256,1536]{1,0:T(8,128)(2,1)}, bf16[256,1536]{1,0:T(8,128)(2,1)}, u32[]{:S(2)}, u32[]{:S(2)}) collective-permute-start(bf16[256,1536]{1,0:T(8,128)(2,1)} %param.69), channel_id=1, source_target_pairs={{0,8},{4,12},{8,0},{12,4},{16,24},{20,28},{24,16},{28,20},{1,9},{5... | collective-permute-start | bytes 2359304 | tf_op jit(solution)/shard_map/swap_dp_2/ppermute | solution.py:122
  89.1 58.5 %collective-permute-start.54 = (bf16[384,1152]{1,0:T(8,128)(2,1)}, bf16[384,1152]{1,0:T(8,128)(2,1)}, u32[]{:S(2)}, u32[]{:S(2)}) collective-permute-start(bf16[384,1152]{1,0:T(8,128)(2,1)} %get-tuple-element.1130), channel_id=1, source_target_pairs={{0,16},{4,20},{8,24},{12,28},{16,0},{20,4},{24,8},{28,12},{1,17},{... | collective-permute-start | bytes 2654216 | tf_op jit(solution)/shard_map/swap_dp_4/ppermute | solution.py:122
  93.5 19.1 %collective-permute-start.6 = (bf16[256,1536]{1,0:T(8,128)(2,1)}, bf16[256,1536]{1,0:T(8,128)(2,1)}, u32[]{:S(2)}, u32[]{:S(2)}) collective-permute-start(bf16[256,1536]{1,0:T(8,128)(2,1)} %part_sum.4), channel_id=1, source_target_pairs={{0,2},{1,3},{2,0},{3,1},{4,6},{5,7},{6,4},{7,5},{8,10},{9,11},{10,... | collective-permute-start | bytes 2359304 | tf_op jit(solution)/shard_map/cond/branch_1_fun/swap_tensor_2/ppermute | solution.py:122
  124.4 23.4 %collective-permute-start.53 = (bf16[384,1152]{1,0:T(8,128)(2,1)}, bf16[384,1152]{1,0:T(8,128)(2,1)}, u32[]{:S(2)}, u32[]{:S(2)}) collective-permute-start(bf16[384,1152]{1,0:T(8,128)(2,1)} %collective-permute-done.51), channel_id=1, source_target_pairs={{0,4},{4,0},{8,12},{12,8},{16,20},{20,16},{24,28},{28,24},{1,5},{5... | collective-permute-start | bytes 2654216 | tf_op jit(solution)/shard_map/swap_dp_1/ppermute | solution.py:122
  125.1 18.6 %collective-permute-start.7 = (bf16[256,1536]{1,0:T(8,128)(2,1)}, bf16[256,1536]{1,0:T(8,128)(2,1)}, u32[]{:S(2)}, u32[]{:S(2)}) collective-permute-start(bf16[256,1536]{1,0:T(8,128)(2,1)} %get-tuple-element.549), channel_id=1, source_target_pairs={{0,2},{1,3},{2,0},{3,1},{4,6},{5,7},{6,4},{7,5},{8,10},{9,11},{10,... | collective-permute-start | bytes 2359304 | tf_op jit(solution)/shard_map/cond/branch_1_fun/swap_tensor_2/ppermute | solution.py:122
  126.5 21.1 %collective-permute-start.8 = (bf16[256,1536]{1,0:T(8,128)(2,1)}, bf16[256,1536]{1,0:T(8,128)(2,1)}, u32[]{:S(2)}, u32[]{:S(2)}) collective-permute-start(bf16[256,1536]{1,0:T(8,128)(2,1)} %get-tuple-element.549), channel_id=1, source_target_pairs={{0,8},{4,12},{8,0},{12,4},{16,24},{20,28},{24,16},{28,20},{1,9},{5... | collective-permute-start | bytes 2359304 | tf_op jit(solution)/shard_map/cond/branch_1_fun/swap_dp_2/ppermute | solution.py:122
  147.8 21.8 %collective-permute-start.55 = (bf16[384,1152]{1,0:T(8,128)(2,1)}, bf16[384,1152]{1,0:T(8,128)(2,1)}, u32[]{:S(2)}, u32[]{:S(2)}) collective-permute-start(bf16[384,1152]{1,0:T(8,128)(2,1)} %collective-permute-done.54), channel_id=1, source_target_pairs={{0,4},{4,0},{8,12},{12,8},{16,20},{20,16},{24,28},{28,24},{1,5},{5... | collective-permute-start | bytes 2654216 | tf_op jit(solution)/shard_map/swap_dp_1/ppermute | solution.py:122
  151.3 10.4 %collective-permute-start.12 = (bf16[128,1536]{1,0:T(8,128)(2,1)}, bf16[128,1536]{1,0:T(8,128)(2,1)}, u32[]{:S(2)}, u32[]{:S(2)}) collective-permute-start(bf16[128,1536]{1,0:T(8,128)(2,1)} %get-tuple-element.565), channel_id=1, source_target_pairs={{0,2},{1,3},{2,0},{3,1},{4,6},{5,7},{6,4},{7,5},{8,10},{9,11},{10,... | collective-permute-start | bytes 1179656 | tf_op jit(solution)/shard_map/cond/branch_1_fun/swap_tensor_2/ppermute | solution.py:122
  153.1 10.1 %collective-permute-start.13 = (bf16[128,1536]{1,0:T(8,128)(2,1)}, bf16[128,1536]{1,0:T(8,128)(2,1)}, u32[]{:S(2)}, u32[]{:S(2)}) collective-permute-start(bf16[128,1536]{1,0:T(8,128)(2,1)} %get-tuple-element.566), channel_id=1, source_target_pairs={{0,8},{4,12},{8,0},{12,4},{16,24},{20,28},{24,16},{28,20},{1,9},{5... | collective-permute-start | bytes 1179656 | tf_op jit(solution)/shard_map/cond/branch_1_fun/swap_dp_2/ppermute | solution.py:122
  169.6 41.2 %collective-permute-start.56 = (bf16[384,1152]{1,0:T(8,128)(2,1)}, bf16[384,1152]{1,0:T(8,128)(2,1)}, u32[]{:S(2)}, u32[]{:S(2)}) collective-permute-start(bf16[384,1152]{1,0:T(8,128)(2,1)} %get-tuple-element.1144), channel_id=1, source_target_pairs={{0,16},{4,20},{8,24},{12,28},{16,0},{20,4},{24,8},{28,12},{1,17},{... | collective-permute-start | bytes 2654216 | tf_op jit(solution)/shard_map/swap_dp_4/ppermute | solution.py:122
  172.2 22.0 %collective-permute-start.16 = (bf16[384,1152]{1,0:T(8,128)(2,1)}, bf16[384,1152]{1,0:T(8,128)(2,1)}, u32[]{:S(2)}, u32[]{:S(2)}) collective-permute-start(bf16[384,1152]{1,0:T(8,128)(2,1)} %get-tuple-element.590), channel_id=1, source_target_pairs={{0,4},{4,0},{8,12},{12,8},{16,20},{20,16},{24,28},{28,24},{1,5},{5... | collective-permute-start | bytes 2654216 | tf_op jit(solution)/shard_map/cond/branch_1_fun/swap_dp_1/ppermute | solution.py:122
  172.9 19.7 %collective-permute-start.17 = (bf16[256,1536]{1,0:T(8,128)(2,1)}, bf16[256,1536]{1,0:T(8,128)(2,1)}, u32[]{:S(2)}, u32[]{:S(2)}) collective-permute-start(bf16[256,1536]{1,0:T(8,128)(2,1)} %get-tuple-element.591), channel_id=1, source_target_pairs={{0,2},{1,3},{2,0},{3,1},{4,6},{5,7},{6,4},{7,5},{8,10},{9,11},{10,... | collective-permute-start | bytes 2359304 | tf_op jit(solution)/shard_map/cond/branch_1_fun/swap_tensor_2/ppermute | solution.py:122
  174.7 17.9 %collective-permute-start.18 = (bf16[256,1536]{1,0:T(8,128)(2,1)}, bf16[256,1536]{1,0:T(8,128)(2,1)}, u32[]{:S(2)}, u32[]{:S(2)}) collective-permute-start(bf16[256,1536]{1,0:T(8,128)(2,1)} %get-tuple-element.592), channel_id=1, source_target_pairs={{0,1},{1,0},{2,3},{3,2},{4,5},{5,4},{6,7},{7,6},{8,9},{9,8},{10,11... | collective-permute-start | bytes 2359304 | tf_op jit(solution)/shard_map/cond/branch_1_fun/swap_tensor_1/ppermute | solution.py:122
  194.2 16.5 %collective-permute-start.19 = (bf16[256,1536]{1,0:T(8,128)(2,1)}, bf16[256,1536]{1,0:T(8,128)(2,1)}, u32[]{:S(2)}, u32[]{:S(2)}) collective-permute-start(bf16[256,1536]{1,0:T(8,128)(2,1)} %get-tuple-element.613), channel_id=1, source_target_pairs={{0,1},{1,0},{2,3},{3,2},{4,5},{5,4},{6,7},{7,6},{8,9},{9,8},{10,11... | collective-permute-start | bytes 2359304 | tf_op jit(solution)/shard_map/cond/branch_1_fun/swap_tensor_1/ppermute | solution.py:122
  194.2 16.5 %collective-permute-start.20 = (bf16[256,1536]{1,0:T(8,128)(2,1)}, bf16[256,1536]{1,0:T(8,128)(2,1)}, u32[]{:S(2)}, u32[]{:S(2)}) collective-permute-start(bf16[256,1536]{1,0:T(8,128)(2,1)} %get-tuple-element.614), channel_id=1, source_target_pairs={{0,1},{1,0},{2,3},{3,2},{4,5},{5,4},{6,7},{7,6},{8,9},{9,8},{10,11... | collective-permute-start | bytes 2359304 | tf_op jit(solution)/shard_map/cond/branch_1_fun/swap_tensor_1/ppermute | solution.py:122
  210.7 21.9 %collective-permute-start.57 = (bf16[384,1152]{1,0:T(8,128)(2,1)}, bf16[384,1152]{1,0:T(8,128)(2,1)}, u32[]{:S(2)}, u32[]{:S(2)}) collective-permute-start(bf16[384,1152]{1,0:T(8,128)(2,1)} %collective-permute-done.56), channel_id=1, source_target_pairs={{0,4},{4,0},{8,12},{12,8},{16,20},{20,16},{24,28},{28,24},{1,5},{5... | collective-permute-start | bytes 2654216 | tf_op jit(solution)/shard_map/swap_dp_1/ppermute | solution.py:122
  232.7 78.5 %collective-permute-start.58 = (bf16[768,1152]{1,0:T(8,128)(2,1)}, bf16[768,1152]{1,0:T(8,128)(2,1)}, u32[]{:S(2)}, u32[]{:S(2)}) collective-permute-start(bf16[768,1152]{1,0:T(8,128)(2,1)} %get-tuple-element.1186), channel_id=1, source_target_pairs={{0,4},{4,0},{8,12},{12,8},{16,20},{20,16},{24,28},{28,24},{1,5},{5... | collective-permute-start | bytes 5308424 | tf_op jit(solution)/shard_map/swap_dp_1/ppermute | solution.py:122
  257.7 24.7 %collective-permute-start.21 = (bf16[1024,1536]{1,0:T(8,128)(2,1)}, bf16[1024,1536]{1,0:T(8,128)(2,1)}, u32[]{:S(2)}, u32[]{:S(2)}) collective-permute-start(bf16[1024,1536]{1,0:T(8,128)(2,1)} %get-tuple-element.657), channel_id=1, source_target_pairs={{0,1},{1,0},{2,3},{3,2},{4,5},{5,4},{6,7},{7,6},{8,9},{9,8},{10,11... | collective-permute-start | bytes 9437192 | tf_op jit(solution)/shard_map/cond/branch_1_fun/swap_tensor_1/ppermute | solution.py:122
  284.8 21.9 %collective-permute-start.23 = (bf16[128,1536]{1,0:T(8,128)(2,1)}, bf16[128,1536]{1,0:T(8,128)(2,1)}, u32[]{:S(2)}, u32[]{:S(2)}) collective-permute-start(bf16[128,1536]{1,0:T(8,128)(2,1)} %get-tuple-element.676), channel_id=1, source_target_pairs={{0,2},{1,3},{2,0},{3,1},{4,6},{5,7},{6,4},{7,5},{8,10},{9,11},{10,... | collective-permute-start | bytes 1179656 | tf_op jit(solution)/shard_map/cond/branch_1_fun/swap_tensor_2/ppermute | solution.py:122
  286.6 20.1 %collective-permute-start.24 = (bf16[128,1536]{1,0:T(8,128)(2,1)}, bf16[128,1536]{1,0:T(8,128)(2,1)}, u32[]{:S(2)}, u32[]{:S(2)}) collective-permute-start(bf16[128,1536]{1,0:T(8,128)(2,1)} %get-tuple-element.677), channel_id=1, source_target_pairs={{0,8},{4,12},{8,0},{12,4},{16,24},{20,28},{24,16},{28,20},{1,9},{5... | collective-permute-start | bytes 1179656 | tf_op jit(solution)/shard_map/cond/branch_1_fun/swap_dp_2/ppermute | solution.py:122
  297.6 9.1 %collective-permute-start.22 = (bf16[1024,1536]{1,0:T(8,128)(2,1)}, bf16[1024,1536]{1,0:T(8,128)(2,1)}, u32[]{:S(2)}, u32[]{:S(2)}) collective-permute-start(bf16[1024,1536]{1,0:T(8,128)(2,1)} %block_rows.3), channel_id=1, source_target_pairs={{0,1},{1,0},{2,3},{3,2},{4,5},{5,4},{6,7},{7,6},{8,9},{9,8},{10,11... | collective-permute-start | bytes 9437192 | tf_op jit(solution)/shard_map/cond/branch_1_fun/cond/branch_1_fun/swap_tensor_1/ppermute | solution.py:122
  311.2 21.2 %collective-permute-start.25 = (bf16[256,1536]{1,0:T(8,128)(2,1)}, bf16[256,1536]{1,0:T(8,128)(2,1)}, u32[]{:S(2)}, u32[]{:S(2)}) collective-permute-start(bf16[256,1536]{1,0:T(8,128)(2,1)} %get-tuple-element.701), channel_id=1, source_target_pairs={{0,2},{1,3},{2,0},{3,1},{4,6},{5,7},{6,4},{7,5},{8,10},{9,11},{10,... | collective-permute-start | bytes 2359304 | tf_op jit(solution)/shard_map/cond/branch_1_fun/swap_tensor_2/ppermute | solution.py:122
  311.6 20.9 %collective-permute-start.26 = (bf16[256,1536]{1,0:T(8,128)(2,1)}, bf16[256,1536]{1,0:T(8,128)(2,1)}, u32[]{:S(2)}, u32[]{:S(2)}) collective-permute-start(bf16[256,1536]{1,0:T(8,128)(2,1)} %get-tuple-element.702), channel_id=1, source_target_pairs={{0,8},{4,12},{8,0},{12,4},{16,24},{20,28},{24,16},{28,20},{1,9},{5... | collective-permute-start | bytes 2359304 | tf_op jit(solution)/shard_map/cond/branch_1_fun/swap_dp_2/ppermute | solution.py:122
  337.1 56.7 %collective-permute-start.60 = (bf16[768,1152]{1,0:T(8,128)(2,1)}, bf16[768,1152]{1,0:T(8,128)(2,1)}, u32[]{:S(2)}, u32[]{:S(2)}) collective-permute-start(bf16[768,1152]{1,0:T(8,128)(2,1)} %get-tuple-element.1210), channel_id=1, source_target_pairs={{0,4},{4,0},{8,12},{12,8},{16,20},{20,16},{24,28},{28,24},{1,5},{5... | collective-permute-start | bytes 5308424 | tf_op jit(solution)/shard_map/swap_dp_1/ppermute | solution.py:122
  338.6 55.2 %collective-permute-start.61 = (bf16[512,1536]{1,0:T(8,128)(2,1)}, bf16[512,1536]{1,0:T(8,128)(2,1)}, u32[]{:S(2)}, u32[]{:S(2)}) collective-permute-start(bf16[512,1536]{1,0:T(8,128)(2,1)} %get-tuple-element.1211), channel_id=1, source_target_pairs={{0,8},{4,12},{8,0},{12,4},{16,24},{20,28},{24,16},{28,20},{1,9},{5... | collective-permute-start | bytes 4718600 | tf_op jit(solution)/shard_map/swap_dp_2/ppermute | solution.py:122
  340.2 52.9 %collective-permute-start.59 = (bf16[384,1152]{1,0:T(8,128)(2,1)}, bf16[384,1152]{1,0:T(8,128)(2,1)}, u32[]{:S(2)}, u32[]{:S(2)}) collective-permute-start(bf16[384,1152]{1,0:T(8,128)(2,1)} %get-tuple-element.1209), channel_id=1, source_target_pairs={{0,16},{4,20},{8,24},{12,28},{16,0},{20,4},{24,8},{28,12},{1,17},{... | collective-permute-start | bytes 2654216 | tf_op jit(solution)/shard_map/swap_dp_4/ppermute | solution.py:122
  341.3 19.0 %collective-permute-start.27 = (bf16[256,1536]{1,0:T(8,128)(2,1)}, bf16[256,1536]{1,0:T(8,128)(2,1)}, u32[]{:S(2)}, u32[]{:S(2)}) collective-permute-start(bf16[256,1536]{1,0:T(8,128)(2,1)} %get-tuple-element.718), channel_id=1, source_target_pairs={{0,2},{1,3},{2,0},{3,1},{4,6},{5,7},{6,4},{7,5},{8,10},{9,11},{10,... | collective-permute-start | bytes 2359304 | tf_op jit(solution)/shard_map/cond/branch_1_fun/cond/branch_1_fun/swap_tensor_2/ppermute | solution.py:122
  342.2 18.1 %collective-permute-start.28 = (bf16[256,1536]{1,0:T(8,128)(2,1)}, bf16[256,1536]{1,0:T(8,128)(2,1)}, u32[]{:S(2)}, u32[]{:S(2)}) collective-permute-start(bf16[256,1536]{1,0:T(8,128)(2,1)} %get-tuple-element.718), channel_id=1, source_target_pairs={{0,1},{1,0},{2,3},{3,2},{4,5},{5,4},{6,7},{7,6},{8,9},{9,8},{10,11... | collective-permute-start | bytes 2359304 | tf_op jit(solution)/shard_map/cond/branch_1_fun/cond/branch_1_fun/swap_tensor_1/ppermute | solution.py:122
  393.8 61.2 %collective-permute-start.62 = (bf16[768,384]{1,0:T(8,128)(2,1)}, bf16[768,384]{1,0:T(8,128)(2,1)}, u32[]{:S(2)}, u32[]{:S(2)}) collective-permute-start(bf16[768,384]{1,0:T(8,128)(2,1)} %get-tuple-element.1225), channel_id=1, source_target_pairs={{0,8},{4,12},{8,0},{12,4},{16,24},{20,28},{24,16},{28,20},{1,9},{5... | collective-permute-start | bytes 1769480 | tf_op jit(solution)/shard_map/swap_dp_2/ppermute | solution.py:122
  400.2 54.8 %collective-permute-start.37 = (bf16[768,1152]{1,0:T(8,128)(2,1)}, bf16[768,1152]{1,0:T(8,128)(2,1)}, u32[]{:S(2)}, u32[]{:S(2)}) collective-permute-start(bf16[768,1152]{1,0:T(8,128)(2,1)} %get-tuple-element.844), channel_id=1, source_target_pairs={{0,4},{4,0},{8,12},{12,8},{16,20},{20,16},{24,28},{28,24},{1,5},{5... | collective-permute-start | bytes 5308424 | tf_op jit(solution)/shard_map/cond/branch_1_fun/swap_dp_1/ppermute | solution.py:122
  401.0 54.0 %collective-permute-start.38 = (bf16[384,1152]{1,0:T(8,128)(2,1)}, bf16[384,1152]{1,0:T(8,128)(2,1)}, u32[]{:S(2)}, u32[]{:S(2)}) collective-permute-start(bf16[384,1152]{1,0:T(8,128)(2,1)} %get-tuple-element.845), channel_id=1, source_target_pairs={{0,16},{4,20},{8,24},{12,28},{16,0},{20,4},{24,8},{28,12},{1,17},{... | collective-permute-start | bytes 2654216 | tf_op jit(solution)/shard_map/cond/branch_1_fun/swap_dp_4/ppermute | solution.py:122
  401.3 2.7 collective-permute-start.35
  413.2 6.3 %collective-permute-start.36 = (bf16[512,1536]{1,0:T(8,128)(2,1)}, bf16[512,1536]{1,0:T(8,128)(2,1)}, u32[]{:S(2)}, u32[]{:S(2)}) collective-permute-start(bf16[512,1536]{1,0:T(8,128)(2,1)} %get-tuple-element.798), channel_id=1, source_target_pairs={{0,1},{1,0},{2,3},{3,2},{4,5},{5,4},{6,7},{7,6},{8,9},{9,8},{10,11... | collective-permute-start | bytes 4718600 | tf_op jit(solution)/shard_map/cond/branch_1_fun/cond/branch_1_fun/swap_tensor_1/ppermute | solution.py:122
  422.1 19.8 %collective-permute-start.33 = (bf16[256,1536]{1,0:T(8,128)(2,1)}, bf16[256,1536]{1,0:T(8,128)(2,1)}, u32[]{:S(2)}, u32[]{:S(2)}) collective-permute-start(bf16[256,1536]{1,0:T(8,128)(2,1)} %get-tuple-element.762), channel_id=1, source_target_pairs={{0,2},{1,3},{2,0},{3,1},{4,6},{5,7},{6,4},{7,5},{8,10},{9,11},{10,... | collective-permute-start | bytes 2359304 | tf_op jit(solution)/shard_map/cond/branch_1_fun/cond/branch_1_fun/cond/branch_1_fun/swap_tensor_2/ppermute | solution.py:122
  423.8 31.2 %collective-permute-start.34 = (bf16[768,512]{1,0:T(8,128)(2,1)}, bf16[768,512]{1,0:T(8,128)(2,1)}, u32[]{:S(2)}, u32[]{:S(2)}) collective-permute-start(bf16[768,512]{1,0:T(8,128)(2,1)} %get-tuple-element.765), channel_id=1, source_target_pairs={{0,8},{4,12},{8,0},{12,4},{16,24},{20,28},{24,16},{28,20},{1,9},{5... | collective-permute-start | bytes 2359304 | tf_op jit(solution)/shard_map/cond/branch_1_fun/cond/branch_1_fun/cond/branch_1_fun/swap_dp_2/ppermute | solution.py:122
  458.8 41.7 %collective-permute-start.63 = (bf16[384,1152]{1,0:T(8,128)(2,1)}, bf16[384,1152]{1,0:T(8,128)(2,1)}, u32[]{:S(2)}, u32[]{:S(2)}) collective-permute-start(bf16[384,1152]{1,0:T(8,128)(2,1)} %get-tuple-element.1245), channel_id=1, source_target_pairs={{0,16},{4,20},{8,24},{12,28},{16,0},{20,4},{24,8},{28,12},{1,17},{... | collective-permute-start | bytes 2654216 | tf_op jit(solution)/shard_map/swap_dp_4/ppermute | solution.py:122
  460.2 40.3 %all-to-all-start = ((f32[32,1,160]{2,1,0:T(1,128)}), f32[32,1,160]{2,1,0:T(1,128)S(1)}, u32[]{:S(2)}, u32[]{:S(2)}) async-start(f32[32,1,160]{2,1,0:T(1,128)} %all_to_all.8), calls=%async_computation | async-start | bytes 65536 | tf_op jit(solution)/shard_map/all_to_all | solution.py:1323
  465.1 27.3 %collective-permute-start.31 = (bf16[256,1536]{1,0:T(8,128)(2,1)}, bf16[256,1536]{1,0:T(8,128)(2,1)}, u32[]{:S(2)}, u32[]{:S(2)}) collective-permute-start(bf16[256,1536]{1,0:T(8,128)(2,1)} %get-tuple-element.880), channel_id=1, source_target_pairs={{0,2},{1,3},{2,0},{3,1},{4,6},{5,7},{6,4},{7,5},{8,10},{9,11},{10,... | collective-permute-start | bytes 2359304 | tf_op jit(solution)/shard_map/cond/branch_1_fun/swap_tensor_2/ppermute | solution.py:122
  467.0 25.4 %collective-permute-start.32 = (bf16[192,1152]{1,0:T(8,128)(2,1)}, bf16[192,1152]{1,0:T(8,128)(2,1)S(1)}, u32[]{:S(2)}, u32[]{:S(2)}) collective-permute-start(bf16[192,1152]{1,0:T(8,128)(2,1)} %get-tuple-element.881), channel_id=1, source_target_pairs={{0,8},{4,12},{8,0},{12,4},{16,24},{20,28},{24,16},{28,20},{1,9},{5... | collective-permute-start | bytes 1327112 | tf_op jit(solution)/shard_map/cond/branch_1_fun/swap_dp_2/ppermute | solution.py:122
  471.9 17.2 %collective-permute-start.30 = (bf16[384,896]{1,0:T(8,128)(2,1)}, bf16[384,896]{1,0:T(8,128)(2,1)S(1)}, u32[]{:S(2)}, u32[]{:S(2)}) collective-permute-start(bf16[384,896]{1,0:T(8,128)(2,1)} %get-tuple-element.865), channel_id=1, source_target_pairs={{0,4},{4,0},{8,12},{12,8},{16,20},{20,16},{24,28},{28,24},{1,5},{5... | collective-permute-start | bytes 2064392 | tf_op jit(solution)/shard_map/cond/branch_1_fun/cond/branch_1_fun/swap_dp_1/ppermute | solution.py:122
  500.5 20.4 %collective-permute-start.64 = (bf16[192,1152]{1,0:T(8,128)(2,1)S(1)}, bf16[192,1152]{1,0:T(8,128)(2,1)S(1)}, u32[]{:S(2)}, u32[]{:S(2)}) collective-permute-start(bf16[192,1152]{1,0:T(8,128)(2,1)S(1)} %get-tuple-element.1255), channel_id=1, source_target_pairs={{0,8},{4,12},{8,0},{12,4},{16,24},{20,28},{24,16},{28,20},{1,9},{5... | collective-permute-start | bytes 1327112 | tf_op jit(solution)/shard_map/swap_dp_2/ppermute | solution.py:122
  501.1 23.0 %collective-permute-start.65 = (bf16[192,896]{1,0:T(8,128)(2,1)}, bf16[192,896]{1,0:T(8,128)(2,1)S(1)}, u32[]{:S(2)}, u32[]{:S(2)}) collective-permute-start(bf16[192,896]{1,0:T(8,128)(2,1)} %get-tuple-element.1257), channel_id=1, source_target_pairs={{0,16},{4,20},{8,24},{12,28},{16,0},{20,4},{24,8},{28,12},{1,17},{... | collective-permute-start | bytes 1032200 | tf_op jit(solution)/shard_map/swap_dp_4/ppermute | solution.py:122
  511.5 18.0 %collective-permute-start.66 = (bf16[192,1152]{1,0:T(8,128)(2,1)}, bf16[192,1152]{1,0:T(8,128)(2,1)S(1)}, u32[]{:S(2)}, u32[]{:S(2)}) collective-permute-start(bf16[192,1152]{1,0:T(8,128)(2,1)} %get-tuple-element.1254), channel_id=1, source_target_pairs={{0,8},{4,12},{8,0},{12,4},{16,24},{20,28},{24,16},{28,20},{1,9},{5... | collective-permute-start | bytes 1327112 | tf_op jit(solution)/shard_map/swap_dp_2/ppermute | solution.py:122
  525.9 3.6 collective-permute-start.67
  526.0 3.9 collective-permute-start.68
  527.5 3.3 collective-permute-start.69
  (39 other events, 411.7 us)

commit v5 on v4

--- a/solution.py
+++ b/solution.py
@@ -836,57 +836,61 @@
             *arrays_of(pieces),
         )
 
-    def project_back(scalars, grad_query, kv_kept, kv_arrived, pieces, pair, core):
+    def project_back(scalars, grad_query, kv_kept, kv_arrived, pieces):
         tokens, width = grad_query.shape
-        model, columns = pair.shape[1], pieces[0][0].shape[1]
+        columns = pieces[0][0].shape[1]
+        model = dp_size * shard_rows(pieces)
         rows = tokens // 4
 
-        def kernel(
-            scal, query_ref, kept_kv_ref, arrived_ref, pair_ref, core_ref, *refs
-        ):
-            (
-                grads_ref, kept_ref, sent_ref, gain_ref, held, part, acts, sems, out_sems,
-            ) = refs[dp_size:]
-            copies = start_all(
-                attn_jobs(scal[0], refs[:dp_size], pieces, held)
-                + token_jobs(scal[1], pair_ref, core_ref, acts),
-                sems,
-            )
+        def kernel(scal, query_ref, kept_kv_ref, arrived_ref, *refs):
+            grads_ref, kept_ref, sent_ref, held, part, sems, out_sems = refs[dp_size:]
+            copies = start_all(attn_jobs(scal[0], refs[:dp_size], pieces, held), sems)
             grads_ref[:, :width] = query_ref[...]
             grads_ref[:, width:] = (kept_kv_ref[...] + arrived_ref[...].astype(f32)).astype(bf16)
             wait_all(copies)
             for at in range(4):
                 spot = pl.ds(at * rows, rows)
                 part[spot, :] = mm_nt(grads_ref[spot, :], held[...]).astype(bf16)
-            copies = start_all(back(token_jobs(scal[1], kept_ref, sent_ref, part)), out_sems)
-            gain_ref[...] = jnp.zeros_like(gain_ref)
-            for at in range(8):
-                spot = pl.ds(at * rows // 2, rows // 2)
-                gain_ref[0:1, :] += jnp.sum(
-                    part[spot, :].astype(f32) * acts[spot, :].astype(f32), axis=0, keepdims=True
-                )
-            wait_all(copies)
+            wait_all(start_all(back(token_jobs(scal[1], kept_ref, sent_ref, part)), out_sems))
 
         half = jax.ShapeDtypeStruct((tokens // 2, model), bf16)
         return pl.pallas_call(
             kernel,
-            in_specs=[SCALARS, WHOLE, WHOLE, WHOLE, ANY, ANY] + [ANY] * dp_size,
-            out_specs=[WHOLE, ANY, ANY, WHOLE],
-            out_shape=[
-                jax.ShapeDtypeStruct((tokens, columns), bf16),
-                half,
-                half,
-                jax.ShapeDtypeStruct((8, model), f32),
-            ],
+            in_specs=[SCALARS, WHOLE, WHOLE, WHOLE] + [ANY] * dp_size,
+            out_specs=[WHOLE, ANY, ANY],
+            out_shape=[jax.ShapeDtypeStruct((tokens, columns), bf16), half, half],
             scratch_shapes=[
                 pltpu.VMEM((model, columns), bf16),
                 pltpu.VMEM((tokens, model), bf16),
-                pltpu.VMEM((tokens, model), bf16),
-                pltpu.SemaphoreType.DMA((dp_size + 4,)),
+                pltpu.SemaphoreType.DMA((dp_size,)),
                 pltpu.SemaphoreType.DMA((4,)),
             ],
             name="project_back",
-        )(scalars, grad_query, kv_kept, kv_arrived, pair, core, *arrays_of(pieces))
+        )(scalars, grad_query, kv_kept, kv_arrived, *arrays_of(pieces))
+
+    def shard_rows(pieces):
+        return min(piece[0].shape[0] for piece in pieces)
+
+    def gain_rows_of(scalars, kept, sent, pair, core):
+        rows, model = kept.shape[0] // 4, kept.shape[1]
+
+        def kernel(scal, kept_ref, sent_ref, pair_ref, core_ref, gain_ref):
+            @pl.when(pl.program_id(0) == 0)
+            def _():
+                gain_ref[...] = jnp.zeros_like(gain_ref)
+
+            total = kept_ref[...].astype(f32) * pair_ref[...].astype(f32)
+            total = total + sent_ref[...].astype(f32) * core_ref[...].astype(f32)
+            gain_ref[0:1, :] += jnp.sum(total, axis=0, keepdims=True)
+
+        return pl.pallas_call(
+            kernel,
+            grid=(4,),
+            in_specs=[SCALARS] + [pl.BlockSpec((rows, model), lambda i: (i, 0))] * 4,
+            out_specs=pl.BlockSpec((8, model), lambda i: (0, 0)),
+            out_shape=jax.ShapeDtypeStruct((8, model), f32),
+            name="gain_rows",
+        )(scalars, kept, sent, pair, core)
 
     def project_grad(scalars, pair, core, grads):
         tokens, columns = grads.shape
@@ -1253,29 +1257,36 @@
         gate_kept, gate_sent, outs = section(attention_back)
         grad_query_low, kv_kept, kv_given, bias_rows, wout_kept, wout_sent = outs
 
-        kv_given, wout_sent, gate_sent, down_sent, up_sent, block_from_l = hold(
-            [], [kv_given, wout_sent, gate_sent, down_sent, up_sent, block_from_l]
+        kv_given, up_sent = hold([], [kv_given, up_sent])
+
+        def pass_keys():
+            kv_arrived = swap(kv_given, "tensor", 1)
+            up_pair = fold_sum(scalars, up_kept, up_sent, far_bits[0], 1)
+            (kv_arrived,) = hold([up_pair], [kv_arrived])
+            return kv_arrived, *up_pair
+
+        kv_arrived, up_own, up_given = section(pass_keys)
+        kv_arrived, up_given, wout_sent, gate_sent, down_sent, block_from_l = hold(
+            [], [kv_arrived, up_given, wout_sent, gate_sent, down_sent, block_from_l]
         )
         wout_arrived = swap(wout_sent, "dp", pair_bit)
         devices = dp_size * tensor_size
 
         def input_grads():
-            up_own, up_given = fold_sum(scalars, up_kept, up_sent, far_bits[0], 1)
-            kv_in, gate_in, up_given = hold([], [kv_given, gate_sent, up_given])
+            kv_in, gate_in, up_in = hold([], [kv_arrived, gate_sent, up_given])
             gate_y = swap(gate_in, "dp", 1)
-            up_own, up_far_sum = far_rest(up_own, up_given)
+            up_sum, up_far_sum = far_rest(up_own, up_in)
 
             def project_all():
-                kv_arrived = swap(kv_in, "tensor", 1)
-                down_pair = fold_sum(scalars, down_kept, down_sent, pair_bit, 1)
-                (kv_arrived,) = hold([down_pair], [kv_arrived])
-                grad_qkv, one_kept, one_sent, gain_rows = project_back(
-                    scalars, grad_query_low, kv_kept, kv_arrived, qkv_pieces, act_pair, act_c
+                grad_qkv, one_kept, one_sent = project_back(
+                    scalars, grad_query_low, kv_kept, kv_in, qkv_pieces
                 )
+                one_sent, grad_qkv = hold([], [one_sent, grad_qkv])
                 arrived = swap(one_sent, "tensor", 1)
                 wqkv_pair = project_grad(scalars, act_pair, act_c, grad_qkv)
                 (arrived,) = hold([wqkv_pair], [arrived])
                 wqkv_kept, wqkv_sent = wqkv_pair
+                one_partner = one_sent
                 (one_given,) = part_sum(scalars, one_kept, arrived, block_input.shape[0], 1, 1)
                 one_arrived = arrived
 
@@ -1283,6 +1294,8 @@
                     arrived = swap(one_given, "tensor", 2)
                     wqkv_arrived = swap(wqkv_sent, "dp", pair_bit)
                     block = block_x_sum(scalars, block_kept, block_arrived, block_from_l)
+                    down_pair = fold_sum(scalars, down_kept, down_sent, pair_bit, 1)
+                    gain_rows = gain_rows_of(scalars, one_kept, one_partner, act_pair, act_c)
                     bias_keyval = jnp.zeros((2 * KV * HD,), f32)
                     bias_keyval = lax.dynamic_update_slice_in_dim(
                         bias_keyval, bias_rows[0, width : width + HD], head_kv * HD, 0
@@ -1295,19 +1308,19 @@
                     )
                     parts = (gain_rows[0] / gain_attn, gain_two[0], bias_query, bias_keyval)
                     small = jnp.concatenate([part.reshape(devices, -1) for part in parts], axis=1)
-                    (arrived,) = hold([block, small], [arrived])
+                    (arrived,) = hold([block, small, down_pair], [arrived])
                     grad_rows = norm_one_back(
                         scalars, block_input, one_kept, one_arrived, arrived, gain_attn[None, :],
                         grad_hidden,
                     )
                     (wqkv_arrived,) = hold([grad_rows], [wqkv_arrived])
-                    return grad_rows, small, block, wqkv_arrived
-
-                return (*down_pair, wqkv_kept, *section(first_norm_back))
+                    return (*down_pair, wqkv_kept, grad_rows, small, block, wqkv_arrived)
+
+                return section(first_norm_back)
 
             outs = section(project_all)
             outs, gate_y, up_far_sum = hold([], [outs, gate_y, up_far_sum])
-            return (up_own, up_far_sum, gate_y, *outs)
+            return (up_sum, up_far_sum, gate_y, *outs)
 
         (
             up_kept, up_sent, gate_sent, down_mine, down_given, wqkv_kept, grad_rows, small,

time: 544 us -> 537 us (0.987)
  the two profiles are of different devices: /device:TPU:0 before, /device:TPU:29 now
where the time goes in v5:
time: 537 us; the launch traced here: 527 us
  Pallas kernels  279 us (52%)
  waiting for transfers between devices  140 us (26%)
  starting transfers between devices  76 us (14%)
  local copies, waits for them, and re-layouts  16.3 us (3%)
  other arithmetic  13.7 us (3%)
    ppermute x70, waiting for transfers between devices, swap(): return lax.ppermute(array, axis, [(i, i ^ bit) for i in range(size)])  140 us
    ppermute x70, starting transfers between devices, swap(): return lax.ppermute(array, axis, [(i, i ^ bit) for i in range(size)])  67.3 us
    pallas_call x19, Pallas kernels, whole_call(): pl.pallas_call(kernel, in_specs=[SCALARS] + [WHOLE] * (len(args) - 1), ou...  61.3 us
    pallas_call x2, Pallas kernels, ffn_back(): pl.pallas_call(kernel, grid=(2,), in_specs=[SCALARS] + [ANY] * (many + 3...  49 us
    pallas_call x3, Pallas kernels, ffn_grad(): pl.pallas_call(kernel, grid=(model // wide,), in_specs=[SCALARS] + [pl.Bl...  38.9 us
    pallas_call x2, Pallas kernels, ffn_up(): pl.pallas_call(kernel, grid=(2,), in_specs=[SCALARS] + [ANY] * (many + 2...  31.3 us
    pallas_call x9, Pallas kernels, part_call(): pl.pallas_call(kernel, grid=(1,), in_specs=[SCALARS] + [rows_block(rows,...  28.6 us
    pallas_call x1, Pallas kernels, attend_back(): pl.pallas_call(kernel, in_specs=[SCALARS] + [WHOLE] * 4 + [ANY] * 4 + [WH...  21 us
  transfers between devices with their start and end apart: 71, of which 35 were waited for; matrix products, arithmetic and copies ran while one was open for 4% of the time, Pallas kernels for 51%

profile of v5, /device:TPU:29, one launch (start us, length us, event | category | flops | bytes accessed | tf_op | source)
XLA Modules:
  0.0 526.8 jit_solution(10880896952665277235)
XLA Ops:
  10.5 3.9 collective-permute-done.39
  21.2 3.4 split_cols.3
  31.4 10.4 %conditional.23 = (bf16[192,512]{1,0:T(8,128)(2,1)}, bf16[512,1536]{1,0:T(8,128)(2,1)}, bf16[384,384]{1,0:T(8,128)(2,1)}, bf16[384,1152]{1,0:T(8,128)(2,1)}) conditional(s32[]{:T(128)} %convert_element_type.63, () %tuple.242, (bf16[192,512]{1,0:T(8,128)(2,1)}, bf16[512,1536]{1,0:T(8,128)(2,1)S(1)}, bf16[384,384]{1,0:T(8,128)(2,1)}, s32[2]{0:T(128)S(1)}, ...), branch_computations={%region_3.4_spmd, %region_4.5_spmd} | conditional | bytes 8257688 | solution.py:101
  37.2 3.4 collective-permute-done
  46.6 18.6 %conditional.24 = (bf16[1024,384]{1,0:T(8,128)(2,1)}, bf16[1024,128]{1,0:T(8,128)(2,1)}, bf16[1024,128]{1,0:T(8,128)(2,1)}, bf16[1024,384]{1,0:T(8,128)(2,1)S(1)}, bf16[256,1536]{1,0:T(8,128)(2,1)}) conditional(s32[]{:T(128)} %convert_element_type.63, () %tuple.247, (f32[512]{0:T(512)S(1)}, s32[2]{0:T(128)S(1)}, bf16[512,1536]{1,0:T(8,128)(2,1)S(1)}, ...), branch_computations={%region_5.6_spmd, %region_6.7_spmd} | conditional | bytes 4194424 | solution.py:101
  46.6 6.8 %project.1 = (bf16[1024,384]{1,0:T(8,128)(2,1)}, bf16[1024,128]{1,0:T(8,128)(2,1)}) custom-call(s32[2]{0:T(128)S(1)} %get-tuple-element.534.scal, bf16[512,1536]{1,0:T(8,128)(2,1)S(1)} %get-tuple-element.535.pair_ref, bf16[512,1536]{1,0:T(8,128)(2,1)} %get-tuple-element.536.core_ref, f32[1,512]{1,0:T(1,128)S(1)} %bitcast.29, ...), custom_call_target="tpu_custom_call" | custom-call | tf_op jit(solution)/shard_map/cond/branch_1_fun/project/pallas_call | solution.py:676
  57.2 8.1 %attend.1 = bf16[1024,384]{1,0:T(8,128)(2,1)S(1)} custom-call(s32[2]{0:T(128)S(1)} %get-tuple-element.534.scal, bf16[1024,384]{1,0:T(8,128)(2,1)} %get-tuple-element.1379.query_ref, bf16[1024,128]{1,0:T(8,128)(2,1)} %get-tuple-element.1380.own_ref, bf16[1024,128]{1,0:T(8,128)(2,1)} %collective-permute-done.3.other_ref, s32[1024,1]{1,0:T(8,128)} %get-tuple-element.551.start_ref), custom_call_target="tpu_custom_call" | custom-call | tf_op jit(solution)/shard_map/cond/branch_1_fun/attend/pallas_call | solution.py:400
  65.3 5.9 %out_rows.1 = (bf16[512,1536]{1,0:T(8,128)(2,1)}, bf16[512,1536]{1,0:T(8,128)(2,1)}) custom-call(s32[2]{0:T(128)S(1)} %pad_add_fusion.scal, bf16[1024,384]{1,0:T(8,128)(2,1)S(1)} %get-tuple-element.1142.context_ref, bf16[768,384]{1,0:T(8,128)(2,1)S(1)} %pad_maximum_fusion.2.refs_0_.refs_2_.refs_4_.refs_6_, ...), custom_call_target="tpu_custom_call" | custom-call | tf_op jit(solution)/shard_map/out_rows/pallas_call | solution.py:738
  71.2 8.1 %collective-permute-done.49 = bf16[384,1152]{1,0:T(8,128)(2,1)} collective-permute-done((bf16[384,1152]{1,0:T(8,128)(2,1)}, bf16[384,1152]{1,0:T(8,128)(2,1)}, u32[]{:S(2)}, u32[]{:S(2)}) %collective-permute-start.49) | collective-permute-done | bytes 884768 | tf_op jit(solution)/shard_map/swap_dp_2/ppermute | solution.py:122
  79.3 4.9 conditional.25
  87.2 24.3 %conditional.26 = ((f32[256,1536]{1,0:T(8,128)}, bf16[256,1536]{1,0:T(8,128)(2,1)})) conditional(s32[]{:T(128)} %convert_element_type.63, () %tuple.251, (s32[2]{0:T(128)S(1)}, bf16[512,1536]{1,0:T(8,128)(2,1)}, bf16[512,1536]{1,0:T(8,128)(2,1)}, f32[1536]{0:T(1024)S(1)}, bf16[256,1536]{1,0:T(8,128)(2,1)}) %tuple.368), branch_computations={%region_9.10_spmd, %region_10.11_spmd} | conditional | bytes 3158064 | solution.py:101
  91.2 16.5 %collective-permute-done.6.arrived_ref = bf16[256,1536]{1,0:T(8,128)(2,1)} collective-permute-done((bf16[256,1536]{1,0:T(8,128)(2,1)}, bf16[256,1536]{1,0:T(8,128)(2,1)}, u32[]{:S(2)}, u32[]{:S(2)}) %collective-permute-start.6) | collective-permute-done | bytes 786464 | tf_op jit(solution)/shard_map/cond/branch_1_fun/swap_tensor_2/ppermute | solution.py:122
  107.8 3.7 norm_two.1
  111.5 10.2 %collective-permute-done.50 = bf16[256,1536]{1,0:T(8,128)(2,1)} collective-permute-done((bf16[256,1536]{1,0:T(8,128)(2,1)}, bf16[256,1536]{1,0:T(8,128)(2,1)}, u32[]{:S(2)}, u32[]{:S(2)}) %collective-permute-start.50) | collective-permute-done | bytes 786464 | tf_op jit(solution)/shard_map/swap_dp_2/ppermute | solution.py:122
  123.1 18.8 %conditional.27 = (bf16[256,1536]{1,0:T(8,128)(2,1)}, bf16[256,1536]{1,0:T(8,128)(2,1)}, bf16[384,1152]{1,0:T(8,128)(2,1)}) conditional(s32[]{:T(128)} %convert_element_type.63, () %tuple.256, (bf16[256,1536]{1,0:T(8,128)(2,1)}, s32[2]{0:T(128)S(1)}, bf16[384,1152]{1,0:T(8,128)(2,1)}, bf16[384,1152]{1,0:T(8,128)(2,1)}) %tuple.257), branch_computations={%region_11.12_spmd, %region_12.13_spmd} | conditional | bytes 6291560 | solution.py:101
  125.5 16.2 %collective-permute-done.7 = bf16[256,1536]{1,0:T(8,128)(2,1)} collective-permute-done((bf16[256,1536]{1,0:T(8,128)(2,1)}, bf16[256,1536]{1,0:T(8,128)(2,1)}, u32[]{:S(2)}, u32[]{:S(2)}) %collective-permute-start.7) | collective-permute-done | bytes 786464 | tf_op jit(solution)/shard_map/cond/branch_1_fun/swap_tensor_2/ppermute | solution.py:122
  144.1 14.0 %conditional.28 = (bf16[128,1536]{1,0:T(8,128)(2,1)}, bf16[128,1536]{1,0:T(8,128)(2,1)}, bf16[256,1536]{1,0:T(8,128)(2,1)}, bf16[256,1536]{1,0:T(8,128)(2,1)}, bf16[256,1536]{1,0:T(8,128)(2,1)}) conditional(s32[]{:T(128)} %convert_element_type.63, () %tuple.259, (s32[2]{0:T(128)S(1)}, bf16[256,1536]{1,0:T(8,128)(2,1)}, ...), branch_computations={%region_13.14_spmd, %region_14.17_spmd} | conditional | flops 1 | bytes 12583205 | solution.py:101
  148.3 8.6 %conditional = (bf16[256,1536]{1,0:T(8,128)(2,1)}, bf16[256,1536]{1,0:T(8,128)(2,1)}, bf16[256,1536]{1,0:T(8,128)(2,1)}) conditional(s32[]{:T(128)} %convert_element_type.15, () %tuple.119, (bf16[256,1536]{1,0:T(8,128)(2,1)}, bf16[256,1536]{1,0:T(8,128)(2,1)}, bf16[256,1536]{1,0:T(8,128)(2,1)}) %tuple.120), branch_computations={%region_15.15_spmd, %region_16.16_spmd} | conditional | bytes 9437328 | solution.py:101
  158.1 5.7 %collective-permute-done.55 = bf16[384,1152]{1,0:T(8,128)(2,1)} collective-permute-done((bf16[384,1152]{1,0:T(8,128)(2,1)}, bf16[384,1152]{1,0:T(8,128)(2,1)}, u32[]{:S(2)}, u32[]{:S(2)}) %collective-permute-start.55) | collective-permute-done | bytes 884768 | tf_op jit(solution)/shard_map/swap_dp_1/ppermute | solution.py:122
  163.8 4.7 conditional.29
  168.5 21.2 %conditional.30 = (bf16[384,1152]{1,0:T(8,128)(2,1)}, bf16[256,1536]{1,0:T(8,128)(2,1)}, bf16[256,1536]{1,0:T(8,128)(2,1)}, bf16[1024,1536]{1,0:T(8,128)(2,1)}, ...) conditional(s32[]{:T(128)} %convert_element_type.63, () %tuple.241, ...), branch_computations={%region_19.20_spmd, %region_20.21_spmd} | conditional | bytes 12681286 | solution.py:101
  171.6 15.4 %ffn_up.2 = (bf16[1024,1536]{1,0:T(8,128)(2,1)}, bf16[1024,1152]{1,0:T(8,128)(2,1)}, bf16[1024,1152]{1,0:T(8,128)(2,1)}, bf16[1024,1152]{1,0:T(8,128)(2,1)}) custom-call(s32[2]{0:T(128)S(1)} %get-tuple-element.591.scal, bf16[256,1536]{1,0:T(8,128)(2,1)} %get-tuple-element.592.refs_0_, bf16[256,1536]{1,0:T(8,128)(2,1)} %get-tuple-element.593.refs_1_, ...), custom_call_target="tpu_custom_call" | custom-call | tf_op jit(solution)/shard_map/cond/branch_1_fun/ffn_up/pallas_call | solution.py:252
  189.7 17.1 %conditional.31 = (bf16[256,1536]{1,0:T(8,128)(2,1)}, bf16[256,1536]{1,0:T(8,128)(2,1)}, bf16[1024,1536]{1,0:T(8,128)(2,1)}, bf16[1024,1152]{1,0:T(8,128)(2,1)},...) conditional(s32[]{:T(128)} %convert_element_type.63, () %tuple.266, (s32[2]{0:T(128)S(1)}, ...), branch_computations={%region_21.22_spmd, %region_22.23_spmd} | conditional | bytes 11796540 | solution.py:101
  190.9 15.9 %ffn_up.3 = (bf16[1024,1536]{1,0:T(8,128)(2,1)}, bf16[1024,1152]{1,0:T(8,128)(2,1)}, bf16[1024,1152]{1,0:T(8,128)(2,1)}, bf16[1024,1152]{1,0:T(8,128)(2,1)}) custom-call(s32[2]{0:T(128)S(1)} %get-tuple-element.614.scal, bf16[256,1536]{1,0:T(8,128)(2,1)} %get-tuple-element.615.refs_0_, bf16[256,1536]{1,0:T(8,128)(2,1)} %get-tuple-element.616.refs_1_, ...), custom_call_target="tpu_custom_call" | custom-call | tf_op jit(solution)/shard_map/cond/branch_1_fun/ffn_up/pallas_call | solution.py:252
  207.9 13.2 %conditional.32 = ((bf16[768,1152]{1,0:T(8,128)(2,1)}, bf16[768,1152]{1,0:T(8,128)(2,1)})) conditional(s32[]{:T(128)} %convert_element_type.63, () %tuple.270, (s32[2]{0:T(128)S(1)}, bf16[256,1536]{1,0:T(8,128)(2,1)}, bf16[256,1536]{1,0:T(8,128)(2,1)}, bf16[256,1536]{1,0:T(8,128)(2,1)}, bf16[256,1536]{1,0:T(8,128)(2,1)}, ...), branch_computations={%region_23.24_spmd, %region_24.25_spmd} | conditional | bytes 3538972 | solution.py:101
  207.9 13.2 %grad_down.1 = (bf16[768,1152]{1,0:T(8,128)(2,1)}, bf16[768,1152]{1,0:T(8,128)(2,1)}) custom-call(s32[2]{0:T(128)S(1)} %get-tuple-element.635.scal, bf16[256,1536]{1,0:T(8,128)(2,1)} %get-tuple-element.636.refs_0_, bf16[256,1536]{1,0:T(8,128)(2,1)} %get-tuple-element.637.refs_1_, bf16[256,1536]{1,0:T(8,128)(2,1)} %get-tuple-element.638.refs_2_, ...), custom_call_target="tpu_custom_call" | custom-call | tf_op jit(solution)/shard_map/cond/branch_1_fun/grad_down/pallas_call | solution.py:385
  221.2 6.7 %collective-permute-done.57 = bf16[384,1152]{1,0:T(8,128)(2,1)} collective-permute-done((bf16[384,1152]{1,0:T(8,128)(2,1)}, bf16[384,1152]{1,0:T(8,128)(2,1)}, u32[]{:S(2)}, u32[]{:S(2)}) %collective-permute-start.57) | collective-permute-done | bytes 884768 | tf_op jit(solution)/shard_map/swap_dp_1/ppermute | solution.py:122
  229.0 53.1 %conditional.33 = (bf16[1024,1152]{1,0:T(8,128)(2,1)}, bf16[1024,1152]{1,0:T(8,128)(2,1)}, bf16[1024,1152]{1,0:T(8,128)(2,1)}, bf16[1024,1152]{1,0:T(8,128)(2,1)...) conditional(s32[]{:T(128)} %convert_element_type.63, () %tuple.269, ...), branch_computations={%region_25.26_spmd, %region_26.27_spmd} | conditional | bytes 16515152 | solution.py:101
  229.0 24.4 %ffn_back.3 = (bf16[1024,1152]{1,0:T(8,128)(2,1)}, bf16[1024,1152]{1,0:T(8,128)(2,1)}, bf16[1024,1536]{1,0:T(8,128)(2,1)}) custom-call(s32[2]{0:T(128)S(1)} %get-tuple-element.646.scal, bf16[256,1536]{1,0:T(8,128)(2,1)} %get-tuple-element.666.refs_0_, bf16[256,1536]{1,0:T(8,128)(2,1)} %get-tuple-element.667.refs_1_, ...), custom_call_target="tpu_custom_call" | custom-call | tf_op jit(solution)/shard_map/cond/branch_1_fun/ffn_back/pallas_call | solution.py:315
  255.1 24.6 %ffn_back.2 = (bf16[1024,1152]{1,0:T(8,128)(2,1)}, bf16[1024,1152]{1,0:T(8,128)(2,1)}, bf16[1024,1536]{1,0:T(8,128)(2,1)}) custom-call(s32[2]{0:T(128)S(1)} %get-tuple-element.646.scal, bf16[256,1536]{1,0:T(8,128)(2,1)} %get-tuple-element.647.refs_0_, bf16[256,1536]{1,0:T(8,128)(2,1)} %get-tuple-element.648.refs_1_, ...), custom_call_target="tpu_custom_call" | custom-call | tf_op jit(solution)/shard_map/cond/branch_1_fun/ffn_back/pallas_call | solution.py:315
  282.1 26.1 %conditional.34 = (bf16[1024,1536]{1,0:T(8,128)(2,1)}, bf16[1024,1536]{1,0:T(8,128)(2,1)}, f32[256,1536]{1,0:T(8,128)}, bf16[256,1536]{1,0:T(8,128)(2,1)}, bf16[256,1536]{1,0:T(8,128)(2,1)}) conditional(s32[]{:T(128)} %convert_element_type.63, () %tuple.276, (s32[2]{0:T(128)S(1)}, bf16[1024,1152]{1,0:T(8,128)(2,1)}, bf16[384,1152]{1,0:T(8,128)(2,1)}, ...), branch_computations={%region_27.28_spmd, %region_28.31_spmd} | conditional | flops 1 | bytes 15728877 | solution.py:101
  284.9 18.8 %conditional.1 = (bf16[1024,1536]{1,0:T(8,128)(2,1)}, bf16[1024,1536]{1,0:T(8,128)(2,1)}) conditional(s32[]{:T(128)} %convert_element_type.16, () %tuple.136, (s32[2]{0:T(128)S(1)}, bf16[1024,1152]{1,0:T(8,128)(2,1)}, bf16[384,1152]{1,0:T(8,128)(2,1)}, bf16[384,1152]{1,0:T(8,128)(2,1)}, bf16[384,1152]{1,0:T(8,128)(2,1)}, ...), branch_computations={%region_29.29_spmd, %region_30.30_spmd} | conditional | bytes 12582968 | solution.py:101
  284.9 9.0 %block_rows.3 = bf16[1024,1536]{1,0:T(8,128)(2,1)} custom-call(s32[2]{0:T(128)S(1)} %get-tuple-element.678.scal, bf16[1024,1152]{1,0:T(8,128)(2,1)} %get-tuple-element.684.left_ref, bf16[384,1152]{1,0:T(8,128)(2,1)} %get-tuple-element.680.refs_0_, bf16[384,1152]{1,0:T(8,128)(2,1)} %get-tuple-element.681.refs_1_, ...), custom_call_target="tpu_custom_call" | custom-call | tf_op jit(solution)/shard_map/cond/branch_1_fun/cond/branch_1_fun/block_rows/pallas_call | solution.py:343
  294.6 9.1 %block_rows.2 = bf16[1024,1536]{1,0:T(8,128)(2,1)} custom-call(s32[2]{0:T(128)S(1)} %get-tuple-element.678.scal, bf16[1024,1152]{1,0:T(8,128)(2,1)} %get-tuple-element.679.left_ref, bf16[384,1152]{1,0:T(8,128)(2,1)} %get-tuple-element.680.refs_0_, bf16[384,1152]{1,0:T(8,128)(2,1)} %get-tuple-element.681.refs_1_, ...), custom_call_target="tpu_custom_call" | custom-call | tf_op jit(solution)/shard_map/cond/branch_1_fun/cond/branch_1_fun/block_rows/pallas_call | solution.py:343
  303.7 4.4 spread_rest.1
  308.1 26.2 %conditional.35 = (bf16[768,1152]{1,0:T(8,128)(2,1)}, bf16[768,1152]{1,0:T(8,128)(2,1)}, bf16[384,1152]{1,0:T(8,128)(2,1)}, bf16[384,1152]{1,0:T(8,128)(2,1)}, b...) conditional(s32[]{:T(128)} %convert_element_type.63, () %tuple.240, ...), branch_computations={%region_31.32_spmd, %region_32.33_spmd} | conditional | bytes 9289812 | solution.py:101
  309.7 3.7 fold_sum.7
  313.4 3.4 part_sum.6
  316.8 12.9 %grad_up.1 = (bf16[768,1152]{1,0:T(8,128)(2,1)}, bf16[768,1152]{1,0:T(8,128)(2,1)}) custom-call(s32[2]{0:T(128)S(1)} %get-tuple-element.705.scal, bf16[1024,1536]{1,0:T(8,128)(2,1)} %get-tuple-element.706.refs_0_, bf16[1024,1536]{1,0:T(8,128)(2,1)} %get-tuple-element.707.refs_1_, bf16[1024,1152]{1,0:T(8,128)(2,1)} %get-tuple-element.708.refs_2_, ...), custom_call_target="tpu_custom_call" | custom-call | tf_op jit(solution)/shard_map/cond/branch_1_fun/grad_up/pallas_call | solution.py:385
  329.6 4.7 norm_two_back.1
  336.3 43.6 %conditional.36 = (bf16[768,1152]{1,0:T(8,128)(2,1)}, bf16[768,1152]{1,0:T(8,128)(2,1)}, bf16[1024,384]{1,0:T(8,128)(2,1)}, f32[1024,128]{1,0:T(8,128)}, bf16[10...) conditional(s32[]{:T(128)} %convert_element_type.63, () %tuple.281, ...), branch_computations={%region_33.34_spmd, %region_34.37_spmd} | conditional | flops 1 | bytes 15728965 | solution.py:101
  336.3 18.2 %conditional.2 = (bf16[256,1536]{1,0:T(8,128)(2,1)}, bf16[256,1536]{1,0:T(8,128)(2,1)}, bf16[768,1152]{1,0:T(8,128)(2,1)}, bf16[768,1152]{1,0:T(8,128)(2,1)}) conditional(s32[]{:T(128)} %convert_element_type.26, () %tuple.147, (s32[2]{0:T(128)S(1)}, bf16[1024,1536]{1,0:T(8,128)(2,1)}, bf16[1024,1536]{1,0:T(8,128)(2,1)}, ...), branch_computations={%region_35.35_spmd, %region_36.36_spmd} | conditional | bytes 6291568 | solution.py:101
  339.2 12.8 %grad_gate.1 = (bf16[768,1152]{1,0:T(8,128)(2,1)}, bf16[768,1152]{1,0:T(8,128)(2,1)}) custom-call(s32[2]{0:T(128)S(1)} %get-tuple-element.729.scal, bf16[1024,1536]{1,0:T(8,128)(2,1)} %get-tuple-element.730.refs_0_, bf16[1024,1536]{1,0:T(8,128)(2,1)} %get-tuple-element.731.refs_1_, bf16[1024,1152]{1,0:T(8,128)(2,1)} %get-tuple-element.732.refs_2_, ...), custom_call_target="tpu_custom_call" | custom-call | tf_op jit(solution)/shard_map/cond/branch_1_fun/cond/branch_1_fun/grad_gate/pallas_call | solution.py:385
  358.9 21.0 %attend_back.1 = (bf16[1024,384]{1,0:T(8,128)(2,1)}, f32[1024,128]{1,0:T(8,128)}, bf16[1024,128]{1,0:T(8,128)(2,1)}, f32[8,640]{1,0:T(8,128)}, bf16[768,384]{1,0:T(8,128)(2,1)}, /*index=5*/bf16[768,384]{1,0:T(8,128)(2,1)}) custom-call(s32[2]{0:T(128)S(1)} %get-tuple-element.739.scal, bf16[1024,384]{1,0:T(8,128)(2,1)S(1)} %copy-done.9, ...), custom_call_target="tpu_custom_call" | custom-call | tf_op jit(solution)/shard_map/cond/branch_1_fun/attend_back/pallas_call | solution.py:813
  380.0 4.5 conditional.37
  380.4 4.0 fold_sum.8
  384.5 4.1 collective-permute-done.60
  390.6 49.6 %conditional.38 = (bf16[384,1152]{1,0:T(8,128)(2,1)}, bf16[384,1152]{1,0:T(8,128)(2,1)}, bf16[768,1152]{1,0:T(8,128)(2,1)}, bf16[192,1152]{1,0:T(8,128)(2,1)}, b...) conditional(s32[]{:T(128)} %convert_element_type.63, () %tuple.238, ...), branch_computations={%region_39.40_spmd, %region_40.45_spmd} | conditional | flops 16910 | bytes 29645708 | solution.py:101
  392.6 47.7 %conditional.4 = ((bf16[192,1152]{1,0:T(8,128)(2,1)}, bf16[192,1152]{1,0:T(8,128)(2,1)}, bf16[768,512]{1,0:T(8,128)(2,1)}, bf16[256,1536]{1,0:T(8,128)(2,1)}, f3...) conditional(s32[]{:T(128)} %convert_element_type.30, () %tuple.164, ...), branch_computations={%region_41.41_spmd, %region_42.44_spmd} | conditional | flops 16909 | bytes 19028512 | solution.py:101
  392.6 8.5 %project_back.1 = (bf16[1024,512]{1,0:T(8,128)(2,1)}, bf16[512,1536]{1,0:T(8,128)(2,1)}, bf16[512,1536]{1,0:T(8,128)(2,1)}) custom-call(s32[2]{0:T(128)S(1)} %get-tuple-element.799.scal, bf16[1024,384]{1,0:T(8,128)(2,1)} %get-tuple-element.805.query_ref, f32[1024,128]{1,0:T(8,128)} %get-tuple-element.806.kept_kv_ref, ...), custom_call_target="tpu_custom_call" | custom-call | tf_op jit(solution)/shard_map/cond/branch_1_fun/cond/branch_1_fun/project_back/pallas_call | solution.py:857
  403.5 5.8 %project_grad.1 = (bf16[768,512]{1,0:T(8,128)(2,1)}, bf16[768,512]{1,0:T(8,128)(2,1)}) custom-call(s32[2]{0:T(128)S(1)} %get-tuple-element.799.scal, bf16[512,1536]{1,0:T(8,128)(2,1)S(1)} %get-tuple-element.819.pair_ref, bf16[512,1536]{1,0:T(8,128)(2,1)} %get-tuple-element.820.core_ref, bf16[1024,512]{1,0:T(8,128)(2,1)} %get-tuple-element.826.grads_ref), custom_call_target="tpu_custom_call" | custom-call | tf_op jit(solution)/shard_map/cond/branch_1_fun/cond/branch_1_fun/project_grad/pallas_call | solution.py:903
  411.7 28.5 %conditional.3 = (bf16[192,1152]{1,0:T(8,128)(2,1)}, bf16[192,1152]{1,0:T(8,128)(2,1)}, bf16[768,512]{1,0:T(8,128)(2,1)}, bf16[256,1536]{1,0:T(8,128)(2,1)}, f32...) conditional(s32[]{:T(128)} %convert_element_type.27, () %tuple.160, ...), branch_computations={%region_43.42_spmd, %region_44.43_spmd} | conditional | flops 16908 | bytes 12736834 | solution.py:101
  418.3 4.2 gain_rows.1
  431.2 3.7 norm_one_back.1
  434.9 5.3 %collective-permute-done.35 = bf16[768,512]{1,0:T(8,128)(2,1)} collective-permute-done((bf16[768,512]{1,0:T(8,128)(2,1)}, bf16[768,512]{1,0:T(8,128)(2,1)}, u32[]{:S(2)}, u32[]{:S(2)}) %collective-permute-start.35) | collective-permute-done | bytes 786464 | tf_op jit(solution)/shard_map/cond/branch_1_fun/cond/branch_1_fun/cond/branch_1_fun/swap_dp_2/ppermute | solution.py:122
  440.3 3.8 fold_sum.12
  446.2 8.7 %all-to-all-start = ((f32[32,1,160]{2,1,0:T(1,128)}), f32[32,1,160]{2,1,0:T(1,128)S(1)}, u32[]{:S(2)}, u32[]{:S(2)}) async-start(f32[32,1,160]{2,1,0:T(1,128)} %all_to_all.8), calls=%async_computation | async-start | bytes 65536 | tf_op jit(solution)/shard_map/all_to_all | solution.py:1336
  454.9 38.4 %conditional.39 = (bf16[192,896]{1,0:T(8,128)(2,1)}, bf16[192,1152]{1,0:T(8,128)(2,1)S(1)}, bf16[192,1152]{1,0:T(8,128)(2,1)S(1)}, bf16[256,1536]{1,0:T(8,128)(2...) conditional(s32[]{:T(128)} %convert_element_type.63, () %tuple.237, (s32[2]{0:T(128)S(1)}, ...), branch_computations={%region_45.46_spmd, %region_46.49_spmd} | conditional | flops 172033 | bytes 16761205 | solution.py:101
  456.4 23.1 %conditional.5 = (bf16[192,896]{1,0:T(8,128)(2,1)S(1)}, bf16[192,896]{1,0:T(8,128)(2,1)}, bf16[192,1152]{1,0:T(8,128)(2,1)}, bf16[192,1152]{1,0:T(8,128)(2,1)}) conditional(s32[]{:T(128)} %convert_element_type.31, () %tuple.173, (s32[2]{0:T(128)S(1)}, bf16[768,512]{1,0:T(8,128)(2,1)}, bf16[768,512]{1,0:T(8,128)(2,1)}, bf16[768,384]{1,0:T(8,128)(2,1)}, ...), branch_computations={%region_47.47_spmd, %region_48.48_spmd} | conditional | bytes 5505124 | solution.py:101
  456.4 3.4 fold_both.1
  462.7 13.5 %collective-permute-done.31.arrived_ref = bf16[384,896]{1,0:T(8,128)(2,1)S(1)} collective-permute-done((bf16[384,896]{1,0:T(8,128)(2,1)}, bf16[384,896]{1,0:T(8,128)(2,1)S(1)}, u32[]{:S(2)}, u32[]{:S(2)}) %collective-permute-start.31) | collective-permute-done | bytes 688160 | tf_op jit(solution)/shard_map/cond/branch_1_fun/cond/branch_1_fun/swap_dp_1/ppermute | solution.py:122
  479.5 7.2 %collective-permute-done.33.theirs_ref = bf16[192,1152]{1,0:T(8,128)(2,1)S(1)} collective-permute-done((bf16[192,1152]{1,0:T(8,128)(2,1)}, bf16[192,1152]{1,0:T(8,128)(2,1)S(1)}, u32[]{:S(2)}, u32[]{:S(2)}) %collective-permute-start.33) | collective-permute-done | bytes 442400 | tf_op jit(solution)/shard_map/cond/branch_1_fun/swap_dp_2/ppermute | solution.py:122
  498.6 8.5 %collective-permute-done.64.theirs_ref = bf16[192,1152]{1,0:T(8,128)(2,1)S(1)} collective-permute-done((bf16[192,1152]{1,0:T(8,128)(2,1)S(1)}, bf16[192,1152]{1,0:T(8,128)(2,1)S(1)}, u32[]{:S(2)}, u32[]{:S(2)}) %collective-permute-start.64) | collective-permute-done | bytes 442400 | tf_op jit(solution)/shard_map/swap_dp_2/ppermute | solution.py:122
  512.3 7.4 %collective-permute-start.67 = (f32[48,128]{1,0:T(8,128)S(1)}, f32[48,128]{1,0:T(8,128)S(1)}, u32[]{:S(2)}, u32[]{:S(2)}) collective-permute-start(f32[48,128]{1,0:T(8,128)S(1)} %get-tuple-element.1307), channel_id=1, source_target_pairs={{0,1},{1,0},{2,3},{3,2},{4,5},{5,4},{6,7},{7,6},{8,9},{9,8},{10,11... | collective-permute-start | bytes 73736 | tf_op jit(solution)/shard_map/swap_tensor_1/ppermute | solution.py:122
  (269 shorter events, 163.8 us)
Async XLA Ops:
  2.5 11.9 %collective-permute-start.39 = (bf16[192,512]{1,0:T(8,128)(2,1)S(1)}, bf16[192,512]{1,0:T(8,128)(2,1)S(1)}, u32[]{:S(2)}, u32[]{:S(2)}) collective-permute-start(bf16[192,512]{1,0:T(8,128)(2,1)S(1)} %pad_maximum_fusion.6), channel_id=1, source_target_pairs={{0,16},{4,20},{8,24},{12,28},{16,0},{20,4},{24,8},{28,12},{1,17},{... | collective-permute-start | bytes 589832 | tf_op jit(solution)/shard_map/swap_dp_4/ppermute | solution.py:122
  2.6 11.8 %collective-permute-start.40 = (bf16[192,512]{1,0:T(8,128)(2,1)S(1)}, bf16[192,512]{1,0:T(8,128)(2,1)S(1)}, u32[]{:S(2)}, u32[]{:S(2)}) collective-permute-start(bf16[192,512]{1,0:T(8,128)(2,1)S(1)} %pad_maximum_fusion.6), channel_id=1, source_target_pairs={{0,8},{4,12},{8,0},{12,4},{16,24},{20,28},{24,16},{28,20},{1,9},{5... | collective-permute-start | bytes 589832 | tf_op jit(solution)/shard_map/swap_dp_2/ppermute | solution.py:122
  2.8 11.6 %collective-permute-start.41 = (bf16[192,512]{1,0:T(8,128)(2,1)S(1)}, bf16[192,512]{1,0:T(8,128)(2,1)S(1)}, u32[]{:S(2)}, u32[]{:S(2)}) collective-permute-start(bf16[192,512]{1,0:T(8,128)(2,1)S(1)} %pad_maximum_fusion.6), channel_id=1, source_target_pairs={{0,4},{4,0},{8,12},{12,8},{16,20},{20,16},{24,28},{28,24},{1,5},{5... | collective-permute-start | bytes 589832 | tf_op jit(solution)/shard_map/swap_dp_1/ppermute | solution.py:122
  5.5 21.8 %collective-permute-start.44 = (bf16[256,1536]{1,0:T(8,128)(2,1)S(1)}, bf16[256,1536]{1,0:T(8,128)(2,1)}, u32[]{:S(2)}, u32[]{:S(2)}) collective-permute-start(bf16[256,1536]{1,0:T(8,128)(2,1)S(1)} %fusion.2), channel_id=1, source_target_pairs={{0,2},{1,3},{2,0},{3,1},{4,6},{5,7},{6,4},{7,5},{8,10},{9,11},{10,... | collective-permute-start | bytes 2359304 | tf_op jit(solution)/shard_map/swap_tensor_2/ppermute | solution.py:122
  9.2 22.1 %collective-permute-start.45 = (bf16[192,1152]{1,0:T(8,128)(2,1)}, bf16[192,1152]{1,0:T(8,128)(2,1)}, u32[]{:S(2)}, u32[]{:S(2)}) collective-permute-start(bf16[192,1152]{1,0:T(8,128)(2,1)} %get-tuple-element.1114), channel_id=1, source_target_pairs={{0,8},{4,12},{8,0},{12,4},{16,24},{20,28},{24,16},{28,20},{1,9},{5... | collective-permute-start | bytes 1327112 | tf_op jit(solution)/shard_map/swap_dp_2/ppermute | solution.py:122
  14.5 16.9 %collective-permute-start.43 = (bf16[192,512]{1,0:T(8,128)(2,1)S(1)}, bf16[192,512]{1,0:T(8,128)(2,1)}, u32[]{:S(2)}, u32[]{:S(2)}) collective-permute-start(bf16[192,512]{1,0:T(8,128)(2,1)S(1)} %collective-permute-done.39), channel_id=1, source_target_pairs={{0,8},{4,12},{8,0},{12,4},{16,24},{20,28},{24,16},{28,20},{1,9},{5... | collective-permute-start | bytes 589832 | tf_op jit(solution)/shard_map/swap_dp_2/ppermute | solution.py:122
  16.0 15.4 %collective-permute-start.42 = (bf16[384,512]{1,0:T(8,128)(2,1)}, bf16[384,512]{1,0:T(8,128)(2,1)S(1)}, u32[]{:S(2)}, u32[]{:S(2)}) collective-permute-start(bf16[384,512]{1,0:T(8,128)(2,1)} %pad_maximum_fusion.4), channel_id=1, source_target_pairs={{0,4},{4,0},{8,12},{12,8},{16,20},{20,16},{24,28},{28,24},{1,5},{5... | collective-permute-start | bytes 1179656 | tf_op jit(solution)/shard_map/swap_dp_1/ppermute | solution.py:122
  16.2 10.4 %collective-permute-start.46 = (bf16[192,384]{1,0:T(8,128)(2,1)S(1)}, bf16[192,384]{1,0:T(8,128)(2,1)S(1)}, u32[]{:S(2)}, u32[]{:S(2)}) collective-permute-start(bf16[192,384]{1,0:T(8,128)(2,1)S(1)} %bitcast.25), channel_id=1, source_target_pairs={{0,16},{4,20},{8,24},{12,28},{16,0},{20,4},{24,8},{28,12},{1,17},{... | collective-permute-start | bytes 442376 | tf_op jit(solution)/shard_map/swap_dp_4/ppermute | solution.py:122
  31.4 10.4 %collective-permute-start.1 = (bf16[512,1536]{1,0:T(8,128)(2,1)S(1)}, bf16[512,1536]{1,0:T(8,128)(2,1)}, u32[]{:S(2)}, u32[]{:S(2)}) collective-permute-start(bf16[512,1536]{1,0:T(8,128)(2,1)S(1)} %get-tuple-element.529), channel_id=1, source_target_pairs={{0,1},{1,0},{2,3},{3,2},{4,5},{5,4},{6,7},{7,6},{8,9},{9,8},{10,11... | collective-permute-start | bytes 4718600 | tf_op jit(solution)/shard_map/cond/branch_1_fun/swap_tensor_1/ppermute | solution.py:122
  31.9 9.9 %collective-permute-start.2 = (bf16[384,384]{1,0:T(8,128)(2,1)}, bf16[384,384]{1,0:T(8,128)(2,1)}, u32[]{:S(2)}, u32[]{:S(2)}) collective-permute-start(bf16[384,384]{1,0:T(8,128)(2,1)} %get-tuple-element.530), channel_id=1, source_target_pairs={{0,8},{4,12},{8,0},{12,4},{16,24},{20,28},{24,16},{28,20},{1,9},{5... | collective-permute-start | bytes 884744 | tf_op jit(solution)/shard_map/cond/branch_1_fun/swap_dp_2/ppermute | solution.py:122
  34.2 6.5 %collective-permute-start = (bf16[192,512]{1,0:T(8,128)(2,1)}, bf16[192,512]{1,0:T(8,128)(2,1)}, u32[]{:S(2)}, u32[]{:S(2)}) collective-permute-start(bf16[192,512]{1,0:T(8,128)(2,1)} %get-tuple-element.528), channel_id=1, source_target_pairs={{0,4},{4,0},{8,12},{12,8},{16,20},{20,16},{24,28},{28,24},{1,5},{5... | collective-permute-start | bytes 589832 | tf_op jit(solution)/shard_map/cond/branch_1_fun/swap_dp_1/ppermute | solution.py:122
  42.9 36.4 %collective-permute-start.49 = (bf16[384,1152]{1,0:T(8,128)(2,1)}, bf16[384,1152]{1,0:T(8,128)(2,1)}, u32[]{:S(2)}, u32[]{:S(2)}) collective-permute-start(bf16[384,1152]{1,0:T(8,128)(2,1)} %get-tuple-element.1145), channel_id=1, source_target_pairs={{0,8},{4,12},{8,0},{12,4},{16,24},{20,28},{24,16},{28,20},{1,9},{5... | collective-permute-start | bytes 2654216 | tf_op jit(solution)/shard_map/swap_dp_2/ppermute | solution.py:122
  44.3 26.9 %collective-permute-start.47 = (bf16[256,1536]{1,0:T(8,128)(2,1)}, bf16[256,1536]{1,0:T(8,128)(2,1)}, u32[]{:S(2)}, u32[]{:S(2)}) collective-permute-start(bf16[256,1536]{1,0:T(8,128)(2,1)} %param.71), channel_id=1, source_target_pairs={{0,2},{1,3},{2,0},{3,1},{4,6},{5,7},{6,4},{7,5},{8,10},{9,11},{10,... | collective-permute-start | bytes 2359304 | tf_op jit(solution)/shard_map/swap_tensor_2/ppermute | solution.py:122
  45.5 19.8 %collective-permute-start.48 = (bf16[768,384]{1,0:T(8,128)(2,1)S(1)}, bf16[768,384]{1,0:T(8,128)(2,1)S(1)}, u32[]{:S(2)}, u32[]{:S(2)}) collective-permute-start(bf16[768,384]{1,0:T(8,128)(2,1)S(1)} %pad_maximum_fusion.2.refs_0_.refs_2_.refs_4_.refs_6_), channel_id=1, source_target_pairs={{0,4},{4,0},{8,12},{12,8},{16,20},{20,16},{24,28},{28,24},{1,5},{5... | collective-permute-start | bytes 1769480 | tf_op jit(solution)/shard_map/swap_dp_1/ppermute | solution.py:122
  46.5 65.0 %collective-permute-start.51 = (bf16[384,1152]{1,0:T(8,128)(2,1)}, bf16[384,1152]{1,0:T(8,128)(2,1)}, u32[]{:S(2)}, u32[]{:S(2)}) collective-permute-start(bf16[384,1152]{1,0:T(8,128)(2,1)} %get-tuple-element.1149), channel_id=1, source_target_pairs={{0,16},{4,20},{8,24},{12,28},{16,0},{20,4},{24,8},{28,12},{1,17},{... | collective-permute-start | bytes 2654216 | tf_op jit(solution)/shard_map/swap_dp_4/ppermute | solution.py:122
  56.8 8.4 %collective-permute-start.4 = (bf16[256,1536]{1,0:T(8,128)(2,1)}, bf16[256,1536]{1,0:T(8,128)(2,1)}, u32[]{:S(2)}, u32[]{:S(2)}) collective-permute-start(bf16[256,1536]{1,0:T(8,128)(2,1)} %get-tuple-element.552), channel_id=1, source_target_pairs={{0,1},{1,0},{2,3},{3,2},{4,5},{5,4},{6,7},{7,6},{8,9},{9,8},{10,11... | collective-permute-start | bytes 2359304 | tf_op jit(solution)/shard_map/cond/branch_1_fun/swap_tensor_1/ppermute | solution.py:122
  79.3 4.9 collective-permute-start.5
  84.2 59.2 %collective-permute-start.52 = (bf16[768,1152]{1,0:T(8,128)(2,1)}, bf16[768,1152]{1,0:T(8,128)(2,1)S(1)}, u32[]{:S(2)}, u32[]{:S(2)}) collective-permute-start(bf16[768,1152]{1,0:T(8,128)(2,1)} %get-tuple-element.1155), channel_id=1, source_target_pairs={{0,4},{4,0},{8,12},{12,8},{16,20},{20,16},{24,28},{28,24},{1,5},{5... | collective-permute-start | bytes 5308424 | tf_op jit(solution)/shard_map/swap_dp_1/ppermute | solution.py:122
  84.7 37.0 %collective-permute-start.50 = (bf16[256,1536]{1,0:T(8,128)(2,1)}, bf16[256,1536]{1,0:T(8,128)(2,1)}, u32[]{:S(2)}, u32[]{:S(2)}) collective-permute-start(bf16[256,1536]{1,0:T(8,128)(2,1)} %param.71), channel_id=1, source_target_pairs={{0,8},{4,12},{8,0},{12,4},{16,24},{20,28},{24,16},{28,20},{1,9},{5... | collective-permute-start | bytes 2359304 | tf_op jit(solution)/shard_map/swap_dp_2/ppermute | solution.py:122
  84.7 57.2 %collective-permute-start.54 = (bf16[384,1152]{1,0:T(8,128)(2,1)}, bf16[384,1152]{1,0:T(8,128)(2,1)}, u32[]{:S(2)}, u32[]{:S(2)}) collective-permute-start(bf16[384,1152]{1,0:T(8,128)(2,1)} %get-tuple-element.1159), channel_id=1, source_target_pairs={{0,16},{4,20},{8,24},{12,28},{16,0},{20,4},{24,8},{28,12},{1,17},{... | collective-permute-start | bytes 2654216 | tf_op jit(solution)/shard_map/swap_dp_4/ppermute | solution.py:122
  89.6 18.1 %collective-permute-start.6 = (bf16[256,1536]{1,0:T(8,128)(2,1)}, bf16[256,1536]{1,0:T(8,128)(2,1)}, u32[]{:S(2)}, u32[]{:S(2)}) collective-permute-start(bf16[256,1536]{1,0:T(8,128)(2,1)} %part_sum.4), channel_id=1, source_target_pairs={{0,2},{1,3},{2,0},{3,1},{4,6},{5,7},{6,4},{7,5},{8,10},{9,11},{10,... | collective-permute-start | bytes 2359304 | tf_op jit(solution)/shard_map/cond/branch_1_fun/swap_tensor_2/ppermute | solution.py:122
  121.7 21.7 %collective-permute-start.53 = (bf16[384,1152]{1,0:T(8,128)(2,1)}, bf16[384,1152]{1,0:T(8,128)(2,1)}, u32[]{:S(2)}, u32[]{:S(2)}) collective-permute-start(bf16[384,1152]{1,0:T(8,128)(2,1)} %collective-permute-done.51), channel_id=1, source_target_pairs={{0,4},{4,0},{8,12},{12,8},{16,20},{20,16},{24,28},{28,24},{1,5},{5... | collective-permute-start | bytes 2654216 | tf_op jit(solution)/shard_map/swap_dp_1/ppermute | solution.py:122
  123.1 18.6 %collective-permute-start.7 = (bf16[256,1536]{1,0:T(8,128)(2,1)}, bf16[256,1536]{1,0:T(8,128)(2,1)}, u32[]{:S(2)}, u32[]{:S(2)}) collective-permute-start(bf16[256,1536]{1,0:T(8,128)(2,1)} %get-tuple-element.567), channel_id=1, source_target_pairs={{0,2},{1,3},{2,0},{3,1},{4,6},{5,7},{6,4},{7,5},{8,10},{9,11},{10,... | collective-permute-start | bytes 2359304 | tf_op jit(solution)/shard_map/cond/branch_1_fun/swap_tensor_2/ppermute | solution.py:122
  123.1 18.8 %collective-permute-start.8 = (bf16[256,1536]{1,0:T(8,128)(2,1)}, bf16[256,1536]{1,0:T(8,128)(2,1)}, u32[]{:S(2)}, u32[]{:S(2)}) collective-permute-start(bf16[256,1536]{1,0:T(8,128)(2,1)} %get-tuple-element.567), channel_id=1, source_target_pairs={{0,8},{4,12},{8,0},{12,4},{16,24},{20,28},{24,16},{28,20},{1,9},{5... | collective-permute-start | bytes 2359304 | tf_op jit(solution)/shard_map/cond/branch_1_fun/swap_dp_2/ppermute | solution.py:122
  143.4 20.4 %collective-permute-start.55 = (bf16[384,1152]{1,0:T(8,128)(2,1)}, bf16[384,1152]{1,0:T(8,128)(2,1)}, u32[]{:S(2)}, u32[]{:S(2)}) collective-permute-start(bf16[384,1152]{1,0:T(8,128)(2,1)} %collective-permute-done.54), channel_id=1, source_target_pairs={{0,4},{4,0},{8,12},{12,8},{16,20},{20,16},{24,28},{28,24},{1,5},{5... | collective-permute-start | bytes 2654216 | tf_op jit(solution)/shard_map/swap_dp_1/ppermute | solution.py:122
  146.4 10.5 %collective-permute-start.12 = (bf16[128,1536]{1,0:T(8,128)(2,1)}, bf16[128,1536]{1,0:T(8,128)(2,1)}, u32[]{:S(2)}, u32[]{:S(2)}) collective-permute-start(bf16[128,1536]{1,0:T(8,128)(2,1)} %get-tuple-element.583), channel_id=1, source_target_pairs={{0,2},{1,3},{2,0},{3,1},{4,6},{5,7},{6,4},{7,5},{8,10},{9,11},{10,... | collective-permute-start | bytes 1179656 | tf_op jit(solution)/shard_map/cond/branch_1_fun/swap_tensor_2/ppermute | solution.py:122
  148.3 9.8 %collective-permute-start.13 = (bf16[128,1536]{1,0:T(8,128)(2,1)}, bf16[128,1536]{1,0:T(8,128)(2,1)}, u32[]{:S(2)}, u32[]{:S(2)}) collective-permute-start(bf16[128,1536]{1,0:T(8,128)(2,1)} %get-tuple-element.584), channel_id=1, source_target_pairs={{0,8},{4,12},{8,0},{12,4},{16,24},{20,28},{24,16},{28,20},{1,9},{5... | collective-permute-start | bytes 1179656 | tf_op jit(solution)/shard_map/cond/branch_1_fun/swap_dp_2/ppermute | solution.py:122
  163.8 43.0 %collective-permute-start.56 = (bf16[384,1152]{1,0:T(8,128)(2,1)}, bf16[384,1152]{1,0:T(8,128)(2,1)}, u32[]{:S(2)}, u32[]{:S(2)}) collective-permute-start(bf16[384,1152]{1,0:T(8,128)(2,1)} %get-tuple-element.1173), channel_id=1, source_target_pairs={{0,16},{4,20},{8,24},{12,28},{16,0},{20,4},{24,8},{28,12},{1,17},{... | collective-permute-start | bytes 2654216 | tf_op jit(solution)/shard_map/swap_dp_4/ppermute | solution.py:122
  163.8 4.1 collective-permute-start.14
  168.5 21.2 %collective-permute-start.16 = (bf16[384,1152]{1,0:T(8,128)(2,1)}, bf16[384,1152]{1,0:T(8,128)(2,1)}, u32[]{:S(2)}, u32[]{:S(2)}) collective-permute-start(bf16[384,1152]{1,0:T(8,128)(2,1)} %get-tuple-element.608), channel_id=1, source_target_pairs={{0,4},{4,0},{8,12},{12,8},{16,20},{20,16},{24,28},{28,24},{1,5},{5... | collective-permute-start | bytes 2654216 | tf_op jit(solution)/shard_map/cond/branch_1_fun/swap_dp_1/ppermute | solution.py:122
  169.6 18.8 %collective-permute-start.17 = (bf16[256,1536]{1,0:T(8,128)(2,1)}, bf16[256,1536]{1,0:T(8,128)(2,1)}, u32[]{:S(2)}, u32[]{:S(2)}) collective-permute-start(bf16[256,1536]{1,0:T(8,128)(2,1)} %get-tuple-element.609), channel_id=1, source_target_pairs={{0,2},{1,3},{2,0},{3,1},{4,6},{5,7},{6,4},{7,5},{8,10},{9,11},{10,... | collective-permute-start | bytes 2359304 | tf_op jit(solution)/shard_map/cond/branch_1_fun/swap_tensor_2/ppermute | solution.py:122
  170.6 17.7 %collective-permute-start.18 = (bf16[256,1536]{1,0:T(8,128)(2,1)}, bf16[256,1536]{1,0:T(8,128)(2,1)}, u32[]{:S(2)}, u32[]{:S(2)}) collective-permute-start(bf16[256,1536]{1,0:T(8,128)(2,1)} %get-tuple-element.610), channel_id=1, source_target_pairs={{0,1},{1,0},{2,3},{3,2},{4,5},{5,4},{6,7},{7,6},{8,9},{9,8},{10,11... | collective-permute-start | bytes 2359304 | tf_op jit(solution)/shard_map/cond/branch_1_fun/swap_tensor_1/ppermute | solution.py:122
  189.7 17.1 %collective-permute-start.19 = (bf16[256,1536]{1,0:T(8,128)(2,1)}, bf16[256,1536]{1,0:T(8,128)(2,1)}, u32[]{:S(2)}, u32[]{:S(2)}) collective-permute-start(bf16[256,1536]{1,0:T(8,128)(2,1)} %get-tuple-element.631), channel_id=1, source_target_pairs={{0,1},{1,0},{2,3},{3,2},{4,5},{5,4},{6,7},{7,6},{8,9},{9,8},{10,11... | collective-permute-start | bytes 2359304 | tf_op jit(solution)/shard_map/cond/branch_1_fun/swap_tensor_1/ppermute | solution.py:122
  190.9 15.9 %collective-permute-start.20 = (bf16[256,1536]{1,0:T(8,128)(2,1)}, bf16[256,1536]{1,0:T(8,128)(2,1)}, u32[]{:S(2)}, u32[]{:S(2)}) collective-permute-start(bf16[256,1536]{1,0:T(8,128)(2,1)} %get-tuple-element.632), channel_id=1, source_target_pairs={{0,1},{1,0},{2,3},{3,2},{4,5},{5,4},{6,7},{7,6},{8,9},{9,8},{10,11... | collective-permute-start | bytes 2359304 | tf_op jit(solution)/shard_map/cond/branch_1_fun/swap_tensor_1/ppermute | solution.py:122
  206.8 21.1 %collective-permute-start.57 = (bf16[384,1152]{1,0:T(8,128)(2,1)}, bf16[384,1152]{1,0:T(8,128)(2,1)}, u32[]{:S(2)}, u32[]{:S(2)}) collective-permute-start(bf16[384,1152]{1,0:T(8,128)(2,1)} %collective-permute-done.56), channel_id=1, source_target_pairs={{0,4},{4,0},{8,12},{12,8},{16,20},{20,16},{24,28},{28,24},{1,5},{5... | collective-permute-start | bytes 2654216 | tf_op jit(solution)/shard_map/swap_dp_1/ppermute | solution.py:122
  227.9 80.2 %collective-permute-start.58 = (bf16[768,1152]{1,0:T(8,128)(2,1)}, bf16[768,1152]{1,0:T(8,128)(2,1)}, u32[]{:S(2)}, u32[]{:S(2)}) collective-permute-start(bf16[768,1152]{1,0:T(8,128)(2,1)} %get-tuple-element.1215), channel_id=1, source_target_pairs={{0,4},{4,0},{8,12},{12,8},{16,20},{20,16},{24,28},{28,24},{1,5},{5... | collective-permute-start | bytes 5308424 | tf_op jit(solution)/shard_map/swap_dp_1/ppermute | solution.py:122
  253.4 26.3 %collective-permute-start.21 = (bf16[1024,1536]{1,0:T(8,128)(2,1)}, bf16[1024,1536]{1,0:T(8,128)(2,1)}, u32[]{:S(2)}, u32[]{:S(2)}) collective-permute-start(bf16[1024,1536]{1,0:T(8,128)(2,1)} %get-tuple-element.675), channel_id=1, source_target_pairs={{0,1},{1,0},{2,3},{3,2},{4,5},{5,4},{6,7},{7,6},{8,9},{9,8},{10,11... | collective-permute-start | bytes 9437192 | tf_op jit(solution)/shard_map/cond/branch_1_fun/swap_tensor_1/ppermute | solution.py:122
  282.1 21.6 %collective-permute-start.23 = (bf16[128,1536]{1,0:T(8,128)(2,1)}, bf16[128,1536]{1,0:T(8,128)(2,1)}, u32[]{:S(2)}, u32[]{:S(2)}) collective-permute-start(bf16[128,1536]{1,0:T(8,128)(2,1)} %get-tuple-element.694), channel_id=1, source_target_pairs={{0,2},{1,3},{2,0},{3,1},{4,6},{5,7},{6,4},{7,5},{8,10},{9,11},{10,... | collective-permute-start | bytes 1179656 | tf_op jit(solution)/shard_map/cond/branch_1_fun/swap_tensor_2/ppermute | solution.py:122
  283.1 20.6 %collective-permute-start.24 = (bf16[128,1536]{1,0:T(8,128)(2,1)}, bf16[128,1536]{1,0:T(8,128)(2,1)}, u32[]{:S(2)}, u32[]{:S(2)}) collective-permute-start(bf16[128,1536]{1,0:T(8,128)(2,1)} %get-tuple-element.695), channel_id=1, source_target_pairs={{0,8},{4,12},{8,0},{12,4},{16,24},{20,28},{24,16},{28,20},{1,9},{5... | collective-permute-start | bytes 1179656 | tf_op jit(solution)/shard_map/cond/branch_1_fun/swap_dp_2/ppermute | solution.py:122
  293.9 9.7 %collective-permute-start.22 = (bf16[1024,1536]{1,0:T(8,128)(2,1)}, bf16[1024,1536]{1,0:T(8,128)(2,1)}, u32[]{:S(2)}, u32[]{:S(2)}) collective-permute-start(bf16[1024,1536]{1,0:T(8,128)(2,1)} %block_rows.3), channel_id=1, source_target_pairs={{0,1},{1,0},{2,3},{3,2},{4,5},{5,4},{6,7},{7,6},{8,9},{9,8},{10,11... | collective-permute-start | bytes 9437192 | tf_op jit(solution)/shard_map/cond/branch_1_fun/cond/branch_1_fun/swap_tensor_1/ppermute | solution.py:122
  308.1 21.5 %collective-permute-start.25 = (bf16[256,1536]{1,0:T(8,128)(2,1)}, bf16[256,1536]{1,0:T(8,128)(2,1)}, u32[]{:S(2)}, u32[]{:S(2)}) collective-permute-start(bf16[256,1536]{1,0:T(8,128)(2,1)} %get-tuple-element.719), channel_id=1, source_target_pairs={{0,2},{1,3},{2,0},{3,1},{4,6},{5,7},{6,4},{7,5},{8,10},{9,11},{10,... | collective-permute-start | bytes 2359304 | tf_op jit(solution)/shard_map/cond/branch_1_fun/swap_tensor_2/ppermute | solution.py:122
  309.1 20.6 %collective-permute-start.26 = (bf16[256,1536]{1,0:T(8,128)(2,1)}, bf16[256,1536]{1,0:T(8,128)(2,1)}, u32[]{:S(2)}, u32[]{:S(2)}) collective-permute-start(bf16[256,1536]{1,0:T(8,128)(2,1)} %get-tuple-element.720), channel_id=1, source_target_pairs={{0,8},{4,12},{8,0},{12,4},{16,24},{20,28},{24,16},{28,20},{1,9},{5... | collective-permute-start | bytes 2359304 | tf_op jit(solution)/shard_map/cond/branch_1_fun/swap_dp_2/ppermute | solution.py:122
  334.3 45.6 %collective-permute-start.59 = (bf16[768,1152]{1,0:T(8,128)(2,1)}, bf16[768,1152]{1,0:T(8,128)(2,1)}, u32[]{:S(2)}, u32[]{:S(2)}) collective-permute-start(bf16[768,1152]{1,0:T(8,128)(2,1)} %get-tuple-element.1236), channel_id=1, source_target_pairs={{0,4},{4,0},{8,12},{12,8},{16,20},{20,16},{24,28},{28,24},{1,5},{5... | collective-permute-start | bytes 5308424 | tf_op jit(solution)/shard_map/swap_dp_1/ppermute | solution.py:122
  334.8 54.3 %collective-permute-start.61 = (bf16[512,1536]{1,0:T(8,128)(2,1)}, bf16[512,1536]{1,0:T(8,128)(2,1)}, u32[]{:S(2)}, u32[]{:S(2)}) collective-permute-start(bf16[512,1536]{1,0:T(8,128)(2,1)} %get-tuple-element.1244), channel_id=1, source_target_pairs={{0,8},{4,12},{8,0},{12,4},{16,24},{20,28},{24,16},{28,20},{1,9},{5... | collective-permute-start | bytes 4718600 | tf_op jit(solution)/shard_map/swap_dp_2/ppermute | solution.py:122
  336.3 52.3 %collective-permute-start.60 = (bf16[384,1152]{1,0:T(8,128)(2,1)}, bf16[384,1152]{1,0:T(8,128)(2,1)}, u32[]{:S(2)}, u32[]{:S(2)}) collective-permute-start(bf16[384,1152]{1,0:T(8,128)(2,1)} %get-tuple-element.1243), channel_id=1, source_target_pairs={{0,16},{4,20},{8,24},{12,28},{16,0},{20,4},{24,8},{28,12},{1,17},{... | collective-permute-start | bytes 2654216 | tf_op jit(solution)/shard_map/swap_dp_4/ppermute | solution.py:122
  336.3 18.2 %collective-permute-start.27 = (bf16[256,1536]{1,0:T(8,128)(2,1)}, bf16[256,1536]{1,0:T(8,128)(2,1)}, u32[]{:S(2)}, u32[]{:S(2)}) collective-permute-start(bf16[256,1536]{1,0:T(8,128)(2,1)} %get-tuple-element.736), channel_id=1, source_target_pairs={{0,2},{1,3},{2,0},{3,1},{4,6},{5,7},{6,4},{7,5},{8,10},{9,11},{10,... | collective-permute-start | bytes 2359304 | tf_op jit(solution)/shard_map/cond/branch_1_fun/cond/branch_1_fun/swap_tensor_2/ppermute | solution.py:122
  337.8 16.7 %collective-permute-start.28 = (bf16[256,1536]{1,0:T(8,128)(2,1)}, bf16[256,1536]{1,0:T(8,128)(2,1)}, u32[]{:S(2)}, u32[]{:S(2)}) collective-permute-start(bf16[256,1536]{1,0:T(8,128)(2,1)} %get-tuple-element.736), channel_id=1, source_target_pairs={{0,1},{1,0},{2,3},{3,2},{4,5},{5,4},{6,7},{7,6},{8,9},{9,8},{10,11... | collective-permute-start | bytes 2359304 | tf_op jit(solution)/shard_map/cond/branch_1_fun/cond/branch_1_fun/swap_tensor_1/ppermute | solution.py:122
  354.5 4.4 collective-permute-start.29
  380.0 4.5 collective-permute-start.30
  389.2 51.1 %collective-permute-start.62 = (bf16[768,384]{1,0:T(8,128)(2,1)}, bf16[768,384]{1,0:T(8,128)(2,1)}, u32[]{:S(2)}, u32[]{:S(2)}) collective-permute-start(bf16[768,384]{1,0:T(8,128)(2,1)} %get-tuple-element.1259), channel_id=1, source_target_pairs={{0,8},{4,12},{8,0},{12,4},{16,24},{20,28},{24,16},{28,20},{1,9},{5... | collective-permute-start | bytes 1769480 | tf_op jit(solution)/shard_map/swap_dp_2/ppermute | solution.py:122
  390.6 49.6 %collective-permute-start.37 = (bf16[768,1152]{1,0:T(8,128)(2,1)}, bf16[768,1152]{1,0:T(8,128)(2,1)}, u32[]{:S(2)}, u32[]{:S(2)}) collective-permute-start(bf16[768,1152]{1,0:T(8,128)(2,1)} %get-tuple-element.868), channel_id=1, source_target_pairs={{0,4},{4,0},{8,12},{12,8},{16,20},{20,16},{24,28},{28,24},{1,5},{5... | collective-permute-start | bytes 5308424 | tf_op jit(solution)/shard_map/cond/branch_1_fun/swap_dp_1/ppermute | solution.py:122
  391.9 48.3 %collective-permute-start.38 = (bf16[384,1152]{1,0:T(8,128)(2,1)}, bf16[384,1152]{1,0:T(8,128)(2,1)}, u32[]{:S(2)}, u32[]{:S(2)}) collective-permute-start(bf16[384,1152]{1,0:T(8,128)(2,1)} %get-tuple-element.869), channel_id=1, source_target_pairs={{0,16},{4,20},{8,24},{12,28},{16,0},{20,4},{24,8},{28,12},{1,17},{... | collective-permute-start | bytes 2654216 | tf_op jit(solution)/shard_map/cond/branch_1_fun/swap_dp_4/ppermute | solution.py:122
  401.1 8.2 %collective-permute-start.36 = (bf16[512,1536]{1,0:T(8,128)(2,1)}, bf16[512,1536]{1,0:T(8,128)(2,1)}, u32[]{:S(2)}, u32[]{:S(2)}) collective-permute-start(bf16[512,1536]{1,0:T(8,128)(2,1)} %get-tuple-element.818), channel_id=1, source_target_pairs={{0,1},{1,0},{2,3},{3,2},{4,5},{5,4},{6,7},{7,6},{8,9},{9,8},{10,11... | collective-permute-start | bytes 4718600 | tf_op jit(solution)/shard_map/cond/branch_1_fun/cond/branch_1_fun/swap_tensor_1/ppermute | solution.py:122
  411.7 19.5 %collective-permute-start.34 = (bf16[256,1536]{1,0:T(8,128)(2,1)}, bf16[256,1536]{1,0:T(8,128)(2,1)}, u32[]{:S(2)}, u32[]{:S(2)}) collective-permute-start(bf16[256,1536]{1,0:T(8,128)(2,1)} %get-tuple-element.794), channel_id=1, source_target_pairs={{0,2},{1,3},{2,0},{3,1},{4,6},{5,7},{6,4},{7,5},{8,10},{9,11},{10,... | collective-permute-start | bytes 2359304 | tf_op jit(solution)/shard_map/cond/branch_1_fun/cond/branch_1_fun/cond/branch_1_fun/swap_tensor_2/ppermute | solution.py:122
  412.6 27.7 %collective-permute-start.35 = (bf16[768,512]{1,0:T(8,128)(2,1)}, bf16[768,512]{1,0:T(8,128)(2,1)}, u32[]{:S(2)}, u32[]{:S(2)}) collective-permute-start(bf16[768,512]{1,0:T(8,128)(2,1)} %get-tuple-element.797), channel_id=1, source_target_pairs={{0,8},{4,12},{8,0},{12,4},{16,24},{20,28},{24,16},{28,20},{1,9},{5... | collective-permute-start | bytes 2359304 | tf_op jit(solution)/shard_map/cond/branch_1_fun/cond/branch_1_fun/cond/branch_1_fun/swap_dp_2/ppermute | solution.py:122
  444.1 49.2 %collective-permute-start.63 = (bf16[384,1152]{1,0:T(8,128)(2,1)}, bf16[384,1152]{1,0:T(8,128)(2,1)}, u32[]{:S(2)}, u32[]{:S(2)}) collective-permute-start(bf16[384,1152]{1,0:T(8,128)(2,1)} %get-tuple-element.1279), channel_id=1, source_target_pairs={{0,16},{4,20},{8,24},{12,28},{16,0},{20,4},{24,8},{28,12},{1,17},{... | collective-permute-start | bytes 2654216 | tf_op jit(solution)/shard_map/swap_dp_4/ppermute | solution.py:122
  446.2 47.0 %all-to-all-start = ((f32[32,1,160]{2,1,0:T(1,128)}), f32[32,1,160]{2,1,0:T(1,128)S(1)}, u32[]{:S(2)}, u32[]{:S(2)}) async-start(f32[32,1,160]{2,1,0:T(1,128)} %all_to_all.8), calls=%async_computation | async-start | bytes 65536 | tf_op jit(solution)/shard_map/all_to_all | solution.py:1336
  454.9 31.8 %collective-permute-start.32 = (bf16[256,1536]{1,0:T(8,128)(2,1)}, bf16[256,1536]{1,0:T(8,128)(2,1)}, u32[]{:S(2)}, u32[]{:S(2)}) collective-permute-start(bf16[256,1536]{1,0:T(8,128)(2,1)} %get-tuple-element.904), channel_id=1, source_target_pairs={{0,2},{1,3},{2,0},{3,1},{4,6},{5,7},{6,4},{7,5},{8,10},{9,11},{10,... | collective-permute-start | bytes 2359304 | tf_op jit(solution)/shard_map/cond/branch_1_fun/swap_tensor_2/ppermute | solution.py:122
  456.2 30.5 %collective-permute-start.33 = (bf16[192,1152]{1,0:T(8,128)(2,1)}, bf16[192,1152]{1,0:T(8,128)(2,1)S(1)}, u32[]{:S(2)}, u32[]{:S(2)}) collective-permute-start(bf16[192,1152]{1,0:T(8,128)(2,1)} %get-tuple-element.905), channel_id=1, source_target_pairs={{0,8},{4,12},{8,0},{12,4},{16,24},{20,28},{24,16},{28,20},{1,9},{5... | collective-permute-start | bytes 1327112 | tf_op jit(solution)/shard_map/cond/branch_1_fun/swap_dp_2/ppermute | solution.py:122
  459.8 16.4 %collective-permute-start.31 = (bf16[384,896]{1,0:T(8,128)(2,1)}, bf16[384,896]{1,0:T(8,128)(2,1)S(1)}, u32[]{:S(2)}, u32[]{:S(2)}) collective-permute-start(bf16[384,896]{1,0:T(8,128)(2,1)} %get-tuple-element.889), channel_id=1, source_target_pairs={{0,4},{4,0},{8,12},{12,8},{16,20},{20,16},{24,28},{28,24},{1,5},{5... | collective-permute-start | bytes 2064392 | tf_op jit(solution)/shard_map/cond/branch_1_fun/cond/branch_1_fun/swap_dp_1/ppermute | solution.py:122
  493.3 13.8 %collective-permute-start.64 = (bf16[192,1152]{1,0:T(8,128)(2,1)S(1)}, bf16[192,1152]{1,0:T(8,128)(2,1)S(1)}, u32[]{:S(2)}, u32[]{:S(2)}) collective-permute-start(bf16[192,1152]{1,0:T(8,128)(2,1)S(1)} %get-tuple-element.1289), channel_id=1, source_target_pairs={{0,8},{4,12},{8,0},{12,4},{16,24},{20,28},{24,16},{28,20},{1,9},{5... | collective-permute-start | bytes 1327112 | tf_op jit(solution)/shard_map/swap_dp_2/ppermute | solution.py:122
  493.4 17.1 %collective-permute-start.65 = (bf16[192,896]{1,0:T(8,128)(2,1)}, bf16[192,896]{1,0:T(8,128)(2,1)S(1)}, u32[]{:S(2)}, u32[]{:S(2)}) collective-permute-start(bf16[192,896]{1,0:T(8,128)(2,1)} %get-tuple-element.1291), channel_id=1, source_target_pairs={{0,16},{4,20},{8,24},{12,28},{16,0},{20,4},{24,8},{28,12},{1,17},{... | collective-permute-start | bytes 1032200 | tf_op jit(solution)/shard_map/swap_dp_4/ppermute | solution.py:122
  496.2 26.1 %collective-permute-start.66 = (bf16[192,1152]{1,0:T(8,128)(2,1)}, bf16[192,1152]{1,0:T(8,128)(2,1)S(1)}, u32[]{:S(2)}, u32[]{:S(2)}) collective-permute-start(bf16[192,1152]{1,0:T(8,128)(2,1)} %get-tuple-element.1288), channel_id=1, source_target_pairs={{0,8},{4,12},{8,0},{12,4},{16,24},{20,28},{24,16},{28,20},{1,9},{5... | collective-permute-start | bytes 1327112 | tf_op jit(solution)/shard_map/swap_dp_2/ppermute | solution.py:122
  512.3 10.0 %collective-permute-start.67 = (f32[48,128]{1,0:T(8,128)S(1)}, f32[48,128]{1,0:T(8,128)S(1)}, u32[]{:S(2)}, u32[]{:S(2)}) collective-permute-start(f32[48,128]{1,0:T(8,128)S(1)} %get-tuple-element.1307), channel_id=1, source_target_pairs={{0,1},{1,0},{2,3},{3,2},{4,5},{5,4},{6,7},{7,6},{8,9},{9,8},{10,11... | collective-permute-start | bytes 73736 | tf_op jit(solution)/shard_map/swap_tensor_1/ppermute | solution.py:122
  (41 other events, 337.4 us)

commit v6 on v5

--- a/solution.py
+++ b/solution.py
@@ -729,10 +729,15 @@
         def kernel(scal, context_ref, *refs):
             kept_ref, sent_ref, held, part, sems, out_sems = refs[dp_size:]
             wait_all(start_all(attn_jobs(scal[0], refs[:dp_size], pieces, held), sems))
-            for at in range(4):
-                spot = pl.ds(at * rows, rows)
+            jobs = back(token_jobs(scal[1], kept_ref, sent_ref, part))
+            copies = made(jobs, out_sems)
+            for at in (2, 3, 0, 1):
+                mask = (0, 2, 1, 3)[at]
+                spot = jnp.bitwise_xor(scal[1], mask)
+                spot = pl.ds(pl.multiple_of(spot * rows, rows), rows)
                 part[spot, :] = mm_nt(context_ref[spot, :], held[...]).astype(bf16)
-            wait_all(start_all(back(token_jobs(scal[1], kept_ref, sent_ref, part)), out_sems))
+                copies[at].start()
+            wait_all(copies)
 
         half = jax.ShapeDtypeStruct((tokens // 2, model), bf16)
         return pl.pallas_call(
@@ -848,10 +853,15 @@
             grads_ref[:, :width] = query_ref[...]
             grads_ref[:, width:] = (kept_kv_ref[...] + arrived_ref[...].astype(f32)).astype(bf16)
             wait_all(copies)
-            for at in range(4):
-                spot = pl.ds(at * rows, rows)
+            jobs = back(token_jobs(scal[1], kept_ref, sent_ref, part))
+            copies = made(jobs, out_sems)
+            for at in (2, 3, 0, 1):
+                mask = (0, 2, 1, 3)[at]
+                spot = jnp.bitwise_xor(scal[1], mask)
+                spot = pl.ds(pl.multiple_of(spot * rows, rows), rows)
                 part[spot, :] = mm_nt(grads_ref[spot, :], held[...]).astype(bf16)
-            wait_all(start_all(back(token_jobs(scal[1], kept_ref, sent_ref, part)), out_sems))
+                copies[at].start()
+            wait_all(copies)
 
         half = jax.ShapeDtypeStruct((tokens // 2, model), bf16)
         return pl.pallas_call(
@@ -1115,7 +1125,7 @@
             return hold([], [far_a, far_b, *arrived])
 
         far_a, far_b, two_x_c, two_l_c, two_own_c = section(gather_rest)
-        far_a, far_b, down_piece = hold(up_y2, [far_a, far_b, down_piece])
+        far_a, far_b, down_piece = hold([], [far_a, far_b, down_piece])
         down_far = far_pieces(down_piece)
 
         def gather_far():
@@ -1129,12 +1139,12 @@
         gate_pieces = [(part, 0) for part in [*gate_far]] + [
             (part, 0) for part in [own_y, *gate_y2]
         ]
+        far_a, far_b, far_a_c, far_b_c, down_piece_y, cot_x, cot_l, up_y2 = hold(
+            [], [far_a, far_b, far_a_c, far_b_c, down_piece, cot_x, cot_l, tuple(up_y2)]
+        )
         up_pieces = [(part, 0) for part in [*up_far]] + [(own_y, size)] + [
             (part, 0) for part in up_y2
         ]
-        far_a, far_b, far_a_c, far_b_c, down_piece_y, cot_x, cot_l = hold(
-            [], [far_a, far_b, far_a_c, far_b_c, down_piece, cot_x, cot_l]
-        )
         two_pieces += [far_a, far_b]
         two_pieces_c += [far_a_c, far_b_c]
 

time: 537 us -> 528 us (0.983)
  the two profiles are of different devices: /device:TPU:29 before, /device:TPU:0 now
where the time goes in v6:
time: 528 us; the launch traced here: 518 us
  Pallas kernels  278 us (53%)
  waiting for transfers between devices  137 us (26%)
  starting transfers between devices  72.8 us (14%)
  local copies, waits for them, and re-layouts  15.6 us (3%)
  other arithmetic  13.7 us (3%)
    ppermute x70, waiting for transfers between devices, swap(): return lax.ppermute(array, axis, [(i, i ^ bit) for i in range(size)])  135 us
    ppermute x70, starting transfers between devices, swap(): return lax.ppermute(array, axis, [(i, i ^ bit) for i in range(size)])  69.5 us
    pallas_call x19, Pallas kernels, whole_call(): pl.pallas_call(kernel, in_specs=[SCALARS] + [WHOLE] * (len(args) - 1), ou...  61.2 us
    pallas_call x2, Pallas kernels, ffn_back(): pl.pallas_call(kernel, grid=(2,), in_specs=[SCALARS] + [ANY] * (many + 3...  49 us
    pallas_call x3, Pallas kernels, ffn_grad(): pl.pallas_call(kernel, grid=(model // wide,), in_specs=[SCALARS] + [pl.Bl...  38.9 us
    pallas_call x2, Pallas kernels, ffn_up(): pl.pallas_call(kernel, grid=(2,), in_specs=[SCALARS] + [ANY] * (many + 2...  31.3 us
    pallas_call x9, Pallas kernels, part_call(): pl.pallas_call(kernel, grid=(1,), in_specs=[SCALARS] + [rows_block(rows,...  28.6 us
    pallas_call x1, Pallas kernels, attend_back(): pl.pallas_call(kernel, in_specs=[SCALARS] + [WHOLE] * 4 + [ANY] * 4 + [WH...  21 us
  transfers between devices with their start and end apart: 71, of which 35 were waited for; matrix products, arithmetic and copies ran while one was open for 4% of the time, Pallas kernels for 51%

profile of v6, /device:TPU:0, one launch (start us, length us, event | category | flops | bytes accessed | tf_op | source)
XLA Modules:
  0.0 518.3 jit_solution(2012454601028439944)
XLA Ops:
  2.5 4.1 collective-permute-start.39
  27.4 3.4 split_cols.3
  34.7 10.4 %conditional.23 = (bf16[192,512]{1,0:T(8,128)(2,1)}, bf16[512,1536]{1,0:T(8,128)(2,1)}, bf16[384,384]{1,0:T(8,128)(2,1)}, bf16[384,1152]{1,0:T(8,128)(2,1)}) conditional(s32[]{:T(128)} %convert_element_type.63, () %tuple.242, (bf16[192,512]{1,0:T(8,128)(2,1)}, bf16[512,1536]{1,0:T(8,128)(2,1)S(1)}, bf16[384,384]{1,0:T(8,128)(2,1)}, s32[2]{0:T(128)S(1)}, ...), branch_computations={%region_3.4_spmd, %region_4.5_spmd} | conditional | bytes 8257688 | solution.py:101
  40.1 4.3 collective-permute-done
  52.4 17.0 %conditional.24 = (bf16[1024,384]{1,0:T(8,128)(2,1)}, bf16[1024,128]{1,0:T(8,128)(2,1)}, bf16[1024,128]{1,0:T(8,128)(2,1)}, bf16[1024,384]{1,0:T(8,128)(2,1)S(1)}, bf16[256,1536]{1,0:T(8,128)(2,1)}) conditional(s32[]{:T(128)} %convert_element_type.63, () %tuple.247, (f32[512]{0:T(512)S(1)}, s32[2]{0:T(128)S(1)}, bf16[512,1536]{1,0:T(8,128)(2,1)S(1)}, ...), branch_computations={%region_5.6_spmd, %region_6.7_spmd} | conditional | bytes 4194424 | solution.py:101
  52.4 6.8 %project.1 = (bf16[1024,384]{1,0:T(8,128)(2,1)}, bf16[1024,128]{1,0:T(8,128)(2,1)}) custom-call(s32[2]{0:T(128)S(1)} %get-tuple-element.534.scal, bf16[512,1536]{1,0:T(8,128)(2,1)S(1)} %get-tuple-element.535.pair_ref, bf16[512,1536]{1,0:T(8,128)(2,1)} %get-tuple-element.536.core_ref, f32[1,512]{1,0:T(1,128)S(1)} %bitcast.29, ...), custom_call_target="tpu_custom_call" | custom-call | tf_op jit(solution)/shard_map/cond/branch_1_fun/project/pallas_call | solution.py:676
  61.4 8.1 %attend.1 = bf16[1024,384]{1,0:T(8,128)(2,1)S(1)} custom-call(s32[2]{0:T(128)S(1)} %get-tuple-element.534.scal, bf16[1024,384]{1,0:T(8,128)(2,1)} %get-tuple-element.1381.query_ref, bf16[1024,128]{1,0:T(8,128)(2,1)} %get-tuple-element.1382.own_ref, bf16[1024,128]{1,0:T(8,128)(2,1)} %collective-permute-done.3.other_ref, s32[1024,1]{1,0:T(8,128)} %get-tuple-element.551.start_ref), custom_call_target="tpu_custom_call" | custom-call | tf_op jit(solution)/shard_map/cond/branch_1_fun/attend/pallas_call | solution.py:400
  69.5 5.1 out_rows.1
  74.6 9.5 %collective-permute-done.49 = bf16[384,1152]{1,0:T(8,128)(2,1)} collective-permute-done((bf16[384,1152]{1,0:T(8,128)(2,1)}, bf16[384,1152]{1,0:T(8,128)(2,1)}, u32[]{:S(2)}, u32[]{:S(2)}) %collective-permute-start.49) | collective-permute-done | bytes 884768 | tf_op jit(solution)/shard_map/swap_dp_2/ppermute | solution.py:122
  84.1 3.8 conditional.25
  91.0 25.3 %conditional.26 = ((f32[256,1536]{1,0:T(8,128)}, bf16[256,1536]{1,0:T(8,128)(2,1)})) conditional(s32[]{:T(128)} %convert_element_type.63, () %tuple.251, (s32[2]{0:T(128)S(1)}, bf16[512,1536]{1,0:T(8,128)(2,1)}, bf16[512,1536]{1,0:T(8,128)(2,1)}, f32[1536]{0:T(1024)S(1)}, bf16[256,1536]{1,0:T(8,128)(2,1)}) %tuple.368), branch_computations={%region_9.10_spmd, %region_10.11_spmd} | conditional | bytes 3158064 | solution.py:101
  95.9 16.7 %collective-permute-done.6.arrived_ref = bf16[256,1536]{1,0:T(8,128)(2,1)} collective-permute-done((bf16[256,1536]{1,0:T(8,128)(2,1)}, bf16[256,1536]{1,0:T(8,128)(2,1)}, u32[]{:S(2)}, u32[]{:S(2)}) %collective-permute-start.6) | collective-permute-done | bytes 786464 | tf_op jit(solution)/shard_map/cond/branch_1_fun/swap_tensor_2/ppermute | solution.py:122
  112.6 3.7 norm_two.1
  116.3 8.0 %collective-permute-done.50 = bf16[256,1536]{1,0:T(8,128)(2,1)} collective-permute-done((bf16[256,1536]{1,0:T(8,128)(2,1)}, bf16[256,1536]{1,0:T(8,128)(2,1)}, u32[]{:S(2)}, u32[]{:S(2)}) %collective-permute-start.50) | collective-permute-done | bytes 786464 | tf_op jit(solution)/shard_map/swap_dp_2/ppermute | solution.py:122
  125.1 22.5 %conditional.27 = (bf16[256,1536]{1,0:T(8,128)(2,1)}, bf16[256,1536]{1,0:T(8,128)(2,1)}, bf16[384,1152]{1,0:T(8,128)(2,1)}) conditional(s32[]{:T(128)} %convert_element_type.63, () %tuple.256, (bf16[256,1536]{1,0:T(8,128)(2,1)}, s32[2]{0:T(128)S(1)}, bf16[384,1152]{1,0:T(8,128)(2,1)}, bf16[384,1152]{1,0:T(8,128)(2,1)}) %tuple.257), branch_computations={%region_11.12_spmd, %region_12.13_spmd} | conditional | bytes 6291560 | solution.py:101
  128.9 14.8 %collective-permute-done.7 = bf16[256,1536]{1,0:T(8,128)(2,1)} collective-permute-done((bf16[256,1536]{1,0:T(8,128)(2,1)}, bf16[256,1536]{1,0:T(8,128)(2,1)}, u32[]{:S(2)}, u32[]{:S(2)}) %collective-permute-start.7) | collective-permute-done | bytes 786464 | tf_op jit(solution)/shard_map/cond/branch_1_fun/swap_tensor_2/ppermute | solution.py:122
  143.7 3.9 collective-permute-done.8
  149.1 14.2 %conditional.28 = (bf16[128,1536]{1,0:T(8,128)(2,1)}, bf16[128,1536]{1,0:T(8,128)(2,1)}, bf16[256,1536]{1,0:T(8,128)(2,1)}, bf16[256,1536]{1,0:T(8,128)(2,1)}, bf16[256,1536]{1,0:T(8,128)(2,1)}) conditional(s32[]{:T(128)} %convert_element_type.63, () %tuple.259, (s32[2]{0:T(128)S(1)}, bf16[256,1536]{1,0:T(8,128)(2,1)}, ...), branch_computations={%region_13.14_spmd, %region_14.17_spmd} | conditional | flops 1 | bytes 12583205 | solution.py:101
  153.1 7.9 %conditional = (bf16[256,1536]{1,0:T(8,128)(2,1)}, bf16[256,1536]{1,0:T(8,128)(2,1)}, bf16[256,1536]{1,0:T(8,128)(2,1)}) conditional(s32[]{:T(128)} %convert_element_type.15, () %tuple.119, (bf16[256,1536]{1,0:T(8,128)(2,1)}, bf16[256,1536]{1,0:T(8,128)(2,1)}, bf16[256,1536]{1,0:T(8,128)(2,1)}) %tuple.120), branch_computations={%region_15.15_spmd, %region_16.16_spmd} | conditional | bytes 9437328 | solution.py:101
  166.0 3.5 collective-permute-done.55
  169.6 20.9 %conditional.30 = (bf16[384,1152]{1,0:T(8,128)(2,1)}, bf16[256,1536]{1,0:T(8,128)(2,1)}, bf16[256,1536]{1,0:T(8,128)(2,1)}, bf16[1024,1536]{1,0:T(8,128)(2,1)}, ...) conditional(s32[]{:T(128)} %convert_element_type.63, () %tuple.241, ...), branch_computations={%region_19.20_spmd, %region_20.21_spmd} | conditional | bytes 12681286 | solution.py:101
  172.0 15.4 %ffn_up.2 = (bf16[1024,1536]{1,0:T(8,128)(2,1)}, bf16[1024,1152]{1,0:T(8,128)(2,1)}, bf16[1024,1152]{1,0:T(8,128)(2,1)}, bf16[1024,1152]{1,0:T(8,128)(2,1)}) custom-call(s32[2]{0:T(128)S(1)} %get-tuple-element.591.scal, bf16[256,1536]{1,0:T(8,128)(2,1)} %get-tuple-element.592.refs_0_, bf16[256,1536]{1,0:T(8,128)(2,1)} %get-tuple-element.593.refs_1_, ...), custom_call_target="tpu_custom_call" | custom-call | tf_op jit(solution)/shard_map/cond/branch_1_fun/ffn_up/pallas_call | solution.py:252
  190.5 16.4 %conditional.31 = (bf16[256,1536]{1,0:T(8,128)(2,1)}, bf16[256,1536]{1,0:T(8,128)(2,1)}, bf16[1024,1536]{1,0:T(8,128)(2,1)}, bf16[1024,1152]{1,0:T(8,128)(2,1)},...) conditional(s32[]{:T(128)} %convert_element_type.63, () %tuple.266, (s32[2]{0:T(128)S(1)}, ...), branch_computations={%region_21.22_spmd, %region_22.23_spmd} | conditional | bytes 11796540 | solution.py:101
  191.0 15.9 %ffn_up.3 = (bf16[1024,1536]{1,0:T(8,128)(2,1)}, bf16[1024,1152]{1,0:T(8,128)(2,1)}, bf16[1024,1152]{1,0:T(8,128)(2,1)}, bf16[1024,1152]{1,0:T(8,128)(2,1)}) custom-call(s32[2]{0:T(128)S(1)} %get-tuple-element.614.scal, bf16[256,1536]{1,0:T(8,128)(2,1)} %get-tuple-element.615.refs_0_, bf16[256,1536]{1,0:T(8,128)(2,1)} %get-tuple-element.616.refs_1_, ...), custom_call_target="tpu_custom_call" | custom-call | tf_op jit(solution)/shard_map/cond/branch_1_fun/ffn_up/pallas_call | solution.py:252
  207.2 13.2 %conditional.32 = ((bf16[768,1152]{1,0:T(8,128)(2,1)}, bf16[768,1152]{1,0:T(8,128)(2,1)})) conditional(s32[]{:T(128)} %convert_element_type.63, () %tuple.270, (s32[2]{0:T(128)S(1)}, bf16[256,1536]{1,0:T(8,128)(2,1)}, bf16[256,1536]{1,0:T(8,128)(2,1)}, bf16[256,1536]{1,0:T(8,128)(2,1)}, bf16[256,1536]{1,0:T(8,128)(2,1)}, ...), branch_computations={%region_23.24_spmd, %region_24.25_spmd} | conditional | bytes 3538972 | solution.py:101
  207.2 13.2 %grad_down.1 = (bf16[768,1152]{1,0:T(8,128)(2,1)}, bf16[768,1152]{1,0:T(8,128)(2,1)}) custom-call(s32[2]{0:T(128)S(1)} %get-tuple-element.635.scal, bf16[256,1536]{1,0:T(8,128)(2,1)} %get-tuple-element.636.refs_0_, bf16[256,1536]{1,0:T(8,128)(2,1)} %get-tuple-element.637.refs_1_, bf16[256,1536]{1,0:T(8,128)(2,1)} %get-tuple-element.638.refs_2_, ...), custom_call_target="tpu_custom_call" | custom-call | tf_op jit(solution)/shard_map/cond/branch_1_fun/grad_down/pallas_call | solution.py:385
  220.5 8.4 %collective-permute-done.57 = bf16[384,1152]{1,0:T(8,128)(2,1)} collective-permute-done((bf16[384,1152]{1,0:T(8,128)(2,1)}, bf16[384,1152]{1,0:T(8,128)(2,1)}, u32[]{:S(2)}, u32[]{:S(2)}) %collective-permute-start.57) | collective-permute-done | bytes 884768 | tf_op jit(solution)/shard_map/swap_dp_1/ppermute | solution.py:122
  229.1 51.5 %conditional.33 = (bf16[1024,1152]{1,0:T(8,128)(2,1)}, bf16[1024,1152]{1,0:T(8,128)(2,1)}, bf16[1024,1152]{1,0:T(8,128)(2,1)}, bf16[1024,1152]{1,0:T(8,128)(2,1)...) conditional(s32[]{:T(128)} %convert_element_type.63, () %tuple.269, ...), branch_computations={%region_25.26_spmd, %region_26.27_spmd} | conditional | bytes 16515152 | solution.py:101
  229.1 24.4 %ffn_back.3 = (bf16[1024,1152]{1,0:T(8,128)(2,1)}, bf16[1024,1152]{1,0:T(8,128)(2,1)}, bf16[1024,1536]{1,0:T(8,128)(2,1)}) custom-call(s32[2]{0:T(128)S(1)} %get-tuple-element.646.scal, bf16[256,1536]{1,0:T(8,128)(2,1)} %get-tuple-element.666.refs_0_, bf16[256,1536]{1,0:T(8,128)(2,1)} %get-tuple-element.667.refs_1_, ...), custom_call_target="tpu_custom_call" | custom-call | tf_op jit(solution)/shard_map/cond/branch_1_fun/ffn_back/pallas_call | solution.py:315
  253.6 24.6 %ffn_back.2 = (bf16[1024,1152]{1,0:T(8,128)(2,1)}, bf16[1024,1152]{1,0:T(8,128)(2,1)}, bf16[1024,1536]{1,0:T(8,128)(2,1)}) custom-call(s32[2]{0:T(128)S(1)} %get-tuple-element.646.scal, bf16[256,1536]{1,0:T(8,128)(2,1)} %get-tuple-element.647.refs_0_, bf16[256,1536]{1,0:T(8,128)(2,1)} %get-tuple-element.648.refs_1_, ...), custom_call_target="tpu_custom_call" | custom-call | tf_op jit(solution)/shard_map/cond/branch_1_fun/ffn_back/pallas_call | solution.py:315
  280.6 24.3 %conditional.34 = (bf16[1024,1536]{1,0:T(8,128)(2,1)}, bf16[1024,1536]{1,0:T(8,128)(2,1)}, f32[256,1536]{1,0:T(8,128)}, bf16[256,1536]{1,0:T(8,128)(2,1)}, bf16[256,1536]{1,0:T(8,128)(2,1)}) conditional(s32[]{:T(128)} %convert_element_type.63, () %tuple.276, (s32[2]{0:T(128)S(1)}, bf16[1024,1152]{1,0:T(8,128)(2,1)}, bf16[384,1152]{1,0:T(8,128)(2,1)}, ...), branch_computations={%region_27.28_spmd, %region_28.31_spmd} | conditional | flops 1 | bytes 15728877 | solution.py:101
  282.2 18.3 %conditional.1 = (bf16[1024,1536]{1,0:T(8,128)(2,1)}, bf16[1024,1536]{1,0:T(8,128)(2,1)}) conditional(s32[]{:T(128)} %convert_element_type.16, () %tuple.136, (s32[2]{0:T(128)S(1)}, bf16[1024,1152]{1,0:T(8,128)(2,1)}, bf16[384,1152]{1,0:T(8,128)(2,1)}, bf16[384,1152]{1,0:T(8,128)(2,1)}, bf16[384,1152]{1,0:T(8,128)(2,1)}, ...), branch_computations={%region_29.29_spmd, %region_30.30_spmd} | conditional | bytes 12582968 | solution.py:101
  282.2 9.0 %block_rows.3 = bf16[1024,1536]{1,0:T(8,128)(2,1)} custom-call(s32[2]{0:T(128)S(1)} %get-tuple-element.678.scal, bf16[1024,1152]{1,0:T(8,128)(2,1)} %get-tuple-element.684.left_ref, bf16[384,1152]{1,0:T(8,128)(2,1)} %get-tuple-element.680.refs_0_, bf16[384,1152]{1,0:T(8,128)(2,1)} %get-tuple-element.681.refs_1_, ...), custom_call_target="tpu_custom_call" | custom-call | tf_op jit(solution)/shard_map/cond/branch_1_fun/cond/branch_1_fun/block_rows/pallas_call | solution.py:343
  291.4 9.0 %block_rows.2 = bf16[1024,1536]{1,0:T(8,128)(2,1)} custom-call(s32[2]{0:T(128)S(1)} %get-tuple-element.678.scal, bf16[1024,1152]{1,0:T(8,128)(2,1)} %get-tuple-element.679.left_ref, bf16[384,1152]{1,0:T(8,128)(2,1)} %get-tuple-element.680.refs_0_, bf16[384,1152]{1,0:T(8,128)(2,1)} %get-tuple-element.681.refs_1_, ...), custom_call_target="tpu_custom_call" | custom-call | tf_op jit(solution)/shard_map/cond/branch_1_fun/cond/branch_1_fun/block_rows/pallas_call | solution.py:343
  300.5 4.4 spread_rest.1
  305.0 27.7 %conditional.35 = (bf16[768,1152]{1,0:T(8,128)(2,1)}, bf16[768,1152]{1,0:T(8,128)(2,1)}, bf16[384,1152]{1,0:T(8,128)(2,1)}, bf16[384,1152]{1,0:T(8,128)(2,1)}, b...) conditional(s32[]{:T(128)} %convert_element_type.63, () %tuple.240, ...), branch_computations={%region_31.32_spmd, %region_32.33_spmd} | conditional | bytes 9289812 | solution.py:101
  308.1 3.7 fold_sum.7
  311.8 3.4 part_sum.6
  315.2 12.8 %grad_up.1 = (bf16[768,1152]{1,0:T(8,128)(2,1)}, bf16[768,1152]{1,0:T(8,128)(2,1)}) custom-call(s32[2]{0:T(128)S(1)} %get-tuple-element.705.scal, bf16[1024,1536]{1,0:T(8,128)(2,1)} %get-tuple-element.706.refs_0_, bf16[1024,1536]{1,0:T(8,128)(2,1)} %get-tuple-element.707.refs_1_, bf16[1024,1152]{1,0:T(8,128)(2,1)} %get-tuple-element.708.refs_2_, ...), custom_call_target="tpu_custom_call" | custom-call | tf_op jit(solution)/shard_map/cond/branch_1_fun/grad_up/pallas_call | solution.py:385
  328.0 4.7 norm_two_back.1
  336.5 42.6 %conditional.36 = (bf16[768,1152]{1,0:T(8,128)(2,1)}, bf16[768,1152]{1,0:T(8,128)(2,1)}, bf16[1024,384]{1,0:T(8,128)(2,1)}, f32[1024,128]{1,0:T(8,128)}, bf16[10...) conditional(s32[]{:T(128)} %convert_element_type.63, () %tuple.281, ...), branch_computations={%region_33.34_spmd, %region_34.37_spmd} | conditional | flops 1 | bytes 15728965 | solution.py:101
  336.5 19.0 %conditional.2 = (bf16[256,1536]{1,0:T(8,128)(2,1)}, bf16[256,1536]{1,0:T(8,128)(2,1)}, bf16[768,1152]{1,0:T(8,128)(2,1)}, bf16[768,1152]{1,0:T(8,128)(2,1)}) conditional(s32[]{:T(128)} %convert_element_type.26, () %tuple.147, (s32[2]{0:T(128)S(1)}, bf16[1024,1536]{1,0:T(8,128)(2,1)}, bf16[1024,1536]{1,0:T(8,128)(2,1)}, ...), branch_computations={%region_35.35_spmd, %region_36.36_spmd} | conditional | bytes 6291568 | solution.py:101
  338.3 12.9 %grad_gate.1 = (bf16[768,1152]{1,0:T(8,128)(2,1)}, bf16[768,1152]{1,0:T(8,128)(2,1)}) custom-call(s32[2]{0:T(128)S(1)} %get-tuple-element.729.scal, bf16[1024,1536]{1,0:T(8,128)(2,1)} %get-tuple-element.730.refs_0_, bf16[1024,1536]{1,0:T(8,128)(2,1)} %get-tuple-element.731.refs_1_, bf16[1024,1152]{1,0:T(8,128)(2,1)} %get-tuple-element.732.refs_2_, ...), custom_call_target="tpu_custom_call" | custom-call | tf_op jit(solution)/shard_map/cond/branch_1_fun/cond/branch_1_fun/grad_gate/pallas_call | solution.py:385
  351.2 4.3 collective-permute-done.27
  358.1 21.0 %attend_back.1 = (bf16[1024,384]{1,0:T(8,128)(2,1)}, f32[1024,128]{1,0:T(8,128)}, bf16[1024,128]{1,0:T(8,128)(2,1)}, f32[8,640]{1,0:T(8,128)}, bf16[768,384]{1,0:T(8,128)(2,1)}, /*index=5*/bf16[768,384]{1,0:T(8,128)(2,1)}) custom-call(s32[2]{0:T(128)S(1)} %get-tuple-element.739.scal, bf16[1024,384]{1,0:T(8,128)(2,1)S(1)} %copy-done.9, ...), custom_call_target="tpu_custom_call" | custom-call | tf_op jit(solution)/shard_map/cond/branch_1_fun/attend_back/pallas_call | solution.py:818
  379.2 4.1 conditional.37
  379.4 3.9 fold_sum.8
  383.3 4.1 collective-permute-done.60
  390.1 49.9 %conditional.38 = (bf16[384,1152]{1,0:T(8,128)(2,1)}, bf16[384,1152]{1,0:T(8,128)(2,1)}, bf16[768,1152]{1,0:T(8,128)(2,1)}, bf16[192,1152]{1,0:T(8,128)(2,1)}, b...) conditional(s32[]{:T(128)} %convert_element_type.63, () %tuple.238, ...), branch_computations={%region_39.40_spmd, %region_40.45_spmd} | conditional | flops 16910 | bytes 29645708 | solution.py:101
  392.2 47.8 %conditional.4 = ((bf16[192,1152]{1,0:T(8,128)(2,1)}, bf16[192,1152]{1,0:T(8,128)(2,1)}, bf16[768,512]{1,0:T(8,128)(2,1)}, bf16[256,1536]{1,0:T(8,128)(2,1)}, f3...) conditional(s32[]{:T(128)} %convert_element_type.30, () %tuple.164, ...), branch_computations={%region_41.41_spmd, %region_42.44_spmd} | conditional | flops 16909 | bytes 19028512 | solution.py:101
  392.2 7.7 %project_back.1 = (bf16[1024,512]{1,0:T(8,128)(2,1)}, bf16[512,1536]{1,0:T(8,128)(2,1)}, bf16[512,1536]{1,0:T(8,128)(2,1)}) custom-call(s32[2]{0:T(128)S(1)} %get-tuple-element.799.scal, bf16[1024,384]{1,0:T(8,128)(2,1)} %get-tuple-element.805.query_ref, f32[1024,128]{1,0:T(8,128)} %get-tuple-element.806.kept_kv_ref, ...), custom_call_target="tpu_custom_call" | custom-call | tf_op jit(solution)/shard_map/cond/branch_1_fun/cond/branch_1_fun/project_back/pallas_call | solution.py:867
  400.0 5.8 %project_grad.1 = (bf16[768,512]{1,0:T(8,128)(2,1)}, bf16[768,512]{1,0:T(8,128)(2,1)}) custom-call(s32[2]{0:T(128)S(1)} %get-tuple-element.799.scal, bf16[512,1536]{1,0:T(8,128)(2,1)S(1)} %get-tuple-element.819.pair_ref, bf16[512,1536]{1,0:T(8,128)(2,1)} %get-tuple-element.820.core_ref, bf16[1024,512]{1,0:T(8,128)(2,1)} %get-tuple-element.826.grads_ref), custom_call_target="tpu_custom_call" | custom-call | tf_op jit(solution)/shard_map/cond/branch_1_fun/cond/branch_1_fun/project_grad/pallas_call | solution.py:913
  408.3 31.8 %conditional.3 = (bf16[192,1152]{1,0:T(8,128)(2,1)}, bf16[192,1152]{1,0:T(8,128)(2,1)}, bf16[768,512]{1,0:T(8,128)(2,1)}, bf16[256,1536]{1,0:T(8,128)(2,1)}, f32...) conditional(s32[]{:T(128)} %convert_element_type.27, () %tuple.160, ...), branch_computations={%region_43.42_spmd, %region_44.43_spmd} | conditional | flops 16908 | bytes 12736834 | solution.py:101
  415.0 4.2 gain_rows.1
  428.6 3.7 norm_one_back.1
  432.2 7.8 %collective-permute-done.35 = bf16[768,512]{1,0:T(8,128)(2,1)} collective-permute-done((bf16[768,512]{1,0:T(8,128)(2,1)}, bf16[768,512]{1,0:T(8,128)(2,1)}, u32[]{:S(2)}, u32[]{:S(2)}) %collective-permute-start.35) | collective-permute-done | bytes 786464 | tf_op jit(solution)/shard_map/cond/branch_1_fun/cond/branch_1_fun/cond/branch_1_fun/swap_dp_2/ppermute | solution.py:122
  440.1 3.8 fold_sum.12
  446.4 3.3 all-to-all-start
  449.7 33.9 %conditional.39 = (bf16[192,896]{1,0:T(8,128)(2,1)}, bf16[192,1152]{1,0:T(8,128)(2,1)S(1)}, bf16[192,1152]{1,0:T(8,128)(2,1)S(1)}, bf16[256,1536]{1,0:T(8,128)(2...) conditional(s32[]{:T(128)} %convert_element_type.63, () %tuple.237, (s32[2]{0:T(128)S(1)}, ...), branch_computations={%region_45.46_spmd, %region_46.49_spmd} | conditional | flops 172033 | bytes 16761205 | solution.py:101
  453.1 23.9 %conditional.5 = (bf16[192,896]{1,0:T(8,128)(2,1)S(1)}, bf16[192,896]{1,0:T(8,128)(2,1)}, bf16[192,1152]{1,0:T(8,128)(2,1)}, bf16[192,1152]{1,0:T(8,128)(2,1)}) conditional(s32[]{:T(128)} %convert_element_type.31, () %tuple.173, (s32[2]{0:T(128)S(1)}, bf16[768,512]{1,0:T(8,128)(2,1)}, bf16[768,512]{1,0:T(8,128)(2,1)}, bf16[768,384]{1,0:T(8,128)(2,1)}, ...), branch_computations={%region_47.47_spmd, %region_48.48_spmd} | conditional | bytes 5505124 | solution.py:101
  453.1 3.4 fold_both.1
  460.6 13.1 %collective-permute-done.31.arrived_ref = bf16[384,896]{1,0:T(8,128)(2,1)S(1)} collective-permute-done((bf16[384,896]{1,0:T(8,128)(2,1)}, bf16[384,896]{1,0:T(8,128)(2,1)S(1)}, u32[]{:S(2)}, u32[]{:S(2)}) %collective-permute-start.31) | collective-permute-done | bytes 688160 | tf_op jit(solution)/shard_map/cond/branch_1_fun/cond/branch_1_fun/swap_dp_1/ppermute | solution.py:122
  485.6 7.9 %collective-permute-start.65 = (bf16[192,896]{1,0:T(8,128)(2,1)}, bf16[192,896]{1,0:T(8,128)(2,1)S(1)}, u32[]{:S(2)}, u32[]{:S(2)}) collective-permute-start(bf16[192,896]{1,0:T(8,128)(2,1)} %get-tuple-element.1293), channel_id=1, source_target_pairs={{0,16},{4,20},{8,24},{12,28},{16,0},{20,4},{24,8},{28,12},{1,17},{... | collective-permute-start | bytes 1032200 | tf_op jit(solution)/shard_map/swap_dp_4/ppermute | solution.py:122
  497.4 8.1 %collective-permute-done.64.theirs_ref = bf16[192,1152]{1,0:T(8,128)(2,1)S(1)} collective-permute-done((bf16[192,1152]{1,0:T(8,128)(2,1)S(1)}, bf16[192,1152]{1,0:T(8,128)(2,1)S(1)}, u32[]{:S(2)}, u32[]{:S(2)}) %collective-permute-start.64) | collective-permute-done | bytes 442400 | tf_op jit(solution)/shard_map/swap_dp_2/ppermute | solution.py:122
  (269 shorter events, 163.2 us)
Async XLA Ops:
  2.5 14.1 %collective-permute-start.39 = (bf16[192,512]{1,0:T(8,128)(2,1)S(1)}, bf16[192,512]{1,0:T(8,128)(2,1)S(1)}, u32[]{:S(2)}, u32[]{:S(2)}) collective-permute-start(bf16[192,512]{1,0:T(8,128)(2,1)S(1)} %pad_maximum_fusion.6), channel_id=1, source_target_pairs={{0,16},{4,20},{8,24},{12,28},{16,0},{20,4},{24,8},{28,12},{1,17},{... | collective-permute-start | bytes 589832 | tf_op jit(solution)/shard_map/swap_dp_4/ppermute | solution.py:122
  6.6 10.0 %collective-permute-start.40 = (bf16[192,512]{1,0:T(8,128)(2,1)S(1)}, bf16[192,512]{1,0:T(8,128)(2,1)S(1)}, u32[]{:S(2)}, u32[]{:S(2)}) collective-permute-start(bf16[192,512]{1,0:T(8,128)(2,1)S(1)} %pad_maximum_fusion.6), channel_id=1, source_target_pairs={{0,8},{4,12},{8,0},{12,4},{16,24},{20,28},{24,16},{28,20},{1,9},{5... | collective-permute-start | bytes 589832 | tf_op jit(solution)/shard_map/swap_dp_2/ppermute | solution.py:122
  8.2 8.5 %collective-permute-start.41 = (bf16[192,512]{1,0:T(8,128)(2,1)S(1)}, bf16[192,512]{1,0:T(8,128)(2,1)S(1)}, u32[]{:S(2)}, u32[]{:S(2)}) collective-permute-start(bf16[192,512]{1,0:T(8,128)(2,1)S(1)} %pad_maximum_fusion.6), channel_id=1, source_target_pairs={{0,4},{4,0},{8,12},{12,8},{16,20},{20,16},{24,28},{28,24},{1,5},{5... | collective-permute-start | bytes 589832 | tf_op jit(solution)/shard_map/swap_dp_1/ppermute | solution.py:122
  12.1 21.1 %collective-permute-start.44 = (bf16[256,1536]{1,0:T(8,128)(2,1)S(1)}, bf16[256,1536]{1,0:T(8,128)(2,1)}, u32[]{:S(2)}, u32[]{:S(2)}) collective-permute-start(bf16[256,1536]{1,0:T(8,128)(2,1)S(1)} %fusion.2), channel_id=1, source_target_pairs={{0,2},{1,3},{2,0},{3,1},{4,6},{5,7},{6,4},{7,5},{8,10},{9,11},{10,... | collective-permute-start | bytes 2359304 | tf_op jit(solution)/shard_map/swap_tensor_2/ppermute | solution.py:122
  16.2 18.5 %collective-permute-start.45 = (bf16[192,1152]{1,0:T(8,128)(2,1)}, bf16[192,1152]{1,0:T(8,128)(2,1)}, u32[]{:S(2)}, u32[]{:S(2)}) collective-permute-start(bf16[192,1152]{1,0:T(8,128)(2,1)} %get-tuple-element.1115), channel_id=1, source_target_pairs={{0,8},{4,12},{8,0},{12,4},{16,24},{20,28},{24,16},{28,20},{1,9},{5... | collective-permute-start | bytes 1327112 | tf_op jit(solution)/shard_map/swap_dp_2/ppermute | solution.py:122
  16.7 18.0 %collective-permute-start.43 = (bf16[192,512]{1,0:T(8,128)(2,1)S(1)}, bf16[192,512]{1,0:T(8,128)(2,1)}, u32[]{:S(2)}, u32[]{:S(2)}) collective-permute-start(bf16[192,512]{1,0:T(8,128)(2,1)S(1)} %collective-permute-done.39), channel_id=1, source_target_pairs={{0,8},{4,12},{8,0},{12,4},{16,24},{20,28},{24,16},{28,20},{1,9},{5... | collective-permute-start | bytes 589832 | tf_op jit(solution)/shard_map/swap_dp_2/ppermute | solution.py:122
  19.1 15.5 %collective-permute-start.42 = (bf16[384,512]{1,0:T(8,128)(2,1)}, bf16[384,512]{1,0:T(8,128)(2,1)S(1)}, u32[]{:S(2)}, u32[]{:S(2)}) collective-permute-start(bf16[384,512]{1,0:T(8,128)(2,1)} %pad_maximum_fusion.4), channel_id=1, source_target_pairs={{0,4},{4,0},{8,12},{12,8},{16,20},{20,16},{24,28},{28,24},{1,5},{5... | collective-permute-start | bytes 1179656 | tf_op jit(solution)/shard_map/swap_dp_1/ppermute | solution.py:122
  20.2 12.3 %collective-permute-start.46 = (bf16[192,384]{1,0:T(8,128)(2,1)S(1)}, bf16[192,384]{1,0:T(8,128)(2,1)S(1)}, u32[]{:S(2)}, u32[]{:S(2)}) collective-permute-start(bf16[192,384]{1,0:T(8,128)(2,1)S(1)} %bitcast.25), channel_id=1, source_target_pairs={{0,16},{4,20},{8,24},{12,28},{16,0},{20,4},{24,8},{28,12},{1,17},{... | collective-permute-start | bytes 442376 | tf_op jit(solution)/shard_map/swap_dp_4/ppermute | solution.py:122
  34.7 10.3 %collective-permute-start.1 = (bf16[512,1536]{1,0:T(8,128)(2,1)S(1)}, bf16[512,1536]{1,0:T(8,128)(2,1)}, u32[]{:S(2)}, u32[]{:S(2)}) collective-permute-start(bf16[512,1536]{1,0:T(8,128)(2,1)S(1)} %get-tuple-element.529), channel_id=1, source_target_pairs={{0,1},{1,0},{2,3},{3,2},{4,5},{5,4},{6,7},{7,6},{8,9},{9,8},{10,11... | collective-permute-start | bytes 4718600 | tf_op jit(solution)/shard_map/cond/branch_1_fun/swap_tensor_1/ppermute | solution.py:122
  34.7 10.3 %collective-permute-start.2 = (bf16[384,384]{1,0:T(8,128)(2,1)}, bf16[384,384]{1,0:T(8,128)(2,1)}, u32[]{:S(2)}, u32[]{:S(2)}) collective-permute-start(bf16[384,384]{1,0:T(8,128)(2,1)} %get-tuple-element.530), channel_id=1, source_target_pairs={{0,8},{4,12},{8,0},{12,4},{16,24},{20,28},{24,16},{28,20},{1,9},{5... | collective-permute-start | bytes 884744 | tf_op jit(solution)/shard_map/cond/branch_1_fun/swap_dp_2/ppermute | solution.py:122
  37.1 7.3 %collective-permute-start = (bf16[192,512]{1,0:T(8,128)(2,1)}, bf16[192,512]{1,0:T(8,128)(2,1)}, u32[]{:S(2)}, u32[]{:S(2)}) collective-permute-start(bf16[192,512]{1,0:T(8,128)(2,1)} %get-tuple-element.528), channel_id=1, source_target_pairs={{0,4},{4,0},{8,12},{12,8},{16,20},{20,16},{24,28},{28,24},{1,5},{5... | collective-permute-start | bytes 589832 | tf_op jit(solution)/shard_map/cond/branch_1_fun/swap_dp_1/ppermute | solution.py:122
  46.1 38.0 %collective-permute-start.49 = (bf16[384,1152]{1,0:T(8,128)(2,1)}, bf16[384,1152]{1,0:T(8,128)(2,1)}, u32[]{:S(2)}, u32[]{:S(2)}) collective-permute-start(bf16[384,1152]{1,0:T(8,128)(2,1)} %get-tuple-element.1146), channel_id=1, source_target_pairs={{0,8},{4,12},{8,0},{12,4},{16,24},{20,28},{24,16},{28,20},{1,9},{5... | collective-permute-start | bytes 2654216 | tf_op jit(solution)/shard_map/swap_dp_2/ppermute | solution.py:122
  48.0 26.7 %collective-permute-start.47 = (bf16[256,1536]{1,0:T(8,128)(2,1)}, bf16[256,1536]{1,0:T(8,128)(2,1)}, u32[]{:S(2)}, u32[]{:S(2)}) collective-permute-start(bf16[256,1536]{1,0:T(8,128)(2,1)} %param.71), channel_id=1, source_target_pairs={{0,2},{1,3},{2,0},{3,1},{4,6},{5,7},{6,4},{7,5},{8,10},{9,11},{10,... | collective-permute-start | bytes 2359304 | tf_op jit(solution)/shard_map/swap_tensor_2/ppermute | solution.py:122
  48.8 20.6 %collective-permute-start.48 = (bf16[768,384]{1,0:T(8,128)(2,1)S(1)}, bf16[768,384]{1,0:T(8,128)(2,1)S(1)}, u32[]{:S(2)}, u32[]{:S(2)}) collective-permute-start(bf16[768,384]{1,0:T(8,128)(2,1)S(1)} %pad_maximum_fusion.2.refs_0_.refs_2_.refs_4_.refs_6_), channel_id=1, source_target_pairs={{0,4},{4,0},{8,12},{12,8},{16,20},{20,16},{24,28},{28,24},{1,5},{5... | collective-permute-start | bytes 1769480 | tf_op jit(solution)/shard_map/swap_dp_1/ppermute | solution.py:122
  51.1 65.2 %collective-permute-start.51 = (bf16[384,1152]{1,0:T(8,128)(2,1)}, bf16[384,1152]{1,0:T(8,128)(2,1)}, u32[]{:S(2)}, u32[]{:S(2)}) collective-permute-start(bf16[384,1152]{1,0:T(8,128)(2,1)} %get-tuple-element.1150), channel_id=1, source_target_pairs={{0,16},{4,20},{8,24},{12,28},{16,0},{20,4},{24,8},{28,12},{1,17},{... | collective-permute-start | bytes 2654216 | tf_op jit(solution)/shard_map/swap_dp_4/ppermute | solution.py:122
  61.2 8.2 %collective-permute-start.4 = (bf16[256,1536]{1,0:T(8,128)(2,1)}, bf16[256,1536]{1,0:T(8,128)(2,1)}, u32[]{:S(2)}, u32[]{:S(2)}) collective-permute-start(bf16[256,1536]{1,0:T(8,128)(2,1)} %get-tuple-element.552), channel_id=1, source_target_pairs={{0,1},{1,0},{2,3},{3,2},{4,5},{5,4},{6,7},{7,6},{8,9},{9,8},{10,11... | collective-permute-start | bytes 2359304 | tf_op jit(solution)/shard_map/cond/branch_1_fun/swap_tensor_1/ppermute | solution.py:122
  84.1 3.8 collective-permute-start.5
  87.9 59.9 %collective-permute-start.52 = (bf16[768,1152]{1,0:T(8,128)(2,1)}, bf16[768,1152]{1,0:T(8,128)(2,1)S(1)}, u32[]{:S(2)}, u32[]{:S(2)}) collective-permute-start(bf16[768,1152]{1,0:T(8,128)(2,1)} %get-tuple-element.1156), channel_id=1, source_target_pairs={{0,4},{4,0},{8,12},{12,8},{16,20},{20,16},{24,28},{28,24},{1,5},{5... | collective-permute-start | bytes 5308424 | tf_op jit(solution)/shard_map/swap_dp_1/ppermute | solution.py:122
  89.1 35.2 %collective-permute-start.50 = (bf16[256,1536]{1,0:T(8,128)(2,1)}, bf16[256,1536]{1,0:T(8,128)(2,1)}, u32[]{:S(2)}, u32[]{:S(2)}) collective-permute-start(bf16[256,1536]{1,0:T(8,128)(2,1)} %param.71), channel_id=1, source_target_pairs={{0,8},{4,12},{8,0},{12,4},{16,24},{20,28},{24,16},{28,20},{1,9},{5... | collective-permute-start | bytes 2359304 | tf_op jit(solution)/shard_map/swap_dp_2/ppermute | solution.py:122
  89.1 58.5 %collective-permute-start.54 = (bf16[384,1152]{1,0:T(8,128)(2,1)}, bf16[384,1152]{1,0:T(8,128)(2,1)}, u32[]{:S(2)}, u32[]{:S(2)}) collective-permute-start(bf16[384,1152]{1,0:T(8,128)(2,1)} %get-tuple-element.1160), channel_id=1, source_target_pairs={{0,16},{4,20},{8,24},{12,28},{16,0},{20,4},{24,8},{28,12},{1,17},{... | collective-permute-start | bytes 2654216 | tf_op jit(solution)/shard_map/swap_dp_4/ppermute | solution.py:122
  93.5 19.1 %collective-permute-start.6 = (bf16[256,1536]{1,0:T(8,128)(2,1)}, bf16[256,1536]{1,0:T(8,128)(2,1)}, u32[]{:S(2)}, u32[]{:S(2)}) collective-permute-start(bf16[256,1536]{1,0:T(8,128)(2,1)} %part_sum.4), channel_id=1, source_target_pairs={{0,2},{1,3},{2,0},{3,1},{4,6},{5,7},{6,4},{7,5},{8,10},{9,11},{10,... | collective-permute-start | bytes 2359304 | tf_op jit(solution)/shard_map/cond/branch_1_fun/swap_tensor_2/ppermute | solution.py:122
  124.4 23.4 %collective-permute-start.53 = (bf16[384,1152]{1,0:T(8,128)(2,1)}, bf16[384,1152]{1,0:T(8,128)(2,1)}, u32[]{:S(2)}, u32[]{:S(2)}) collective-permute-start(bf16[384,1152]{1,0:T(8,128)(2,1)} %collective-permute-done.51), channel_id=1, source_target_pairs={{0,4},{4,0},{8,12},{12,8},{16,20},{20,16},{24,28},{28,24},{1,5},{5... | collective-permute-start | bytes 2654216 | tf_op jit(solution)/shard_map/swap_dp_1/ppermute | solution.py:122
  125.1 18.6 %collective-permute-start.7 = (bf16[256,1536]{1,0:T(8,128)(2,1)}, bf16[256,1536]{1,0:T(8,128)(2,1)}, u32[]{:S(2)}, u32[]{:S(2)}) collective-permute-start(bf16[256,1536]{1,0:T(8,128)(2,1)} %get-tuple-element.567), channel_id=1, source_target_pairs={{0,2},{1,3},{2,0},{3,1},{4,6},{5,7},{6,4},{7,5},{8,10},{9,11},{10,... | collective-permute-start | bytes 2359304 | tf_op jit(solution)/shard_map/cond/branch_1_fun/swap_tensor_2/ppermute | solution.py:122
  126.5 21.1 %collective-permute-start.8 = (bf16[256,1536]{1,0:T(8,128)(2,1)}, bf16[256,1536]{1,0:T(8,128)(2,1)}, u32[]{:S(2)}, u32[]{:S(2)}) collective-permute-start(bf16[256,1536]{1,0:T(8,128)(2,1)} %get-tuple-element.567), channel_id=1, source_target_pairs={{0,8},{4,12},{8,0},{12,4},{16,24},{20,28},{24,16},{28,20},{1,9},{5... | collective-permute-start | bytes 2359304 | tf_op jit(solution)/shard_map/cond/branch_1_fun/swap_dp_2/ppermute | solution.py:122
  147.8 21.8 %collective-permute-start.55 = (bf16[384,1152]{1,0:T(8,128)(2,1)}, bf16[384,1152]{1,0:T(8,128)(2,1)}, u32[]{:S(2)}, u32[]{:S(2)}) collective-permute-start(bf16[384,1152]{1,0:T(8,128)(2,1)} %collective-permute-done.54), channel_id=1, source_target_pairs={{0,4},{4,0},{8,12},{12,8},{16,20},{20,16},{24,28},{28,24},{1,5},{5... | collective-permute-start | bytes 2654216 | tf_op jit(solution)/shard_map/swap_dp_1/ppermute | solution.py:122
  151.3 10.4 %collective-permute-start.12 = (bf16[128,1536]{1,0:T(8,128)(2,1)}, bf16[128,1536]{1,0:T(8,128)(2,1)}, u32[]{:S(2)}, u32[]{:S(2)}) collective-permute-start(bf16[128,1536]{1,0:T(8,128)(2,1)} %get-tuple-element.583), channel_id=1, source_target_pairs={{0,2},{1,3},{2,0},{3,1},{4,6},{5,7},{6,4},{7,5},{8,10},{9,11},{10,... | collective-permute-start | bytes 1179656 | tf_op jit(solution)/shard_map/cond/branch_1_fun/swap_tensor_2/ppermute | solution.py:122
  153.1 10.1 %collective-permute-start.13 = (bf16[128,1536]{1,0:T(8,128)(2,1)}, bf16[128,1536]{1,0:T(8,128)(2,1)}, u32[]{:S(2)}, u32[]{:S(2)}) collective-permute-start(bf16[128,1536]{1,0:T(8,128)(2,1)} %get-tuple-element.584), channel_id=1, source_target_pairs={{0,8},{4,12},{8,0},{12,4},{16,24},{20,28},{24,16},{28,20},{1,9},{5... | collective-permute-start | bytes 1179656 | tf_op jit(solution)/shard_map/cond/branch_1_fun/swap_dp_2/ppermute | solution.py:122
  163.2 43.7 %collective-permute-start.56 = (bf16[384,1152]{1,0:T(8,128)(2,1)}, bf16[384,1152]{1,0:T(8,128)(2,1)}, u32[]{:S(2)}, u32[]{:S(2)}) collective-permute-start(bf16[384,1152]{1,0:T(8,128)(2,1)} %get-tuple-element.1175), channel_id=1, source_target_pairs={{0,16},{4,20},{8,24},{12,28},{16,0},{20,4},{24,8},{28,12},{1,17},{... | collective-permute-start | bytes 2654216 | tf_op jit(solution)/shard_map/swap_dp_4/ppermute | solution.py:122
  169.6 20.9 %collective-permute-start.16 = (bf16[384,1152]{1,0:T(8,128)(2,1)}, bf16[384,1152]{1,0:T(8,128)(2,1)}, u32[]{:S(2)}, u32[]{:S(2)}) collective-permute-start(bf16[384,1152]{1,0:T(8,128)(2,1)} %get-tuple-element.608), channel_id=1, source_target_pairs={{0,4},{4,0},{8,12},{12,8},{16,20},{20,16},{24,28},{28,24},{1,5},{5... | collective-permute-start | bytes 2654216 | tf_op jit(solution)/shard_map/cond/branch_1_fun/swap_dp_1/ppermute | solution.py:122
  170.2 18.2 %collective-permute-start.17 = (bf16[256,1536]{1,0:T(8,128)(2,1)}, bf16[256,1536]{1,0:T(8,128)(2,1)}, u32[]{:S(2)}, u32[]{:S(2)}) collective-permute-start(bf16[256,1536]{1,0:T(8,128)(2,1)} %get-tuple-element.609), channel_id=1, source_target_pairs={{0,2},{1,3},{2,0},{3,1},{4,6},{5,7},{6,4},{7,5},{8,10},{9,11},{10,... | collective-permute-start | bytes 2359304 | tf_op jit(solution)/shard_map/cond/branch_1_fun/swap_tensor_2/ppermute | solution.py:122
  172.0 16.4 %collective-permute-start.18 = (bf16[256,1536]{1,0:T(8,128)(2,1)}, bf16[256,1536]{1,0:T(8,128)(2,1)}, u32[]{:S(2)}, u32[]{:S(2)}) collective-permute-start(bf16[256,1536]{1,0:T(8,128)(2,1)} %get-tuple-element.610), channel_id=1, source_target_pairs={{0,1},{1,0},{2,3},{3,2},{4,5},{5,4},{6,7},{7,6},{8,9},{9,8},{10,11... | collective-permute-start | bytes 2359304 | tf_op jit(solution)/shard_map/cond/branch_1_fun/swap_tensor_1/ppermute | solution.py:122
  190.5 16.4 %collective-permute-start.19 = (bf16[256,1536]{1,0:T(8,128)(2,1)}, bf16[256,1536]{1,0:T(8,128)(2,1)}, u32[]{:S(2)}, u32[]{:S(2)}) collective-permute-start(bf16[256,1536]{1,0:T(8,128)(2,1)} %get-tuple-element.631), channel_id=1, source_target_pairs={{0,1},{1,0},{2,3},{3,2},{4,5},{5,4},{6,7},{7,6},{8,9},{9,8},{10,11... | collective-permute-start | bytes 2359304 | tf_op jit(solution)/shard_map/cond/branch_1_fun/swap_tensor_1/ppermute | solution.py:122
  190.5 16.4 %collective-permute-start.20 = (bf16[256,1536]{1,0:T(8,128)(2,1)}, bf16[256,1536]{1,0:T(8,128)(2,1)}, u32[]{:S(2)}, u32[]{:S(2)}) collective-permute-start(bf16[256,1536]{1,0:T(8,128)(2,1)} %get-tuple-element.632), channel_id=1, source_target_pairs={{0,1},{1,0},{2,3},{3,2},{4,5},{5,4},{6,7},{7,6},{8,9},{9,8},{10,11... | collective-permute-start | bytes 2359304 | tf_op jit(solution)/shard_map/cond/branch_1_fun/swap_tensor_1/ppermute | solution.py:122
  206.9 21.9 %collective-permute-start.57 = (bf16[384,1152]{1,0:T(8,128)(2,1)}, bf16[384,1152]{1,0:T(8,128)(2,1)}, u32[]{:S(2)}, u32[]{:S(2)}) collective-permute-start(bf16[384,1152]{1,0:T(8,128)(2,1)} %collective-permute-done.56), channel_id=1, source_target_pairs={{0,4},{4,0},{8,12},{12,8},{16,20},{20,16},{24,28},{28,24},{1,5},{5... | collective-permute-start | bytes 2654216 | tf_op jit(solution)/shard_map/swap_dp_1/ppermute | solution.py:122
  228.8 76.1 %collective-permute-start.58 = (bf16[768,1152]{1,0:T(8,128)(2,1)}, bf16[768,1152]{1,0:T(8,128)(2,1)}, u32[]{:S(2)}, u32[]{:S(2)}) collective-permute-start(bf16[768,1152]{1,0:T(8,128)(2,1)} %get-tuple-element.1217), channel_id=1, source_target_pairs={{0,4},{4,0},{8,12},{12,8},{16,20},{20,16},{24,28},{28,24},{1,5},{5... | collective-permute-start | bytes 5308424 | tf_op jit(solution)/shard_map/swap_dp_1/ppermute | solution.py:122
  253.5 24.7 %collective-permute-start.21 = (bf16[1024,1536]{1,0:T(8,128)(2,1)}, bf16[1024,1536]{1,0:T(8,128)(2,1)}, u32[]{:S(2)}, u32[]{:S(2)}) collective-permute-start(bf16[1024,1536]{1,0:T(8,128)(2,1)} %get-tuple-element.675), channel_id=1, source_target_pairs={{0,1},{1,0},{2,3},{3,2},{4,5},{5,4},{6,7},{7,6},{8,9},{9,8},{10,11... | collective-permute-start | bytes 9437192 | tf_op jit(solution)/shard_map/cond/branch_1_fun/swap_tensor_1/ppermute | solution.py:122
  280.6 19.9 %collective-permute-start.23 = (bf16[128,1536]{1,0:T(8,128)(2,1)}, bf16[128,1536]{1,0:T(8,128)(2,1)}, u32[]{:S(2)}, u32[]{:S(2)}) collective-permute-start(bf16[128,1536]{1,0:T(8,128)(2,1)} %get-tuple-element.694), channel_id=1, source_target_pairs={{0,2},{1,3},{2,0},{3,1},{4,6},{5,7},{6,4},{7,5},{8,10},{9,11},{10,... | collective-permute-start | bytes 1179656 | tf_op jit(solution)/shard_map/cond/branch_1_fun/swap_tensor_2/ppermute | solution.py:122
  282.2 18.4 %collective-permute-start.24 = (bf16[128,1536]{1,0:T(8,128)(2,1)}, bf16[128,1536]{1,0:T(8,128)(2,1)}, u32[]{:S(2)}, u32[]{:S(2)}) collective-permute-start(bf16[128,1536]{1,0:T(8,128)(2,1)} %get-tuple-element.695), channel_id=1, source_target_pairs={{0,8},{4,12},{8,0},{12,4},{16,24},{20,28},{24,16},{28,20},{1,9},{5... | collective-permute-start | bytes 1179656 | tf_op jit(solution)/shard_map/cond/branch_1_fun/swap_dp_2/ppermute | solution.py:122
  291.2 9.3 %collective-permute-start.22 = (bf16[1024,1536]{1,0:T(8,128)(2,1)}, bf16[1024,1536]{1,0:T(8,128)(2,1)}, u32[]{:S(2)}, u32[]{:S(2)}) collective-permute-start(bf16[1024,1536]{1,0:T(8,128)(2,1)} %block_rows.3), channel_id=1, source_target_pairs={{0,1},{1,0},{2,3},{3,2},{4,5},{5,4},{6,7},{7,6},{8,9},{9,8},{10,11... | collective-permute-start | bytes 9437192 | tf_op jit(solution)/shard_map/cond/branch_1_fun/cond/branch_1_fun/swap_tensor_1/ppermute | solution.py:122
  305.0 23.0 %collective-permute-start.25 = (bf16[256,1536]{1,0:T(8,128)(2,1)}, bf16[256,1536]{1,0:T(8,128)(2,1)}, u32[]{:S(2)}, u32[]{:S(2)}) collective-permute-start(bf16[256,1536]{1,0:T(8,128)(2,1)} %get-tuple-element.719), channel_id=1, source_target_pairs={{0,2},{1,3},{2,0},{3,1},{4,6},{5,7},{6,4},{7,5},{8,10},{9,11},{10,... | collective-permute-start | bytes 2359304 | tf_op jit(solution)/shard_map/cond/branch_1_fun/swap_tensor_2/ppermute | solution.py:122
  305.9 22.1 %collective-permute-start.26 = (bf16[256,1536]{1,0:T(8,128)(2,1)}, bf16[256,1536]{1,0:T(8,128)(2,1)}, u32[]{:S(2)}, u32[]{:S(2)}) collective-permute-start(bf16[256,1536]{1,0:T(8,128)(2,1)} %get-tuple-element.720), channel_id=1, source_target_pairs={{0,8},{4,12},{8,0},{12,4},{16,24},{20,28},{24,16},{28,20},{1,9},{5... | collective-permute-start | bytes 2359304 | tf_op jit(solution)/shard_map/cond/branch_1_fun/swap_dp_2/ppermute | solution.py:122
  332.7 46.4 %collective-permute-start.59 = (bf16[768,1152]{1,0:T(8,128)(2,1)}, bf16[768,1152]{1,0:T(8,128)(2,1)}, u32[]{:S(2)}, u32[]{:S(2)}) collective-permute-start(bf16[768,1152]{1,0:T(8,128)(2,1)} %get-tuple-element.1238), channel_id=1, source_target_pairs={{0,4},{4,0},{8,12},{12,8},{16,20},{20,16},{24,28},{28,24},{1,5},{5... | collective-permute-start | bytes 5308424 | tf_op jit(solution)/shard_map/swap_dp_1/ppermute | solution.py:122
  334.4 55.2 %collective-permute-start.61 = (bf16[512,1536]{1,0:T(8,128)(2,1)}, bf16[512,1536]{1,0:T(8,128)(2,1)}, u32[]{:S(2)}, u32[]{:S(2)}) collective-permute-start(bf16[512,1536]{1,0:T(8,128)(2,1)} %get-tuple-element.1246), channel_id=1, source_target_pairs={{0,8},{4,12},{8,0},{12,4},{16,24},{20,28},{24,16},{28,20},{1,9},{5... | collective-permute-start | bytes 4718600 | tf_op jit(solution)/shard_map/swap_dp_2/ppermute | solution.py:122
  334.6 52.9 %collective-permute-start.60 = (bf16[384,1152]{1,0:T(8,128)(2,1)}, bf16[384,1152]{1,0:T(8,128)(2,1)}, u32[]{:S(2)}, u32[]{:S(2)}) collective-permute-start(bf16[384,1152]{1,0:T(8,128)(2,1)} %get-tuple-element.1245), channel_id=1, source_target_pairs={{0,16},{4,20},{8,24},{12,28},{16,0},{20,4},{24,8},{28,12},{1,17},{... | collective-permute-start | bytes 2654216 | tf_op jit(solution)/shard_map/swap_dp_4/ppermute | solution.py:122
  336.5 19.0 %collective-permute-start.27 = (bf16[256,1536]{1,0:T(8,128)(2,1)}, bf16[256,1536]{1,0:T(8,128)(2,1)}, u32[]{:S(2)}, u32[]{:S(2)}) collective-permute-start(bf16[256,1536]{1,0:T(8,128)(2,1)} %get-tuple-element.736), channel_id=1, source_target_pairs={{0,2},{1,3},{2,0},{3,1},{4,6},{5,7},{6,4},{7,5},{8,10},{9,11},{10,... | collective-permute-start | bytes 2359304 | tf_op jit(solution)/shard_map/cond/branch_1_fun/cond/branch_1_fun/swap_tensor_2/ppermute | solution.py:122
  338.3 17.2 %collective-permute-start.28 = (bf16[256,1536]{1,0:T(8,128)(2,1)}, bf16[256,1536]{1,0:T(8,128)(2,1)}, u32[]{:S(2)}, u32[]{:S(2)}) collective-permute-start(bf16[256,1536]{1,0:T(8,128)(2,1)} %get-tuple-element.736), channel_id=1, source_target_pairs={{0,1},{1,0},{2,3},{3,2},{4,5},{5,4},{6,7},{7,6},{8,9},{9,8},{10,11... | collective-permute-start | bytes 2359304 | tf_op jit(solution)/shard_map/cond/branch_1_fun/cond/branch_1_fun/swap_tensor_1/ppermute | solution.py:122
  379.2 4.1 collective-permute-start.30
  389.6 50.4 %collective-permute-start.62 = (bf16[768,384]{1,0:T(8,128)(2,1)}, bf16[768,384]{1,0:T(8,128)(2,1)}, u32[]{:S(2)}, u32[]{:S(2)}) collective-permute-start(bf16[768,384]{1,0:T(8,128)(2,1)} %get-tuple-element.1261), channel_id=1, source_target_pairs={{0,8},{4,12},{8,0},{12,4},{16,24},{20,28},{24,16},{28,20},{1,9},{5... | collective-permute-start | bytes 1769480 | tf_op jit(solution)/shard_map/swap_dp_2/ppermute | solution.py:122
  390.1 49.9 %collective-permute-start.37 = (bf16[768,1152]{1,0:T(8,128)(2,1)}, bf16[768,1152]{1,0:T(8,128)(2,1)}, u32[]{:S(2)}, u32[]{:S(2)}) collective-permute-start(bf16[768,1152]{1,0:T(8,128)(2,1)} %get-tuple-element.868), channel_id=1, source_target_pairs={{0,4},{4,0},{8,12},{12,8},{16,20},{20,16},{24,28},{28,24},{1,5},{5... | collective-permute-start | bytes 5308424 | tf_op jit(solution)/shard_map/cond/branch_1_fun/swap_dp_1/ppermute | solution.py:122
  390.5 49.6 %collective-permute-start.38 = (bf16[384,1152]{1,0:T(8,128)(2,1)}, bf16[384,1152]{1,0:T(8,128)(2,1)}, u32[]{:S(2)}, u32[]{:S(2)}) collective-permute-start(bf16[384,1152]{1,0:T(8,128)(2,1)} %get-tuple-element.869), channel_id=1, source_target_pairs={{0,16},{4,20},{8,24},{12,28},{16,0},{20,4},{24,8},{28,12},{1,17},{... | collective-permute-start | bytes 2654216 | tf_op jit(solution)/shard_map/cond/branch_1_fun/swap_dp_4/ppermute | solution.py:122
  399.9 5.9 %collective-permute-start.36 = (bf16[512,1536]{1,0:T(8,128)(2,1)}, bf16[512,1536]{1,0:T(8,128)(2,1)}, u32[]{:S(2)}, u32[]{:S(2)}) collective-permute-start(bf16[512,1536]{1,0:T(8,128)(2,1)} %get-tuple-element.818), channel_id=1, source_target_pairs={{0,1},{1,0},{2,3},{3,2},{4,5},{5,4},{6,7},{7,6},{8,9},{9,8},{10,11... | collective-permute-start | bytes 4718600 | tf_op jit(solution)/shard_map/cond/branch_1_fun/cond/branch_1_fun/swap_tensor_1/ppermute | solution.py:122
  408.3 20.3 %collective-permute-start.34 = (bf16[256,1536]{1,0:T(8,128)(2,1)}, bf16[256,1536]{1,0:T(8,128)(2,1)}, u32[]{:S(2)}, u32[]{:S(2)}) collective-permute-start(bf16[256,1536]{1,0:T(8,128)(2,1)} %get-tuple-element.794), channel_id=1, source_target_pairs={{0,2},{1,3},{2,0},{3,1},{4,6},{5,7},{6,4},{7,5},{8,10},{9,11},{10,... | collective-permute-start | bytes 2359304 | tf_op jit(solution)/shard_map/cond/branch_1_fun/cond/branch_1_fun/cond/branch_1_fun/swap_tensor_2/ppermute | solution.py:122
  410.0 30.1 %collective-permute-start.35 = (bf16[768,512]{1,0:T(8,128)(2,1)}, bf16[768,512]{1,0:T(8,128)(2,1)}, u32[]{:S(2)}, u32[]{:S(2)}) collective-permute-start(bf16[768,512]{1,0:T(8,128)(2,1)} %get-tuple-element.797), channel_id=1, source_target_pairs={{0,8},{4,12},{8,0},{12,4},{16,24},{20,28},{24,16},{28,20},{1,9},{5... | collective-permute-start | bytes 2359304 | tf_op jit(solution)/shard_map/cond/branch_1_fun/cond/branch_1_fun/cond/branch_1_fun/swap_dp_2/ppermute | solution.py:122
  443.9 41.1 %collective-permute-start.63 = (bf16[384,1152]{1,0:T(8,128)(2,1)}, bf16[384,1152]{1,0:T(8,128)(2,1)}, u32[]{:S(2)}, u32[]{:S(2)}) collective-permute-start(bf16[384,1152]{1,0:T(8,128)(2,1)} %get-tuple-element.1281), channel_id=1, source_target_pairs={{0,16},{4,20},{8,24},{12,28},{16,0},{20,4},{24,8},{28,12},{1,17},{... | collective-permute-start | bytes 2654216 | tf_op jit(solution)/shard_map/swap_dp_4/ppermute | solution.py:122
  446.4 38.7 %all-to-all-start = ((f32[32,1,160]{2,1,0:T(1,128)}), f32[32,1,160]{2,1,0:T(1,128)S(1)}, u32[]{:S(2)}, u32[]{:S(2)}) async-start(f32[32,1,160]{2,1,0:T(1,128)} %all_to_all.8), calls=%async_computation | async-start | bytes 65536 | tf_op jit(solution)/shard_map/all_to_all | solution.py:1346
  449.7 27.3 %collective-permute-start.32 = (bf16[256,1536]{1,0:T(8,128)(2,1)}, bf16[256,1536]{1,0:T(8,128)(2,1)}, u32[]{:S(2)}, u32[]{:S(2)}) collective-permute-start(bf16[256,1536]{1,0:T(8,128)(2,1)} %get-tuple-element.904), channel_id=1, source_target_pairs={{0,2},{1,3},{2,0},{3,1},{4,6},{5,7},{6,4},{7,5},{8,10},{9,11},{10,... | collective-permute-start | bytes 2359304 | tf_op jit(solution)/shard_map/cond/branch_1_fun/swap_tensor_2/ppermute | solution.py:122
  451.6 25.4 %collective-permute-start.33 = (bf16[192,1152]{1,0:T(8,128)(2,1)}, bf16[192,1152]{1,0:T(8,128)(2,1)S(1)}, u32[]{:S(2)}, u32[]{:S(2)}) collective-permute-start(bf16[192,1152]{1,0:T(8,128)(2,1)} %get-tuple-element.905), channel_id=1, source_target_pairs={{0,8},{4,12},{8,0},{12,4},{16,24},{20,28},{24,16},{28,20},{1,9},{5... | collective-permute-start | bytes 1327112 | tf_op jit(solution)/shard_map/cond/branch_1_fun/swap_dp_2/ppermute | solution.py:122
  456.5 17.2 %collective-permute-start.31 = (bf16[384,896]{1,0:T(8,128)(2,1)}, bf16[384,896]{1,0:T(8,128)(2,1)S(1)}, u32[]{:S(2)}, u32[]{:S(2)}) collective-permute-start(bf16[384,896]{1,0:T(8,128)(2,1)} %get-tuple-element.889), channel_id=1, source_target_pairs={{0,4},{4,0},{8,12},{12,8},{16,20},{20,16},{24,28},{28,24},{1,5},{5... | collective-permute-start | bytes 2064392 | tf_op jit(solution)/shard_map/cond/branch_1_fun/cond/branch_1_fun/swap_dp_1/ppermute | solution.py:122
  485.0 20.4 %collective-permute-start.64 = (bf16[192,1152]{1,0:T(8,128)(2,1)S(1)}, bf16[192,1152]{1,0:T(8,128)(2,1)S(1)}, u32[]{:S(2)}, u32[]{:S(2)}) collective-permute-start(bf16[192,1152]{1,0:T(8,128)(2,1)S(1)} %get-tuple-element.1291), channel_id=1, source_target_pairs={{0,8},{4,12},{8,0},{12,4},{16,24},{20,28},{24,16},{28,20},{1,9},{5... | collective-permute-start | bytes 1327112 | tf_op jit(solution)/shard_map/swap_dp_2/ppermute | solution.py:122
  485.6 23.1 %collective-permute-start.65 = (bf16[192,896]{1,0:T(8,128)(2,1)}, bf16[192,896]{1,0:T(8,128)(2,1)S(1)}, u32[]{:S(2)}, u32[]{:S(2)}) collective-permute-start(bf16[192,896]{1,0:T(8,128)(2,1)} %get-tuple-element.1293), channel_id=1, source_target_pairs={{0,16},{4,20},{8,24},{12,28},{16,0},{20,4},{24,8},{28,12},{1,17},{... | collective-permute-start | bytes 1032200 | tf_op jit(solution)/shard_map/swap_dp_4/ppermute | solution.py:122
  496.1 17.7 %collective-permute-start.66 = (bf16[192,1152]{1,0:T(8,128)(2,1)}, bf16[192,1152]{1,0:T(8,128)(2,1)S(1)}, u32[]{:S(2)}, u32[]{:S(2)}) collective-permute-start(bf16[192,1152]{1,0:T(8,128)(2,1)} %get-tuple-element.1290), channel_id=1, source_target_pairs={{0,8},{4,12},{8,0},{12,4},{16,24},{20,28},{24,16},{28,20},{1,9},{5... | collective-permute-start | bytes 1327112 | tf_op jit(solution)/shard_map/swap_dp_2/ppermute | solution.py:122
  510.5 3.3 collective-permute-start.67
  510.6 3.9 collective-permute-start.68
  511.5 3.3 collective-permute-start.69
  (41 other events, 339.8 us)

commit v7 on v6

--- a/solution.py
+++ b/solution.py
@@ -466,9 +466,16 @@
                 own_ref[spot, :] = jnp.where(flag, high, low).astype(bf16)
                 sent_ref[spot, :] = jnp.where(flag, low, high).astype(bf16)
 
-        return whole_call(
-            kernel, [((rows, columns), bf16)] * 2, "fold_sum", scalars, kept, arrived
-        )
+        wide = 384 if columns % 384 == 0 else columns
+        spec = pl.BlockSpec((2 * rows, wide), lambda i: (0, i))
+        return pl.pallas_call(
+            kernel,
+            grid=(columns // wide,),
+            in_specs=[SCALARS, spec, spec],
+            out_specs=[pl.BlockSpec((rows, wide), lambda i: (0, i))] * 2,
+            out_shape=[jax.ShapeDtypeStruct((rows, columns), bf16)] * 2,
+            name="fold_sum",
+        )(scalars, kept, arrived)
 
     def norm_two(scalars, rows_in, kept, sums, arrived, gain):
         rows, columns = rows_in.shape
@@ -479,7 +486,7 @@
             hidden_ref[...] = hidden
             out_ref[...] = (norm_forward(hidden)[0] * gain_ref[...]).astype(bf16)
 
-        return part_call(
+        return row_call(
             kernel, [((rows, columns), f32), ((rows, columns), bf16)], "norm_two", scalars,
             [(kept, rows, 0), (sums, rows, 0)], [rows_in, arrived, gain],
         )
@@ -497,7 +504,7 @@
             )
             out_ref[...] = (given_ref[...] + grad_in).astype(bf16)
 
-        return part_call(
+        return row_call(
             kernel, [((rows, columns), bf16)], "norm_one_back", scalars,
             [(kept, rows, 0), (sums, rows, 0)], [rows_in, arrived, gain, given],
         )[0]
@@ -568,6 +575,29 @@
             + [rows_block(rows, array.shape[1], at) for array, rows, at in parts]
             + [WHOLE] * len(rest),
             out_specs=[WHOLE] * len(outs),
+            out_shape=[jax.ShapeDtypeStruct(shape, kind) for shape, kind in outs],
+            name=name,
+        )(scalars, *[array for array, _, _ in parts], *rest)
+
+    def row_call(kernel, outs, name, scalars, parts, rest):
+        steps, rows = 4, parts[0][1]
+        size = rows // steps
+
+        def part_spec(columns, at):
+            return pl.BlockSpec((size, columns), lambda i: (at * steps + i, 0))
+
+        def rest_spec(array):
+            if array.shape[0] == 1:
+                return pl.BlockSpec(array.shape, lambda i: (0, 0))
+            return part_spec(array.shape[1], 0)
+
+        return pl.pallas_call(
+            kernel,
+            grid=(steps,),
+            in_specs=[SCALARS]
+            + [part_spec(array.shape[1], at) for array, _, at in parts]
+            + [rest_spec(array) for array in rest],
+            out_specs=[part_spec(shape[1], 0) for shape, _ in outs],
             out_shape=[jax.ShapeDtypeStruct(shape, kind) for shape, kind in outs],
             name=name,
         )(scalars, *[array for array, _, _ in parts], *rest)
@@ -935,12 +965,26 @@
             total = given_ref[...].astype(f32) + grad_in
             out_ref[...] = total
             low_ref[...] = total.astype(bf16)
-            sum_ref[0:1, :] = jnp.sum(grad_out * normed, axis=0, keepdims=True)
-
-        outs = [((rows, model), f32), ((rows, model), bf16), ((8, model), f32)]
-        return whole_call(
-            kernel, outs, "norm_two_back", scalars, own, from_x, from_l, hidden, gain, given
-        )
+
+            @pl.when(pl.program_id(0) == 0)
+            def _():
+                sum_ref[...] = jnp.zeros_like(sum_ref)
+
+            sum_ref[0:1, :] += jnp.sum(grad_out * normed, axis=0, keepdims=True)
+
+        spec = pl.BlockSpec((rows // 4, model), lambda i: (i, 0))
+        return pl.pallas_call(
+            kernel,
+            grid=(4,),
+            in_specs=[SCALARS] + [spec] * 4 + [pl.BlockSpec((1, model), lambda i: (0, 0)), spec],
+            out_specs=[spec, spec, pl.BlockSpec((8, model), lambda i: (0, 0))],
+            out_shape=[
+                jax.ShapeDtypeStruct((rows, model), f32),
+                jax.ShapeDtypeStruct((rows, model), bf16),
+                jax.ShapeDtypeStruct((8, model), f32),
+            ],
+            name="norm_two_back",
+        )(scalars, own, from_x, from_l, hidden, gain, given)
 
     def local(
         block_input,

time: 528 us -> 530 us (level)
  starting transfers between devices: 72.8 us -> 67.1 us
    pallas_call x0 -> x10, Pallas kernels: none -> 38.3 us  [the longest x7 25.1 us: fold_sum(): pl.pallas_call(kernel, grid=(columns // wide,), in_specs=[SCALARS, spec,...]
    pallas_call x19 -> x11, Pallas kernels: 61.2 us -> 34.9 us  [whole_call(): pl.pallas_call(kernel, in_specs=[SCALARS] + [WHOLE] * (len(args) - 1), ou...]
    pallas_call x9 -> x7, Pallas kernels: 28.6 us -> 21.2 us  [part_call(): pl.pallas_call(kernel, grid=(1,), in_specs=[SCALARS] + [rows_block(rows,...]
    ppermute x70, starting transfers between devices: 69.5 us -> 64 us  [swap(): return lax.ppermute(array, axis, [(i, i ^ bit) for i in range(size)])]
  transfers between devices with their start and end apart: 71 -> 71, of which waited for: 35 -> 35; matrix products, arithmetic and copies ran while one was open for 4% -> 4% of each run, Pallas kernels for 51% -> 52%
where the time goes in v7:
time: 530 us; the launch traced here: 520 us
  Pallas kernels  282 us (53%)
  waiting for transfers between devices  139 us (26%)
  starting transfers between devices  67.1 us (13%)
  local copies, waits for them, and re-layouts  15.6 us (3%)
  other arithmetic  13.7 us (3%)
    ppermute x70, waiting for transfers between devices, swap(): return lax.ppermute(array, axis, [(i, i ^ bit) for i in range(size)])  137 us
    ppermute x70, starting transfers between devices, swap(): return lax.ppermute(array, axis, [(i, i ^ bit) for i in range(size)])  64 us
    pallas_call x2, Pallas kernels, ffn_back(): pl.pallas_call(kernel, grid=(2,), in_specs=[SCALARS] + [ANY] * (many + 3...  49.3 us
    pallas_call x3, Pallas kernels, ffn_grad(): pl.pallas_call(kernel, grid=(model // wide,), in_specs=[SCALARS] + [pl.Bl...  38.9 us
    pallas_call x11, Pallas kernels, whole_call(): pl.pallas_call(kernel, in_specs=[SCALARS] + [WHOLE] * (len(args) - 1), ou...  34.9 us
    pallas_call x2, Pallas kernels, ffn_up(): pl.pallas_call(kernel, grid=(2,), in_specs=[SCALARS] + [ANY] * (many + 2...  31.1 us
    pallas_call x7, Pallas kernels, fold_sum(): pl.pallas_call(kernel, grid=(columns // wide,), in_specs=[SCALARS, spec,...  25.1 us
    pallas_call x7, Pallas kernels, part_call(): pl.pallas_call(kernel, grid=(1,), in_specs=[SCALARS] + [rows_block(rows,...  21.2 us
  transfers between devices with their start and end apart: 71, of which 35 were waited for; matrix products, arithmetic and copies ran while one was open for 4% of the time, Pallas kernels for 52%

profile of v7, /device:TPU:0, one launch (start us, length us, event | category | flops | bytes accessed | tf_op | source)
XLA Modules:
  0.0 519.5 jit_solution(3852476879350132222)
XLA Ops:
  2.5 4.1 collective-permute-start.39
  27.4 3.4 split_cols.3
  34.7 10.4 %conditional.23 = (bf16[192,512]{1,0:T(8,128)(2,1)}, bf16[512,1536]{1,0:T(8,128)(2,1)}, bf16[384,384]{1,0:T(8,128)(2,1)}, bf16[384,1152]{1,0:T(8,128)(2,1)}) conditional(s32[]{:T(128)} %convert_element_type.63, () %tuple.242, (bf16[192,512]{1,0:T(8,128)(2,1)}, bf16[512,1536]{1,0:T(8,128)(2,1)S(1)}, bf16[384,384]{1,0:T(8,128)(2,1)}, s32[2]{0:T(128)S(1)}, ...), branch_computations={%region_3.4_spmd, %region_4.5_spmd} | conditional | bytes 8257688 | solution.py:101
  40.1 4.3 collective-permute-done
  52.4 17.0 %conditional.24 = (bf16[1024,384]{1,0:T(8,128)(2,1)}, bf16[1024,128]{1,0:T(8,128)(2,1)}, bf16[1024,128]{1,0:T(8,128)(2,1)}, bf16[1024,384]{1,0:T(8,128)(2,1)S(1)}, bf16[256,1536]{1,0:T(8,128)(2,1)}) conditional(s32[]{:T(128)} %convert_element_type.63, () %tuple.247, (f32[512]{0:T(512)S(1)}, s32[2]{0:T(128)S(1)}, bf16[512,1536]{1,0:T(8,128)(2,1)S(1)}, ...), branch_computations={%region_5.6_spmd, %region_6.7_spmd} | conditional | bytes 4194424 | solution.py:101
  52.4 6.8 %project.1 = (bf16[1024,384]{1,0:T(8,128)(2,1)}, bf16[1024,128]{1,0:T(8,128)(2,1)}) custom-call(s32[2]{0:T(128)S(1)} %get-tuple-element.534.scal, bf16[512,1536]{1,0:T(8,128)(2,1)S(1)} %get-tuple-element.535.pair_ref, bf16[512,1536]{1,0:T(8,128)(2,1)} %get-tuple-element.536.core_ref, f32[1,512]{1,0:T(1,128)S(1)} %bitcast.29, ...), custom_call_target="tpu_custom_call" | custom-call | tf_op jit(solution)/shard_map/cond/branch_1_fun/project/pallas_call | solution.py:706
  61.4 8.0 %attend.1 = bf16[1024,384]{1,0:T(8,128)(2,1)S(1)} custom-call(s32[2]{0:T(128)S(1)} %get-tuple-element.534.scal, bf16[1024,384]{1,0:T(8,128)(2,1)} %get-tuple-element.1381.query_ref, bf16[1024,128]{1,0:T(8,128)(2,1)} %get-tuple-element.1382.own_ref, bf16[1024,128]{1,0:T(8,128)(2,1)} %collective-permute-done.3.other_ref, s32[1024,1]{1,0:T(8,128)} %get-tuple-element.551.start_ref), custom_call_target="tpu_custom_call" | custom-call | tf_op jit(solution)/shard_map/cond/branch_1_fun/attend/pallas_call | solution.py:400
  69.5 5.1 out_rows.1
  74.6 9.5 %collective-permute-done.49 = bf16[384,1152]{1,0:T(8,128)(2,1)} collective-permute-done((bf16[384,1152]{1,0:T(8,128)(2,1)}, bf16[384,1152]{1,0:T(8,128)(2,1)}, u32[]{:S(2)}, u32[]{:S(2)}) %collective-permute-start.49) | collective-permute-done | bytes 884768 | tf_op jit(solution)/shard_map/swap_dp_2/ppermute | solution.py:122
  84.1 3.8 conditional.25
  91.0 25.9 %conditional.26 = ((f32[256,1536]{1,0:T(8,128)}, bf16[256,1536]{1,0:T(8,128)(2,1)})) conditional(s32[]{:T(128)} %convert_element_type.63, () %tuple.251, (s32[2]{0:T(128)S(1)}, bf16[512,1536]{1,0:T(8,128)(2,1)}, bf16[512,1536]{1,0:T(8,128)(2,1)}, f32[1536]{0:T(1024)S(1)}, bf16[256,1536]{1,0:T(8,128)(2,1)}) %tuple.368), branch_computations={%region_9.10_spmd, %region_10.11_spmd} | conditional | bytes 3158064 | solution.py:101
  95.9 16.7 %collective-permute-done.6.arrived_ref = bf16[256,1536]{1,0:T(8,128)(2,1)} collective-permute-done((bf16[256,1536]{1,0:T(8,128)(2,1)}, bf16[256,1536]{1,0:T(8,128)(2,1)}, u32[]{:S(2)}, u32[]{:S(2)}) %collective-permute-start.6) | collective-permute-done | bytes 786464 | tf_op jit(solution)/shard_map/cond/branch_1_fun/swap_tensor_2/ppermute | solution.py:122
  112.6 4.3 norm_two.1
  116.9 7.4 %collective-permute-done.50 = bf16[256,1536]{1,0:T(8,128)(2,1)} collective-permute-done((bf16[256,1536]{1,0:T(8,128)(2,1)}, bf16[256,1536]{1,0:T(8,128)(2,1)}, u32[]{:S(2)}, u32[]{:S(2)}) %collective-permute-start.50) | collective-permute-done | bytes 786464 | tf_op jit(solution)/shard_map/swap_dp_2/ppermute | solution.py:122
  125.1 22.5 %conditional.27 = (bf16[256,1536]{1,0:T(8,128)(2,1)}, bf16[256,1536]{1,0:T(8,128)(2,1)}, bf16[384,1152]{1,0:T(8,128)(2,1)}) conditional(s32[]{:T(128)} %convert_element_type.63, () %tuple.256, (bf16[256,1536]{1,0:T(8,128)(2,1)}, s32[2]{0:T(128)S(1)}, bf16[384,1152]{1,0:T(8,128)(2,1)}, bf16[384,1152]{1,0:T(8,128)(2,1)}) %tuple.257), branch_computations={%region_11.12_spmd, %region_12.13_spmd} | conditional | bytes 6291560 | solution.py:101
  128.9 14.8 %collective-permute-done.7 = bf16[256,1536]{1,0:T(8,128)(2,1)} collective-permute-done((bf16[256,1536]{1,0:T(8,128)(2,1)}, bf16[256,1536]{1,0:T(8,128)(2,1)}, u32[]{:S(2)}, u32[]{:S(2)}) %collective-permute-start.7) | collective-permute-done | bytes 786464 | tf_op jit(solution)/shard_map/cond/branch_1_fun/swap_tensor_2/ppermute | solution.py:122
  143.7 3.9 collective-permute-done.8
  149.1 14.2 %conditional.28 = (bf16[128,1536]{1,0:T(8,128)(2,1)}, bf16[128,1536]{1,0:T(8,128)(2,1)}, bf16[256,1536]{1,0:T(8,128)(2,1)}, bf16[256,1536]{1,0:T(8,128)(2,1)}, bf16[256,1536]{1,0:T(8,128)(2,1)}) conditional(s32[]{:T(128)} %convert_element_type.63, () %tuple.259, (s32[2]{0:T(128)S(1)}, bf16[256,1536]{1,0:T(8,128)(2,1)}, ...), branch_computations={%region_13.14_spmd, %region_14.17_spmd} | conditional | flops 1 | bytes 12583205 | solution.py:101
  153.1 7.9 %conditional = (bf16[256,1536]{1,0:T(8,128)(2,1)}, bf16[256,1536]{1,0:T(8,128)(2,1)}, bf16[256,1536]{1,0:T(8,128)(2,1)}) conditional(s32[]{:T(128)} %convert_element_type.15, () %tuple.119, (bf16[256,1536]{1,0:T(8,128)(2,1)}, bf16[256,1536]{1,0:T(8,128)(2,1)}, bf16[256,1536]{1,0:T(8,128)(2,1)}) %tuple.120), branch_computations={%region_15.15_spmd, %region_16.16_spmd} | conditional | bytes 9437328 | solution.py:101
  166.0 3.5 collective-permute-done.55
  169.6 20.9 %conditional.30 = (bf16[384,1152]{1,0:T(8,128)(2,1)}, bf16[256,1536]{1,0:T(8,128)(2,1)}, bf16[256,1536]{1,0:T(8,128)(2,1)}, bf16[1024,1536]{1,0:T(8,128)(2,1)}, ...) conditional(s32[]{:T(128)} %convert_element_type.63, () %tuple.241, ...), branch_computations={%region_19.20_spmd, %region_20.21_spmd} | conditional | bytes 12681286 | solution.py:101
  172.0 15.4 %ffn_up.2 = (bf16[1024,1536]{1,0:T(8,128)(2,1)}, bf16[1024,1152]{1,0:T(8,128)(2,1)}, bf16[1024,1152]{1,0:T(8,128)(2,1)}, bf16[1024,1152]{1,0:T(8,128)(2,1)}) custom-call(s32[2]{0:T(128)S(1)} %get-tuple-element.591.scal, bf16[256,1536]{1,0:T(8,128)(2,1)} %get-tuple-element.592.refs_0_, bf16[256,1536]{1,0:T(8,128)(2,1)} %get-tuple-element.593.refs_1_, ...), custom_call_target="tpu_custom_call" | custom-call | tf_op jit(solution)/shard_map/cond/branch_1_fun/ffn_up/pallas_call | solution.py:252
  190.5 16.2 %conditional.31 = (bf16[256,1536]{1,0:T(8,128)(2,1)}, bf16[256,1536]{1,0:T(8,128)(2,1)}, bf16[1024,1536]{1,0:T(8,128)(2,1)}, bf16[1024,1152]{1,0:T(8,128)(2,1)},...) conditional(s32[]{:T(128)} %convert_element_type.63, () %tuple.266, (s32[2]{0:T(128)S(1)}, ...), branch_computations={%region_21.22_spmd, %region_22.23_spmd} | conditional | bytes 11796540 | solution.py:101
  191.0 15.7 %ffn_up.3 = (bf16[1024,1536]{1,0:T(8,128)(2,1)}, bf16[1024,1152]{1,0:T(8,128)(2,1)}, bf16[1024,1152]{1,0:T(8,128)(2,1)}, bf16[1024,1152]{1,0:T(8,128)(2,1)}) custom-call(s32[2]{0:T(128)S(1)} %get-tuple-element.614.scal, bf16[256,1536]{1,0:T(8,128)(2,1)} %get-tuple-element.615.refs_0_, bf16[256,1536]{1,0:T(8,128)(2,1)} %get-tuple-element.616.refs_1_, ...), custom_call_target="tpu_custom_call" | custom-call | tf_op jit(solution)/shard_map/cond/branch_1_fun/ffn_up/pallas_call | solution.py:252
  207.1 13.2 %conditional.32 = ((bf16[768,1152]{1,0:T(8,128)(2,1)}, bf16[768,1152]{1,0:T(8,128)(2,1)})) conditional(s32[]{:T(128)} %convert_element_type.63, () %tuple.270, (s32[2]{0:T(128)S(1)}, bf16[256,1536]{1,0:T(8,128)(2,1)}, bf16[256,1536]{1,0:T(8,128)(2,1)}, bf16[256,1536]{1,0:T(8,128)(2,1)}, bf16[256,1536]{1,0:T(8,128)(2,1)}, ...), branch_computations={%region_23.24_spmd, %region_24.25_spmd} | conditional | bytes 3538972 | solution.py:101
  207.1 13.2 %grad_down.1 = (bf16[768,1152]{1,0:T(8,128)(2,1)}, bf16[768,1152]{1,0:T(8,128)(2,1)}) custom-call(s32[2]{0:T(128)S(1)} %get-tuple-element.635.scal, bf16[256,1536]{1,0:T(8,128)(2,1)} %get-tuple-element.636.refs_0_, bf16[256,1536]{1,0:T(8,128)(2,1)} %get-tuple-element.637.refs_1_, bf16[256,1536]{1,0:T(8,128)(2,1)} %get-tuple-element.638.refs_2_, ...), custom_call_target="tpu_custom_call" | custom-call | tf_op jit(solution)/shard_map/cond/branch_1_fun/grad_down/pallas_call | solution.py:385
  220.3 8.4 %collective-permute-done.57 = bf16[384,1152]{1,0:T(8,128)(2,1)} collective-permute-done((bf16[384,1152]{1,0:T(8,128)(2,1)}, bf16[384,1152]{1,0:T(8,128)(2,1)}, u32[]{:S(2)}, u32[]{:S(2)}) %collective-permute-start.57) | collective-permute-done | bytes 884768 | tf_op jit(solution)/shard_map/swap_dp_1/ppermute | solution.py:122
  228.9 51.8 %conditional.33 = (bf16[1024,1152]{1,0:T(8,128)(2,1)}, bf16[1024,1152]{1,0:T(8,128)(2,1)}, bf16[1024,1152]{1,0:T(8,128)(2,1)}, bf16[1024,1152]{1,0:T(8,128)(2,1)...) conditional(s32[]{:T(128)} %convert_element_type.63, () %tuple.269, ...), branch_computations={%region_25.26_spmd, %region_26.27_spmd} | conditional | bytes 16515152 | solution.py:101
  228.9 24.4 %ffn_back.3 = (bf16[1024,1152]{1,0:T(8,128)(2,1)}, bf16[1024,1152]{1,0:T(8,128)(2,1)}, bf16[1024,1536]{1,0:T(8,128)(2,1)}) custom-call(s32[2]{0:T(128)S(1)} %get-tuple-element.646.scal, bf16[256,1536]{1,0:T(8,128)(2,1)} %get-tuple-element.666.refs_0_, bf16[256,1536]{1,0:T(8,128)(2,1)} %get-tuple-element.667.refs_1_, ...), custom_call_target="tpu_custom_call" | custom-call | tf_op jit(solution)/shard_map/cond/branch_1_fun/ffn_back/pallas_call | solution.py:315
  253.4 24.9 %ffn_back.2 = (bf16[1024,1152]{1,0:T(8,128)(2,1)}, bf16[1024,1152]{1,0:T(8,128)(2,1)}, bf16[1024,1536]{1,0:T(8,128)(2,1)}) custom-call(s32[2]{0:T(128)S(1)} %get-tuple-element.646.scal, bf16[256,1536]{1,0:T(8,128)(2,1)} %get-tuple-element.647.refs_0_, bf16[256,1536]{1,0:T(8,128)(2,1)} %get-tuple-element.648.refs_1_, ...), custom_call_target="tpu_custom_call" | custom-call | tf_op jit(solution)/shard_map/cond/branch_1_fun/ffn_back/pallas_call | solution.py:315
  280.7 24.3 %conditional.34 = (bf16[1024,1536]{1,0:T(8,128)(2,1)}, bf16[1024,1536]{1,0:T(8,128)(2,1)}, f32[256,1536]{1,0:T(8,128)}, bf16[256,1536]{1,0:T(8,128)(2,1)}, bf16[256,1536]{1,0:T(8,128)(2,1)}) conditional(s32[]{:T(128)} %convert_element_type.63, () %tuple.276, (s32[2]{0:T(128)S(1)}, bf16[1024,1152]{1,0:T(8,128)(2,1)}, bf16[384,1152]{1,0:T(8,128)(2,1)}, ...), branch_computations={%region_27.28_spmd, %region_28.31_spmd} | conditional | flops 1 | bytes 15728877 | solution.py:101
  282.3 18.3 %conditional.1 = (bf16[1024,1536]{1,0:T(8,128)(2,1)}, bf16[1024,1536]{1,0:T(8,128)(2,1)}) conditional(s32[]{:T(128)} %convert_element_type.16, () %tuple.136, (s32[2]{0:T(128)S(1)}, bf16[1024,1152]{1,0:T(8,128)(2,1)}, bf16[384,1152]{1,0:T(8,128)(2,1)}, bf16[384,1152]{1,0:T(8,128)(2,1)}, bf16[384,1152]{1,0:T(8,128)(2,1)}, ...), branch_computations={%region_29.29_spmd, %region_30.30_spmd} | conditional | bytes 12582968 | solution.py:101
  282.3 9.0 %block_rows.3 = bf16[1024,1536]{1,0:T(8,128)(2,1)} custom-call(s32[2]{0:T(128)S(1)} %get-tuple-element.678.scal, bf16[1024,1152]{1,0:T(8,128)(2,1)} %get-tuple-element.684.left_ref, bf16[384,1152]{1,0:T(8,128)(2,1)} %get-tuple-element.680.refs_0_, bf16[384,1152]{1,0:T(8,128)(2,1)} %get-tuple-element.681.refs_1_, ...), custom_call_target="tpu_custom_call" | custom-call | tf_op jit(solution)/shard_map/cond/branch_1_fun/cond/branch_1_fun/block_rows/pallas_call | solution.py:343
  291.5 9.0 %block_rows.2 = bf16[1024,1536]{1,0:T(8,128)(2,1)} custom-call(s32[2]{0:T(128)S(1)} %get-tuple-element.678.scal, bf16[1024,1152]{1,0:T(8,128)(2,1)} %get-tuple-element.679.left_ref, bf16[384,1152]{1,0:T(8,128)(2,1)} %get-tuple-element.680.refs_0_, bf16[384,1152]{1,0:T(8,128)(2,1)} %get-tuple-element.681.refs_1_, ...), custom_call_target="tpu_custom_call" | custom-call | tf_op jit(solution)/shard_map/cond/branch_1_fun/cond/branch_1_fun/block_rows/pallas_call | solution.py:343
  300.6 4.4 spread_rest.1
  305.1 28.2 %conditional.35 = (bf16[768,1152]{1,0:T(8,128)(2,1)}, bf16[768,1152]{1,0:T(8,128)(2,1)}, bf16[384,1152]{1,0:T(8,128)(2,1)}, bf16[384,1152]{1,0:T(8,128)(2,1)}, b...) conditional(s32[]{:T(128)} %convert_element_type.63, () %tuple.240, ...), branch_computations={%region_31.32_spmd, %region_32.33_spmd} | conditional | bytes 9289812 | solution.py:101
  308.2 4.2 fold_sum.7
  312.3 3.4 part_sum.6
  315.7 12.9 %grad_up.1 = (bf16[768,1152]{1,0:T(8,128)(2,1)}, bf16[768,1152]{1,0:T(8,128)(2,1)}) custom-call(s32[2]{0:T(128)S(1)} %get-tuple-element.705.scal, bf16[1024,1536]{1,0:T(8,128)(2,1)} %get-tuple-element.706.refs_0_, bf16[1024,1536]{1,0:T(8,128)(2,1)} %get-tuple-element.707.refs_1_, bf16[1024,1152]{1,0:T(8,128)(2,1)} %get-tuple-element.708.refs_2_, ...), custom_call_target="tpu_custom_call" | custom-call | tf_op jit(solution)/shard_map/cond/branch_1_fun/grad_up/pallas_call | solution.py:385
  328.6 4.7 norm_two_back.1
  337.1 42.4 %conditional.36 = (bf16[768,1152]{1,0:T(8,128)(2,1)}, bf16[768,1152]{1,0:T(8,128)(2,1)}, bf16[1024,384]{1,0:T(8,128)(2,1)}, f32[1024,128]{1,0:T(8,128)}, bf16[10...) conditional(s32[]{:T(128)} %convert_element_type.63, () %tuple.281, ...), branch_computations={%region_33.34_spmd, %region_34.37_spmd} | conditional | flops 1 | bytes 15728965 | solution.py:101
  337.2 19.0 %conditional.2 = (bf16[256,1536]{1,0:T(8,128)(2,1)}, bf16[256,1536]{1,0:T(8,128)(2,1)}, bf16[768,1152]{1,0:T(8,128)(2,1)}, bf16[768,1152]{1,0:T(8,128)(2,1)}) conditional(s32[]{:T(128)} %convert_element_type.26, () %tuple.147, (s32[2]{0:T(128)S(1)}, bf16[1024,1536]{1,0:T(8,128)(2,1)}, bf16[1024,1536]{1,0:T(8,128)(2,1)}, ...), branch_computations={%region_35.35_spmd, %region_36.36_spmd} | conditional | bytes 6291568 | solution.py:101
  339.0 12.9 %grad_gate.1 = (bf16[768,1152]{1,0:T(8,128)(2,1)}, bf16[768,1152]{1,0:T(8,128)(2,1)}) custom-call(s32[2]{0:T(128)S(1)} %get-tuple-element.729.scal, bf16[1024,1536]{1,0:T(8,128)(2,1)} %get-tuple-element.730.refs_0_, bf16[1024,1536]{1,0:T(8,128)(2,1)} %get-tuple-element.731.refs_1_, bf16[1024,1152]{1,0:T(8,128)(2,1)} %get-tuple-element.732.refs_2_, ...), custom_call_target="tpu_custom_call" | custom-call | tf_op jit(solution)/shard_map/cond/branch_1_fun/cond/branch_1_fun/grad_gate/pallas_call | solution.py:385
  351.8 4.3 collective-permute-done.27
  358.8 20.8 %attend_back.1 = (bf16[1024,384]{1,0:T(8,128)(2,1)}, f32[1024,128]{1,0:T(8,128)}, bf16[1024,128]{1,0:T(8,128)(2,1)}, f32[8,640]{1,0:T(8,128)}, bf16[768,384]{1,0:T(8,128)(2,1)}, /*index=5*/bf16[768,384]{1,0:T(8,128)(2,1)}) custom-call(s32[2]{0:T(128)S(1)} %get-tuple-element.739.scal, bf16[1024,384]{1,0:T(8,128)(2,1)S(1)} %copy-done.9, ...), custom_call_target="tpu_custom_call" | custom-call | tf_op jit(solution)/shard_map/cond/branch_1_fun/attend_back/pallas_call | solution.py:848
  379.7 4.5 conditional.37
  379.9 4.3 fold_sum.8
  384.2 3.9 collective-permute-done.60
  390.8 49.9 %conditional.38 = (bf16[384,1152]{1,0:T(8,128)(2,1)}, bf16[384,1152]{1,0:T(8,128)(2,1)}, bf16[768,1152]{1,0:T(8,128)(2,1)}, bf16[192,1152]{1,0:T(8,128)(2,1)}, b...) conditional(s32[]{:T(128)} %convert_element_type.63, () %tuple.238, ...), branch_computations={%region_39.40_spmd, %region_40.45_spmd} | conditional | flops 16910 | bytes 29645708 | solution.py:101
  393.0 47.8 %conditional.4 = ((bf16[192,1152]{1,0:T(8,128)(2,1)}, bf16[192,1152]{1,0:T(8,128)(2,1)}, bf16[768,512]{1,0:T(8,128)(2,1)}, bf16[256,1536]{1,0:T(8,128)(2,1)}, f3...) conditional(s32[]{:T(128)} %convert_element_type.30, () %tuple.164, ...), branch_computations={%region_41.41_spmd, %region_42.44_spmd} | conditional | flops 16909 | bytes 19028512 | solution.py:101
  393.0 7.7 %project_back.1 = (bf16[1024,512]{1,0:T(8,128)(2,1)}, bf16[512,1536]{1,0:T(8,128)(2,1)}, bf16[512,1536]{1,0:T(8,128)(2,1)}) custom-call(s32[2]{0:T(128)S(1)} %get-tuple-element.799.scal, bf16[1024,384]{1,0:T(8,128)(2,1)} %get-tuple-element.805.query_ref, f32[1024,128]{1,0:T(8,128)} %get-tuple-element.806.kept_kv_ref, ...), custom_call_target="tpu_custom_call" | custom-call | tf_op jit(solution)/shard_map/cond/branch_1_fun/cond/branch_1_fun/project_back/pallas_call | solution.py:897
  400.8 5.8 %project_grad.1 = (bf16[768,512]{1,0:T(8,128)(2,1)}, bf16[768,512]{1,0:T(8,128)(2,1)}) custom-call(s32[2]{0:T(128)S(1)} %get-tuple-element.799.scal, bf16[512,1536]{1,0:T(8,128)(2,1)S(1)} %get-tuple-element.819.pair_ref, bf16[512,1536]{1,0:T(8,128)(2,1)} %get-tuple-element.820.core_ref, bf16[1024,512]{1,0:T(8,128)(2,1)} %get-tuple-element.826.grads_ref), custom_call_target="tpu_custom_call" | custom-call | tf_op jit(solution)/shard_map/cond/branch_1_fun/cond/branch_1_fun/project_grad/pallas_call | solution.py:943
  409.0 31.7 %conditional.3 = (bf16[192,1152]{1,0:T(8,128)(2,1)}, bf16[192,1152]{1,0:T(8,128)(2,1)}, bf16[768,512]{1,0:T(8,128)(2,1)}, bf16[256,1536]{1,0:T(8,128)(2,1)}, f32...) conditional(s32[]{:T(128)} %convert_element_type.27, () %tuple.160, ...), branch_computations={%region_43.42_spmd, %region_44.43_spmd} | conditional | flops 16908 | bytes 12736834 | solution.py:101
  415.7 4.2 gain_rows.1
  420.8 3.3 fold_sum.9
  429.3 4.3 norm_one_back.1
  433.6 7.2 %collective-permute-done.35 = bf16[768,512]{1,0:T(8,128)(2,1)} collective-permute-done((bf16[768,512]{1,0:T(8,128)(2,1)}, bf16[768,512]{1,0:T(8,128)(2,1)}, u32[]{:S(2)}, u32[]{:S(2)}) %collective-permute-start.35) | collective-permute-done | bytes 786464 | tf_op jit(solution)/shard_map/cond/branch_1_fun/cond/branch_1_fun/cond/branch_1_fun/swap_dp_2/ppermute | solution.py:122
  440.8 4.3 fold_sum.12
  450.6 33.8 %conditional.39 = (bf16[192,896]{1,0:T(8,128)(2,1)}, bf16[192,1152]{1,0:T(8,128)(2,1)S(1)}, bf16[192,1152]{1,0:T(8,128)(2,1)S(1)}, bf16[256,1536]{1,0:T(8,128)(2...) conditional(s32[]{:T(128)} %convert_element_type.63, () %tuple.237, (s32[2]{0:T(128)S(1)}, ...), branch_computations={%region_45.46_spmd, %region_46.49_spmd} | conditional | flops 172033 | bytes 16761205 | solution.py:101
  453.9 23.9 %conditional.5 = (bf16[192,896]{1,0:T(8,128)(2,1)S(1)}, bf16[192,896]{1,0:T(8,128)(2,1)}, bf16[192,1152]{1,0:T(8,128)(2,1)}, bf16[192,1152]{1,0:T(8,128)(2,1)}) conditional(s32[]{:T(128)} %convert_element_type.31, () %tuple.173, (s32[2]{0:T(128)S(1)}, bf16[768,512]{1,0:T(8,128)(2,1)}, bf16[768,512]{1,0:T(8,128)(2,1)}, bf16[768,384]{1,0:T(8,128)(2,1)}, ...), branch_computations={%region_47.47_spmd, %region_48.48_spmd} | conditional | bytes 5505124 | solution.py:101
  453.9 3.4 fold_both.1
  458.8 3.3 fold_sum.10
  462.1 12.4 %collective-permute-done.31.arrived_ref = bf16[384,896]{1,0:T(8,128)(2,1)S(1)} collective-permute-done((bf16[384,896]{1,0:T(8,128)(2,1)}, bf16[384,896]{1,0:T(8,128)(2,1)S(1)}, u32[]{:S(2)}, u32[]{:S(2)}) %collective-permute-start.31) | collective-permute-done | bytes 688160 | tf_op jit(solution)/shard_map/cond/branch_1_fun/cond/branch_1_fun/swap_dp_1/ppermute | solution.py:122
  493.7 12.9 %collective-permute-done.64.theirs_ref = bf16[192,1152]{1,0:T(8,128)(2,1)S(1)} collective-permute-done((bf16[192,1152]{1,0:T(8,128)(2,1)S(1)}, bf16[192,1152]{1,0:T(8,128)(2,1)S(1)}, u32[]{:S(2)}, u32[]{:S(2)}) %collective-permute-start.64) | collective-permute-done | bytes 442400 | tf_op jit(solution)/shard_map/swap_dp_2/ppermute | solution.py:122
  (269 shorter events, 163.8 us)
Async XLA Ops:
  2.5 14.1 %collective-permute-start.39 = (bf16[192,512]{1,0:T(8,128)(2,1)S(1)}, bf16[192,512]{1,0:T(8,128)(2,1)S(1)}, u32[]{:S(2)}, u32[]{:S(2)}) collective-permute-start(bf16[192,512]{1,0:T(8,128)(2,1)S(1)} %pad_maximum_fusion.6), channel_id=1, source_target_pairs={{0,16},{4,20},{8,24},{12,28},{16,0},{20,4},{24,8},{28,12},{1,17},{... | collective-permute-start | bytes 589832 | tf_op jit(solution)/shard_map/swap_dp_4/ppermute | solution.py:122
  6.6 10.0 %collective-permute-start.40 = (bf16[192,512]{1,0:T(8,128)(2,1)S(1)}, bf16[192,512]{1,0:T(8,128)(2,1)S(1)}, u32[]{:S(2)}, u32[]{:S(2)}) collective-permute-start(bf16[192,512]{1,0:T(8,128)(2,1)S(1)} %pad_maximum_fusion.6), channel_id=1, source_target_pairs={{0,8},{4,12},{8,0},{12,4},{16,24},{20,28},{24,16},{28,20},{1,9},{5... | collective-permute-start | bytes 589832 | tf_op jit(solution)/shard_map/swap_dp_2/ppermute | solution.py:122
  8.2 8.5 %collective-permute-start.41 = (bf16[192,512]{1,0:T(8,128)(2,1)S(1)}, bf16[192,512]{1,0:T(8,128)(2,1)S(1)}, u32[]{:S(2)}, u32[]{:S(2)}) collective-permute-start(bf16[192,512]{1,0:T(8,128)(2,1)S(1)} %pad_maximum_fusion.6), channel_id=1, source_target_pairs={{0,4},{4,0},{8,12},{12,8},{16,20},{20,16},{24,28},{28,24},{1,5},{5... | collective-permute-start | bytes 589832 | tf_op jit(solution)/shard_map/swap_dp_1/ppermute | solution.py:122
  12.1 21.1 %collective-permute-start.44 = (bf16[256,1536]{1,0:T(8,128)(2,1)S(1)}, bf16[256,1536]{1,0:T(8,128)(2,1)}, u32[]{:S(2)}, u32[]{:S(2)}) collective-permute-start(bf16[256,1536]{1,0:T(8,128)(2,1)S(1)} %fusion.2), channel_id=1, source_target_pairs={{0,2},{1,3},{2,0},{3,1},{4,6},{5,7},{6,4},{7,5},{8,10},{9,11},{10,... | collective-permute-start | bytes 2359304 | tf_op jit(solution)/shard_map/swap_tensor_2/ppermute | solution.py:122
  16.2 18.5 %collective-permute-start.45 = (bf16[192,1152]{1,0:T(8,128)(2,1)}, bf16[192,1152]{1,0:T(8,128)(2,1)}, u32[]{:S(2)}, u32[]{:S(2)}) collective-permute-start(bf16[192,1152]{1,0:T(8,128)(2,1)} %get-tuple-element.1115), channel_id=1, source_target_pairs={{0,8},{4,12},{8,0},{12,4},{16,24},{20,28},{24,16},{28,20},{1,9},{5... | collective-permute-start | bytes 1327112 | tf_op jit(solution)/shard_map/swap_dp_2/ppermute | solution.py:122
  16.7 18.0 %collective-permute-start.43 = (bf16[192,512]{1,0:T(8,128)(2,1)S(1)}, bf16[192,512]{1,0:T(8,128)(2,1)}, u32[]{:S(2)}, u32[]{:S(2)}) collective-permute-start(bf16[192,512]{1,0:T(8,128)(2,1)S(1)} %collective-permute-done.39), channel_id=1, source_target_pairs={{0,8},{4,12},{8,0},{12,4},{16,24},{20,28},{24,16},{28,20},{1,9},{5... | collective-permute-start | bytes 589832 | tf_op jit(solution)/shard_map/swap_dp_2/ppermute | solution.py:122
  19.1 15.5 %collective-permute-start.42 = (bf16[384,512]{1,0:T(8,128)(2,1)}, bf16[384,512]{1,0:T(8,128)(2,1)S(1)}, u32[]{:S(2)}, u32[]{:S(2)}) collective-permute-start(bf16[384,512]{1,0:T(8,128)(2,1)} %pad_maximum_fusion.4), channel_id=1, source_target_pairs={{0,4},{4,0},{8,12},{12,8},{16,20},{20,16},{24,28},{28,24},{1,5},{5... | collective-permute-start | bytes 1179656 | tf_op jit(solution)/shard_map/swap_dp_1/ppermute | solution.py:122
  20.2 12.3 %collective-permute-start.46 = (bf16[192,384]{1,0:T(8,128)(2,1)S(1)}, bf16[192,384]{1,0:T(8,128)(2,1)S(1)}, u32[]{:S(2)}, u32[]{:S(2)}) collective-permute-start(bf16[192,384]{1,0:T(8,128)(2,1)S(1)} %bitcast.25), channel_id=1, source_target_pairs={{0,16},{4,20},{8,24},{12,28},{16,0},{20,4},{24,8},{28,12},{1,17},{... | collective-permute-start | bytes 442376 | tf_op jit(solution)/shard_map/swap_dp_4/ppermute | solution.py:122
  34.7 10.3 %collective-permute-start.1 = (bf16[512,1536]{1,0:T(8,128)(2,1)S(1)}, bf16[512,1536]{1,0:T(8,128)(2,1)}, u32[]{:S(2)}, u32[]{:S(2)}) collective-permute-start(bf16[512,1536]{1,0:T(8,128)(2,1)S(1)} %get-tuple-element.529), channel_id=1, source_target_pairs={{0,1},{1,0},{2,3},{3,2},{4,5},{5,4},{6,7},{7,6},{8,9},{9,8},{10,11... | collective-permute-start | bytes 4718600 | tf_op jit(solution)/shard_map/cond/branch_1_fun/swap_tensor_1/ppermute | solution.py:122
  34.7 10.3 %collective-permute-start.2 = (bf16[384,384]{1,0:T(8,128)(2,1)}, bf16[384,384]{1,0:T(8,128)(2,1)}, u32[]{:S(2)}, u32[]{:S(2)}) collective-permute-start(bf16[384,384]{1,0:T(8,128)(2,1)} %get-tuple-element.530), channel_id=1, source_target_pairs={{0,8},{4,12},{8,0},{12,4},{16,24},{20,28},{24,16},{28,20},{1,9},{5... | collective-permute-start | bytes 884744 | tf_op jit(solution)/shard_map/cond/branch_1_fun/swap_dp_2/ppermute | solution.py:122
  37.1 7.3 %collective-permute-start = (bf16[192,512]{1,0:T(8,128)(2,1)}, bf16[192,512]{1,0:T(8,128)(2,1)}, u32[]{:S(2)}, u32[]{:S(2)}) collective-permute-start(bf16[192,512]{1,0:T(8,128)(2,1)} %get-tuple-element.528), channel_id=1, source_target_pairs={{0,4},{4,0},{8,12},{12,8},{16,20},{20,16},{24,28},{28,24},{1,5},{5... | collective-permute-start | bytes 589832 | tf_op jit(solution)/shard_map/cond/branch_1_fun/swap_dp_1/ppermute | solution.py:122
  46.1 38.0 %collective-permute-start.49 = (bf16[384,1152]{1,0:T(8,128)(2,1)}, bf16[384,1152]{1,0:T(8,128)(2,1)}, u32[]{:S(2)}, u32[]{:S(2)}) collective-permute-start(bf16[384,1152]{1,0:T(8,128)(2,1)} %get-tuple-element.1146), channel_id=1, source_target_pairs={{0,8},{4,12},{8,0},{12,4},{16,24},{20,28},{24,16},{28,20},{1,9},{5... | collective-permute-start | bytes 2654216 | tf_op jit(solution)/shard_map/swap_dp_2/ppermute | solution.py:122
  48.0 26.6 %collective-permute-start.47 = (bf16[256,1536]{1,0:T(8,128)(2,1)}, bf16[256,1536]{1,0:T(8,128)(2,1)}, u32[]{:S(2)}, u32[]{:S(2)}) collective-permute-start(bf16[256,1536]{1,0:T(8,128)(2,1)} %param.71), channel_id=1, source_target_pairs={{0,2},{1,3},{2,0},{3,1},{4,6},{5,7},{6,4},{7,5},{8,10},{9,11},{10,... | collective-permute-start | bytes 2359304 | tf_op jit(solution)/shard_map/swap_tensor_2/ppermute | solution.py:122
  48.8 20.6 %collective-permute-start.48 = (bf16[768,384]{1,0:T(8,128)(2,1)S(1)}, bf16[768,384]{1,0:T(8,128)(2,1)S(1)}, u32[]{:S(2)}, u32[]{:S(2)}) collective-permute-start(bf16[768,384]{1,0:T(8,128)(2,1)S(1)} %pad_maximum_fusion.2.refs_0_.refs_2_.refs_4_.refs_6_), channel_id=1, source_target_pairs={{0,4},{4,0},{8,12},{12,8},{16,20},{20,16},{24,28},{28,24},{1,5},{5... | collective-permute-start | bytes 1769480 | tf_op jit(solution)/shard_map/swap_dp_1/ppermute | solution.py:122
  51.1 65.8 %collective-permute-start.51 = (bf16[384,1152]{1,0:T(8,128)(2,1)}, bf16[384,1152]{1,0:T(8,128)(2,1)}, u32[]{:S(2)}, u32[]{:S(2)}) collective-permute-start(bf16[384,1152]{1,0:T(8,128)(2,1)} %get-tuple-element.1150), channel_id=1, source_target_pairs={{0,16},{4,20},{8,24},{12,28},{16,0},{20,4},{24,8},{28,12},{1,17},{... | collective-permute-start | bytes 2654216 | tf_op jit(solution)/shard_map/swap_dp_4/ppermute | solution.py:122
  61.2 8.2 %collective-permute-start.4 = (bf16[256,1536]{1,0:T(8,128)(2,1)}, bf16[256,1536]{1,0:T(8,128)(2,1)}, u32[]{:S(2)}, u32[]{:S(2)}) collective-permute-start(bf16[256,1536]{1,0:T(8,128)(2,1)} %get-tuple-element.552), channel_id=1, source_target_pairs={{0,1},{1,0},{2,3},{3,2},{4,5},{5,4},{6,7},{7,6},{8,9},{9,8},{10,11... | collective-permute-start | bytes 2359304 | tf_op jit(solution)/shard_map/cond/branch_1_fun/swap_tensor_1/ppermute | solution.py:122
  84.1 3.8 collective-permute-start.5
  87.9 59.9 %collective-permute-start.52 = (bf16[768,1152]{1,0:T(8,128)(2,1)}, bf16[768,1152]{1,0:T(8,128)(2,1)S(1)}, u32[]{:S(2)}, u32[]{:S(2)}) collective-permute-start(bf16[768,1152]{1,0:T(8,128)(2,1)} %get-tuple-element.1156), channel_id=1, source_target_pairs={{0,4},{4,0},{8,12},{12,8},{16,20},{20,16},{24,28},{28,24},{1,5},{5... | collective-permute-start | bytes 5308424 | tf_op jit(solution)/shard_map/swap_dp_1/ppermute | solution.py:122
  89.1 35.2 %collective-permute-start.50 = (bf16[256,1536]{1,0:T(8,128)(2,1)}, bf16[256,1536]{1,0:T(8,128)(2,1)}, u32[]{:S(2)}, u32[]{:S(2)}) collective-permute-start(bf16[256,1536]{1,0:T(8,128)(2,1)} %param.71), channel_id=1, source_target_pairs={{0,8},{4,12},{8,0},{12,4},{16,24},{20,28},{24,16},{28,20},{1,9},{5... | collective-permute-start | bytes 2359304 | tf_op jit(solution)/shard_map/swap_dp_2/ppermute | solution.py:122
  89.1 58.5 %collective-permute-start.54 = (bf16[384,1152]{1,0:T(8,128)(2,1)}, bf16[384,1152]{1,0:T(8,128)(2,1)}, u32[]{:S(2)}, u32[]{:S(2)}) collective-permute-start(bf16[384,1152]{1,0:T(8,128)(2,1)} %get-tuple-element.1160), channel_id=1, source_target_pairs={{0,16},{4,20},{8,24},{12,28},{16,0},{20,4},{24,8},{28,12},{1,17},{... | collective-permute-start | bytes 2654216 | tf_op jit(solution)/shard_map/swap_dp_4/ppermute | solution.py:122
  93.5 19.1 %collective-permute-start.6 = (bf16[256,1536]{1,0:T(8,128)(2,1)}, bf16[256,1536]{1,0:T(8,128)(2,1)}, u32[]{:S(2)}, u32[]{:S(2)}) collective-permute-start(bf16[256,1536]{1,0:T(8,128)(2,1)} %part_sum.4), channel_id=1, source_target_pairs={{0,2},{1,3},{2,0},{3,1},{4,6},{5,7},{6,4},{7,5},{8,10},{9,11},{10,... | collective-permute-start | bytes 2359304 | tf_op jit(solution)/shard_map/cond/branch_1_fun/swap_tensor_2/ppermute | solution.py:122
  124.4 23.4 %collective-permute-start.53 = (bf16[384,1152]{1,0:T(8,128)(2,1)}, bf16[384,1152]{1,0:T(8,128)(2,1)}, u32[]{:S(2)}, u32[]{:S(2)}) collective-permute-start(bf16[384,1152]{1,0:T(8,128)(2,1)} %collective-permute-done.51), channel_id=1, source_target_pairs={{0,4},{4,0},{8,12},{12,8},{16,20},{20,16},{24,28},{28,24},{1,5},{5... | collective-permute-start | bytes 2654216 | tf_op jit(solution)/shard_map/swap_dp_1/ppermute | solution.py:122
  125.1 18.6 %collective-permute-start.7 = (bf16[256,1536]{1,0:T(8,128)(2,1)}, bf16[256,1536]{1,0:T(8,128)(2,1)}, u32[]{:S(2)}, u32[]{:S(2)}) collective-permute-start(bf16[256,1536]{1,0:T(8,128)(2,1)} %get-tuple-element.567), channel_id=1, source_target_pairs={{0,2},{1,3},{2,0},{3,1},{4,6},{5,7},{6,4},{7,5},{8,10},{9,11},{10,... | collective-permute-start | bytes 2359304 | tf_op jit(solution)/shard_map/cond/branch_1_fun/swap_tensor_2/ppermute | solution.py:122
  126.5 21.1 %collective-permute-start.8 = (bf16[256,1536]{1,0:T(8,128)(2,1)}, bf16[256,1536]{1,0:T(8,128)(2,1)}, u32[]{:S(2)}, u32[]{:S(2)}) collective-permute-start(bf16[256,1536]{1,0:T(8,128)(2,1)} %get-tuple-element.567), channel_id=1, source_target_pairs={{0,8},{4,12},{8,0},{12,4},{16,24},{20,28},{24,16},{28,20},{1,9},{5... | collective-permute-start | bytes 2359304 | tf_op jit(solution)/shard_map/cond/branch_1_fun/swap_dp_2/ppermute | solution.py:122
  147.8 21.8 %collective-permute-start.55 = (bf16[384,1152]{1,0:T(8,128)(2,1)}, bf16[384,1152]{1,0:T(8,128)(2,1)}, u32[]{:S(2)}, u32[]{:S(2)}) collective-permute-start(bf16[384,1152]{1,0:T(8,128)(2,1)} %collective-permute-done.54), channel_id=1, source_target_pairs={{0,4},{4,0},{8,12},{12,8},{16,20},{20,16},{24,28},{28,24},{1,5},{5... | collective-permute-start | bytes 2654216 | tf_op jit(solution)/shard_map/swap_dp_1/ppermute | solution.py:122
  151.3 10.4 %collective-permute-start.12 = (bf16[128,1536]{1,0:T(8,128)(2,1)}, bf16[128,1536]{1,0:T(8,128)(2,1)}, u32[]{:S(2)}, u32[]{:S(2)}) collective-permute-start(bf16[128,1536]{1,0:T(8,128)(2,1)} %get-tuple-element.583), channel_id=1, source_target_pairs={{0,2},{1,3},{2,0},{3,1},{4,6},{5,7},{6,4},{7,5},{8,10},{9,11},{10,... | collective-permute-start | bytes 1179656 | tf_op jit(solution)/shard_map/cond/branch_1_fun/swap_tensor_2/ppermute | solution.py:122
  153.1 10.1 %collective-permute-start.13 = (bf16[128,1536]{1,0:T(8,128)(2,1)}, bf16[128,1536]{1,0:T(8,128)(2,1)}, u32[]{:S(2)}, u32[]{:S(2)}) collective-permute-start(bf16[128,1536]{1,0:T(8,128)(2,1)} %get-tuple-element.584), channel_id=1, source_target_pairs={{0,8},{4,12},{8,0},{12,4},{16,24},{20,28},{24,16},{28,20},{1,9},{5... | collective-permute-start | bytes 1179656 | tf_op jit(solution)/shard_map/cond/branch_1_fun/swap_dp_2/ppermute | solution.py:122
  163.2 43.5 %collective-permute-start.56 = (bf16[384,1152]{1,0:T(8,128)(2,1)}, bf16[384,1152]{1,0:T(8,128)(2,1)}, u32[]{:S(2)}, u32[]{:S(2)}) collective-permute-start(bf16[384,1152]{1,0:T(8,128)(2,1)} %get-tuple-element.1175), channel_id=1, source_target_pairs={{0,16},{4,20},{8,24},{12,28},{16,0},{20,4},{24,8},{28,12},{1,17},{... | collective-permute-start | bytes 2654216 | tf_op jit(solution)/shard_map/swap_dp_4/ppermute | solution.py:122
  169.6 20.9 %collective-permute-start.16 = (bf16[384,1152]{1,0:T(8,128)(2,1)}, bf16[384,1152]{1,0:T(8,128)(2,1)}, u32[]{:S(2)}, u32[]{:S(2)}) collective-permute-start(bf16[384,1152]{1,0:T(8,128)(2,1)} %get-tuple-element.608), channel_id=1, source_target_pairs={{0,4},{4,0},{8,12},{12,8},{16,20},{20,16},{24,28},{28,24},{1,5},{5... | collective-permute-start | bytes 2654216 | tf_op jit(solution)/shard_map/cond/branch_1_fun/swap_dp_1/ppermute | solution.py:122
  170.2 18.2 %collective-permute-start.17 = (bf16[256,1536]{1,0:T(8,128)(2,1)}, bf16[256,1536]{1,0:T(8,128)(2,1)}, u32[]{:S(2)}, u32[]{:S(2)}) collective-permute-start(bf16[256,1536]{1,0:T(8,128)(2,1)} %get-tuple-element.609), channel_id=1, source_target_pairs={{0,2},{1,3},{2,0},{3,1},{4,6},{5,7},{6,4},{7,5},{8,10},{9,11},{10,... | collective-permute-start | bytes 2359304 | tf_op jit(solution)/shard_map/cond/branch_1_fun/swap_tensor_2/ppermute | solution.py:122
  172.0 16.4 %collective-permute-start.18 = (bf16[256,1536]{1,0:T(8,128)(2,1)}, bf16[256,1536]{1,0:T(8,128)(2,1)}, u32[]{:S(2)}, u32[]{:S(2)}) collective-permute-start(bf16[256,1536]{1,0:T(8,128)(2,1)} %get-tuple-element.610), channel_id=1, source_target_pairs={{0,1},{1,0},{2,3},{3,2},{4,5},{5,4},{6,7},{7,6},{8,9},{9,8},{10,11... | collective-permute-start | bytes 2359304 | tf_op jit(solution)/shard_map/cond/branch_1_fun/swap_tensor_1/ppermute | solution.py:122
  190.5 16.2 %collective-permute-start.19 = (bf16[256,1536]{1,0:T(8,128)(2,1)}, bf16[256,1536]{1,0:T(8,128)(2,1)}, u32[]{:S(2)}, u32[]{:S(2)}) collective-permute-start(bf16[256,1536]{1,0:T(8,128)(2,1)} %get-tuple-element.631), channel_id=1, source_target_pairs={{0,1},{1,0},{2,3},{3,2},{4,5},{5,4},{6,7},{7,6},{8,9},{9,8},{10,11... | collective-permute-start | bytes 2359304 | tf_op jit(solution)/shard_map/cond/branch_1_fun/swap_tensor_1/ppermute | solution.py:122
  190.5 16.2 %collective-permute-start.20 = (bf16[256,1536]{1,0:T(8,128)(2,1)}, bf16[256,1536]{1,0:T(8,128)(2,1)}, u32[]{:S(2)}, u32[]{:S(2)}) collective-permute-start(bf16[256,1536]{1,0:T(8,128)(2,1)} %get-tuple-element.632), channel_id=1, source_target_pairs={{0,1},{1,0},{2,3},{3,2},{4,5},{5,4},{6,7},{7,6},{8,9},{9,8},{10,11... | collective-permute-start | bytes 2359304 | tf_op jit(solution)/shard_map/cond/branch_1_fun/swap_tensor_1/ppermute | solution.py:122
  206.7 21.9 %collective-permute-start.57 = (bf16[384,1152]{1,0:T(8,128)(2,1)}, bf16[384,1152]{1,0:T(8,128)(2,1)}, u32[]{:S(2)}, u32[]{:S(2)}) collective-permute-start(bf16[384,1152]{1,0:T(8,128)(2,1)} %collective-permute-done.56), channel_id=1, source_target_pairs={{0,4},{4,0},{8,12},{12,8},{16,20},{20,16},{24,28},{28,24},{1,5},{5... | collective-permute-start | bytes 2654216 | tf_op jit(solution)/shard_map/swap_dp_1/ppermute | solution.py:122
  228.6 76.4 %collective-permute-start.58 = (bf16[768,1152]{1,0:T(8,128)(2,1)}, bf16[768,1152]{1,0:T(8,128)(2,1)}, u32[]{:S(2)}, u32[]{:S(2)}) collective-permute-start(bf16[768,1152]{1,0:T(8,128)(2,1)} %get-tuple-element.1217), channel_id=1, source_target_pairs={{0,4},{4,0},{8,12},{12,8},{16,20},{20,16},{24,28},{28,24},{1,5},{5... | collective-permute-start | bytes 5308424 | tf_op jit(solution)/shard_map/swap_dp_1/ppermute | solution.py:122
  253.3 25.0 %collective-permute-start.21 = (bf16[1024,1536]{1,0:T(8,128)(2,1)}, bf16[1024,1536]{1,0:T(8,128)(2,1)}, u32[]{:S(2)}, u32[]{:S(2)}) collective-permute-start(bf16[1024,1536]{1,0:T(8,128)(2,1)} %get-tuple-element.675), channel_id=1, source_target_pairs={{0,1},{1,0},{2,3},{3,2},{4,5},{5,4},{6,7},{7,6},{8,9},{9,8},{10,11... | collective-permute-start | bytes 9437192 | tf_op jit(solution)/shard_map/cond/branch_1_fun/swap_tensor_1/ppermute | solution.py:122
  280.7 19.9 %collective-permute-start.23 = (bf16[128,1536]{1,0:T(8,128)(2,1)}, bf16[128,1536]{1,0:T(8,128)(2,1)}, u32[]{:S(2)}, u32[]{:S(2)}) collective-permute-start(bf16[128,1536]{1,0:T(8,128)(2,1)} %get-tuple-element.694), channel_id=1, source_target_pairs={{0,2},{1,3},{2,0},{3,1},{4,6},{5,7},{6,4},{7,5},{8,10},{9,11},{10,... | collective-permute-start | bytes 1179656 | tf_op jit(solution)/shard_map/cond/branch_1_fun/swap_tensor_2/ppermute | solution.py:122
  282.3 18.4 %collective-permute-start.24 = (bf16[128,1536]{1,0:T(8,128)(2,1)}, bf16[128,1536]{1,0:T(8,128)(2,1)}, u32[]{:S(2)}, u32[]{:S(2)}) collective-permute-start(bf16[128,1536]{1,0:T(8,128)(2,1)} %get-tuple-element.695), channel_id=1, source_target_pairs={{0,8},{4,12},{8,0},{12,4},{16,24},{20,28},{24,16},{28,20},{1,9},{5... | collective-permute-start | bytes 1179656 | tf_op jit(solution)/shard_map/cond/branch_1_fun/swap_dp_2/ppermute | solution.py:122
  291.3 9.3 %collective-permute-start.22 = (bf16[1024,1536]{1,0:T(8,128)(2,1)}, bf16[1024,1536]{1,0:T(8,128)(2,1)}, u32[]{:S(2)}, u32[]{:S(2)}) collective-permute-start(bf16[1024,1536]{1,0:T(8,128)(2,1)} %block_rows.3), channel_id=1, source_target_pairs={{0,1},{1,0},{2,3},{3,2},{4,5},{5,4},{6,7},{7,6},{8,9},{9,8},{10,11... | collective-permute-start | bytes 9437192 | tf_op jit(solution)/shard_map/cond/branch_1_fun/cond/branch_1_fun/swap_tensor_1/ppermute | solution.py:122
  305.1 23.5 %collective-permute-start.25 = (bf16[256,1536]{1,0:T(8,128)(2,1)}, bf16[256,1536]{1,0:T(8,128)(2,1)}, u32[]{:S(2)}, u32[]{:S(2)}) collective-permute-start(bf16[256,1536]{1,0:T(8,128)(2,1)} %get-tuple-element.719), channel_id=1, source_target_pairs={{0,2},{1,3},{2,0},{3,1},{4,6},{5,7},{6,4},{7,5},{8,10},{9,11},{10,... | collective-permute-start | bytes 2359304 | tf_op jit(solution)/shard_map/cond/branch_1_fun/swap_tensor_2/ppermute | solution.py:122
  306.0 22.6 %collective-permute-start.26 = (bf16[256,1536]{1,0:T(8,128)(2,1)}, bf16[256,1536]{1,0:T(8,128)(2,1)}, u32[]{:S(2)}, u32[]{:S(2)}) collective-permute-start(bf16[256,1536]{1,0:T(8,128)(2,1)} %get-tuple-element.720), channel_id=1, source_target_pairs={{0,8},{4,12},{8,0},{12,4},{16,24},{20,28},{24,16},{28,20},{1,9},{5... | collective-permute-start | bytes 2359304 | tf_op jit(solution)/shard_map/cond/branch_1_fun/swap_dp_2/ppermute | solution.py:122
  333.3 46.3 %collective-permute-start.59 = (bf16[768,1152]{1,0:T(8,128)(2,1)}, bf16[768,1152]{1,0:T(8,128)(2,1)}, u32[]{:S(2)}, u32[]{:S(2)}) collective-permute-start(bf16[768,1152]{1,0:T(8,128)(2,1)} %get-tuple-element.1238), channel_id=1, source_target_pairs={{0,4},{4,0},{8,12},{12,8},{16,20},{20,16},{24,28},{28,24},{1,5},{5... | collective-permute-start | bytes 5308424 | tf_op jit(solution)/shard_map/swap_dp_1/ppermute | solution.py:122
  335.1 55.2 %collective-permute-start.61 = (bf16[512,1536]{1,0:T(8,128)(2,1)}, bf16[512,1536]{1,0:T(8,128)(2,1)}, u32[]{:S(2)}, u32[]{:S(2)}) collective-permute-start(bf16[512,1536]{1,0:T(8,128)(2,1)} %get-tuple-element.1246), channel_id=1, source_target_pairs={{0,8},{4,12},{8,0},{12,4},{16,24},{20,28},{24,16},{28,20},{1,9},{5... | collective-permute-start | bytes 4718600 | tf_op jit(solution)/shard_map/swap_dp_2/ppermute | solution.py:122
  335.2 52.9 %collective-permute-start.60 = (bf16[384,1152]{1,0:T(8,128)(2,1)}, bf16[384,1152]{1,0:T(8,128)(2,1)}, u32[]{:S(2)}, u32[]{:S(2)}) collective-permute-start(bf16[384,1152]{1,0:T(8,128)(2,1)} %get-tuple-element.1245), channel_id=1, source_target_pairs={{0,16},{4,20},{8,24},{12,28},{16,0},{20,4},{24,8},{28,12},{1,17},{... | collective-permute-start | bytes 2654216 | tf_op jit(solution)/shard_map/swap_dp_4/ppermute | solution.py:122
  337.2 19.0 %collective-permute-start.27 = (bf16[256,1536]{1,0:T(8,128)(2,1)}, bf16[256,1536]{1,0:T(8,128)(2,1)}, u32[]{:S(2)}, u32[]{:S(2)}) collective-permute-start(bf16[256,1536]{1,0:T(8,128)(2,1)} %get-tuple-element.736), channel_id=1, source_target_pairs={{0,2},{1,3},{2,0},{3,1},{4,6},{5,7},{6,4},{7,5},{8,10},{9,11},{10,... | collective-permute-start | bytes 2359304 | tf_op jit(solution)/shard_map/cond/branch_1_fun/cond/branch_1_fun/swap_tensor_2/ppermute | solution.py:122
  339.0 17.2 %collective-permute-start.28 = (bf16[256,1536]{1,0:T(8,128)(2,1)}, bf16[256,1536]{1,0:T(8,128)(2,1)}, u32[]{:S(2)}, u32[]{:S(2)}) collective-permute-start(bf16[256,1536]{1,0:T(8,128)(2,1)} %get-tuple-element.736), channel_id=1, source_target_pairs={{0,1},{1,0},{2,3},{3,2},{4,5},{5,4},{6,7},{7,6},{8,9},{9,8},{10,11... | collective-permute-start | bytes 2359304 | tf_op jit(solution)/shard_map/cond/branch_1_fun/cond/branch_1_fun/swap_tensor_1/ppermute | solution.py:122
  379.7 4.5 collective-permute-start.30
  390.3 50.4 %collective-permute-start.62 = (bf16[768,384]{1,0:T(8,128)(2,1)}, bf16[768,384]{1,0:T(8,128)(2,1)}, u32[]{:S(2)}, u32[]{:S(2)}) collective-permute-start(bf16[768,384]{1,0:T(8,128)(2,1)} %get-tuple-element.1261), channel_id=1, source_target_pairs={{0,8},{4,12},{8,0},{12,4},{16,24},{20,28},{24,16},{28,20},{1,9},{5... | collective-permute-start | bytes 1769480 | tf_op jit(solution)/shard_map/swap_dp_2/ppermute | solution.py:122
  390.8 49.9 %collective-permute-start.37 = (bf16[768,1152]{1,0:T(8,128)(2,1)}, bf16[768,1152]{1,0:T(8,128)(2,1)}, u32[]{:S(2)}, u32[]{:S(2)}) collective-permute-start(bf16[768,1152]{1,0:T(8,128)(2,1)} %get-tuple-element.868), channel_id=1, source_target_pairs={{0,4},{4,0},{8,12},{12,8},{16,20},{20,16},{24,28},{28,24},{1,5},{5... | collective-permute-start | bytes 5308424 | tf_op jit(solution)/shard_map/cond/branch_1_fun/swap_dp_1/ppermute | solution.py:122
  391.3 49.5 %collective-permute-start.38 = (bf16[384,1152]{1,0:T(8,128)(2,1)}, bf16[384,1152]{1,0:T(8,128)(2,1)}, u32[]{:S(2)}, u32[]{:S(2)}) collective-permute-start(bf16[384,1152]{1,0:T(8,128)(2,1)} %get-tuple-element.869), channel_id=1, source_target_pairs={{0,16},{4,20},{8,24},{12,28},{16,0},{20,4},{24,8},{28,12},{1,17},{... | collective-permute-start | bytes 2654216 | tf_op jit(solution)/shard_map/cond/branch_1_fun/swap_dp_4/ppermute | solution.py:122
  400.7 5.9 %collective-permute-start.36 = (bf16[512,1536]{1,0:T(8,128)(2,1)}, bf16[512,1536]{1,0:T(8,128)(2,1)}, u32[]{:S(2)}, u32[]{:S(2)}) collective-permute-start(bf16[512,1536]{1,0:T(8,128)(2,1)} %get-tuple-element.818), channel_id=1, source_target_pairs={{0,1},{1,0},{2,3},{3,2},{4,5},{5,4},{6,7},{7,6},{8,9},{9,8},{10,11... | collective-permute-start | bytes 4718600 | tf_op jit(solution)/shard_map/cond/branch_1_fun/cond/branch_1_fun/swap_tensor_1/ppermute | solution.py:122
  409.0 20.3 %collective-permute-start.34 = (bf16[256,1536]{1,0:T(8,128)(2,1)}, bf16[256,1536]{1,0:T(8,128)(2,1)}, u32[]{:S(2)}, u32[]{:S(2)}) collective-permute-start(bf16[256,1536]{1,0:T(8,128)(2,1)} %get-tuple-element.794), channel_id=1, source_target_pairs={{0,2},{1,3},{2,0},{3,1},{4,6},{5,7},{6,4},{7,5},{8,10},{9,11},{10,... | collective-permute-start | bytes 2359304 | tf_op jit(solution)/shard_map/cond/branch_1_fun/cond/branch_1_fun/cond/branch_1_fun/swap_tensor_2/ppermute | solution.py:122
  410.7 30.0 %collective-permute-start.35 = (bf16[768,512]{1,0:T(8,128)(2,1)}, bf16[768,512]{1,0:T(8,128)(2,1)}, u32[]{:S(2)}, u32[]{:S(2)}) collective-permute-start(bf16[768,512]{1,0:T(8,128)(2,1)} %get-tuple-element.797), channel_id=1, source_target_pairs={{0,8},{4,12},{8,0},{12,4},{16,24},{20,28},{24,16},{28,20},{1,9},{5... | collective-permute-start | bytes 2359304 | tf_op jit(solution)/shard_map/cond/branch_1_fun/cond/branch_1_fun/cond/branch_1_fun/swap_dp_2/ppermute | solution.py:122
  445.1 41.1 %collective-permute-start.63 = (bf16[384,1152]{1,0:T(8,128)(2,1)}, bf16[384,1152]{1,0:T(8,128)(2,1)}, u32[]{:S(2)}, u32[]{:S(2)}) collective-permute-start(bf16[384,1152]{1,0:T(8,128)(2,1)} %get-tuple-element.1281), channel_id=1, source_target_pairs={{0,16},{4,20},{8,24},{12,28},{16,0},{20,4},{24,8},{28,12},{1,17},{... | collective-permute-start | bytes 2654216 | tf_op jit(solution)/shard_map/swap_dp_4/ppermute | solution.py:122
  447.5 38.7 %all-to-all-start = ((f32[32,1,160]{2,1,0:T(1,128)}), f32[32,1,160]{2,1,0:T(1,128)S(1)}, u32[]{:S(2)}, u32[]{:S(2)}) async-start(f32[32,1,160]{2,1,0:T(1,128)} %all_to_all.8), calls=%async_computation | async-start | bytes 65536 | tf_op jit(solution)/shard_map/all_to_all | solution.py:1390
  450.6 27.2 %collective-permute-start.32 = (bf16[256,1536]{1,0:T(8,128)(2,1)}, bf16[256,1536]{1,0:T(8,128)(2,1)}, u32[]{:S(2)}, u32[]{:S(2)}) collective-permute-start(bf16[256,1536]{1,0:T(8,128)(2,1)} %get-tuple-element.904), channel_id=1, source_target_pairs={{0,2},{1,3},{2,0},{3,1},{4,6},{5,7},{6,4},{7,5},{8,10},{9,11},{10,... | collective-permute-start | bytes 2359304 | tf_op jit(solution)/shard_map/cond/branch_1_fun/swap_tensor_2/ppermute | solution.py:122
  452.5 25.4 %collective-permute-start.33 = (bf16[192,1152]{1,0:T(8,128)(2,1)}, bf16[192,1152]{1,0:T(8,128)(2,1)S(1)}, u32[]{:S(2)}, u32[]{:S(2)}) collective-permute-start(bf16[192,1152]{1,0:T(8,128)(2,1)} %get-tuple-element.905), channel_id=1, source_target_pairs={{0,8},{4,12},{8,0},{12,4},{16,24},{20,28},{24,16},{28,20},{1,9},{5... | collective-permute-start | bytes 1327112 | tf_op jit(solution)/shard_map/cond/branch_1_fun/swap_dp_2/ppermute | solution.py:122
  457.4 17.2 %collective-permute-start.31 = (bf16[384,896]{1,0:T(8,128)(2,1)}, bf16[384,896]{1,0:T(8,128)(2,1)S(1)}, u32[]{:S(2)}, u32[]{:S(2)}) collective-permute-start(bf16[384,896]{1,0:T(8,128)(2,1)} %get-tuple-element.889), channel_id=1, source_target_pairs={{0,4},{4,0},{8,12},{12,8},{16,20},{20,16},{24,28},{28,24},{1,5},{5... | collective-permute-start | bytes 2064392 | tf_op jit(solution)/shard_map/cond/branch_1_fun/cond/branch_1_fun/swap_dp_1/ppermute | solution.py:122
  486.2 20.4 %collective-permute-start.64 = (bf16[192,1152]{1,0:T(8,128)(2,1)S(1)}, bf16[192,1152]{1,0:T(8,128)(2,1)S(1)}, u32[]{:S(2)}, u32[]{:S(2)}) collective-permute-start(bf16[192,1152]{1,0:T(8,128)(2,1)S(1)} %get-tuple-element.1291), channel_id=1, source_target_pairs={{0,8},{4,12},{8,0},{12,4},{16,24},{20,28},{24,16},{28,20},{1,9},{5... | collective-permute-start | bytes 1327112 | tf_op jit(solution)/shard_map/swap_dp_2/ppermute | solution.py:122
  486.8 23.1 %collective-permute-start.65 = (bf16[192,896]{1,0:T(8,128)(2,1)}, bf16[192,896]{1,0:T(8,128)(2,1)S(1)}, u32[]{:S(2)}, u32[]{:S(2)}) collective-permute-start(bf16[192,896]{1,0:T(8,128)(2,1)} %get-tuple-element.1293), channel_id=1, source_target_pairs={{0,16},{4,20},{8,24},{12,28},{16,0},{20,4},{24,8},{28,12},{1,17},{... | collective-permute-start | bytes 1032200 | tf_op jit(solution)/shard_map/swap_dp_4/ppermute | solution.py:122
  492.0 22.9 %collective-permute-start.66 = (bf16[192,1152]{1,0:T(8,128)(2,1)}, bf16[192,1152]{1,0:T(8,128)(2,1)S(1)}, u32[]{:S(2)}, u32[]{:S(2)}) collective-permute-start(bf16[192,1152]{1,0:T(8,128)(2,1)} %get-tuple-element.1290), channel_id=1, source_target_pairs={{0,8},{4,12},{8,0},{12,4},{16,24},{20,28},{24,16},{28,20},{1,9},{5... | collective-permute-start | bytes 1327112 | tf_op jit(solution)/shard_map/swap_dp_2/ppermute | solution.py:122
  511.6 3.3 collective-permute-start.67
  511.7 3.9 collective-permute-start.68
  512.7 3.3 collective-permute-start.69
  (41 other events, 340.7 us)
